TPU v7x, 32 devices: a whole 2x2x4 slice. The times are simulated.
32 devices in a mesh: items: 8 (over y, x, core), rows: 4 (over z).
Axes of the slice: x: 2, y: 2, z: 4, core: 2. Of those that a mesh axis runs over, the one named last changes fastest.
Arguments:
- latents: bfloat16 [8, 576, 1536], P('items', 'rows'), may hold values from -6 to 6
- clip_tokens: bfloat16 [8, 80, 1280], P('items', 'rows'), may hold values from -6 to 6
- time_embed: bfloat16 [8, 64], P('items'), may hold values from -6 to 6
- bucket_ids: int32 [8], P('items'), may hold values from 0 to 2, as said below
- heights: int32 [8], P('items'), may hold values from 9 to 32, as said below
- widths: int32 [8], P('items'), may hold values from 10 to 36, as said below
- text_mask: int32 [8, 80], P('items'), may hold values 0 or 1
- conv_weight: bfloat16 [9, 1536], P(None, ('items', 'rows')), may hold values from -2 to 2
- conv_bias: bfloat16 [1536], P(('items', 'rows')), may hold values from -3 to 3
- in_weight: bfloat16 [1536, 6144], P(('items', 'rows')), may hold values from -0.15625 to 0.15625
- in_bias: bfloat16 [6144], P(('items', 'rows')), may hold values from -3 to 3
- grn_gain: bfloat16 [6144], P(('items', 'rows')), may hold values from -3 to 3
- grn_bias: bfloat16 [6144], P(('items', 'rows')), may hold values from -2 to 2
- out_weight: bfloat16 [6144, 1536], P(('items', 'rows')), may hold values from -0.078125 to 0.078125
- out_bias: bfloat16 [1536], P(('items', 'rows')), may hold values from -2 to 2
- time_weight: bfloat16 [64, 3072], P(None, ('items', 'rows')), may hold values from -0.375 to 0.375
- time_bias: bfloat16 [3072], P(('items', 'rows')), may hold values from -2 to 2
- map_weight: bfloat16 [1280, 1536], P(('items', 'rows')), may hold values from -0.15625 to 0.15625
- map_bias: bfloat16 [1536], P(('items', 'rows')), may hold values from -2 to 2
- qkv_weight: bfloat16 [1536, 4608], P(('items', 'rows')), may hold values from -0.15625 to 0.15625
- qv_bias: bfloat16 [3072], P(('items', 'rows')), may hold values from -2 to 2
- proj_weight: bfloat16 [1536, 1536], P(('items', 'rows')), may hold values from -1.25 to 1.25
- proj_bias: bfloat16 [1536], P(('items', 'rows')), may hold values from -2 to 2
- cotangent: bfloat16 [8, 576, 1536], P('items', 'rows'), may hold values from -6 to 6
Outputs:
- output: bfloat16 [8, 576, 1536], P('items', 'rows')
- grad_latents: float32 [8, 576, 1536], P('items', 'rows')
- grad_conv_weight: float32 [9, 1536], P(None, ('items', 'rows'))
- grad_conv_bias: float32 [1536], P(('items', 'rows'))
- grad_in_weight: float32 [1536, 6144], P(('items', 'rows'))
- grad_in_bias: float32 [6144], P(('items', 'rows'))
- grad_grn_gain: float32 [6144], P(('items', 'rows'))
- grad_grn_bias: float32 [6144], P(('items', 'rows'))
- grad_out_weight: float32 [6144, 1536], P(('items', 'rows'))
- grad_out_bias: float32 [1536], P(('items', 'rows'))
- grad_time_weight: float32 [64, 3072], P(None, ('items', 'rows'))
- grad_time_bias: float32 [3072], P(('items', 'rows'))
- grad_map_weight: float32 [1280, 1536], P(('items', 'rows'))
- grad_map_bias: float32 [1536], P(('items', 'rows'))
- grad_qkv_weight: float32 [1536, 4608], P(('items', 'rows'))
- grad_qv_bias: float32 [3072], P(('items', 'rows'))
- grad_proj_weight: float32 [1536, 1536], P(('items', 'rows'))
- grad_proj_bias: float32 [1536], P(('items', 'rows'))
Inputs may be any that keep to these rules, and one draw needn't show every extreme that they name: `bucket_ids`: items 0, 1 and 2 lie in buckets 0, 1 and 2. `heights`: an item's height is more than half of its bucket's rows and at most all of them; item 2 and every item whose index is a multiple of 16 have all rows of their bucket. `widths`: an item's width is more than half of its bucket's W and at most W; item 2 and every item whose index is a multiple of 16 have all columns of their bucket.
All inputs are finite; a program needn't handle non-finite values. No bound on the sum of `text_mask` on one device may be relied on, other than what follows from the above.
Results may differ from a plain program's by a relative error of at most 0.012.
Values may be sent and summed in bfloat16 or wider, within the bound.
A program may use at most 256 MiB of HBM per device.

v0:
```python
import jax
import jax.numpy as jnp
from jax import lax
from jax.sharding import PartitionSpec as P

HEAD = 64
TXT = 77
UNIT = 8
HALO = 36


norm_eps = 1e-06
grn_eps = 1e-06
masked_score = -1000000000.0


def with_halo(block, sides, width):
    for axis, dim in sides:
        count = lax.axis_size(axis)
        forward = [(i, i + 1) for i in range(count - 1)]
        backward = [(target, source) for source, target in forward]
        low = lax.ppermute(
            lax.slice_in_dim(block, block.shape[dim] - width, None, axis=dim), axis, forward
        )
        high = lax.ppermute(lax.slice_in_dim(block, 0, width, axis=dim), axis, backward)
        block = jnp.concatenate([low, block, high], axis=dim)
    return block


def bucket_shape(bucket_ids):
    bucket_rows = (bucket_ids + 2) * UNIT
    bucket_cols = jnp.where(
        bucket_ids == 0, 9 * UNIT // 2, jnp.where(bucket_ids == 1, 3 * UNIT, 9 * UNIT // 4)
    )
    return (bucket_rows, bucket_cols)


def pixel_mask(start_pixel, pixel_count, heights, widths, bucket_cols):
    positions = start_pixel + jnp.arange(pixel_count, dtype=jnp.int32)
    row_at = positions[None, :] // bucket_cols[:, None]
    col_at = positions[None, :] % bucket_cols[:, None]
    inside = (row_at < heights[:, None]) & (col_at < widths[:, None])
    return inside.astype(jnp.float32)


def tap_values(extended, bucket_cols, pixel_count, tap_index):
    shift_y = tap_index // 3 - 1
    shift_x = tap_index % 3 - 1
    positions = jnp.arange(pixel_count, dtype=jnp.int32)
    column = positions[None, :] % bucket_cols[:, None]
    source = HALO + positions[None, :] + shift_y * bucket_cols[:, None] + shift_x
    source = jnp.clip(source, 0, extended.shape[1] - 1)
    picked = jax.vmap(lambda item_rows, item_index: item_rows[item_index])(extended, source).astype(
        jnp.float32
    )
    is_valid = (column + shift_x >= 0) & (column + shift_x < bucket_cols[:, None])
    return jnp.where(is_valid[:, :, None], picked, 0.0)


def depthwise(extended, kernel, bucket_cols, pixel_count):
    running = jnp.zeros((extended.shape[0], pixel_count, extended.shape[2]), jnp.float32)
    for tap_index in range(9):
        running = (
            running + tap_values(extended, bucket_cols, pixel_count, tap_index) * kernel[tap_index]
        )
    return running


def tap_grads(extended, grad_conv, bucket_cols, pixel_count):
    tap_rows = []
    for tap_index in range(9):
        tap_rows.append(
            jnp.sum(
                tap_values(extended, bucket_cols, pixel_count, tap_index) * grad_conv, axis=(0, 1)
            )
        )
    return jnp.stack(tap_rows)


def layer_norm(values):
    center = values - jnp.mean(values, axis=-1, keepdims=True)
    spread = jnp.mean(center * center, axis=-1, keepdims=True)
    return center * lax.rsqrt(spread + norm_eps)


def exact_gelu(values):
    return jax.nn.gelu(values, approximate=False)


def flat_dot(operand, factor):
    product = jnp.dot(
        operand.reshape(-1, operand.shape[-1]), factor, preferred_element_type=jnp.float32
    )
    return product.reshape(operand.shape[:-1] + (factor.shape[-1],))


def back_dot(grad_rows, weight):
    product = lax.dot_general(
        grad_rows.reshape(-1, grad_rows.shape[-1]),
        weight,
        (((1,), (1,)), ((), ())),
        preferred_element_type=jnp.float32,
    )
    return product.reshape(grad_rows.shape[:-1] + (weight.shape[0],))


def cross_dot(operand, factor):
    return lax.dot_general(
        operand.reshape(-1, operand.shape[-1]),
        factor.reshape(-1, factor.shape[-1]),
        (((0,), (0,)), ((), ())),
        preferred_element_type=jnp.float32,
    )


def body(
    latents,
    clip_tokens,
    time_embed,
    bucket_ids,
    heights,
    widths,
    text_mask,
    conv_weight,
    conv_bias,
    in_weight,
    in_bias,
    grn_gain,
    grn_bias,
    out_weight,
    out_bias,
    time_weight,
    time_bias,
    map_weight,
    map_bias,
    qkv_weight,
    qv_bias,
    proj_weight,
    proj_bias,
    cotangent,
):
    (
        kernel_full,
        conv_bias_full,
        in_full,
        in_bias_full,
        gain_full,
        grn_bias_full,
        out_full,
        out_bias_full,
        time_full,
        time_bias_full,
        map_full,
        map_bias_full,
        qkv_full,
        qv_bias_full,
        proj_full,
        proj_bias_full,
    ) = (
        lax.all_gather(conv_weight, ("items", "rows"), axis=1, tiled=True),
        lax.all_gather(conv_bias, ("items", "rows"), axis=0, tiled=True),
        lax.all_gather(in_weight, ("items", "rows"), axis=0, tiled=True),
        lax.all_gather(in_bias, ("items", "rows"), axis=0, tiled=True),
        lax.all_gather(grn_gain, ("items", "rows"), axis=0, tiled=True),
        lax.all_gather(grn_bias, ("items", "rows"), axis=0, tiled=True),
        lax.all_gather(out_weight, ("items", "rows"), axis=0, tiled=True),
        lax.all_gather(out_bias, ("items", "rows"), axis=0, tiled=True),
        lax.all_gather(time_weight, ("items", "rows"), axis=1, tiled=True),
        lax.all_gather(time_bias, ("items", "rows"), axis=0, tiled=True),
        lax.all_gather(map_weight, ("items", "rows"), axis=0, tiled=True),
        lax.all_gather(map_bias, ("items", "rows"), axis=0, tiled=True),
        lax.all_gather(qkv_weight, ("items", "rows"), axis=0, tiled=True),
        lax.all_gather(qv_bias, ("items", "rows"), axis=0, tiled=True),
        lax.all_gather(proj_weight, ("items", "rows"), axis=0, tiled=True),
        lax.all_gather(proj_bias, ("items", "rows"), axis=0, tiled=True),
    )
    row_index = lax.axis_index("rows")
    row_devices = lax.axis_size("rows")
    items_here = latents.shape[0]
    pixel_count = latents.shape[1]
    channels = latents.shape[2]
    text_slots = clip_tokens.shape[1]
    bucket_cols = bucket_shape(bucket_ids)[1]
    pixel_keep = pixel_mask(row_index * pixel_count, pixel_count, heights, widths, bucket_cols)
    keep_col = pixel_keep[:, :, None]
    masked = latents * keep_col.astype(jnp.bfloat16)
    extended = with_halo(masked, (("rows", 1),), HALO)
    conv_out = depthwise(
        extended, kernel_full.astype(jnp.float32), bucket_cols, pixel_count
    ) + conv_bias_full.astype(jnp.float32)
    normed_hat, norm_back = jax.vjp(layer_norm, conv_out)
    normed = normed_hat.astype(jnp.bfloat16)
    hidden = flat_dot(normed, in_full) + in_bias_full.astype(jnp.float32)
    active, gelu_back = jax.vjp(exact_gelu, hidden)
    squares = lax.psum(jnp.sum(keep_col * active * active, axis=1), "rows")
    grn_norms = jnp.sqrt(squares)
    norm_mean = jnp.mean(grn_norms, axis=-1, keepdims=True) + grn_eps
    grn_ratio = grn_norms / norm_mean
    grn_out = (
        gain_full.astype(jnp.float32) * (active * grn_ratio[:, None, :])
        + grn_bias_full.astype(jnp.float32)
        + active
    ).astype(jnp.bfloat16)
    branch = flat_dot(grn_out, out_full) + out_bias_full.astype(jnp.float32)
    after_res = latents.astype(jnp.float32) + keep_col * branch
    modulate = jnp.dot(
        time_embed, time_full, preferred_element_type=jnp.float32
    ) + time_bias_full.astype(jnp.float32)
    scale_by = 1.0 + modulate[:, None, :channels]
    second = after_res * scale_by + modulate[:, None, channels:]
    two_hat, two_back = jax.vjp(layer_norm, second)
    normed_two = two_hat.astype(jnp.bfloat16)
    projected = flat_dot(normed_two, qkv_full)
    qv_float = qv_bias_full.astype(jnp.float32)
    queries = (projected[:, :, :channels] + qv_float[:channels]).astype(jnp.bfloat16)
    pixel_keys = projected[:, :, channels : 2 * channels].astype(jnp.bfloat16)
    pixel_values = (projected[:, :, 2 * channels :] + qv_float[channels:]).astype(jnp.bfloat16)
    silu_text = jax.nn.silu(clip_tokens.astype(jnp.float32)).astype(jnp.bfloat16)
    mapped = (flat_dot(silu_text, map_full) + map_bias_full.astype(jnp.float32)).astype(
        jnp.bfloat16
    )
    text_kv = flat_dot(mapped, qkv_full)
    text_keys = text_kv[:, :, channels : 2 * channels].astype(jnp.bfloat16)
    text_values = (text_kv[:, :, 2 * channels :] + qv_float[channels:]).astype(jnp.bfloat16)
    local_keys = jnp.concatenate([pixel_keys, text_keys], axis=1)
    local_values = jnp.concatenate([pixel_values, text_values], axis=1)
    all_keys, all_values = (
        lax.all_gather(local_keys, "rows", axis=1, tiled=True),
        lax.all_gather(local_values, "rows", axis=1, tiled=True),
    )
    all_pixels = pixel_mask(0, row_devices * pixel_count, heights, widths, bucket_cols).reshape(
        items_here, row_devices, pixel_count
    )
    text_keep = (
        text_mask.astype(jnp.float32)
        * (jnp.arange(row_devices * text_slots, dtype=jnp.int32) < TXT).astype(jnp.float32)[None, :]
    )
    key_keep = jnp.concatenate(
        [all_pixels, text_keep.reshape(items_here, row_devices, text_slots)], axis=2
    ).reshape(items_here, -1)
    key_total = all_keys.shape[1]
    score_scale = HEAD ** (-0.5)
    pair_width = 2 * HEAD
    pair_count = channels // pair_width

    def head_slice(stacked, pair_index):
        piece = lax.dynamic_slice_in_dim(stacked, pair_index * pair_width, pair_width, axis=2)
        return piece.reshape(piece.shape[0], piece.shape[1], 2, HEAD)

    def pair_scores(pair_index):
        raw_scores = (
            jnp.einsum(
                "iqhd,ikhd->ihqk",
                head_slice(queries, pair_index),
                head_slice(all_keys, pair_index),
                preferred_element_type=jnp.float32,
            )
            * score_scale
        )
        return jnp.where(key_keep[:, None, None, :] > 0, raw_scores, masked_score)

    def forward_pair(pair_index, carry):
        attended, log_norm = carry
        scores = pair_scores(pair_index)
        biggest = jnp.max(scores, axis=-1, keepdims=True)
        weights = jnp.exp(scores - biggest)
        totals = jnp.sum(weights, axis=-1, keepdims=True)
        probs = (weights / totals).astype(jnp.bfloat16)
        mixed_heads = jnp.einsum(
            "ihqk,ikhd->iqhd",
            probs,
            head_slice(all_values, pair_index),
            preferred_element_type=jnp.float32,
        )
        attended = lax.dynamic_update_slice_in_dim(
            attended,
            mixed_heads.reshape(items_here, pixel_count, pair_width),
            pair_index * pair_width,
            axis=2,
        )
        log_norm = lax.dynamic_update_slice_in_dim(
            log_norm, (biggest + jnp.log(totals))[..., 0], 2 * pair_index, axis=1
        )
        return (attended, log_norm)

    attended, log_norm = lax.fori_loop(
        0,
        pair_count,
        forward_pair,
        (
            jnp.zeros((items_here, pixel_count, channels), jnp.float32),
            jnp.zeros((items_here, 2 * pair_count, pixel_count), jnp.float32),
        ),
    )
    attended = attended.astype(jnp.bfloat16)
    result = flat_dot(attended, proj_full) + proj_bias_full.astype(jnp.float32)
    output = (second + keep_col * result).astype(jnp.bfloat16)
    kernel_back, gain_back, in_back, out_back, qkv_back, proj_back = (
        lax.all_gather(conv_weight, ("items", "rows"), axis=1, tiled=True),
        lax.all_gather(grn_gain, ("items", "rows"), axis=0, tiled=True),
        lax.all_gather(in_weight, ("items", "rows"), axis=0, tiled=True),
        lax.all_gather(out_weight, ("items", "rows"), axis=0, tiled=True),
        lax.all_gather(qkv_weight, ("items", "rows"), axis=0, tiled=True),
        lax.all_gather(proj_weight, ("items", "rows"), axis=0, tiled=True),
    )
    grad_output = cotangent.astype(jnp.float32)
    grad_result = (keep_col * grad_output).astype(jnp.bfloat16)
    grad_proj_bias = jnp.sum(grad_result.astype(jnp.float32), axis=(0, 1))
    grad_proj = cross_dot(attended, grad_result)
    grad_att = back_dot(grad_result, proj_back).astype(jnp.bfloat16)

    def backward_pair(pair_index, carry):
        grad_query, grad_key, grad_value = carry
        scores = pair_scores(pair_index)
        log_total = lax.dynamic_slice_in_dim(log_norm, 2 * pair_index, 2, axis=1)[..., None]
        probs = jnp.exp(scores - log_total)
        grad_pair = head_slice(grad_att, pair_index)
        grad_probs = jnp.einsum(
            "iqhd,ikhd->ihqk",
            grad_pair,
            head_slice(all_values, pair_index),
            preferred_element_type=jnp.float32,
        )
        value_term = jnp.einsum(
            "ihqk,iqhd->ikhd",
            probs.astype(jnp.bfloat16),
            grad_pair,
            preferred_element_type=jnp.float32,
        )
        row_sums = jnp.sum(probs * grad_probs, axis=-1, keepdims=True)
        grad_scores = (probs * (grad_probs - row_sums)).astype(jnp.bfloat16)
        query_term = (
            jnp.einsum(
                "ihqk,ikhd->iqhd",
                grad_scores,
                head_slice(all_keys, pair_index),
                preferred_element_type=jnp.float32,
            )
            * score_scale
        )
        key_term = (
            jnp.einsum(
                "ihqk,iqhd->ikhd",
                grad_scores,
                head_slice(queries, pair_index),
                preferred_element_type=jnp.float32,
            )
            * score_scale
        )
        lane_start = pair_index * pair_width
        grad_query = lax.dynamic_update_slice_in_dim(
            grad_query, query_term.reshape(items_here, pixel_count, pair_width), lane_start, axis=2
        )
        grad_key = lax.dynamic_update_slice_in_dim(
            grad_key, key_term.reshape(items_here, key_total, pair_width), lane_start, axis=2
        )
        grad_value = lax.dynamic_update_slice_in_dim(
            grad_value, value_term.reshape(items_here, key_total, pair_width), lane_start, axis=2
        )
        return (grad_query, grad_key, grad_value)

    grad_query, grad_key, grad_value = lax.fori_loop(
        0,
        pair_count,
        backward_pair,
        (
            jnp.zeros((items_here, pixel_count, channels), jnp.float32),
            jnp.zeros((items_here, key_total, channels), jnp.float32),
            jnp.zeros((items_here, key_total, channels), jnp.float32),
        ),
    )
    own_keys, own_values = (
        lax.psum_scatter(
            grad_key.astype(jnp.bfloat16), "rows", scatter_dimension=1, tiled=True
        ).astype(jnp.float32),
        lax.psum_scatter(
            grad_value.astype(jnp.bfloat16), "rows", scatter_dimension=1, tiled=True
        ).astype(jnp.float32),
    )
    own_keys = own_keys.astype(jnp.bfloat16)
    own_values = own_values.astype(jnp.bfloat16)
    grad_query = grad_query.astype(jnp.bfloat16)
    grad_pixel_qkv = jnp.concatenate(
        [grad_query, own_keys[:, :pixel_count], own_values[:, :pixel_count]], axis=2
    )
    grad_text_keys = own_keys[:, pixel_count:]
    grad_text_qkv = jnp.concatenate(
        [jnp.zeros_like(grad_text_keys), grad_text_keys, own_values[:, pixel_count:]], axis=2
    )
    grad_qkv = cross_dot(
        jnp.concatenate([normed_two.reshape(-1, channels), mapped.reshape(-1, channels)], axis=0),
        jnp.concatenate(
            [grad_pixel_qkv.reshape(-1, 3 * channels), grad_text_qkv.reshape(-1, 3 * channels)],
            axis=0,
        ),
    )
    grad_qv_bias = jnp.concatenate(
        [
            jnp.sum(grad_query.astype(jnp.float32), axis=(0, 1)),
            jnp.sum(own_values.astype(jnp.float32), axis=(0, 1)),
        ]
    )
    grad_mapped = back_dot(grad_text_qkv, qkv_back).astype(jnp.bfloat16)
    grad_map = cross_dot(silu_text, grad_mapped)
    grad_map_bias = jnp.sum(grad_mapped.astype(jnp.float32), axis=(0, 1))
    grad_two = back_dot(grad_pixel_qkv, qkv_back)
    grad_second = grad_output + two_back(grad_two)[0]
    grad_modulate = jnp.concatenate(
        [jnp.sum(grad_second * after_res, axis=1), jnp.sum(grad_second, axis=1)], axis=1
    )
    grad_time = lax.dot_general(
        time_embed.astype(jnp.float32),
        grad_modulate,
        (((0,), (0,)), ((), ())),
        precision=lax.Precision.HIGHEST,
    )
    grad_time_bias = jnp.sum(grad_modulate, axis=0)
    grad_after = grad_second * scale_by
    grad_branch = (keep_col * grad_after).astype(jnp.bfloat16)
    grad_out_bias = jnp.sum(grad_branch.astype(jnp.float32), axis=(0, 1))
    grad_out = cross_dot(grn_out, grad_branch)
    grad_grn = back_dot(grad_branch, out_back)
    gain_float = gain_back.astype(jnp.float32)
    grad_gain = jnp.sum(grad_grn * active * grn_ratio[:, None, :], axis=(0, 1))
    grad_grn_bias = jnp.sum(grad_grn, axis=(0, 1))
    ratio_grad = lax.psum(jnp.sum(grad_grn * gain_float * active, axis=1), "rows")
    grad_norms = ratio_grad / norm_mean - jnp.sum(
        ratio_grad * grn_norms, axis=-1, keepdims=True
    ) / (grn_norms.shape[-1] * norm_mean * norm_mean)
    grad_active = (
        grad_grn * (gain_float * grn_ratio[:, None, :] + 1.0)
        + keep_col * active * (grad_norms / grn_norms)[:, None, :]
    )
    grad_hidden = gelu_back(grad_active)[0].astype(jnp.bfloat16)
    grad_in_bias = jnp.sum(grad_hidden.astype(jnp.float32), axis=(0, 1))
    grad_in = cross_dot(normed, grad_hidden)
    grad_conv = norm_back(back_dot(grad_hidden, in_back))[0]
    grad_conv_bias = jnp.sum(grad_conv, axis=(0, 1))
    grad_kernel = tap_grads(extended, grad_conv, bucket_cols, pixel_count)
    grad_extended = with_halo(grad_conv.astype(jnp.bfloat16), (("rows", 1),), HALO).astype(
        grad_conv.dtype
    )
    flipped = kernel_back.astype(jnp.float32)[::-1]
    grad_latents = grad_after + keep_col * depthwise(
        grad_extended, flipped, bucket_cols, pixel_count
    )
    grad_shards = (
        lax.psum_scatter(grad_kernel, ("items", "rows"), scatter_dimension=1, tiled=True),
        lax.psum_scatter(grad_conv_bias, ("items", "rows"), scatter_dimension=0, tiled=True),
        lax.psum_scatter(grad_in, ("items", "rows"), scatter_dimension=0, tiled=True),
        lax.psum_scatter(grad_in_bias, ("items", "rows"), scatter_dimension=0, tiled=True),
        lax.psum_scatter(grad_gain, ("items", "rows"), scatter_dimension=0, tiled=True),
        lax.psum_scatter(grad_grn_bias, ("items", "rows"), scatter_dimension=0, tiled=True),
        lax.psum_scatter(grad_out, ("items", "rows"), scatter_dimension=0, tiled=True),
        lax.psum_scatter(grad_out_bias, ("items", "rows"), scatter_dimension=0, tiled=True),
        lax.psum_scatter(grad_time, ("items", "rows"), scatter_dimension=1, tiled=True),
        lax.psum_scatter(grad_time_bias, ("items", "rows"), scatter_dimension=0, tiled=True),
        lax.psum_scatter(grad_map, ("items", "rows"), scatter_dimension=0, tiled=True),
        lax.psum_scatter(grad_map_bias, ("items", "rows"), scatter_dimension=0, tiled=True),
        lax.psum_scatter(grad_qkv, ("items", "rows"), scatter_dimension=0, tiled=True),
        lax.psum_scatter(grad_qv_bias, ("items", "rows"), scatter_dimension=0, tiled=True),
        lax.psum_scatter(grad_proj, ("items", "rows"), scatter_dimension=0, tiled=True),
        lax.psum_scatter(grad_proj_bias, ("items", "rows"), scatter_dimension=0, tiled=True),
    )
    return (output, grad_latents) + tuple(grad_shards)


def solution(mesh):
    return jax.shard_map(
        body,
        mesh=mesh,
        in_specs=(
            P("items", "rows", None),
            P("items", "rows", None),
            P("items", None),
            P("items"),
            P("items"),
            P("items"),
            P("items", None),
            P(None, ("items", "rows")),
            P(("items", "rows")),
            P(("items", "rows"), None),
            P(("items", "rows")),
            P(("items", "rows")),
            P(("items", "rows")),
            P(("items", "rows"), None),
            P(("items", "rows")),
            P(None, ("items", "rows")),
            P(("items", "rows")),
            P(("items", "rows"), None),
            P(("items", "rows")),
            P(("items", "rows"), None),
            P(("items", "rows")),
            P(("items", "rows"), None),
            P(("items", "rows")),
            P("items", "rows", None),
        ),
        out_specs=(
            P("items", "rows", None),
            P("items", "rows", None),
            P(None, ("items", "rows")),
            P(("items", "rows")),
            P(("items", "rows"), None),
            P(("items", "rows")),
            P(("items", "rows")),
            P(("items", "rows")),
            P(("items", "rows"), None),
            P(("items", "rows")),
            P(None, ("items", "rows")),
            P(("items", "rows")),
            P(("items", "rows"), None),
            P(("items", "rows")),
            P(("items", "rows"), None),
            P(("items", "rows")),
            P(("items", "rows"), None),
            P(("items", "rows")),
        ),
        check_vma=False,
    )
```

profile of v0, /device:TPU:0, one launch (start us, length us, event | category | flops | bytes accessed | tf_op | source)
XLA Modules:
  0.0 2626.2 jit_solution(1771894623415452256)
XLA Ops:
  28.5 43.1 %all-reduce.21 = (bf16[1536]{0:T(1024)(128)(2,1)}, bf16[1536]{0:T(1024)(128)(2,1)S(1)}, bf16[3072]{0:T(1024)(128)(2,1)S(1)}, bf16[3072]{0:T(1024)(128)(2,1)S(1)}...) all-reduce(bf16[1536]{0:T(1024)(128)(2,1)S(1)} %dynamic-update-slic, ...), channel_id=1, replica_groups=mesh['items'=8,'rows'=4] {'items','rows'}, use_global_device_ids=true, to_apply=%add.8 | all-reduce | flops 30720 | bytes 122880
  72.2 74.5 %all-gather.1 = bf16[32,96,64]{1,2,0:T(8,128)(2,1)S(1)} all-gather(bf16[1,96,64]{1,2,0:T(8,128)(2,1)S(1)} %bitcast.486), channel_id=1, replica_groups=mesh['items'=8,'rows'=4] {'items','rows'}, dimensions={0}, use_global_device_ids=true | all-gather | bytes 405504 | tf_op jit(solution)/shard_map/all_gather | solution.py:168
  149.3 66.3 %all-gather = bf16[32,48,9]{1,2,0:T(8,128)(2,1)S(1)} all-gather(bf16[1,48,9]{1,2,0:T(8,128)(2,1)S(1)} %bitcast.487), channel_id=1, replica_groups=mesh['items'=8,'rows'=4] {'items','rows'}, dimensions={0}, use_global_device_ids=true | all-gather | bytes 28512 | tf_op jit(solution)/shard_map/all_gather | solution.py:160
  267.7 42.5 %all-gather.10.cloned.1.call-done = bf16[1536,6144]{1,0:T(8,128)(2,1)} async-done(((bf16[48,6144]{1,0:T(8,128)(2,1)}), bf16[1536,6144]{1,0:T(8,128)(2,1)}) %all-gather.10.cloned.1.call-update) | async-done | bytes 18874384 | tf_op jit(solution)/shard_map/all_gather | solution.py:162
  310.2 17.3 fusion.8
  327.5 18.9 psum.14
  349.9 86.1 %all-gather.12.cloned.1.call-done = bf16[6144,1536]{1,0:T(8,128)(2,1)} async-done(((bf16[192,1536]{1,0:T(8,128)(2,1)}), bf16[6144,1536]{1,0:T(8,128)(2,1)}) %all-gather.12.cloned.1.call-update) | async-done | bytes 18874384 | tf_op jit(solution)/shard_map/all_gather | solution.py:166
  455.6 44.9 %all-gather.22.cloned.1.call-done = bf16[1536,1536]{1,0:T(8,128)(2,1)} async-done(((bf16[48,1536]{1,0:T(8,128)(2,1)}), bf16[1536,1536]{1,0:T(8,128)(2,1)}) %all-gather.22.cloned.1.call-update) | async-done | bytes 4718608 | tf_op jit(solution)/shard_map/all_gather | solution.py:174
  505.5 73.8 %all-gather.18.cloned.1.call-done = bf16[1,656,1536]{2,0,1:T(2,128)(2,1)} async-done(((bf16[1,164,1536]{2,0,1:T(2,128)(2,1)}), bf16[1,656,1536]{2,0,1:T(2,128)(2,1)}) %all-gather.18.cloned.1.call-update) | async-done | bytes 2015248 | tf_op jit(solution)/shard_map/all_gather | solution.py:229
  588.4 69.7 %all-gather.20.cloned.1.call-done = bf16[1,656,1536]{2,0,1:T(2,128)(2,1)} async-done(((bf16[1,164,1536]{2,0,1:T(2,128)(2,1)}), bf16[1,656,1536]{2,0,1:T(2,128)(2,1)}) %all-gather.20.cloned.1.call-update) | async-done | bytes 2015248 | tf_op jit(solution)/shard_map/all_gather | solution.py:228
  666.9 30.2 %while.32 = (s32[]{:T(128)}, bf16[1,144,1536]{1,2,0:T(8,128)(2,1)S(1)}, f32[1,24,144]{2,1,0:T(8,128)S(1)}, bf16[1,656,1536]{1,2,0:T(8,128)(2,1)}, f32[1,4,164]{2...) while((s32[]{:T(128)}, ...), condition=%wide.region_10.12_spmd, body=%wide.region_7.11_spmd.sunk | while | flops 49877364 | bytes 3570673 | solution.py:286
  700.3 65.3 %while.33 = (s32[]{:T(128)}, bf16[1,144,1536]{1,2,0:T(8,128)(2,1)S(1)}, bf16[1,656,1536]{1,2,0:T(8,128)(2,1)}, bf16[1,656,1536]{1,2,0:T(8,128)(2,1)}, bf16[1,656...) while((s32[]{:T(128)}, ...), condition=%wide.region_13.15_spmd, body=%wide.region_11.14_spmd.sunk | while | flops 122819440 | bytes 8456213 | solution.py:362
  770.1 166.6 %all-reduce.28.cloned.1.call-done = (bf16[1,656,1536]{1,2,0:T(8,128)(2,1)}, bf16[1,656,1536]{1,2,0:T(8,128)(2,1)}) async-done(((bf16[1,656,1536]{1,2,0:T(8,128)(2,1)}, bf16[1,656,1536]{1,2,0:T(8,128)(2,1)}), (bf16[1,656,1536]{1,2,0:T(8,128)(2,1)}, bf16[1,656,1536]{1,2,0:T(8,128)(2,1)})) %all-reduce.28.cloned.1.call-update) | async-done | bytes 4030480
  974.3 18.1 psum.15
  1092.6 16.4 fusion.188
  1109.1 15.8 fusion.123
  1136.1 29.7 %all-reduce.26.cloned.1.call-done = (f32[1536]{0:T(1024)}, f32[6144]{0:T(1024)}, f32[6144]{0:T(1024)}, f32[6144]{0:T(1024)}, f32[1536]{0:T(1024)}, /*index=5*/f3...) async-done(((f32[1536]{0:T(1024)}, f32[6144]{0:T(1024)}, f32[6144]{0:T(1024)}, f32[6144]{0:T(1024)}, f32[1536]{0:T(1024)}, /*index=5*/f32[3072]{0:T(1024)}, ...) | async-done | bytes 122896
  1177.4 88.7 %reduce-scatter.24.cloned.1.call-done = f32[48,9]{1,0:T(8,128)} async-done(((f32[1536,9]{1,0:T(8,128)}), f32[48,9]{1,0:T(8,128)}) %reduce-scatter.24.cloned.1.call-update) | async-done | bytes 1744
  1306.9 61.4 %reduce-scatter.26.cloned.1.call-done = f32[96,64]{1,0:T(8,128)} async-done(((f32[3072,64]{1,0:T(8,128)}), f32[96,64]{1,0:T(8,128)}) %reduce-scatter.26.cloned.1.call-update) | async-done | bytes 24592
  1369.8 140.3 %reduce-scatter.22.cloned.1.call-done = f32[48,1536]{1,0:T(8,128)} async-done(((f32[1536,1536]{1,0:T(8,128)}), f32[48,1536]{1,0:T(8,128)}) %reduce-scatter.22.cloned.1.call-update) | async-done | bytes 294928 | tf_op jit(solution)/shard_map/reduce_scatter | solution.py:462
  1510.1 127.8 %reduce-scatter.18.cloned.1.call-done = f32[40,1536]{1,0:T(8,128)} async-done(((f32[1280,1536]{1,0:T(8,128)}), f32[40,1536]{1,0:T(8,128)}) %reduce-scatter.18.cloned.1.call-update) | async-done | bytes 245776 | tf_op jit(solution)/shard_map/reduce_scatter | solution.py:458
  1637.9 270.8 %reduce-scatter.20.cloned.1.call-done = f32[48,4608]{1,0:T(8,128)} async-done(((f32[1536,4608]{1,0:T(8,128)}), f32[48,4608]{1,0:T(8,128)}) %reduce-scatter.20.cloned.1.call-update) | async-done | bytes 884752 | tf_op jit(solution)/shard_map/reduce_scatter | solution.py:460
  1908.7 356.3 %reduce-scatter.14.cloned.1.call-done = f32[48,6144]{1,0:T(8,128)} async-done(((f32[1536,6144]{1,0:T(8,128)}), f32[48,6144]{1,0:T(8,128)}) %reduce-scatter.14.cloned.1.call-update) | async-done | bytes 1179664 | tf_op jit(solution)/shard_map/reduce_scatter | solution.py:450
  2265.0 354.5 %reduce-scatter.16.cloned.1.call-done = f32[192,1536]{1,0:T(8,128)} async-done(((f32[6144,1536]{1,0:T(8,128)}), f32[192,1536]{1,0:T(8,128)}) %reduce-scatter.16.cloned.1.call-update) | async-done | bytes 1179664 | tf_op jit(solution)/shard_map/reduce_scatter | solution.py:454
  (730 shorter events, 421.3 us)
Async XLA Ops:
  7.2 210.0 %copy-start.94 = (bf16[1,64]{1,0:T(2,128)(2,1)S(1)}, bf16[1,64]{1,0:T(2,128)(2,1)}, u32[]{:S(2)}) copy-start(bf16[1,64]{1,0:T(2,128)(2,1)} %param.32) | copy-start | bytes 388
  7.2 249.1 %all-gather.16.cloned.1.call-start = ((), (), s32[]{:S(2)}) async-start(), calls=%async_computation.10 | async-start | bytes 4055040 | tf_op jit(solution)/shard_map/all_gather | solution.py:170
  8.0 251.2 %all-gather.14.cloned.1.call-start = ((), (), s32[]{:S(2)}) async-start(), calls=%async_computation.9 | async-start | bytes 14598144 | tf_op jit(solution)/shard_map/all_gather | solution.py:172
  8.7 301.5 %all-gather.10.cloned.1.call-start = ((), (), s32[]{:S(2)}) async-start(), calls=%async_computation.7 | async-start | bytes 19464192 | tf_op jit(solution)/shard_map/all_gather | solution.py:162
  9.4 426.5 %all-gather.12.cloned.1.call-start = ((), (), s32[]{:S(2)}) async-start(), calls=%async_computation.8 | async-start | bytes 19464192 | tf_op jit(solution)/shard_map/all_gather | solution.py:166
  10.0 490.4 %all-gather.22.cloned.1.call-start = ((), (), s32[]{:S(2)}) async-start(), calls=%async_computation.13 | async-start | bytes 4866048 | tf_op jit(solution)/shard_map/all_gather | solution.py:174
  13.4 204.7 %collective-permute-start.1 = (bf16[1,36,1536]{2,1,0:T(8,128)(2,1)S(1)}, bf16[1,36,1536]{2,1,0:T(8,128)(2,1)S(1)}, u32[]{:S(2)}, u32[]{:S(2)}) collective-permute-start(bf16[1,36,1536]{2,1,0:T(8,128)(2,1)S(1)} %get-tuple-element.519), channel_id=1, source_target_pairs={{1,0},{2,1},{3,2},{5,4},{6,5},{7,6},{9,8},{10,9},{11,10},{13,12},{... | collective-permute-start | bytes 331784 | tf_op jit(solution)/shard_map/ppermute | solution.py:25
  14.7 203.4 %collective-permute-start = (bf16[1,36,1536]{2,1,0:T(8,128)(2,1)S(1)}, bf16[1,36,1536]{2,1,0:T(8,128)(2,1)S(1)}, u32[]{:S(2)}, u32[]{:S(2)}) collective-permute-start(bf16[1,36,1536]{2,1,0:T(8,128)(2,1)S(1)} %get-tuple-element.518), channel_id=1, source_target_pairs={{0,1},{1,2},{2,3},{4,5},{5,6},{6,7},{8,9},{9,10},{10,11},{12,13},{... | collective-permute-start | bytes 331784 | tf_op jit(solution)/shard_map/ppermute | solution.py:22
  20.3 559.1 %all-gather.18.cloned.1.call-start = ((), (), s32[]{:S(2)}) async-start(), calls=%async_computation.11 | async-start | bytes 5038080 | tf_op jit(solution)/shard_map/all_gather | solution.py:229
  20.6 233.0 %copy-start.83 = (pred[144]{0:T(512)(128)(4,1)}, pred[144]{0:T(512)(128)(4,1)S(1)}, u32[]{:S(2)}) copy-start(pred[144]{0:T(512)(128)(4,1)S(1)} %get-tuple-element.532) | copy-start | bytes 436
  20.6 233.0 %copy-start.84 = (pred[144]{0:T(512)(128)(4,1)}, pred[144]{0:T(512)(128)(4,1)S(1)}, u32[]{:S(2)}) copy-start(pred[144]{0:T(512)(128)(4,1)S(1)} %get-tuple-element.533) | copy-start | bytes 436
  20.8 232.8 %copy-start.85 = (pred[144]{0:T(512)(128)(4,1)}, pred[144]{0:T(512)(128)(4,1)S(1)}, u32[]{:S(2)}) copy-start(pred[144]{0:T(512)(128)(4,1)S(1)} %and_reduce_fusion.2) | copy-start | bytes 436
  451.6 206.5 %all-gather.20.cloned.1.call-start = ((), (), s32[]{:S(2)}) async-start(), calls=%async_computation.12 | async-start | bytes 5038080 | tf_op jit(solution)/shard_map/all_gather | solution.py:228
  454.5 482.2 %all-reduce.28.cloned.1.call-start = ((), (), s32[]{:S(2)}) async-start(), calls=%async_computation.22 | async-start | bytes 9437184
  1027.6 138.1 %all-reduce.26.cloned.1.call-start = ((), (), s32[]{:S(2)}) async-start(), calls=%async_computation.21 | async-start | bytes 262144
  1040.2 225.9 %reduce-scatter.24.cloned.1.call-start = ((), (), s32[]{:S(2)}) async-start(), calls=%async_computation.19 | async-start | bytes 811008
  1057.2 311.0 %reduce-scatter.26.cloned.1.call-start = ((), (), s32[]{:S(2)}) async-start(), calls=%async_computation.20 | async-start | bytes 1622016
  1060.1 450.0 %reduce-scatter.22.cloned.1.call-start = ((), (), s32[]{:S(2)}) async-start(), calls=%async_computation.18 | async-start | bytes 9732096 | tf_op jit(solution)/shard_map/reduce_scatter | solution.py:462
  1066.4 571.5 %reduce-scatter.18.cloned.1.call-start = ((), (), s32[]{:S(2)}) async-start(), calls=%async_computation.16 | async-start | bytes 8110080 | tf_op jit(solution)/shard_map/reduce_scatter | solution.py:458
  1071.8 836.9 %reduce-scatter.20.cloned.1.call-start = ((), (), s32[]{:S(2)}) async-start(), calls=%async_computation.17 | async-start | bytes 29196288 | tf_op jit(solution)/shard_map/reduce_scatter | solution.py:460
  1092.5 1172.4 %reduce-scatter.14.cloned.1.call-start = ((), (), s32[]{:S(2)}) async-start(), calls=%async_computation.14 | async-start | bytes 38928384 | tf_op jit(solution)/shard_map/reduce_scatter | solution.py:450
  1109.0 1510.4 %reduce-scatter.16.cloned.1.call-start = ((), (), s32[]{:S(2)}) async-start(), calls=%async_computation.15 | async-start | bytes 38928384 | tf_op jit(solution)/shard_map/reduce_scatter | solution.py:454
  1126.0 141.5 %collective-permute-start.3 = (bf16[1,36,1536]{2,1,0:T(8,128)(2,1)S(1)}, bf16[1,36,1536]{2,1,0:T(8,128)(2,1)S(1)}, u32[]{:S(2)}, u32[]{:S(2)}) collective-permute-start(bf16[1,36,1536]{2,1,0:T(8,128)(2,1)S(1)} %get-tuple-element.517), channel_id=1, source_target_pairs={{1,0},{2,1},{3,2},{5,4},{6,5},{7,6},{9,8},{10,9},{11,10},{13,12},{... | collective-permute-start | bytes 331784 | tf_op jit(solution)/shard_map/ppermute | solution.py:25
  1127.3 140.2 %collective-permute-start.2 = (bf16[1,36,1536]{2,1,0:T(8,128)(2,1)S(1)}, bf16[1,36,1536]{2,1,0:T(8,128)(2,1)S(1)}, u32[]{:S(2)}, u32[]{:S(2)}) collective-permute-start(bf16[1,36,1536]{2,1,0:T(8,128)(2,1)S(1)} %get-tuple-element.516), channel_id=1, source_target_pairs={{0,1},{1,2},{2,3},{4,5},{5,6},{6,7},{8,9},{9,10},{10,11},{12,13},{... | collective-permute-start | bytes 331784 | tf_op jit(solution)/shard_map/ppermute | solution.py:22
  (98 other events, 3209.2 us)
Sparse Core Ops, SparseCore 0:
  10.9 64.3 all-gather.15
  78.0 105.7 all-gather.13
  186.7 123.4 all-gather.9
  312.8 123.0 all-gather.11
  438.6 61.7 all-gather.21
  502.5 76.8 all-gather.17
  581.5 76.6 all-gather.19
  765.8 170.8 all-reduce.27
  1040.3 125.3 all-reduce.25
  1171.5 94.5 reduce-scatter.23
  1272.2 96.0 reduce-scatter.25
  1375.6 134.4 reduce-scatter.21
  1516.3 121.5 reduce-scatter.17
  1645.9 262.7 reduce-scatter.19
  1916.7 348.2 reduce-scatter.13
  2271.8 347.5 reduce-scatter.15
where the time goes:
time: 2640 us; the launch traced here: 2630 us
  waiting for transfers between devices  1920 us (73%)
  blocking collectives  221 us (8%)
  local copies, waits for them, and re-layouts  206 us (8%)
  matrix products  183 us (7%)
  other arithmetic  65.1 us (2%)
    reduce_scatter x1, waiting for transfers between devices, body(): lax.psum_scatter(grad_in, ('items', 'rows'), scatter_dimension=0, tiled=T...  356 us
    reduce_scatter x1, waiting for transfers between devices, body(): lax.psum_scatter(grad_out, ('items', 'rows'), scatter_dimension=0, tiled=...  354 us
    unnamed x20, waiting for transfers between devices  349 us
    reduce_scatter x1, waiting for transfers between devices, body(): lax.psum_scatter(grad_qkv, ('items', 'rows'), scatter_dimension=0, tiled=...  271 us
    reduce_scatter x1, waiting for transfers between devices, body(): lax.psum_scatter(grad_proj, ('items', 'rows'), scatter_dimension=0, tiled...  140 us
    reduce_scatter x1, waiting for transfers between devices, body(): lax.psum_scatter(grad_map, ('items', 'rows'), scatter_dimension=0, tiled=...  128 us
    all_gather x1, waiting for transfers between devices, body(): lax.all_gather(out_weight, ('items', 'rows'), axis=0, tiled=True)  86.1 us
    all_gather x1, blocking collectives, body(): lax.all_gather(time_weight, ('items', 'rows'), axis=1, tiled=True)  74.5 us
  transfers between devices with their start and end apart: 20, of which 14 were waited for; matrix products, arithmetic and copies ran while one was open for 10% of the time, Pallas kernels for 0%

commit v1 on v0

v1 whole, which is shorter than its diff:
```python
import functools

import jax
import jax.numpy as jnp
from jax import lax
from jax.experimental import pallas as pl
from jax.experimental.pallas import tpu as pltpu
from jax.sharding import Mesh, PartitionSpec as P

HEAD = 64
TXT = 77
UNIT = 8
EDGE = 48

norm_eps = 1e-06
grn_eps = 1e-06
masked_score = -1000000000.0

AXES = ("grp", "duo", "rows")
MESH_ID = pl.DeviceIdType.MESH
F32 = jnp.float32
BF16 = jnp.bfloat16


class Place:
    def __init__(self):
        self.q, self.c, self.z = (lax.axis_index(axis) for axis in AXES)
        self.G, self.D, self.R = (lax.axis_size(axis) for axis in AXES)

    def team(self):
        for step in range(1, self.D * self.R):
            dc, dz = step // self.R, step % self.R
            yield lax.rem(self.c + dc, self.D), lax.rem(self.z + dz, self.R)

    def groups(self):
        for step in range(1, self.G):
            yield lax.rem(self.q + step, self.G)


def signal_all(barrier, targets):
    for target in targets:
        pl.semaphore_signal(barrier, inc=1, device_id=target, device_id_type=MESH_ID)


def run_plan(plan, count_in, count_out, *refs):
    ins, outs = refs[:count_in], refs[count_in : count_in + count_out]
    send_sem, recv_sem, local_sem = refs[count_in + count_out :]
    place = Place()
    greet, messages, local = plan(place, ins, outs)
    barrier = pltpu.get_barrier_semaphore()
    waits = 0
    for target, when in greet:
        if when is None:
            signal_all(barrier, [target])
            waits += 1
        else:

            @pl.when(when)
            def _():
                signal_all(barrier, [target])

    for _, when in greet:
        if when is not None:
            waits = waits + jnp.where(when, 1, 0).astype(jnp.int32)
    pl.semaphore_wait(barrier, waits)
    copies = []
    arrived = set()

    def guarded(when, act):
        if when is None:
            act()
        else:
            pl.when(when)(act)

    for number, (src, dst, target, after, when) in enumerate(messages):
        for earlier in after:
            if earlier not in arrived:
                arrived.add(earlier)
                guarded(copies[earlier][1], copies[earlier][0].wait_recv)
        copy = pltpu.make_async_remote_copy(
            src_ref=src,
            dst_ref=dst,
            send_sem=send_sem.at[number],
            recv_sem=recv_sem.at[number],
            device_id=target,
            device_id_type=MESH_ID,
        )
        guarded(when, copy.start)
        copies.append((copy, when))
    stays = []
    for number, (src, dst, when) in enumerate(local):
        copy = pltpu.make_async_copy(src, dst, local_sem.at[number])
        guarded(when, copy.start)
        stays.append((copy, when))
    for copy, when in stays:
        guarded(when, copy.wait)
    for number, (copy, when) in enumerate(copies):
        if number not in arrived:
            guarded(when, copy.wait_recv)
    for copy, when in copies:
        guarded(when, copy.wait_send)


def exchange(ident, name, plan, arrays, results, messages, local):
    spot = pl.BlockSpec(memory_space=pl.ANY)
    return pl.pallas_call(
        functools.partial(run_plan, plan, len(arrays), len(results)),
        out_shape=[jax.ShapeDtypeStruct(shape, kind) for shape, kind in results],
        in_specs=[spot] * len(arrays),
        out_specs=[spot] * len(results),
        scratch_shapes=[
            pltpu.SemaphoreType.DMA((messages,)),
            pltpu.SemaphoreType.DMA((messages,)),
            pltpu.SemaphoreType.DMA((max(local, 1),)),
        ],
        compiler_params=pltpu.CompilerParams(collective_id=ident, has_side_effects=True),
        name=name,
    )(*arrays)


def team_greet(p):
    return [({"duo": c, "rows": z}, None) for c, z in p.team()]


def group_greet(p):
    return [({"grp": q}, None) for q in p.groups()]


def rows_greet(p):
    return [({"rows": lax.rem(p.z + step, p.R)}, None) for step in range(1, p.R)]


def duo_greet(p):
    return [({"duo": lax.rem(p.c + step, p.D)}, None) for step in range(1, p.D)]


def team_swap(p, src, dst, slot=None):
    mine = p.c * p.R + p.z
    return (
        [
            (src.at[c * p.R + z], dst.at[mine], {"duo": c, "rows": z}, (), None)
            for c, z in p.team()
        ],
        [(src.at[mine], dst.at[mine], None)],
    )


def team_gather(p, src, dst):
    mine = p.c * p.R + p.z
    return (
        [(src, dst.at[mine], {"duo": c, "rows": z}, (), None) for c, z in p.team()],
        [(src, dst.at[mine], None)],
    )


def group_gather(p, src, dst):
    return (
        [(src, dst.at[p.q], {"grp": q}, (), None) for q in p.groups()],
        [(src, dst.at[p.q], None)],
    )


def group_swap(p, src, dst):
    return (
        [(src.at[q], dst.at[p.q], {"grp": q}, (), None) for q in p.groups()],
        [(src.at[p.q], dst.at[p.q], None)],
    )


def item_gather(p, src, dst, base):
    messages = []
    for step in range(1, p.R):
        messages.append((src, dst.at[p.c, p.z], {"rows": lax.rem(p.z + step, p.R)}, (), None))
    other = {"duo": lax.rem(p.c + 1, p.D)}
    messages.append((src, dst.at[p.c, p.z], other, (), None))
    for step in range(1, p.R):
        block = lax.rem(p.z - step + p.R, p.R)
        messages.append(
            (dst.at[p.c, block], dst.at[p.c, block], other, (base + step - 1,), None)
        )
    return messages, [(src, dst.at[p.c, p.z], None)]


def layer_stats(values):
    center = values - jnp.mean(values, axis=-1, keepdims=True)
    spread = jnp.mean(center * center, axis=-1, keepdims=True)
    inverse = lax.rsqrt(spread + norm_eps)
    return center * inverse, inverse


def layer_back(grad, hat, inverse):
    first = jnp.mean(grad, axis=-1, keepdims=True)
    second = jnp.mean(grad * hat, axis=-1, keepdims=True)
    return inverse * (grad - first - hat * second)


def mm(left, right):
    return jnp.dot(left, right, preferred_element_type=F32)


def mm_t(left, right):
    return lax.dot_general(left, right, (((1,), (1,)), ((), ())), preferred_element_type=F32)


def t_mm(left, right):
    return lax.dot_general(left, right, (((0,), (0,)), ((), ())), preferred_element_type=F32)


def columns_of(bucket_ids):
    return jnp.where(
        bucket_ids == 0, 9 * UNIT // 2, jnp.where(bucket_ids == 1, 3 * UNIT, 9 * UNIT // 4)
    )


def pixel_mask(positions, height, width, cols):
    row_at = positions // cols
    col_at = positions % cols
    return ((row_at < height) & (col_at < width)).astype(F32)


def reduce_items(p_kernel_id, name, part):
    duo, rows, count, width = part.shape

    def kernel(part_ref, out_ref, mate, passed, landed, s1, r1, s2, r2):
        p = Place()
        barrier = pltpu.get_barrier_semaphore()
        greet = [target for target, _ in duo_greet(p) + rows_greet(p)]
        signal_all(barrier, greet)
        pl.semaphore_wait(barrier, len(greet))
        other = lax.rem(p.c + 1, duo)
        order = list(range(1, rows)) + [0]
        first = []
        for step in order:
            block = lax.rem(p.z + step, rows)
            copy = pltpu.make_async_remote_copy(
                src_ref=part_ref.at[other, block],
                dst_ref=mate.at[block],
                send_sem=s1.at[step],
                recv_sem=r1.at[step],
                device_id={"duo": other},
                device_id_type=MESH_ID,
            )
            copy.start()
            first.append(copy)
        second = []
        for copy, step in zip(first, order):
            block = lax.rem(p.z + step, rows)
            copy.wait_recv()
            total = part_ref[p.c, block].astype(F32) + mate[block].astype(F32)
            if step == 0:
                out_ref[...] = total
            else:
                passed[block] = total.astype(BF16)
                onward = pltpu.make_async_remote_copy(
                    src_ref=passed.at[block],
                    dst_ref=landed.at[p.z],
                    send_sem=s2.at[step],
                    recv_sem=r2.at[step],
                    device_id={"rows": block},
                    device_id_type=MESH_ID,
                )
                onward.start()
                second.append((onward, step))
        for onward, step in second:
            onward.wait_recv()
            out_ref[...] += landed[lax.rem(p.z - step + rows, rows)].astype(F32)
        for copy in first:
            copy.wait_send()
        for onward, _ in second:
            onward.wait_send()

    spot = pl.BlockSpec(memory_space=pltpu.VMEM)
    block = (rows, count, width)
    return pl.pallas_call(
        kernel,
        out_shape=jax.ShapeDtypeStruct((count, width), F32),
        in_specs=[spot],
        out_specs=spot,
        scratch_shapes=[pltpu.VMEM(block, BF16)] * 3
        + [pltpu.SemaphoreType.DMA((rows,))] * 4,
        compiler_params=pltpu.CompilerParams(
            collective_id=p_kernel_id, has_side_effects=True, vmem_limit_bytes=48 * 2**20
        ),
        name=name,
    )(part)


def pad_rows(values, rows):
    return jnp.pad(values, ((0, rows - values.shape[0]),) + ((0, 0),) * (values.ndim - 1))


def pack_flat(pieces, rows, kind):
    flat = jnp.concatenate([piece.astype(kind).reshape(-1) for piece in pieces])
    return jnp.pad(flat, (0, rows * 128 - flat.shape[0])).reshape(rows, 128)


def body(
    latents,
    clip_tokens,
    time_embed,
    bucket_ids,
    heights,
    widths,
    text_mask,
    conv_weight,
    conv_bias,
    in_weight,
    in_bias,
    grn_gain,
    grn_bias,
    out_weight,
    out_bias,
    time_weight,
    time_bias,
    map_weight,
    map_bias,
    qkv_weight,
    qv_bias,
    proj_weight,
    proj_bias,
    cotangent,
):
    G, D, R = (lax.axis_size(axis) for axis in AXES)
    T = D * R
    q, c, z = (lax.axis_index(axis) for axis in AXES)
    N = latents.shape[1]
    C = latents.shape[2]
    pixels = R * N
    FFS = in_bias.shape[0]
    FL = G * FFS
    FF = in_weight.shape[1]
    cs = conv_bias.shape[0]
    ms = map_weight.shape[0]
    slots = clip_tokens.shape[1]
    text_all = R * slots
    HW = C // T
    even = G == R
    head_slice = R and (D * z + c)

    latents = latents[0]
    cotangent = cotangent[0]
    cols = columns_of(bucket_ids)[0]
    positions = z * N + jnp.arange(N, dtype=jnp.int32)
    keep = pixel_mask(positions, heights[0], widths[0], cols)[:, None]
    masked = latents * keep.astype(BF16)

    in_cut = in_weight.reshape(cs, G, T, FFS).transpose(2, 0, 1, 3).reshape(T, cs, FL)
    qkv_cut = qkv_weight.reshape(cs, 3, R, D, HW).transpose(3, 2, 0, 1, 4).reshape(T, cs, 3 * HW)
    mp = -(-ms // 16) * 16
    map_cut = jnp.pad(
        map_weight.reshape(ms, T, HW).transpose(1, 0, 2), ((0, 0), (0, mp - ms), (0, 0))
    )
    sp = -(-slots // 16) * 16
    clip_pad = pad_rows(clip_tokens[0], sp)
    meta = [
        conv_weight,
        conv_bias,
        out_bias,
        time_bias,
        map_bias,
        qv_bias,
        proj_bias,
        time_weight,
        time_embed,
        heights,
        widths,
        bucket_ids,
        text_mask,
    ]
    sizes = [piece.size for piece in meta]
    mrows = -(-sum(sizes) // 2048) * 16
    small = pack_flat(meta, mrows, BF16)
    frows = -(-3 * FFS // 2048) * 16
    fvec = pack_flat([in_bias, grn_gain, grn_bias], frows, BF16)

    def plan_start(p, ins, outs):
        edge_ref, small_ref, in_ref, qkv_ref, map_ref, clip_ref, fvec_ref = ins
        edge_out, small_out, in_out, qkv_out, map_out, clip_out, fvec_out = outs
        up, down = lax.rem(p.z + 1, R), lax.rem(p.z + R - 1, R)
        count = edge_ref.shape[0]
        messages = [
            (edge_ref.at[pl.ds(count - EDGE, EDGE)], edge_out.at[0], {"rows": up}, (), None),
            (edge_ref.at[pl.ds(0, EDGE)], edge_out.at[1], {"rows": down}, (), None),
        ]
        local = []
        mine = p.c * R + p.z
        stage, kept = group_gather(p, small_ref, small_out.at[mine])
        base = len(messages)
        messages += stage
        local += kept
        for c2, z2 in p.team():
            messages.append(
                (small_ref, small_out.at[mine, p.q], {"duo": c2, "rows": z2}, (), None)
            )
        for step, q2 in enumerate(range(1, G)):
            block = lax.rem(p.q - q2 + G, G)
            for c2, z2 in p.team():
                messages.append(
                    (
                        small_out.at[mine, block],
                        small_out.at[mine, block],
                        {"duo": c2, "rows": z2},
                        (base + step,),
                        None,
                    )
                )
        for ref, out in ((in_ref, in_out), (qkv_ref, qkv_out), (map_ref, map_out)):
            stage, kept = team_swap(p, ref, out)
            messages += stage
            local += kept
        stage, kept = team_gather(p, clip_ref, clip_out)
        messages += stage
        local += kept
        stage, kept = group_gather(p, fvec_ref, fvec_out)
        messages += stage
        local += kept
        return team_greet(p) + group_greet(p), messages, local

    count = 2 + (G - 1) + (T - 1) * G + 4 * (T - 1) + (G - 1)
    edges, small_all, in_rows, qkv_rows, map_rows, clip_all, fvec_all = exchange(
        0,
        "exchange_start",
        plan_start,
        [masked, small, in_cut, qkv_cut, map_cut, clip_pad, fvec],
        [
            ((2, EDGE, C), BF16),
            ((T, G, mrows, 128), BF16),
            ((T, cs, FL), BF16),
            ((T, cs, 3 * HW), BF16),
            ((T, mp, HW), BF16),
            ((T, sp, clip_tokens.shape[2]), BF16),
            ((G, frows, 128), BF16),
        ],
        count,
        6,
    )
    flat = small_all.reshape(D, R, G, mrows * 128).transpose(2, 0, 1, 3).reshape(T * G, -1)
    parts = []
    at = 0
    for size in sizes:
        parts.append(flat[:, at : at + size])
        at += size
    shards = T * G

    def whole(part):
        return part.reshape(-1)

    kernel_full = parts[0].reshape(shards, 9, cs).transpose(1, 0, 2).reshape(9, C).astype(F32)
    conv_bias_full = whole(parts[1]).astype(F32)
    out_bias_full = whole(parts[2]).astype(F32)
    time_bias_full = whole(parts[3]).astype(F32)
    map_bias_full = whole(parts[4]).astype(F32)
    qv_full = whole(parts[5]).astype(F32)
    proj_bias_full = whole(parts[6]).astype(F32)
    time_full = parts[7].reshape(shards, time_weight.shape[0], -1).transpose(1, 0, 2)
    time_full = time_full.reshape(time_weight.shape[0], -1)
    per_item = [part.reshape(G, D, R, -1)[:, :, 0] for part in parts[8:]]
    embed_all = per_item[0].reshape(G * D, -1).astype(F32)
    pair = [lax.dynamic_index_in_dim(part, q, 0, keepdims=False) for part in per_item[1:]]
    pair_height, pair_width, pair_bucket = (part.astype(jnp.int32) for part in pair[:3])
    pair_cols = columns_of(pair_bucket)
    pair_keep = pixel_mask(
        jnp.arange(pixels, dtype=jnp.int32)[None, :], pair_height, pair_width, pair_cols
    )
    text_keep = pair[3].astype(F32) * (jnp.arange(text_all) < TXT).astype(F32)[None, :]
    key_keep = jnp.concatenate([pair_keep, text_keep], axis=1)
    fv = fvec_all.reshape(G, -1)[:, : 3 * FFS].reshape(G, 3, FFS).transpose(1, 0, 2)
    in_bias_s, gain_s, grn_bias_s = fv.reshape(3, FL).astype(F32)

    def extend(low, mid, high):
        return jnp.concatenate(
            [
                jnp.where(z > 0, low, jnp.zeros_like(low)),
                mid,
                jnp.where(z < R - 1, high, jnp.zeros_like(high)),
            ],
            axis=0,
        )

    column = (positions % cols)[:, None]

    def tap(extended, dy, dx):
        piece = lax.dynamic_slice_in_dim(extended, EDGE + dy * cols + dx, N, axis=0).astype(F32)
        ok = (column + dx >= 0) & (column + dx < cols)
        return jnp.where(ok, piece, 0.0)

    extended = extend(edges[0], masked, edges[1])
    conv_out = jnp.zeros((N, C), F32) + conv_bias_full
    for index in range(9):
        conv_out = conv_out + tap(extended, index // 3 - 1, index % 3 - 1) * kernel_full[index]
    norm_hat, norm_inv = layer_stats(conv_out)
    normed = norm_hat.astype(BF16)

    def plan_first(p, ins, outs):
        messages, local = item_gather(p, ins[0], outs[0], 0)
        for ref, out in zip(ins[1:], outs[1:]):
            stage, kept = group_gather(p, ref, out)
            messages += stage
            local += kept
        return rows_greet(p) + duo_greet(p) + group_greet(p), messages, local

    normed_all, in_full, out_full, map_full = exchange(
        1,
        "exchange_normed",
        plan_first,
        [normed, in_rows, out_weight, map_rows],
        [
            ((D, R, N, C), BF16),
            ((G,) + in_rows.shape, BF16),
            ((G,) + out_weight.shape, BF16),
            ((G,) + map_rows.shape, BF16),
        ],
        2 * R - 1 + 3 * (G - 1),
        4,
    )
    normed_all = normed_all.reshape(D * pixels, C)
    in_full = in_full.reshape(C, FL)
    out_full = out_full.reshape(FL, C)
    map_full = map_full[:, :, :ms].reshape(G * T * ms, HW)
    keep_all = pair_keep.reshape(D, pixels, 1)

    hidden = mm(normed_all, in_full) + in_bias_s
    gate = 0.5 * lax.erfc(-hidden * (0.5**0.5))
    active = hidden * gate
    active3 = active.reshape(D, pixels, FL)
    squares = jnp.sum(keep_all * active3 * active3, axis=1)
    grn_norms = jnp.sqrt(squares)

    def team_total(ident, name, values):
        block = jnp.zeros((8, 128), F32).at[0, :D].set(values)

        def plan(p, ins, outs):
            messages, local = team_gather(p, ins[0], outs[0])
            return team_greet(p), messages, local

        (everyone,) = exchange(
            ident, name, plan, [block], [((T, 8, 128), F32)], T - 1, 1
        )
        return jnp.sum(everyone[:, 0, :D], axis=0)

    norm_mean = (team_total(2, "total_norms", jnp.sum(grn_norms, axis=1)) / FF + grn_eps)[:, None]
    grn_ratio = grn_norms / norm_mean
    grn_out = (
        (gain_s * (active3 * grn_ratio[:, None, :]) + grn_bias_s + active3)
        .astype(BF16)
        .reshape(D * pixels, FL)
    )
    branch = reduce_items(
        3, "reduce_branch", mm(grn_out, out_full).astype(BF16).reshape(D, R, N, C)
    )
    branch = branch + out_bias_full
    after_res = latents.astype(F32) + keep * branch
    modulate = mm(time_embed, time_full) + time_bias_full
    scale_by = 1.0 + modulate[:, :C]
    second = after_res * scale_by + modulate[:, C:]
    two_hat, two_inv = layer_stats(second)
    normed_two = two_hat.astype(BF16)

    silu_text = jax.nn.silu(clip_all[:, :slots].astype(F32)).astype(BF16)
    silu_text = silu_text.reshape(D * text_all, -1)
    map_bias_s = lax.dynamic_slice_in_dim(map_bias_full, (c * R + z) * HW, HW)
    mapped_s = (mm(silu_text, map_full) + map_bias_s).astype(BF16)
    grad_result = (keep * cotangent.astype(F32)).astype(BF16)

    def plan_second(p, ins, outs):
        two, grad, text, qkv = ins[:4]
        messages, local = item_gather(p, two, outs[0], 0)
        stage, kept = team_gather(p, text, outs[2])
        messages += stage
        local += kept
        stage, kept = item_gather(p, grad, outs[1], len(messages))
        messages += stage
        local += kept
        stage, kept = group_gather(p, qkv, outs[3])
        messages += stage
        local += kept
        greet = team_greet(p) + group_greet(p)
        if even:
            proj, proj_out = ins[4], outs[4]
            selfish = p.q == p.z
            for step in range(G):
                to = lax.rem(p.z + step, G)
                where = {"grp": to, "duo": p.c, "rows": p.q}
                when = None if step else p.q != p.z
                messages.append((proj, proj_out.at[p.z], where, (), when))
                source = {"grp": p.z, "duo": p.c, "rows": lax.rem(p.q - step + G, G)}
                greet.append((source, when))
            local.append((proj, proj_out.at[p.z], selfish))
        return greet, messages, local

    arrays = [normed_two, grad_result, mapped_s, qkv_rows]
    results = [
        ((D, R, N, C), BF16),
        ((D, R, N, C), BF16),
        ((T,) + mapped_s.shape, BF16),
        ((G,) + qkv_rows.shape, BF16),
    ]
    if even:
        arrays.append(proj_weight)
        results.append(((R,) + proj_weight.shape, BF16))
    gathered = exchange(
        4,
        "exchange_second",
        plan_second,
        arrays,
        results,
        2 * (2 * R - 1) + T - 1 + G - 1 + (G if even else 0),
        5,
    )
    two_all = gathered[0].reshape(D * pixels, C)
    gres_all = gathered[1].reshape(D * pixels, C)
    mapped = gathered[2].transpose(1, 0, 2).reshape(D * text_all, C)
    qkv_full = gathered[3].reshape(C, 3 * HW)
    if even:
        proj_s = gathered[4].reshape(HW, C)
    else:
        proj_whole = lax.all_gather(proj_weight, AXES, axis=0, tiled=True)
        proj_s = lax.dynamic_slice_in_dim(proj_whole, head_slice * HW, HW, axis=0)

    q_bias = lax.dynamic_slice_in_dim(qv_full, head_slice * HW, HW)
    v_bias = lax.dynamic_slice_in_dim(qv_full, C + head_slice * HW, HW)
    projected = mm(two_all, qkv_full)
    heads = HW // HEAD

    def split(values):
        return values.astype(BF16).reshape(D, -1, heads, HEAD)

    queries = split(projected[:, :HW] + q_bias)
    text_kv = mm(mapped, qkv_full[:, HW:])
    keys = jnp.concatenate([split(projected[:, HW : 2 * HW]), split(text_kv[:, :HW])], axis=1)
    values = jnp.concatenate(
        [split(projected[:, 2 * HW :] + v_bias), split(text_kv[:, HW:] + v_bias)], axis=1
    )
    score_scale = HEAD ** (-0.5)

    def dots(spec, left, right):
        return jnp.einsum(spec, left, right, preferred_element_type=F32)

    scores = dots("iqhd,ikhd->ihqk", queries, keys) * score_scale
    scores = jnp.where(key_keep[:, None, None, :] > 0, scores, masked_score)
    weights = jnp.exp(scores - jnp.max(scores, axis=-1, keepdims=True))
    probs = weights / jnp.sum(weights, axis=-1, keepdims=True)
    probs_low = probs.astype(BF16)
    attended = dots("ihqk,ikhd->iqhd", probs_low, values).astype(BF16).reshape(D * pixels, HW)
    result_part = mm(attended, proj_s).astype(BF16).reshape(D, R, N, C)
    grad_att = split(mm_t(gres_all, proj_s))
    grad_probs = dots("iqhd,ikhd->ihqk", grad_att, values)
    grad_values = dots("ihqk,iqhd->ikhd", probs_low, grad_att).astype(BF16)
    row_sums = jnp.sum(probs * grad_probs, axis=-1, keepdims=True)
    grad_scores = (probs * (grad_probs - row_sums)).astype(BF16)
    grad_queries = (dots("ihqk,ikhd->iqhd", grad_scores, keys) * score_scale).astype(BF16)
    grad_keys = (dots("ihqk,iqhd->ikhd", grad_scores, queries) * score_scale).astype(BF16)
    grad_pixel = jnp.concatenate(
        [
            piece.reshape(D * pixels, HW)
            for piece in (grad_queries, grad_keys[:, :pixels], grad_values[:, :pixels])
        ],
        axis=1,
    )
    grad_text = jnp.concatenate(
        [
            piece.reshape(D * text_all, HW)
            for piece in (grad_keys[:, pixels:], grad_values[:, pixels:])
        ],
        axis=1,
    )
    grad_qkv = t_mm(two_all, grad_pixel) + jnp.pad(t_mm(mapped, grad_text), ((0, 0), (HW, 0)))
    q_bias_grad = jnp.sum(grad_pixel[:, :HW].astype(F32), axis=0)
    v_bias_grad = jnp.sum(grad_pixel[:, 2 * HW :].astype(F32), axis=0) + jnp.sum(
        grad_text[:, HW:].astype(F32), axis=0
    )
    grad_proj = t_mm(attended, gres_all)
    mapped_part = mm_t(grad_text, qkv_full[:, HW:]).astype(BF16)
    mapped_part = mapped_part.reshape(D * text_all, T, HW).transpose(1, 0, 2)
    two_part = mm_t(grad_pixel, qkv_full).astype(BF16).reshape(D, R, N, C)

    result = reduce_items(5, "reduce_result", result_part) + proj_bias_full
    output = (second + keep * result).astype(BF16)
    grad_two = reduce_items(6, "reduce_two", two_part)

    grad_output = cotangent.astype(F32)
    grad_second = grad_output + layer_back(grad_two, two_hat, two_inv)
    grad_modulate = jnp.concatenate(
        [jnp.sum(grad_second * after_res, axis=0), jnp.sum(grad_second, axis=0)]
    )
    grad_after = grad_second * scale_by
    grad_branch = (keep * grad_after).astype(BF16)

    def plan_third(p, ins, outs):
        messages, local = item_gather(p, ins[0], outs[0], 0)
        stage, kept = team_swap(p, ins[1], outs[1])
        messages += stage
        local += kept
        stage, kept = group_swap(p, ins[2], outs[2])
        messages += stage
        local += kept
        greet = team_greet(p) + group_greet(p)
        if even:
            proj, proj_out = ins[3], outs[3]
            for step in range(G):
                to = lax.rem(p.q + step, G)
                where = {"grp": p.z, "duo": p.c, "rows": to}
                when = None if step else p.q != p.z
                messages.append((proj.at[to], proj_out.at[p.q], where, (), when))
                source = {"grp": lax.rem(p.z - step + G, G), "duo": p.c, "rows": p.q}
                greet.append((source, when))
            local.append((proj.at[p.z], proj_out.at[p.q], p.q == p.z))
        return greet, messages, local

    arrays = [grad_branch, mapped_part, grad_qkv.astype(BF16).reshape(G, T * cs, 3 * HW)]
    results = [
        ((D, R, N, C), BF16),
        (mapped_part.shape, BF16),
        ((G, T * cs, 3 * HW), BF16),
    ]
    if even:
        arrays.append(grad_proj.astype(BF16).reshape(R, cs, C))
        results.append(((R, cs, C), BF16))
    gathered = exchange(
        7,
        "exchange_branch",
        plan_third,
        arrays,
        results,
        2 * R - 1 + T - 1 + G - 1 + (G if even else 0),
        4,
    )
    gb_all = gathered[0].reshape(D * pixels, C)
    grad_mapped = jnp.sum(gathered[1].astype(F32), axis=0).astype(BF16)
    qkv_sum = jnp.sum(gathered[2].astype(F32), axis=0).astype(BF16).reshape(T, cs, 3 * HW)
    if even:
        grad_proj_out = jnp.sum(gathered[3].astype(F32), axis=0)
    else:
        spread = jnp.zeros((C, C), F32)
        spread = lax.dynamic_update_slice_in_dim(spread, grad_proj, head_slice * HW, axis=0)
        grad_proj_out = lax.psum_scatter(spread, AXES, scatter_dimension=0, tiled=True)
    grad_map = t_mm(silu_text, grad_mapped).astype(BF16)
    grad_map = jnp.pad(
        grad_map.reshape(G, T, ms, HW), ((0, 0), (0, 0), (0, mp - ms), (0, 0))
    )
    map_bias_grad = jnp.sum(grad_mapped.astype(F32), axis=0)

    grad_out = t_mm(grn_out, gb_all).astype(BF16).reshape(G, FFS, C)
    grad_grn = mm_t(gb_all, out_full)
    grad_grn3 = grad_grn.reshape(D, pixels, FL)
    moment = jnp.sum(grad_grn3 * active3, axis=1)
    grad_gain = jnp.sum(moment * grn_ratio, axis=0)
    grad_grn_bias = jnp.sum(grad_grn, axis=0)
    ratio_grad = moment * gain_s
    cross = team_total(8, "total_cross", jnp.sum(ratio_grad * grn_norms, axis=1))[:, None]
    grad_norms = ratio_grad / norm_mean - cross / (FF * norm_mean * norm_mean)
    grad_active = (
        grad_grn3 * (gain_s * grn_ratio[:, None, :] + 1.0)
        + keep_all * active3 * (grad_norms / grn_norms)[:, None, :]
    ).reshape(D * pixels, FL)
    density = jnp.exp(-0.5 * hidden * hidden) * 0.3989422804014327
    grad_hidden = (grad_active * (gate + hidden * density)).astype(BF16)
    grad_in_bias = jnp.sum(grad_hidden.astype(F32), axis=0)
    grad_in = t_mm(normed_all, grad_hidden).astype(BF16).reshape(G, T * cs, FL)
    back_part = mm_t(grad_hidden, in_full).astype(BF16).reshape(D, R, N, C)

    def plan_fourth(p, ins, outs):
        messages, local = [], []
        for ref, out in zip(ins[:3], outs[:3]):
            stage, kept = group_swap(p, ref, out)
            messages += stage
            local += kept
        stage, kept = team_swap(p, ins[3], outs[3])
        messages += stage
        local += kept
        return team_greet(p) + group_greet(p), messages, local

    fgrads = jnp.stack([grad_in_bias, grad_gain, grad_grn_bias]).reshape(3, G, FFS)
    fgrads = fgrads.transpose(1, 0, 2).reshape(G, -1)
    grows = -(-fgrads.shape[1] // 1024) * 8
    fgrads = jnp.pad(fgrads, ((0, 0), (0, grows * 128 - fgrads.shape[1]))).reshape(G, grows, 128)

    grad_conv_in = reduce_items(9, "reduce_back", back_part)
    out_sum, in_sum, map_sum, qkv_team = exchange(
        10,
        "exchange_grads",
        plan_fourth,
        [grad_out, grad_in, grad_map.reshape(G, T * mp, HW), qkv_sum],
        [
            (grad_out.shape, BF16),
            (grad_in.shape, BF16),
            ((G, T * mp, HW), BF16),
            (qkv_sum.shape, BF16),
        ],
        3 * (G - 1) + T - 1,
        4,
    )
    grad_out_shard = jnp.sum(out_sum.astype(F32), axis=0)
    grad_conv = layer_back(grad_conv_in, norm_hat, norm_inv)
    taps = [
        jnp.sum(tap(extended, index // 3 - 1, index % 3 - 1) * grad_conv, axis=0)
        for index in range(9)
    ]
    in_back = jnp.sum(in_sum.astype(F32), axis=0).astype(BF16).reshape(T, cs, FL)
    map_back = jnp.sum(map_sum.astype(F32), axis=0).astype(BF16).reshape(T, mp, HW)

    def by_shard(values):
        return values.reshape(shards, -1)

    def placed(values, start, size):
        return lax.dynamic_update_slice_in_dim(jnp.zeros((size,), F32), values, start, axis=0)

    map_bias_vec = placed(map_bias_grad, (c * R + z) * HW, C)
    qv_vec = jnp.concatenate(
        [
            placed(q_bias_grad, head_slice * HW, C),
            placed(v_bias_grad, head_slice * HW, C),
        ]
    )
    pieces = [
        jnp.stack(taps).reshape(9, shards, cs).transpose(1, 0, 2).reshape(shards, -1),
        by_shard(jnp.sum(grad_conv, axis=0)),
        by_shard(jnp.sum(grad_branch.astype(F32), axis=0)),
        by_shard(jnp.sum(grad_result.astype(F32), axis=0)),
        by_shard(map_bias_vec),
        by_shard(qv_vec),
        by_shard(grad_modulate),
    ]
    widths_of = [piece.shape[1] for piece in pieces]
    tiny = jnp.concatenate(pieces, axis=1)
    trows = -(-tiny.shape[1] // 1024) * 8
    tiny = jnp.pad(tiny, ((0, 0), (0, trows * 128 - tiny.shape[1])))
    tiny = tiny.reshape(G, T, trows, 128).transpose(1, 0, 2, 3)

    def plan_fifth(p, ins, outs):
        up, down = lax.rem(p.z + 1, R), lax.rem(p.z + R - 1, R)
        conv_ref = ins[0]
        count = conv_ref.shape[0]
        messages = [
            (conv_ref.at[pl.ds(count - EDGE, EDGE)], outs[0].at[0], {"rows": up}, (), None),
            (conv_ref.at[pl.ds(0, EDGE)], outs[0].at[1], {"rows": down}, (), None),
        ]
        local = []
        for ref, out in zip(ins[1:4], outs[1:4]):
            stage, kept = team_swap(p, ref, out)
            messages += stage
            local += kept
        stage, kept = group_swap(p, ins[4], outs[4])
        messages += stage
        local += kept
        return team_greet(p) + group_greet(p), messages, local

    conv_low = grad_conv.astype(BF16)
    conv_edges, tiny_team, in_team, map_team, f_sum = exchange(
        11,
        "exchange_tail",
        plan_fifth,
        [conv_low, tiny, in_back, map_back, fgrads],
        [
            ((2, EDGE, C), BF16),
            (tiny.shape, F32),
            (in_back.shape, BF16),
            (map_back.shape, BF16),
            (fgrads.shape, F32),
        ],
        2 + 3 * (T - 1) + G - 1,
        4,
    )
    tiny_items = jnp.sum(tiny_team.reshape(D, R, G, trows, 128), axis=1).transpose(1, 0, 2, 3)

    def plan_sixth(p, ins, outs):
        messages, local = group_swap(p, ins[0], outs[0])
        return group_greet(p), messages, local

    (tiny_all,) = exchange(
        12,
        "exchange_tiny",
        plan_sixth,
        [tiny_items],
        [((G, D, trows, 128), F32)],
        G - 1,
        1,
    )
    tiny_all = tiny_all.reshape(G * D, -1)
    tiny_sum = jnp.sum(tiny_all, axis=0)
    outs = []
    at = 0
    for width in widths_of[:-1]:
        outs.append(tiny_sum[at : at + width])
        at += width
    modulate_items = tiny_all[:, at : at + widths_of[-1]]
    grad_time = lax.dot_general(
        embed_all,
        modulate_items,
        (((0,), (0,)), ((), ())),
        precision=lax.Precision.HIGHEST,
    )
    grad_time_bias = jnp.sum(modulate_items, axis=0)

    grad_extended = extend(conv_edges[0], conv_low, conv_edges[1])
    spread = jnp.zeros((N, C), F32)
    for index in range(9):
        spread = spread + tap(grad_extended, 1 - index // 3, 1 - index % 3) * kernel_full[index]
    grad_latents = grad_after + keep * spread

    grad_in_shard = in_team.astype(F32).reshape(T, cs, G, FFS).transpose(1, 2, 0, 3).reshape(cs, FF)
    grad_map_shard = map_team[:, :ms].astype(F32).transpose(1, 0, 2).reshape(ms, C)
    grad_qkv_shard = (
        qkv_team.astype(F32)
        .reshape(D, R, cs, 3, HW)
        .transpose(2, 3, 1, 0, 4)
        .reshape(cs, 3 * C)
    )
    f_total = jnp.sum(f_sum, axis=0).reshape(-1)
    return (
        output[None],
        grad_latents[None],
        outs[0].reshape(9, cs),
        outs[1],
        grad_in_shard,
        f_total[:FFS],
        f_total[FFS : 2 * FFS],
        f_total[2 * FFS : 3 * FFS],
        grad_out_shard,
        outs[2],
        grad_time,
        grad_time_bias,
        grad_map_shard,
        outs[4],
        grad_qkv_shard,
        outs[5],
        grad_proj_out,
        outs[3],
    )


def solution(mesh):
    items, rows = mesh.devices.shape
    fine = Mesh(mesh.devices.reshape(items // 2, 2, rows), AXES)
    item = ("grp", "duo")
    full = AXES
    ins = (
        P(item, "rows", None),
        P(item, "rows", None),
        P(item, None),
        P(item),
        P(item),
        P(item),
        P(item, None),
        P(None, full),
        P(full),
        P(full, None),
        P(full),
        P(full),
        P(full),
        P(full, None),
        P(full),
        P(None, full),
        P(full),
        P(full, None),
        P(full),
        P(full, None),
        P(full),
        P(full, None),
        P(full),
        P(item, "rows", None),
    )
    outs = (
        P(item, "rows", None),
        P(item, "rows", None),
        P(None, full),
        P(full),
        P(full, None),
        P(full),
        P(full),
        P(full),
        P(full, None),
        P(full),
        P(None, full),
        P(full),
        P(full, None),
        P(full),
        P(full, None),
        P(full),
        P(full, None),
        P(full),
    )
    return jax.shard_map(body, mesh=fine, in_specs=ins, out_specs=outs, check_vma=False)
```

time: 2640 us -> 975 us (0.37)
  waiting for transfers between devices: 1920 us -> 0 us
  Pallas kernels: 0 us -> 705 us
  blocking collectives: 221 us -> 0 us
  local copies, waits for them, and re-layouts: 206 us -> 83.6 us
  matrix products: 183 us -> 101 us
    reduce_scatter x5 -> x0, waiting for transfers between devices: 1250 us -> none  [the longest x1 356 us: body(): lax.psum_scatter(grad_in, ('items', 'rows'), scatter_dimension=0, tiled=T...]
    pallas_call x0 -> x13, Pallas kernels: none -> 705 us  [the longest x9 544 us: exchange(): pl.pallas_call(functools.partial(run_plan, plan, len(arrays), len(results...]
    unnamed x20 -> x0, waiting for transfers between devices: 349 us -> none
    all_gather x7 -> x0, waiting for transfers between devices: 317 us -> none  [the longest x1 86.1 us: body(): lax.all_gather(out_weight, ('items', 'rows'), axis=0, tiled=True)]
    all_gather x2 -> x0, blocking collectives: 141 us -> none  [the longest x1 74.5 us: body(): lax.all_gather(time_weight, ('items', 'rows'), axis=1, tiled=True)]
    dot_general x101 -> x24, matrix products: 183 us -> 94.2 us  [the longest x7 27.8 us: mm(): return jnp.dot(left, right, preferred_element_type=F32)]
    gather x27 -> x0, local copies, waits for them, and re-layouts: 64.8 us -> none  [tap_values(): item_rows[item_index]]
    dynamic_slice x84 -> x2, local copies, waits for them, and re-layouts: 46.2 us -> 0.72 us  [the longest x1 0.65 us: body(): q_bias = lax.dynamic_slice_in_dim(qv_full, head_slice * HW, HW)]
  transfers between devices with their start and end apart: 20 -> 0, of which waited for: 14 -> 0; matrix products, arithmetic and copies ran while one was open for 10% -> 0% of each run, Pallas kernels for 0% -> 0%
where the time goes in v1:
time: 975 us; the launch traced here: 965 us
  Pallas kernels  705 us (72%)
  matrix products  101 us (10%)
  local copies, waits for them, and re-layouts  83.6 us (9%)
  other arithmetic  69.9 us (7%)
    pallas_call x9, Pallas kernels, exchange(): pl.pallas_call(functools.partial(run_plan, plan, len(arrays), len(results...  544 us
    pallas_call x4, Pallas kernels, reduce_items(): pl.pallas_call(kernel, out_shape=jax.ShapeDtypeStruct((count, width), F32...  161 us
    dot_general x7, matrix products, mm(): return jnp.dot(left, right, preferred_element_type=F32)  27.8 us
    dot_general x5, matrix products, dots(): return jnp.einsum(spec, left, right, preferred_element_type=F32)  24.1 us
    dot_general x6, matrix products, t_mm(): lax.dot_general(left, right, (((0,), (0,)), ((), ())), preferred_element_...  22.5 us

profile of v1, /device:TPU:0, one launch (start us, length us, event | category | flops | bytes accessed | tf_op | source)
XLA Modules:
  0.0 964.6 jit_solution(16625611123213068126)
XLA Ops:
  23.9 64.6 %exchange_start.1 = (bf16[2,48,1536]{2,1,0:T(8,128)(2,1)}, bf16[8,4,64,128]{3,2,1,0:T(8,128)(2,1)}, bf16[8,48,768]{2,1,0:T(8,128)(2,1)}, bf16[8,48,576]{2,1,0:T(...) custom-call(bf16[144,1536]{1,0:T(8,128)(2,1)} %bitcast_multiply_fusion.3.refs_0_, ...), custom_call_target="tpu_custom_call" | custom-call | tf_op jit(solution)/shard_map/exchange_start/pallas_call | solution.py:106
  111.8 96.4 %exchange_normed.1 = (bf16[2,4,144,1536]{3,2,1,0:T(8,128)(2,1)}, bf16[4,8,48,768]{3,2,1,0:T(8,128)(2,1)}, bf16[4,192,1536]{2,1,0:T(8,128)(2,1)}, bf16[4,8,48,192]{3,2,1,0:T(8,128)(2,1)}) custom-call(bf16[144,1536]{1,0:T(8,128)(2,1)} %fusion.58.refs_0_, bf16[8,48,768]{2,1,0:T(8,128)(2,1)} %get-tuple-element.74.refs_1_, bf16[192,1536]{1,0:T(8,128)(2,1)} %refs_2_.1, ...), custom_call_target="tpu_custom_call" | custom-call | tf_op jit(solution)/shard_map/exchange_normed/pallas_call | solution.py:106
  210.2 14.0 %fusion.106 = (f32[1152,768]{1,0:T(8,128)S(1)}, f32[1152,768]{1,0:T(8,128)}, f32[1152,768]{1,0:T(8,128)}) fusion(f32[768]{0:T(1024)S(1)} %add.527, bf16[1152,1536]{1,0:T(8,128)(2,1)} %bitcast.282, bf16[1536,768]{1,0:T(8,128)(2,1)} %bitcast.288), kind=kOutput, calls=%fused_computation.285 | convolution fusion | flops 2775416832 | bytes 16518144 | tf_op jit(solution)/shard_map/dot_general | solution.py:198
  225.8 14.5 %total_norms.1 = f32[8,8,128]{2,1,0:T(8,128)} custom-call(f32[8,128]{1,0:T(8,128)} %scatter.6.refs_0_), custom_call_target="tpu_custom_call" | custom-call | tf_op jit(solution)/shard_map/total_norms/pallas_call | solution.py:106
  248.4 35.4 %reduce_branch.1 = f32[144,1536]{1,0:T(8,128)S(1)} custom-call(bf16[2,4,144,1536]{3,2,1,0:T(8,128)(2,1)S(1)} %bitcast.224), custom_call_target="tpu_custom_call" | custom-call | tf_op jit(solution)/shard_map/reduce_branch/pallas_call | solution.py:274
  286.8 145.0 %exchange_second.1 = (bf16[2,4,144,1536]{3,2,1,0:T(8,128)(2,1)}, bf16[2,4,144,1536]{3,2,1,0:T(8,128)(2,1)}, bf16[8,160,192]{2,1,0:T(8,128)(2,1)}, bf16[4,8,48,576]{3,2,1,0:T(8,128)(2,1)}, bf16[4,48,1536]{2,1,0:T(8,128)(2,1)}) custom-call(bf16[144,1536]{1,0:T(8,128)(2,1)} %fusion.59.refs_0_, bf16[144,1536]{1,0:T(8,128)(2,1)} %get-tuple-element.149.refs_1_, ...), custom_call_target="tpu_custom_call" | custom-call | tf_op jit(solution)/shard_map/exchange_second/pallas_call | solution.py:106
  441.0 5.3 fusion.119
  450.6 6.4 fusion.114
  457.1 4.8 fusion.41
  466.6 5.6 fusion.37
  477.1 46.1 %reduce_result.1 = f32[144,1536]{1,0:T(8,128)S(1)} custom-call(bf16[2,4,144,1536]{3,2,1,0:T(8,128)(2,1)S(1)} %bitcast.221), custom_call_target="tpu_custom_call" | custom-call | tf_op jit(solution)/shard_map/reduce_result/pallas_call | solution.py:274
  523.2 7.7 multiply_reduce_fusion
  530.9 10.2 %multiply_convert_fusion = bf16[2,3,576,656]{2,3,1,0:T(8,128)(2,1)} fusion(f32[2,3,576,656]{2,3,1,0:T(8,128)} %get-tuple-element.194, f32[2,3,576]{2,1,0:T(4,128)S(1)} %get-tuple-element.193, f32[2,3,576,656]{2,3,1,0:T(8,128)} %get-tuple-element.192, f32[2,3,576]{2,1,0:T(4,128)S(1)} %get-tuple-element.191), kind=kLoop, calls=%fused_computation.1 | loop fusion | flops 9068544 | bytes 22699008 | tf_op jit(solution)/shard_map/convert_element_type | solution.py:650
  568.5 44.0 %reduce_two.1 = f32[144,1536]{1,0:T(8,128)S(1)} custom-call(bf16[2,4,144,1536]{3,2,1,0:T(8,128)(2,1)S(1)} %bitcast.223), custom_call_target="tpu_custom_call" | custom-call | tf_op jit(solution)/shard_map/reduce_two/pallas_call | solution.py:274
  621.8 4.9 add_convert_fusion
  629.0 87.7 %exchange_branch.1 = (bf16[2,4,144,1536]{3,2,1,0:T(8,128)(2,1)}, bf16[8,160,192]{2,1,0:T(8,128)(2,1)}, bf16[4,384,576]{2,1,0:T(8,128)(2,1)}, bf16[4,48,1536]{2,1,0:T(8,128)(2,1)}) custom-call(bf16[144,1536]{1,0:T(8,128)(2,1)} %get-tuple-element.151.refs_0_, bf16[8,160,192]{2,1,0:T(8,128)(2,1)} %bitcast.236, bf16[4,384,576]{2,1,0:T(8,128)(2,1)} %bitcast.228, ...), custom_call_target="tpu_custom_call" | custom-call | tf_op jit(solution)/shard_map/exchange_branch/pallas_call | solution.py:106
  724.0 7.3 convolution_convert_fusion.5
  739.3 24.0 %total_cross.1 = f32[8,8,128]{2,1,0:T(8,128)} custom-call(f32[8,128]{1,0:T(8,128)} %scatter.9.refs_0_), custom_call_target="tpu_custom_call" | custom-call | tf_op jit(solution)/shard_map/total_cross/pallas_call | solution.py:106
  765.6 5.3 convert_reduce_fusion.1
  775.6 67.8 %exchange_grads.1 = (bf16[4,192,1536]{2,1,0:T(8,128)(2,1)}, bf16[4,384,768]{2,1,0:T(8,128)(2,1)}, bf16[4,384,192]{2,1,0:T(8,128)(2,1)}, bf16[8,48,576]{2,1,0:T(8,128)(2,1)}) custom-call(bf16[4,192,1536]{2,1,0:T(8,128)(2,1)} %bitcast.240, bf16[4,384,768]{2,1,0:T(8,128)(2,1)} %bitcast.241, bf16[4,384,192]{2,1,0:T(8,128)(2,1)} %bitcast.235, ...), custom_call_target="tpu_custom_call" | custom-call | tf_op jit(solution)/shard_map/exchange_grads/pallas_call | solution.py:106
  850.6 5.0 convolution_convert_fusion
  855.8 35.4 %reduce_back.1 = f32[144,1536]{1,0:T(8,128)S(1)} custom-call(bf16[2,4,144,1536]{3,2,1,0:T(8,128)(2,1)S(1)} %bitcast.222), custom_call_target="tpu_custom_call" | custom-call | tf_op jit(solution)/shard_map/reduce_back/pallas_call | solution.py:274
  897.3 38.4 %exchange_tail.1 = (bf16[2,48,1536]{2,1,0:T(8,128)(2,1)}, f32[8,4,8,128]{3,2,1,0:T(8,128)}, bf16[8,48,768]{2,1,0:T(8,128)(2,1)}, bf16[8,48,192]{2,1,0:T(8,128)(2,1)}, f32[4,8,128]{2,1,0:T(8,128)}) custom-call(bf16[144,1536]{1,0:T(8,128)(2,1)} %get-tuple-element.152.refs_0_, f32[8,4,8,128]{3,2,1,0:T(8,128)} %copy_bitcast_fusion.7.refs_1_, ...), custom_call_target="tpu_custom_call" | custom-call | tf_op jit(solution)/shard_map/exchange_tail/pallas_call | solution.py:106
  939.7 6.0 exchange_tiny.1
  (464 shorter events, 177.7 us)
Async XLA Ops:
  4.1 102.1 %copy-start.92 = (pred[144]{0:T(512)(128)(4,1)}, pred[144]{0:T(512)(128)(4,1)S(1)}, u32[]{:S(2)}) copy-start(pred[144]{0:T(512)(128)(4,1)S(1)} %get-tuple-element.199) | copy-start | bytes 436
  4.2 101.9 %copy-start.88 = (pred[144]{0:T(512)(128)(4,1)}, pred[144]{0:T(512)(128)(4,1)S(1)}, u32[]{:S(2)}) copy-start(pred[144]{0:T(512)(128)(4,1)S(1)} %get-tuple-element.197) | copy-start | bytes 436
  4.2 101.9 %copy-start.90 = (pred[144]{0:T(512)(128)(4,1)}, pred[144]{0:T(512)(128)(4,1)S(1)}, u32[]{:S(2)}) copy-start(pred[144]{0:T(512)(128)(4,1)S(1)} %get-tuple-element.198) | copy-start | bytes 436
  93.4 115.9 %copy-start.15 = (bf16[160,1280]{1,0:T(8,128)(2,1)}, bf16[160,1280]{1,0:T(8,128)(2,1)S(1)}, u32[]{:S(2)}) copy-start(bf16[160,1280]{1,0:T(8,128)(2,1)S(1)} %reshape.986) | copy-start | bytes 1228804
  109.9 99.4 %copy-start.75 = (f32[144]{0:T(256)}, f32[144]{0:T(256)S(1)}, u32[]{:S(2)}) copy-start(f32[144]{0:T(256)S(1)} %broadcast_multiply_fusion.6) | copy-start | bytes 1732
  110.8 98.5 %copy-start.81 = (f32[144]{0:T(256)}, f32[144]{0:T(256)S(1)}, u32[]{:S(2)}) copy-start(f32[144]{0:T(256)S(1)} %add_rsqrt_fusion.1) | copy-start | bytes 1732
  285.0 327.5 %copy-start.77 = (f32[144]{0:T(256)}, f32[144]{0:T(256)S(1)}, u32[]{:S(2)}) copy-start(f32[144]{0:T(256)S(1)} %broadcast_multiply_fusion.5) | copy-start | bytes 1732
  285.2 146.6 %copy-start.84 = (f32[144]{0:T(256)}, f32[144]{0:T(256)S(1)}, u32[]{:S(2)}) copy-start(f32[144]{0:T(256)S(1)} %add_rsqrt_fusion) | copy-start | bytes 1732
  477.1 46.1 %copy-start.36 = (bf16[2,576,3,64]{1,0,3,2:T(2,128)(2,1)S(1)}, bf16[2,576,3,64]{1,0,3,2:T(2,128)(2,1)}, u32[]{:S(2)}) copy-start(bf16[2,576,3,64]{1,0,3,2:T(2,128)(2,1)} %reshape.1001) | copy-start | bytes 1327108
  626.7 91.9 %copy-start.16 = (bf16[160,1280]{1,0:T(8,128)(2,1)S(1)}, bf16[160,1280]{1,0:T(8,128)(2,1)}, u32[]{:S(2)}) copy-start(bf16[160,1280]{1,0:T(8,128)(2,1)} %copy-done.15) | copy-start | bytes 1228804
  775.6 73.0 %copy-start.83 = (f32[1,4,192]{2,0,1:T(1,128)S(1)}, f32[1,4,192]{2,0,1:T(1,128)}, u32[]{:S(2)}) copy-start(f32[1,4,192]{2,0,1:T(1,128)} %stack.53) | copy-start | bytes 9220
  895.1 54.5 %copy-start.87 = (bf16[4,2,1,64]{3,1,2,0:T(2,128)(2,1)S(1)}, bf16[4,2,1,64]{3,1,2,0:T(2,128)(2,1)}, u32[]{:S(2)}) copy-start(bf16[4,2,1,64]{3,1,2,0:T(2,128)(2,1)} %copy.180) | copy-start | bytes 3076
  895.1 57.3 %copy-start.12 = (bf16[144,1536]{1,0:T(8,128)(2,1)S(1)}, bf16[144,1536]{1,0:T(8,128)(2,1)}, u32[]{:S(2)}) copy-start(bf16[144,1536]{1,0:T(8,128)(2,1)} %get-tuple-element.152.refs_0_) | copy-start | bytes 1327108
  896.0 56.4 %copy-start.11 = (f32[144,1536]{1,0:T(8,128)S(1)}, f32[144,1536]{1,0:T(8,128)}, u32[]{:S(2)}) copy-start(f32[144,1536]{1,0:T(8,128)} %copy-done.10) | copy-start | bytes 2654212
  896.0 56.4 %copy-start.44 = (f32[1536]{0:T(1024)S(1)}, f32[1536]{0:T(1024)}, u32[]{:S(2)}) copy-start(f32[1536]{0:T(1024)} %copy-done.43) | copy-start | bytes 18436
  896.1 56.4 %copy-start.46 = (f32[1536]{0:T(1024)S(1)}, f32[1536]{0:T(1024)}, u32[]{:S(2)}) copy-start(f32[1536]{0:T(1024)} %copy-done.45) | copy-start | bytes 18436
  896.1 56.4 %copy-start.48 = (f32[1536]{0:T(1024)S(1)}, f32[1536]{0:T(1024)}, u32[]{:S(2)}) copy-start(f32[1536]{0:T(1024)} %copy-done.47) | copy-start | bytes 18436
  896.1 56.4 %copy-start.50 = (f32[1536]{0:T(1024)S(1)}, f32[1536]{0:T(1024)}, u32[]{:S(2)}) copy-start(f32[1536]{0:T(1024)} %copy-done.49) | copy-start | bytes 18436
  896.1 56.4 %copy-start.52 = (f32[1536]{0:T(1024)S(1)}, f32[1536]{0:T(1024)}, u32[]{:S(2)}) copy-start(f32[1536]{0:T(1024)} %copy-done.51) | copy-start | bytes 18436
  896.1 56.4 %copy-start.54 = (f32[1536]{0:T(1024)S(1)}, f32[1536]{0:T(1024)}, u32[]{:S(2)}) copy-start(f32[1536]{0:T(1024)} %copy-done.53) | copy-start | bytes 18436
  896.1 56.4 %copy-start.56 = (f32[1536]{0:T(1024)S(1)}, f32[1536]{0:T(1024)}, u32[]{:S(2)}) copy-start(f32[1536]{0:T(1024)} %copy-done.55) | copy-start | bytes 18436
  896.1 56.4 %copy-start.58 = (f32[1536]{0:T(1024)S(1)}, f32[1536]{0:T(1024)}, u32[]{:S(2)}) copy-start(f32[1536]{0:T(1024)} %copy-done.57) | copy-start | bytes 18436
  896.1 56.4 %copy-start.60 = (f32[1536]{0:T(1024)S(1)}, f32[1536]{0:T(1024)}, u32[]{:S(2)}) copy-start(f32[1536]{0:T(1024)} %copy-done.59) | copy-start | bytes 18436
  896.1 56.4 %copy-start.80 = (f32[144]{0:T(256)S(1)}, f32[144]{0:T(256)}, u32[]{:S(2)}) copy-start(f32[144]{0:T(256)} %get-tuple-element.162) | copy-start | bytes 1732
  (79 other events, 1232.3 us)

commit v2 on v1

v2 whole, which is shorter than its diff:
```python
import functools

import jax
import jax.numpy as jnp
from jax import lax
from jax.experimental import pallas as pl
from jax.experimental.pallas import tpu as pltpu
from jax.sharding import Mesh, PartitionSpec as P

HEAD = 64
TXT = 77
UNIT = 8
EDGE = 48

norm_eps = 1e-06
grn_eps = 1e-06
masked_score = -1000000000.0

AXES = ("grp", "duo", "rows")
MESH_ID = pl.DeviceIdType.MESH
F32 = jnp.float32
BF16 = jnp.bfloat16


class Place:
    def __init__(self):
        self.q, self.c, self.z = (lax.axis_index(axis) for axis in AXES)
        self.G, self.D, self.R = (lax.axis_size(axis) for axis in AXES)

    def team(self):
        for step in range(1, self.D * self.R):
            dc, dz = step // self.R, step % self.R
            yield lax.rem(self.c + dc, self.D), lax.rem(self.z + dz, self.R)

    def groups(self):
        for step in range(1, self.G):
            yield lax.rem(self.q + step, self.G)


def signal_all(barrier, targets):
    for target in targets:
        pl.semaphore_signal(barrier, inc=1, device_id=target, device_id_type=MESH_ID)


def guarded(when, act):
    if when is None:
        act()
    else:
        pl.when(when)(act)


class Flow:
    def __init__(self, send_sem, recv_sem):
        self.send_sem, self.recv_sem = send_sem, recv_sem
        self.used = 0
        self.open = []

    def take(self, count=1):
        at = self.used
        self.used += count
        return at

    def copy(self, src, dst, target, at):
        return pltpu.make_async_remote_copy(
            src_ref=src,
            dst_ref=dst,
            send_sem=self.send_sem.at[at],
            recv_sem=self.recv_sem.at[at],
            device_id=target,
            device_id_type=MESH_ID,
        )

    def finish(self):
        for act, when in self.open:
            guarded(when, act)


class LineGather:
    def __init__(self, flow, place, src, dst):
        self.flow, self.p, self.src, self.dst = flow, place, src, dst
        self.up = flow.take(place.R - 1)
        self.down = flow.take(place.R - 1)
        self.side = flow.take(2 * place.R - 1)

    def send(self, block, hop, direction):
        p, dst = self.p, self.dst
        src = self.src if hop == 0 else dst.at[p.c, block]
        at = (self.up if direction > 0 else self.down) + hop
        return self.flow.copy(src, dst.at[p.c, block], {"rows": p.z + direction}, at)

    def across(self, block, number):
        p, dst = self.p, self.dst
        src = self.src if number == 0 else dst.at[p.c, block]
        other = {"duo": lax.rem(p.c + 1, p.D)}
        return self.flow.copy(src, dst.at[p.c, block], other, self.side + number)

    def start(self):
        p = self.p
        for direction, ok in ((1, p.z < p.R - 1), (-1, p.z > 0)):
            copy = self.send(p.z, 0, direction)
            guarded(ok, copy.start)
            self.flow.open.append((copy.wait_send, ok))
        copy = self.across(p.z, 0)
        copy.start()
        self.flow.open += [(copy.wait_recv, None), (copy.wait_send, None)]

    def hop(self, step):
        p = self.p
        for direction, number in ((1, step), (-1, p.R - 1 + step)):
            block = p.z - direction * step
            ok = (block >= 0) if direction > 0 else (block < p.R)
            last = (p.z < p.R - 1) if direction > 0 else (p.z > 0)
            arrived = self.send(block, step - 1, direction)
            side = self.across(block, number)

            def relay(arrived=arrived, side=side, block=block, direction=direction, last=last):
                arrived.wait_recv()
                if step < p.R - 1:
                    pl.when(last)(self.send(block, step, direction).start)
                side.start()

            pl.when(ok)(relay)
            if step < p.R - 1:
                self.flow.open.append((self.send(block, step, direction).wait_send, ok & last))
            self.flow.open += [(side.wait_recv, ok), (side.wait_send, ok)]


class LineReduce:
    def __init__(self, flow, place, part, total_ref, mate, passed, landed):
        self.flow, self.p, self.part, self.total = flow, place, part, total_ref
        self.mate, self.passed, self.landed = mate, passed, landed
        self.side = flow.take(place.R)
        self.line = flow.take(2 * place.R)

    def across(self, block):
        p = self.p
        other = lax.rem(p.c + 1, p.D)
        return self.flow.copy(
            self.part.at[other, block], self.mate.at[block], {"duo": other}, self.side + block
        )

    def along(self, upward, block):
        p = self.p
        way = jnp.where(upward, 1, 0)
        target = {"rows": jnp.where(upward, p.z + 1, p.z - 1)}
        return self.flow.copy(
            self.passed.at[way, block],
            self.landed.at[way, block],
            target,
            self.line + way * p.R + block,
        )

    def steps(self):
        p = self.p
        low = p.z < p.R // 2
        for k in range(p.R - 1):
            for first in (True, False):
                upward = low if first else jnp.logical_not(low)
                block = jnp.where(upward, p.R - 1 - k, k)
                yield upward, block, jnp.where(upward, block > p.z, block < p.z)

    def start(self):
        p = self.p
        for k in range(p.R):
            block = jnp.where(p.z < p.R // 2, p.R - 1 - k, k)
            copy = self.across(block)
            copy.start()
            self.flow.open.append((copy.wait_send, None))

    def rows_of(self, act):
        count = self.part.shape[2]
        step = 16

        @pl.loop(0, count // step)
        def _(number):
            act(pl.ds(pl.multiple_of(number * step, step), step))

    def run(self):
        p = self.p
        for number, (upward, block, ok) in enumerate(self.steps()):
            way = jnp.where(upward, 1, 0)
            behind = jnp.where(upward, p.z > 0, p.z < p.R - 1)

            def act(upward=upward, block=block, way=way, behind=behind):
                self.across(block).wait_recv()

                @pl.when(behind)
                def _():
                    self.along(upward, block).wait_recv()

                    def add(rows):
                        self.passed[way, block, rows] = (
                            self.part[p.c, block, rows].astype(F32)
                            + self.mate[block, rows].astype(F32)
                            + self.landed[way, block, rows].astype(F32)
                        ).astype(BF16)

                    self.rows_of(add)

                @pl.when(jnp.logical_not(behind))
                def _():
                    def add(rows):
                        self.passed[way, block, rows] = (
                            self.part[p.c, block, rows].astype(F32)
                            + self.mate[block, rows].astype(F32)
                        ).astype(BF16)

                    self.rows_of(add)

                self.along(upward, block).start()

            pl.when(ok)(act)
            self.flow.open.append((self.along(upward, block).wait_send, ok))
        self.across(p.z).wait_recv()

        def base(rows):
            self.total[rows] = self.part[p.c, p.z, rows].astype(F32) + self.mate[
                p.z, rows
            ].astype(F32)

        self.rows_of(base)
        for way, ok in ((1, p.z > 0), (0, p.z < p.R - 1)):

            def more(way=way):
                self.along(way == 1, p.z).wait_recv()

                def add(rows):
                    self.total[rows] += self.landed[way, p.z, rows].astype(F32)

                self.rows_of(add)

            pl.when(ok)(more)


def team_kernel(
    ident, name, plan, arrays, results, gathers=(), reduces=(), messages=0, local=1, late=None
):
    D, R = lax.axis_size("duo"), lax.axis_size("rows")
    count_a, count_g, count_r = len(arrays), len(gathers), len(reduces)
    extra = 0 if late is None else 1
    total_sems = messages + (count_g + extra) * (4 * R - 3) + count_r * 3 * R

    def kernel(*refs):
        refs = list(refs)
        ins = refs[:count_a]
        g_in = refs[count_a : count_a + count_g]
        r_in = refs[count_a + count_g : count_a + count_g + count_r]
        refs = refs[count_a + count_g + count_r :]
        outs = refs[: len(results)]
        refs = refs[len(results) :]
        late_out = refs[:extra]
        g_out = refs[extra : extra + count_g]
        r_out = refs[extra + count_g : extra + count_g + count_r]
        refs = refs[extra + count_g + count_r :]
        send_sem, recv_sem, local_sem = refs[:3]
        buffers = refs[3:]
        p = Place()
        flow = Flow(send_sem, recv_sem)
        greet, direct, stay = plan(p, ins, outs)
        barrier = pltpu.get_barrier_semaphore()
        waits = 0
        for target, when in greet:
            if when is None:
                waits = waits + 1
            else:
                waits = waits + jnp.where(when, 1, 0).astype(jnp.int32)
            guarded(when, lambda target=target: signal_all(barrier, [target]))
        pl.semaphore_wait(barrier, waits)
        lines = [LineGather(flow, p, src, dst) for src, dst in zip(g_in, g_out)]
        sums = [
            LineReduce(flow, p, src, dst, *buffers[3 * n : 3 * n + 3])
            for n, (src, dst) in enumerate(zip(r_in, r_out))
        ]
        base = flow.take(messages)
        copies = {}
        arrived = set()

        stays = []

        def landed(number):
            if number not in arrived:
                arrived.add(number)
                guarded(copies[number][2], copies[number][0].wait_recv)

        def run_stage(stage):
            for number, (src, dst, target, after, when, when_stage, lands) in enumerate(direct):
                if when_stage != stage:
                    continue
                for earlier in after:
                    landed(earlier)
                copy = flow.copy(src, dst, target, base + number)
                guarded(when, copy.start)
                copies[number] = (copy, when, lands)
            if late is not None and late[1] == stage:
                for number in range(late[2]):
                    landed(number)
                stays[0][0].wait()
                line = LineGather(flow, p, outs[late[0]], late_out[0])
                line.start()
                own = pltpu.make_async_copy(
                    outs[late[0]], late_out[0].at[p.c, p.z], local_sem.at[local + count_g]
                )
                own.start()
                stays[0] = (own, None)
                if stage:
                    for earlier in range(1, stage + 1):
                        line.hop(earlier)
                lines.append(line)

        for item in sums:
            item.start()
        for line in lines:
            line.start()
        for number, (src, dst, when) in enumerate(
            list(stay) + [(src, dst.at[p.c, p.z], None) for src, dst in zip(g_in, g_out)]
        ):
            copy = pltpu.make_async_copy(src, dst, local_sem.at[number])
            guarded(when, copy.start)
            stays.append((copy, when))
        run_stage(0)
        for step in range(1, R):
            for line in lines:
                line.hop(step)
            run_stage(step)
        for item in sums:
            item.run()
        for copy, when in stays:
            guarded(when, copy.wait)
        for number in copies:
            landed(number)
        for copy, when, _ in copies.values():
            guarded(when, copy.wait_send)
        flow.finish()

    spot = pl.BlockSpec(memory_space=pl.ANY)
    near = pl.BlockSpec(memory_space=pltpu.VMEM)
    out_shape = [jax.ShapeDtypeStruct(shape, kind) for shape, kind in results]
    if late is not None:
        shape, kind = results[late[0]]
        out_shape.append(jax.ShapeDtypeStruct((D, R) + shape, kind))
    out_shape += [jax.ShapeDtypeStruct((D, R) + g.shape, g.dtype) for g in gathers]
    out_shape += [jax.ShapeDtypeStruct(r.shape[2:], F32) for r in reduces]
    scratch = [
        pltpu.SemaphoreType.DMA((total_sems,)),
        pltpu.SemaphoreType.DMA((total_sems,)),
        pltpu.SemaphoreType.DMA((local + count_g + extra,)),
    ]
    for r in reduces:
        block = r.shape[1:]
        scratch += [
            pltpu.VMEM(block, BF16),
            pltpu.VMEM((2,) + block, BF16),
            pltpu.VMEM((2,) + block, BF16),
        ]
    return pl.pallas_call(
        kernel,
        out_shape=out_shape,
        in_specs=[spot] * (count_a + count_g) + [near] * count_r,
        out_specs=[spot] * (len(results) + extra + count_g) + [near] * count_r,
        scratch_shapes=scratch,
        compiler_params=pltpu.CompilerParams(
            collective_id=ident, has_side_effects=True, vmem_limit_bytes=56 * 2**20
        ),
        name=name,
    )(*arrays, *gathers, *reduces)


def team_greet(p):
    return [({"duo": c, "rows": z}, None) for c, z in p.team()]


def group_greet(p):
    return [({"grp": q}, None) for q in p.groups()]


class Plan:
    def __init__(self, p):
        self.p = p
        self.messages, self.local, self.greet = [], [], []

    def add(self, src, dst, target, after=(), when=None, stage=0, lands=None):
        self.messages.append((src, dst, target, after, when, stage, when if lands is None else lands))
        return len(self.messages) - 1

    def team_swap(self, src, dst, stage=0):
        p = self.p
        mine = p.c * p.R + p.z
        for c, z in p.team():
            self.add(src.at[c * p.R + z], dst.at[mine], {"duo": c, "rows": z}, stage=stage)
        self.local.append((src.at[mine], dst.at[mine], None))

    def team_gather(self, src, dst, stage=0):
        p = self.p
        mine = p.c * p.R + p.z
        for c, z in p.team():
            self.add(src, dst.at[mine], {"duo": c, "rows": z}, stage=stage)
        self.local.append((src, dst.at[mine], None))

    def group_gather(self, src, dst, late=None):
        p = self.p
        self.local.append((src, dst.at[p.q], None))
        if late is None or p.G != 4:
            for q in p.groups():
                self.add(src, dst.at[p.q], {"grp": q})
            return
        across = p.q + 1 - 2 * lax.rem(p.q, 2)
        along = lax.rem(p.q + 2, 4)
        one = self.add(src, dst.at[p.q], {"grp": across})
        two = self.add(src, dst.at[p.q], {"grp": along})
        half = src.shape[0] // 2
        top, bottom = pl.ds(0, half), pl.ds(half, half)
        self.add(
            dst.at[across, top], dst.at[across, top], {"grp": along}, after=(one,), stage=late
        )
        self.add(
            dst.at[along, bottom],
            dst.at[along, bottom],
            {"grp": across},
            after=(two,),
            stage=late,
        )

    def group_swap(self, src, dst, stage=0):
        p = self.p
        for q in p.groups():
            self.add(src.at[q], dst.at[p.q], {"grp": q}, stage=stage)
        self.local.append((src.at[p.q], dst.at[p.q], None))

    def done(self):
        p = self.p
        return team_greet(p) + group_greet(p) + self.greet, self.messages, self.local


def layer_stats(values):
    center = values - jnp.mean(values, axis=-1, keepdims=True)
    spread = jnp.mean(center * center, axis=-1, keepdims=True)
    inverse = lax.rsqrt(spread + norm_eps)
    return center * inverse, inverse


def layer_back(grad, hat, inverse):
    first = jnp.mean(grad, axis=-1, keepdims=True)
    second = jnp.mean(grad * hat, axis=-1, keepdims=True)
    return inverse * (grad - first - hat * second)


def mm(left, right):
    return jnp.dot(left, right, preferred_element_type=F32)


def mm_t(left, right):
    return lax.dot_general(left, right, (((1,), (1,)), ((), ())), preferred_element_type=F32)


def t_mm(left, right):
    return lax.dot_general(left, right, (((0,), (0,)), ((), ())), preferred_element_type=F32)


def columns_of(bucket_ids):
    return jnp.where(
        bucket_ids == 0, 9 * UNIT // 2, jnp.where(bucket_ids == 1, 3 * UNIT, 9 * UNIT // 4)
    )


def pixel_mask(positions, height, width, cols):
    row_at = positions // cols
    col_at = positions % cols
    return ((row_at < height) & (col_at < width)).astype(F32)


def attention(queries, text_kv, key_keep, grad_att):
    D, pixels, width = queries.shape
    HW = width // 3
    texts = text_kv.shape[1]
    keys = pixels + texts
    heads = HW // HEAD
    scale = HEAD ** (-0.5)

    def kernel(q_ref, t_ref, keep_ref, g_ref, att_ref, dq_ref, dt_ref, k_all, v_all, dk, dv, o_t, dq_t):
        k_all[pl.ds(0, pixels)] = q_ref[0, :, HW : 2 * HW]
        k_all[pl.ds(pixels, texts)] = t_ref[0, :, :HW]
        v_all[pl.ds(0, pixels)] = q_ref[0, :, 2 * HW :]
        v_all[pl.ds(pixels, texts)] = t_ref[0, :, HW:]
        k_t = k_all[...].T
        v_t = v_all[...].T
        dk[...] = jnp.zeros_like(dk)
        dv[...] = jnp.zeros_like(dv)
        o_t[...] = jnp.zeros_like(o_t)
        dq_t[...] = jnp.zeros_like(dq_t)
        lane = lax.broadcasted_iota(jnp.int32, (1, HW), 1)
        line = lax.broadcasted_iota(jnp.int32, (HW, 1), 0)
        alive = keep_ref[0] > 0

        @pl.loop(0, heads)
        def _(head):
            low = head * HEAD
            in_head = (lane >= low) & (lane < low + HEAD)
            in_line = (line >= low) & (line < low + HEAD)
            q_h = jnp.where(in_head, q_ref[0, :, :HW], 0).astype(BF16)
            g_h = jnp.where(in_head, g_ref[0], 0).astype(BF16)
            scores = mm_t(k_all[...], q_h) * scale
            scores = jnp.where(alive, scores, masked_score)
            top = jnp.max(scores, axis=0, keepdims=True)
            weights = jnp.exp(scores - top)
            probs = weights / jnp.sum(weights, axis=0, keepdims=True)
            probs_low = probs.astype(BF16)
            v_h = jnp.where(in_line, v_t, 0).astype(BF16)
            o_t[...] += mm(v_h, probs_low)
            dv[...] += mm(probs_low, g_h)
            grad_probs = mm_t(v_all[...], g_h)
            sums = jnp.sum(probs * grad_probs, axis=0, keepdims=True)
            grad_scores = (probs * (grad_probs - sums)).astype(BF16)
            k_h = jnp.where(in_line, k_t, 0).astype(BF16)
            dq_t[...] += mm(k_h, grad_scores)
            dk[...] += mm(grad_scores, q_h)

        att_ref[0] = o_t[...].T.astype(BF16)
        dq_ref[0, :, :HW] = (dq_t[...].T * scale).astype(BF16)
        dq_ref[0, :, HW : 2 * HW] = (dk[pl.ds(0, pixels)] * scale).astype(BF16)
        dq_ref[0, :, 2 * HW :] = dv[pl.ds(0, pixels)].astype(BF16)
        dt_ref[0, :, :HW] = (dk[pl.ds(pixels, texts)] * scale).astype(BF16)
        dt_ref[0, :, HW:] = dv[pl.ds(pixels, texts)].astype(BF16)

    def one(shape):
        return pl.BlockSpec((1,) + shape, lambda i: (i, 0, 0))

    return pl.pallas_call(
        kernel,
        grid=(D,),
        out_shape=[
            jax.ShapeDtypeStruct((D, pixels, HW), BF16),
            jax.ShapeDtypeStruct((D, pixels, width), BF16),
            jax.ShapeDtypeStruct((D, texts, 2 * HW), BF16),
        ],
        in_specs=[
            one((pixels, width)),
            one((texts, 2 * HW)),
            one((keys, 1)),
            one((pixels, HW)),
        ],
        out_specs=[one((pixels, HW)), one((pixels, width)), one((texts, 2 * HW))],
        scratch_shapes=[
            pltpu.VMEM((keys, HW), BF16),
            pltpu.VMEM((keys, HW), BF16),
            pltpu.VMEM((keys, HW), F32),
            pltpu.VMEM((keys, HW), F32),
            pltpu.VMEM((HW, pixels), F32),
            pltpu.VMEM((HW, pixels), F32),
        ],
        compiler_params=pltpu.CompilerParams(vmem_limit_bytes=56 * 2**20),
        name="attention",
    )(queries, text_kv, key_keep, grad_att)


def pad_rows(values, rows):
    return jnp.pad(values, ((0, rows - values.shape[0]),) + ((0, 0),) * (values.ndim - 1))


def pack_flat(pieces, rows, kind):
    flat = jnp.concatenate([piece.astype(kind).reshape(-1) for piece in pieces])
    return jnp.pad(flat, (0, rows * 128 - flat.shape[0])).reshape(rows, 128)


def body(
    latents,
    clip_tokens,
    time_embed,
    bucket_ids,
    heights,
    widths,
    text_mask,
    conv_weight,
    conv_bias,
    in_weight,
    in_bias,
    grn_gain,
    grn_bias,
    out_weight,
    out_bias,
    time_weight,
    time_bias,
    map_weight,
    map_bias,
    qkv_weight,
    qv_bias,
    proj_weight,
    proj_bias,
    cotangent,
):
    G, D, R = (lax.axis_size(axis) for axis in AXES)
    T = D * R
    q, c, z = (lax.axis_index(axis) for axis in AXES)
    N = latents.shape[1]
    C = latents.shape[2]
    pixels = R * N
    FFS = in_bias.shape[0]
    FL = G * FFS
    FF = in_weight.shape[1]
    cs = conv_bias.shape[0]
    ms = map_weight.shape[0]
    slots = clip_tokens.shape[1]
    text_all = R * slots
    HW = C // T
    even = G == R
    head_slice = R and (D * z + c)

    latents = latents[0]
    cotangent = cotangent[0]
    cols = columns_of(bucket_ids)[0]
    positions = z * N + jnp.arange(N, dtype=jnp.int32)
    keep = pixel_mask(positions, heights[0], widths[0], cols)[:, None]
    masked = latents * keep.astype(BF16)
    grad_result = (keep * cotangent.astype(F32)).astype(BF16)
    gres_all = lax.all_gather(grad_result, ("duo", "rows"), axis=0, tiled=True)

    in_cut = in_weight.reshape(cs, G, T, FFS).transpose(2, 0, 1, 3).reshape(T, cs, FL)
    qkv_cut = qkv_weight.reshape(cs, 3, R, D, HW).transpose(3, 2, 0, 1, 4).reshape(T, cs, 3 * HW)
    mp = -(-ms // 16) * 16
    map_cut = jnp.pad(
        map_weight.reshape(ms, T, HW).transpose(1, 0, 2), ((0, 0), (0, mp - ms), (0, 0))
    )
    sp = -(-slots // 16) * 16
    clip_pad = pad_rows(clip_tokens[0], sp)

    def lanes(piece):
        piece = piece.astype(BF16).reshape(-1, piece.shape[-1])
        return jnp.pad(piece, ((0, 0), (0, 128 - piece.shape[1])))

    numbers = jnp.stack([heights[0], widths[0], bucket_ids[0]]).astype(BF16)[None]
    small = jnp.concatenate(
        [
            lanes(piece)
            for piece in (
                conv_weight,
                conv_bias,
                out_bias,
                map_bias,
                proj_bias,
                qv_bias,
                time_embed,
                numbers,
                text_mask,
            )
        ]
    )
    mrows = 32
    small = pad_rows(small, mrows)
    fvec = pad_rows(jnp.stack([in_bias, grn_gain, grn_bias]), 16)

    def swap_edges(plan, src, dst):
        p = plan.p
        for block, to, sends, lands in (
            (src.at[pl.ds(src.shape[0] - EDGE, EDGE)], p.z + 1, p.z < R - 1, p.z > 0),
            (src.at[pl.ds(0, EDGE)], p.z - 1, p.z > 0, p.z < R - 1),
        ):
            slot = jnp.where(to > p.z, 0, 1)
            plan.add(block, dst.at[slot], {"rows": to}, when=sends, lands=lands)

    def plan_start(p, ins, outs):
        plan = Plan(p)
        plan.group_gather(ins[1], outs[1])
        swap_edges(plan, ins[0], outs[0])
        plan.team_swap(ins[2], outs[2])
        plan.group_gather(ins[3], outs[3])
        return plan.done()

    edges, _, in_rows, fvec_all, small_all = team_kernel(
        0,
        "exchange_start",
        plan_start,
        [masked, small, in_cut, fvec],
        [
            ((2, EDGE, C), BF16),
            ((G, mrows, 128), BF16),
            ((T, cs, FL), BF16),
            ((G, 16, FFS), BF16),
        ],
        messages=2 + 2 * (G - 1) + (T - 1),
        local=3,
        late=(1, 0, G - 1),
    )
    shards = T * G
    by_place = small_all.reshape(D, R, G, mrows, 128).transpose(2, 0, 1, 3, 4)
    by_place = by_place.reshape(shards, mrows, 128)

    def whole(row, width):
        return by_place[:, row, :width].reshape(-1).astype(F32)

    kernel_full = by_place[:, :9, :cs].transpose(1, 0, 2).reshape(9, C).astype(F32)
    conv_bias_full, out_bias_full, map_bias_full, proj_bias_full = (
        whole(9 + row, cs) for row in range(4)
    )
    qv_full = whole(13, 2 * cs)
    per_item = by_place.reshape(G * D, R, mrows, 128)[:, 0]
    embed_all = per_item[:, 14, : time_embed.shape[1]]
    pair = lax.dynamic_slice_in_dim(per_item, q * D, D, axis=0)
    facts = pair[:, 15, :3].astype(jnp.int32)
    pair_height, pair_width, pair_bucket = (facts[:, n : n + 1] for n in range(3))
    pair_cols = columns_of(pair_bucket)
    pair_keep = pixel_mask(
        jnp.arange(pixels, dtype=jnp.int32)[None, :], pair_height, pair_width, pair_cols
    )
    text_keep = (
        pair[:, 16, :text_all].astype(F32) * (jnp.arange(text_all) < TXT).astype(F32)[None, :]
    )
    key_keep = jnp.concatenate([pair_keep, text_keep], axis=1)
    in_bias_s, gain_s, grn_bias_s = (
        fvec_all[:, row].reshape(FL).astype(F32) for row in range(3)
    )
    mod_rows = -(-G * D // 8) * 8
    mod_part = mm(embed_all, time_weight) + time_bias.astype(F32)
    mod_part = pad_rows(jnp.pad(mod_part, ((0, 0), (0, 128 - 2 * cs))), mod_rows)

    def extend(low, mid, high):
        return jnp.concatenate(
            [
                jnp.where(z > 0, low, jnp.zeros_like(low)),
                mid,
                jnp.where(z < R - 1, high, jnp.zeros_like(high)),
            ],
            axis=0,
        )

    column = (positions % cols)[:, None]

    def tap(extended, dy, dx):
        piece = lax.dynamic_slice_in_dim(extended, EDGE + dy * cols + dx, N, axis=0).astype(F32)
        ok = (column + dx >= 0) & (column + dx < cols)
        return jnp.where(ok, piece, 0.0)

    extended = extend(edges[0], masked, edges[1])
    conv_out = jnp.zeros((N, C), F32) + conv_bias_full
    for index in range(9):
        conv_out = conv_out + tap(extended, index // 3 - 1, index % 3 - 1) * kernel_full[index]
    norm_hat, norm_inv = layer_stats(conv_out)
    normed = norm_hat.astype(BF16)

    def plan_first(p, ins, outs):
        plan = Plan(p)
        plan.group_gather(ins[4], outs[4])
        plan.group_gather(ins[0], outs[0], late=1)
        plan.group_gather(ins[1], outs[1], late=2)
        plan.team_swap(ins[2], outs[2])
        plan.team_swap(ins[3], outs[3])
        if even:
            wide = C // G
            for step in range(G):
                to = lax.rem(p.z + step, G)
                when = None if step else p.q != p.z
                piece = ins[5].at[:, pl.ds(pl.multiple_of(to * wide, 128), wide)]
                plan.add(
                    piece, outs[5].at[p.z], {"grp": to, "duo": p.c, "rows": p.q}, when=when
                )
                source = {"grp": p.z, "duo": p.c, "rows": lax.rem(p.q - step + G, G)}
                plan.greet.append((source, when))
            piece = ins[5].at[:, pl.ds(pl.multiple_of(p.z * wide, 128), wide)]
            plan.local.append((piece, outs[5].at[p.z], p.q == p.z))
        return plan.done()

    group_count = 4 if G == 4 else G - 1
    arrays = [in_rows.reshape(T * cs, FL), out_weight, qkv_cut, map_cut, mod_part]
    results = [
        ((G, T * cs, FL), BF16),
        ((G,) + out_weight.shape, BF16),
        ((T, cs, 3 * HW), BF16),
        ((T, mp, HW), BF16),
        ((G,) + mod_part.shape, F32),
    ]
    if even:
        arrays.append(proj_weight)
        results.append(((R, cs, C // G), BF16))
    gathered = team_kernel(
        1,
        "exchange_normed",
        plan_first,
        arrays,
        results,
        gathers=[normed, clip_pad],
        messages=2 * group_count + 2 * (T - 1) + G - 1 + (G if even else 0),
        local=5 + (1 if even else 0),
        late=(4, 1, G - 1),
    )
    in_full, out_full, qkv_rows, map_rows = gathered[:4]
    mod_all, normed_all, clip_all = gathered[-3:]
    clip_all = clip_all.reshape(T, sp, -1)
    modulate = lax.dynamic_index_in_dim(mod_all, q * D + c, 3, keepdims=False)[..., : 2 * cs]
    modulate = modulate.transpose(2, 0, 1, 3).reshape(1, 2 * C)
    normed_all = normed_all.reshape(D * pixels, C)
    in_full = in_full.reshape(C, FL)
    out_full = out_full.reshape(FL, C)
    keep_all = pair_keep.reshape(D, pixels, 1)

    hidden = mm(normed_all, in_full) + in_bias_s
    gate = 0.5 * lax.erfc(-hidden * (0.5**0.5))
    active = hidden * gate
    active3 = active.reshape(D, pixels, FL)
    squares = jnp.sum(keep_all * active3 * active3, axis=1)
    grn_norms = jnp.sqrt(squares)

    def team_total(ident, name, values):
        block = jnp.zeros((8, 128), F32).at[0, :D].set(values)

        def plan(p, ins, outs):
            plan = Plan(p)
            plan.team_gather(ins[0], outs[0])
            return team_greet(p), plan.messages, plan.local

        (everyone,) = team_kernel(
            ident, name, plan, [block], [((T, 8, 128), F32)], messages=T - 1
        )
        return jnp.sum(everyone[:, 0, :D], axis=0)

    norm_mean = (team_total(2, "total_norms", jnp.sum(grn_norms, axis=1)) / FF + grn_eps)[:, None]
    grn_ratio = grn_norms / norm_mean
    grn_out = (
        (gain_s * (active3 * grn_ratio[:, None, :]) + grn_bias_s + active3)
        .astype(BF16)
        .reshape(D * pixels, FL)
    )

    def plan_branch(p, ins, outs):
        plan = Plan(p)
        plan.group_gather(ins[0], outs[0])
        plan.group_gather(ins[1], outs[1])
        if even:
            plan.group_gather(ins[2], outs[2])
        return plan.done()

    arrays = [qkv_rows.reshape(T * cs, 3 * HW), map_rows.reshape(T * mp, HW)]
    results = [((G, T * cs, 3 * HW), BF16), ((G, T * mp, HW), BF16)]
    if even:
        arrays.append(gathered[5].reshape(HW, C // G))
        results.append(((G, HW, C // G), BF16))
    gathered = team_kernel(
        3,
        "reduce_branch",
        plan_branch,
        arrays,
        results,
        reduces=[mm(grn_out, out_full).astype(BF16).reshape(D, R, N, C)],
        messages=(3 if even else 2) * (G - 1),
        local=3,
    )
    qkv_full = gathered[0].reshape(C, 3 * HW)
    map_full = gathered[1].reshape(G * T, mp, HW)[:, :ms].reshape(G * T * ms, HW)
    if even:
        proj_s = gathered[2].transpose(1, 0, 2).reshape(HW, C)
    else:
        proj_whole = lax.all_gather(proj_weight, AXES, axis=0, tiled=True)
        proj_s = lax.dynamic_slice_in_dim(proj_whole, head_slice * HW, HW, axis=0)
    branch = gathered[-1] + out_bias_full
    after_res = latents.astype(F32) + keep * branch
    scale_by = 1.0 + modulate[:, :C]
    second = after_res * scale_by + modulate[:, C:]
    two_hat, two_inv = layer_stats(second)
    normed_two = two_hat.astype(BF16)

    silu_text = jax.nn.silu(clip_all[:, :slots].astype(F32)).astype(BF16)
    silu_text = silu_text.reshape(D * text_all, -1)
    map_bias_s = lax.dynamic_slice_in_dim(map_bias_full, (c * R + z) * HW, HW)
    mapped_s = (mm(silu_text, map_full) + map_bias_s).astype(BF16)

    def plan_none(p, ins, outs):
        return team_greet(p), [], []

    two_all, mapped = team_kernel(
        4, "exchange_second", plan_none, [], [], gathers=[normed_two, mapped_s]
    )
    two_all = two_all.reshape(D * pixels, C)
    mapped = mapped.reshape(T, D * text_all, HW).transpose(1, 0, 2).reshape(D * text_all, C)

    q_bias = lax.dynamic_slice_in_dim(qv_full, head_slice * HW, HW)
    v_bias = lax.dynamic_slice_in_dim(qv_full, C + head_slice * HW, HW)
    projected = mm(two_all, qkv_full)
    bias = jnp.concatenate([q_bias, jnp.zeros_like(q_bias), v_bias])
    queries = (projected + bias).astype(BF16).reshape(D, pixels, 3 * HW)
    text_kv = (mm(mapped, qkv_full[:, HW:]) + bias[HW:]).astype(BF16)
    text_kv = text_kv.reshape(D, text_all, 2 * HW)
    grad_att = mm_t(gres_all, proj_s).astype(BF16).reshape(D, pixels, HW)
    attended, grad_pixel, grad_text = attention(queries, text_kv, key_keep[:, :, None], grad_att)
    attended = attended.reshape(D * pixels, HW)
    grad_pixel = grad_pixel.reshape(D * pixels, 3 * HW)
    grad_text = grad_text.reshape(D * text_all, 2 * HW)
    result_part = mm(attended, proj_s).astype(BF16)
    result = lax.psum_scatter(result_part, ("duo", "rows"), scatter_dimension=0, tiled=True)
    grad_qkv = t_mm(two_all, grad_pixel) + jnp.pad(t_mm(mapped, grad_text), ((0, 0), (HW, 0)))
    q_bias_grad = jnp.sum(grad_pixel[:, :HW].astype(F32), axis=0)
    v_bias_grad = jnp.sum(grad_pixel[:, 2 * HW :].astype(F32), axis=0) + jnp.sum(
        grad_text[:, HW:].astype(F32), axis=0
    )
    grad_proj = t_mm(attended, gres_all)
    mapped_part = mm_t(grad_text, qkv_full[:, HW:]).astype(BF16)
    mapped_part = mapped_part.reshape(D * text_all, T, HW).transpose(1, 0, 2)
    two_part = mm_t(grad_pixel, qkv_full).astype(BF16).reshape(D, R, N, C)


    grad_two, mapped_sum = team_kernel(
        5,
        "reduce_attended",
        plan_none,
        [],
        [],
        reduces=[two_part, mapped_part.reshape(D, R, D * text_all, HW)],
    )
    output = (second + keep * (result.astype(F32) + proj_bias_full)).astype(BF16)
    grad_mapped = mapped_sum.astype(BF16)
    grad_map = t_mm(silu_text, grad_mapped).astype(BF16)
    grad_map = jnp.pad(grad_map.reshape(G, T, ms, HW), ((0, 0), (0, 0), (0, mp - ms), (0, 0)))
    map_bias_grad = jnp.sum(grad_mapped.astype(F32), axis=0)

    grad_output = cotangent.astype(F32)
    grad_second = grad_output + layer_back(grad_two, two_hat, two_inv)
    grad_modulate = jnp.concatenate(
        [jnp.sum(grad_second * after_res, axis=0), jnp.sum(grad_second, axis=0)]
    )
    grad_after = grad_second * scale_by
    grad_branch = (keep * grad_after).astype(BF16)

    def plan_third(p, ins, outs):
        plan = Plan(p)
        plan.group_swap(ins[0], outs[0])
        plan.group_swap(ins[1], outs[1])
        if even:
            plan.group_swap(ins[2], outs[2])
        return plan.done()

    arrays = [grad_qkv.astype(BF16).reshape(G, T * cs, 3 * HW), grad_map.reshape(G, T * mp, HW)]
    if even:
        arrays.append(grad_proj.astype(BF16).reshape(HW, G, C // G).transpose(1, 0, 2))
    gathered = team_kernel(
        7,
        "exchange_branch",
        plan_third,
        arrays,
        [(array.shape, BF16) for array in arrays],
        gathers=[grad_branch],
        messages=(3 if even else 2) * (G - 1),
        local=3,
    )
    gb_all = gathered[-1].reshape(D * pixels, C)
    qkv_sum = jnp.sum(gathered[0].astype(F32), axis=0).astype(BF16).reshape(T, cs, 3 * HW)
    map_back = jnp.sum(gathered[1].astype(F32), axis=0).astype(BF16).reshape(T, mp, HW)
    if even:
        proj_back = jnp.sum(gathered[2].astype(F32), axis=0).astype(BF16).reshape(R, cs, C // G)
    else:
        spread = jnp.zeros((C, C), F32)
        spread = lax.dynamic_update_slice_in_dim(spread, grad_proj, head_slice * HW, axis=0)
        grad_proj_out = lax.psum_scatter(spread, AXES, scatter_dimension=0, tiled=True)

    grad_out = t_mm(grn_out, gb_all).astype(BF16)
    grad_out_shard = lax.psum_scatter(grad_out, "grp", scatter_dimension=0, tiled=True).astype(F32)
    grad_grn = mm_t(gb_all, out_full)
    grad_grn3 = grad_grn.reshape(D, pixels, FL)
    moment = jnp.sum(grad_grn3 * active3, axis=1)
    grad_gain = jnp.sum(moment * grn_ratio, axis=0)
    grad_grn_bias = jnp.sum(grad_grn, axis=0)
    ratio_grad = moment * gain_s
    cross = team_total(8, "total_cross", jnp.sum(ratio_grad * grn_norms, axis=1))[:, None]
    grad_norms = ratio_grad / norm_mean - cross / (FF * norm_mean * norm_mean)
    grad_active = (
        grad_grn3 * (gain_s * grn_ratio[:, None, :] + 1.0)
        + keep_all * active3 * (grad_norms / grn_norms)[:, None, :]
    ).reshape(D * pixels, FL)
    density = jnp.exp(-0.5 * hidden * hidden) * 0.3989422804014327
    grad_hidden = (grad_active * (gate + hidden * density)).astype(BF16)
    grad_in_bias = jnp.sum(grad_hidden.astype(F32), axis=0)
    grad_in = t_mm(normed_all, grad_hidden).astype(BF16).reshape(G, T * cs, FL)
    back_part = mm_t(grad_hidden, in_full).astype(BF16).reshape(D, R, N, C)

    def plan_fourth(p, ins, outs):
        plan = Plan(p)
        plan.group_swap(ins[0], outs[0])
        plan.team_swap(ins[1], outs[1])
        plan.team_swap(ins[2], outs[2])
        plan.group_swap(ins[3], outs[3])
        if even:
            for step in range(G):
                to = lax.rem(p.q + step, G)
                when = None if step else p.q != p.z
                plan.add(
                    ins[4].at[to],
                    outs[4].at[p.q],
                    {"grp": p.z, "duo": p.c, "rows": to},
                    when=when,
                )
                source = {"grp": lax.rem(p.z - step + G, G), "duo": p.c, "rows": p.q}
                plan.greet.append((source, when))
            plan.local.append((ins[4].at[p.z], outs[4].at[p.q], p.q == p.z))
        return plan.done()

    fgrads = jnp.stack([grad_in_bias, grad_gain, grad_grn_bias]).reshape(3, G, FFS)
    fgrads = fgrads.transpose(1, 0, 2).reshape(G, -1)
    grows = -(-fgrads.shape[1] // 1024) * 8
    fgrads = jnp.pad(fgrads, ((0, 0), (0, grows * 128 - fgrads.shape[1]))).reshape(G, grows, 128)

    arrays = [grad_in, qkv_sum, map_back, fgrads]
    results = [(array.shape, array.dtype) for array in arrays]
    if even:
        arrays.append(proj_back)
        results.append(((G, cs, C // G), BF16))
    gathered = team_kernel(
        9,
        "reduce_back",
        plan_fourth,
        arrays,
        results,
        reduces=[back_part],
        messages=2 * (G - 1) + 2 * (T - 1) + (G if even else 0),
        local=5,
    )
    in_sum, qkv_team, map_team, f_sum = gathered[:4]
    if even:
        grad_proj_out = gathered[4].transpose(1, 0, 2).reshape(cs, C).astype(F32)
    grad_conv_in = gathered[-1]
    grad_conv = layer_back(grad_conv_in, norm_hat, norm_inv)
    taps = [
        jnp.sum(tap(extended, index // 3 - 1, index % 3 - 1) * grad_conv, axis=0)
        for index in range(9)
    ]
    in_back = jnp.sum(in_sum.astype(F32), axis=0).astype(BF16).reshape(T, cs, FL)

    def by_shard(values):
        return values.reshape(shards, -1)

    def placed(values, start, size):
        return lax.dynamic_update_slice_in_dim(jnp.zeros((size,), F32), values, start, axis=0)

    map_bias_vec = placed(map_bias_grad, (c * R + z) * HW, C)
    qv_vec = jnp.concatenate(
        [
            placed(q_bias_grad, head_slice * HW, C),
            placed(v_bias_grad, head_slice * HW, C),
        ]
    )
    pieces = [
        jnp.stack(taps).reshape(9, shards, cs).transpose(1, 0, 2).reshape(shards, -1),
        by_shard(jnp.sum(grad_conv, axis=0)),
        by_shard(jnp.sum(grad_branch.astype(F32), axis=0)),
        by_shard(jnp.sum(grad_result.astype(F32), axis=0)),
        by_shard(map_bias_vec),
        by_shard(qv_vec),
        by_shard(grad_modulate),
    ]
    widths_of = [piece.shape[1] for piece in pieces]
    tiny = jnp.concatenate(pieces, axis=1)
    trows = -(-tiny.shape[1] // 1024) * 8
    tiny = jnp.pad(tiny, ((0, 0), (0, trows * 128 - tiny.shape[1])))
    tiny = tiny.reshape(G, T, trows, 128).transpose(1, 0, 2, 3)

    def plan_fifth(p, ins, outs):
        plan = Plan(p)
        swap_edges(plan, ins[0], outs[0])
        plan.team_swap(ins[1], outs[1])
        plan.team_swap(ins[2], outs[2])
        return plan.done()

    conv_low = grad_conv.astype(BF16)
    conv_edges, tiny_team, in_team = team_kernel(
        11,
        "exchange_tail",
        plan_fifth,
        [conv_low, tiny, in_back],
        [((2, EDGE, C), BF16), (tiny.shape, F32), (in_back.shape, BF16)],
        messages=2 + 2 * (T - 1),
        local=2,
    )
    tiny_items = jnp.sum(tiny_team.reshape(D, R, G, trows, 128), axis=1).transpose(1, 0, 2, 3)

    def plan_sixth(p, ins, outs):
        plan = Plan(p)
        plan.group_swap(ins[0], outs[0])
        return group_greet(p), plan.messages, plan.local

    (tiny_all,) = team_kernel(
        12,
        "exchange_tiny",
        plan_sixth,
        [tiny_items],
        [((G, D, trows, 128), F32)],
        messages=G - 1,
    )
    tiny_all = tiny_all.reshape(G * D, -1)
    tiny_sum = jnp.sum(tiny_all, axis=0)
    outs = []
    at = 0
    for width in widths_of[:-1]:
        outs.append(tiny_sum[at : at + width])
        at += width
    modulate_items = tiny_all[:, at : at + widths_of[-1]]
    grad_time = lax.dot_general(
        embed_all.astype(F32),
        modulate_items,
        (((0,), (0,)), ((), ())),
        precision=lax.Precision.HIGHEST,
    )
    grad_time_bias = jnp.sum(modulate_items, axis=0)

    grad_extended = extend(conv_edges[0], conv_low, conv_edges[1])
    spread = jnp.zeros((N, C), F32)
    for index in range(9):
        spread = spread + tap(grad_extended, 1 - index // 3, 1 - index % 3) * kernel_full[index]
    grad_latents = grad_after + keep * spread

    grad_in_shard = in_team.astype(F32).reshape(T, cs, G, FFS).transpose(1, 2, 0, 3).reshape(cs, FF)
    grad_map_shard = map_team[:, :ms].astype(F32).transpose(1, 0, 2).reshape(ms, C)
    grad_qkv_shard = (
        qkv_team.astype(F32)
        .reshape(D, R, cs, 3, HW)
        .transpose(2, 3, 1, 0, 4)
        .reshape(cs, 3 * C)
    )
    f_total = jnp.sum(f_sum, axis=0).reshape(-1)
    return (
        output[None],
        grad_latents[None],
        outs[0].reshape(9, cs),
        outs[1],
        grad_in_shard,
        f_total[:FFS],
        f_total[FFS : 2 * FFS],
        f_total[2 * FFS : 3 * FFS],
        grad_out_shard,
        outs[2],
        grad_time,
        grad_time_bias,
        grad_map_shard,
        outs[4],
        grad_qkv_shard,
        outs[5],
        grad_proj_out,
        outs[3],
    )


def solution(mesh):
    items, rows = mesh.devices.shape
    fine = Mesh(mesh.devices.reshape(items // 2, 2, rows), AXES)
    item = ("grp", "duo")
    full = AXES
    ins = (
        P(item, "rows", None),
        P(item, "rows", None),
        P(item, None),
        P(item),
        P(item),
        P(item),
        P(item, None),
        P(None, full),
        P(full),
        P(full, None),
        P(full),
        P(full),
        P(full),
        P(full, None),
        P(full),
        P(None, full),
        P(full),
        P(full, None),
        P(full),
        P(full, None),
        P(full),
        P(full, None),
        P(full),
        P(item, "rows", None),
    )
    outs = (
        P(item, "rows", None),
        P(item, "rows", None),
        P(None, full),
        P(full),
        P(full, None),
        P(full),
        P(full),
        P(full),
        P(full, None),
        P(full),
        P(None, full),
        P(full),
        P(full, None),
        P(full),
        P(full, None),
        P(full),
        P(full, None),
        P(full),
    )
    return jax.shard_map(body, mesh=fine, in_specs=ins, out_specs=outs, check_vma=False)
```

time: 975 us -> 718 us (0.74)
  Pallas kernels: 705 us -> 412 us
  local copies, waits for them, and re-layouts: 83.6 us -> 115 us
  matrix products: 101 us -> 85.9 us
  between operations: 5.09 us -> 17.8 us
    pallas_call x13 -> x12, Pallas kernels: 705 us -> 412 us  [the longest x11 392 us: team_kernel(): pl.pallas_call(kernel, out_shape=out_shape, in_specs=[spot] * (count_a +...]
    dot_general x6 -> x1, matrix products: 24.9 us -> 0.84 us  [body(): lax.dot_general(embed_all.astype(F32), modulate_items, (((0,), (0,)), (()...]
  transfers between devices with their start and end apart: 0 -> 3, of which waited for: 0 -> 0; matrix products, arithmetic and copies ran while one was open for 0% -> 25% of each run, Pallas kernels for 0% -> 29%
where the time goes in v2:
time: 718 us; the launch traced here: 708 us
  Pallas kernels  412 us (57%)
  local copies, waits for them, and re-layouts  115 us (16%)
  matrix products  85.9 us (12%)
  other arithmetic  76 us (11%)
  between operations  17.8 us (2%)
    pallas_call x11, Pallas kernels, team_kernel(): pl.pallas_call(kernel, out_shape=out_shape, in_specs=[spot] * (count_a +...  392 us
    dot_general x7, matrix products, mm(): return jnp.dot(left, right, preferred_element_type=F32)  33.8 us
    dot_general x5, matrix products, mm_t(): lax.dot_general(left, right, (((1,), (1,)), ((), ())), preferred_element_...  27.3 us
    dot_general x6, matrix products, t_mm(): lax.dot_general(left, right, (((0,), (0,)), ((), ())), preferred_element_...  24 us
    pallas_call x1, Pallas kernels, attention(): pl.pallas_call(kernel, grid=(D,), out_shape=[jax.ShapeDtypeStruct((D, pix...  20.1 us
  transfers between devices with their start and end apart: 3, of which 0 were waited for; matrix products, arithmetic and copies ran while one was open for 25% of the time, Pallas kernels for 29%

profile of v2, /device:TPU:0, one launch (start us, length us, event | category | flops | bytes accessed | tf_op | source)
XLA Modules:
  0.0 707.8 jit_solution(214667295748629620)
XLA Ops:
  24.1 32.0 %exchange_start.1 = (bf16[2,48,1536]{2,1,0:T(8,128)(2,1)}, bf16[4,32,128]{2,1,0:T(8,128)(2,1)}, bf16[8,48,768]{2,1,0:T(8,128)(2,1)}, bf16[4,16,192]{2,1,0:T(8,128)(2,1)}, bf16[2,4,4,32,128]{4,3,2,1,0:T(8,128)(2,1)}) custom-call(bf16[144,1536]{1,0:T(8,128)(2,1)} %bitcast_multiply_fusion.3.refs_0_, bf16[32,128]{1,0:T(8,128)(2,1)} %pad.88.refs_1_, ...), custom_call_target="tpu_custom_call" | custom-call | tf_op jit(solution)/shard_map/exchange_start/pallas_call | solution.py:355
  74.1 65.8 %exchange_normed.1 = (bf16[4,384,768]{2,1,0:T(8,128)(2,1)}, bf16[4,192,1536]{2,1,0:T(8,128)(2,1)}, bf16[8,48,576]{2,1,0:T(8,128)(2,1)}, bf16[8,48,192]{2,1,0:T(8...) custom-call(bf16[384,768]{1,0:T(8,128)(2,1)} %bitcast.255, ...), custom_call_target="tpu_custom_call" | custom-call | tf_op jit(solution)/shard_map/exchange_normed/pallas_call | solution.py:355
  141.1 14.0 %fusion.64 = (f32[1152,768]{1,0:T(8,128)S(1)}, f32[1152,768]{1,0:T(8,128)}, f32[1152,768]{1,0:T(8,128)}) fusion(f32[768]{0:T(1024)} %reshape.936, bf16[1152,1536]{1,0:T(8,128)(2,1)} %bitcast.281, bf16[1536,768]{1,0:T(8,128)(2,1)} %bitcast.287), kind=kOutput, calls=%fused_computation.240 | convolution fusion | flops 2775416832 | bytes 16518144 | tf_op jit(solution)/shard_map/dot_general | solution.py:448
  156.9 5.9 total_norms.1
  165.0 4.4 convolution_convert_fusion.3
  169.4 42.4 %reduce_branch.1 = (bf16[4,384,576]{2,1,0:T(8,128)(2,1)}, bf16[4,384,192]{2,1,0:T(8,128)(2,1)}, bf16[4,192,384]{2,1,0:T(8,128)(2,1)}, f32[144,1536]{1,0:T(8,128)}) custom-call(bf16[384,576]{1,0:T(8,128)(2,1)} %bitcast.259, bf16[384,192]{1,0:T(8,128)(2,1)} %bitcast.264, bf16[192,384]{1,0:T(8,128)(2,1)} %bitcast.265, bf16[2,4,144,1536]{3,2,1,0:T(8,128)(2,1)} %bitcast.218), custom_call_target="tpu_custom_call" | custom-call | tf_op jit(solution)/shard_map/reduce_branch/pallas_call | solution.py:355
  238.7 51.7 %exchange_second.1 = (bf16[2,4,144,1536]{3,2,1,0:T(8,128)(2,1)}, bf16[2,4,160,192]{3,2,1,0:T(8,128)(2,1)}) custom-call(bf16[144,1536]{1,0:T(8,128)(2,1)} %fusion.31.refs_0_, bf16[160,192]{1,0:T(8,128)(2,1)} %fusion.22.refs_1_), custom_call_target="tpu_custom_call" | custom-call | tf_op jit(solution)/shard_map/exchange_second/pallas_call | solution.py:355
  296.7 6.2 fusion.20
  314.5 20.1 %attention.1 = (bf16[2,576,192]{2,1,0:T(8,128)(2,1)}, bf16[2,576,576]{2,1,0:T(8,128)(2,1)}, bf16[2,80,384]{2,1,0:T(8,128)(2,1)}) custom-call(bf16[2,576,576]{2,1,0:T(8,128)(2,1)} %bitcast.216, bf16[2,80,384]{2,1,0:T(8,128)(2,1)} %bitcast.267, f32[2,656,1]{2,1,0:T(8,128)} %copy.99.keep_ref, bf16[2,576,192]{2,1,0:T(8,128)(2,1)} %bitcast.229), custom_call_target="tpu_custom_call" | custom-call | tf_op jit(solution)/shard_map/attention/pallas_call | solution.py:527
  381.3 6.7 convolution_convert_fusion.1
  388.0 66.4 %reduce_attended.1 = (f32[144,1536]{1,0:T(8,128)}, f32[160,192]{1,0:T(8,128)}) custom-call(bf16[2,4,144,1536]{3,2,1,0:T(8,128)(2,1)} %bitcast.219, bf16[2,4,160,192]{3,2,1,0:T(8,128)(2,1)} %bitcast.226), custom_call_target="tpu_custom_call" | custom-call | tf_op jit(solution)/shard_map/reduce_attended/pallas_call | solution.py:355
  467.4 5.7 add_convert_fusion
  481.2 4.4 multiply_reduce_fusion.1
  488.7 43.7 %exchange_branch.1 = (bf16[4,384,576]{2,1,0:T(8,128)(2,1)}, bf16[4,384,192]{2,1,0:T(8,128)(2,1)}, bf16[4,192,384]{2,1,0:T(8,128)(2,1)}, bf16[2,4,144,1536]{3,2,1,0:T(8,128)(2,1)}) custom-call(bf16[4,384,576]{2,1,0:T(8,128)(2,1)} %bitcast.213, bf16[4,384,192]{2,1,0:T(8,128)(2,1)} %bitcast.222, bf16[4,192,384]{2,1,0:T(8,128)(2,1)} %bitcast.230, ...), custom_call_target="tpu_custom_call" | custom-call | tf_op jit(solution)/shard_map/exchange_branch/pallas_call | solution.py:355
  532.4 6.5 convolution_convert_fusion.4
  539.0 7.6 %fusion.73 = f32[1152,768]{1,0:T(8,128)} fusion(bf16[1152,1536]{1,0:T(8,128)(2,1)} %bitcast.286, bf16[768,1536]{1,0:T(8,128)(2,1)} %bitcast.289), kind=kOutput, calls=%fused_computation.248 | convolution fusion | flops 2717908992 | bytes 9437184 | tf_op jit(solution)/shard_map/dot_general | solution.py:452
  561.5 5.9 total_cross.1
  569.7 5.6 convert_reduce_fusion
  575.3 4.9 convolution_convert_fusion.5
  581.1 5.9 convolution_convert_fusion
  587.0 52.7 %reduce_back.1 = (bf16[4,384,768]{2,1,0:T(8,128)(2,1)}, bf16[8,48,576]{2,1,0:T(8,128)(2,1)}, bf16[8,48,192]{2,1,0:T(8,128)(2,1)}, f32[4,8,128]{2,1,0:T(8,128)}, ...) custom-call(bf16[4,384,768]{2,1,0:T(8,128)(2,1)} %bitcast.227, bf16[8,48,576]{2,1,0:T(8,128)(2,1)} %bitcast.233, ...), custom_call_target="tpu_custom_call" | custom-call | tf_op jit(solution)/shard_map/reduce_back/pallas_call | solution.py:355
  643.3 4.2 multiply_reduce_fusion.5
  649.6 20.2 %exchange_tail.1 = (bf16[2,48,1536]{2,1,0:T(8,128)(2,1)}, f32[8,4,8,128]{3,2,1,0:T(8,128)}, bf16[8,48,768]{2,1,0:T(8,128)(2,1)}) custom-call(bf16[144,1536]{1,0:T(8,128)(2,1)} %get-tuple-element.172.refs_0_, f32[8,4,8,128]{3,2,1,0:T(8,128)} %copy_bitcast_fusion.5.refs_1_, bf16[8,48,768]{2,1,0:T(8,128)(2,1)} %bitcast.228), custom_call_target="tpu_custom_call" | custom-call | tf_op jit(solution)/shard_map/exchange_tail/pallas_call | solution.py:355
  671.4 5.5 exchange_tiny.1
  (424 shorter events, 201.5 us)
Async XLA Ops:
  7.2 66.2 %copy-start = (bf16[64,96]{1,0:T(8,128)(2,1)S(1)}, bf16[64,96]{1,0:T(8,128)(2,1)}, u32[]{:S(2)}) copy-start(bf16[64,96]{1,0:T(8,128)(2,1)} %param.43) | copy-start | bytes 36868
  7.2 15.4 %copy-start.11 = (bf16[1,144,1536]{2,1,0:T(8,128)(2,1)S(1)}, bf16[1,144,1536]{2,1,0:T(8,128)(2,1)}, u32[]{:S(2)}) copy-start(bf16[1,144,1536]{2,1,0:T(8,128)(2,1)} %param.28) | copy-start | bytes 1327108
  7.2 301.0 %all-gather.2.cloned.1.call-start = ((), (), s32[]{:S(2)}) async-start(), calls=%async_computation.2 | async-start | bytes 3981312 | tf_op jit(solution)/shard_map/all_gather | solution.py:614
  18.0 40.0 %copy-start.98 = (bf16[96]{0:T(256)(128)(2,1)S(1)}, bf16[96]{0:T(256)(128)(2,1)}, u32[]{:S(2)}) copy-start(bf16[96]{0:T(256)(128)(2,1)} %param.44) | copy-start | bytes 580
  18.0 40.0 %copy-start.59 = (bf16[1,20,1280]{2,1,0:T(8,128)(2,1)S(1)}, bf16[1,20,1280]{2,1,0:T(8,128)(2,1)}, u32[]{:S(2)}) copy-start(bf16[1,20,1280]{2,1,0:T(8,128)(2,1)} %param.29) | copy-start | bytes 153604
  18.0 40.6 %copy-start.33 = (bf16[40,1536]{1,0:T(8,128)(2,1)S(1)}, bf16[40,1536]{1,0:T(8,128)(2,1)}, u32[]{:S(2)}) copy-start(bf16[40,1536]{1,0:T(8,128)(2,1)} %param.45) | copy-start | bytes 368644
  20.0 39.6 %copy-start.26 = (bf16[48,4608]{1,0:T(8,128)(2,1)S(1)}, bf16[48,4608]{1,0:T(8,128)(2,1)}, u32[]{:S(2)}) copy-start(bf16[48,4608]{1,0:T(8,128)(2,1)} %param.47) | copy-start | bytes 1327108
  21.9 45.6 %copy-start.82 = (pred[144]{0:T(512)(128)(4,1)}, pred[144]{0:T(512)(128)(4,1)S(1)}, u32[]{:S(2)}) copy-start(pred[144]{0:T(512)(128)(4,1)S(1)} %get-tuple-element.205) | copy-start | bytes 436
  21.9 45.6 %copy-start.84 = (pred[144]{0:T(512)(128)(4,1)}, pred[144]{0:T(512)(128)(4,1)S(1)}, u32[]{:S(2)}) copy-start(pred[144]{0:T(512)(128)(4,1)S(1)} %get-tuple-element.206) | copy-start | bytes 436
  22.7 44.9 %copy-start.86 = (pred[144]{0:T(512)(128)(4,1)}, pred[144]{0:T(512)(128)(4,1)S(1)}, u32[]{:S(2)}) copy-start(pred[144]{0:T(512)(128)(4,1)S(1)} %get-tuple-element.207) | copy-start | bytes 436
  141.0 344.6 %copy-start.31 = (f32[1536]{0:T(1024)}, f32[1536]{0:T(1024)S(1)}, u32[]{:S(2)}) copy-start(f32[1536]{0:T(1024)S(1)} %get-tuple-element.158) | copy-start | bytes 18436
  141.0 14.1 %copy-start.64 = (s32[576]{0:T(1024)S(1)}, s32[576]{0:T(1024)}, u32[]{:S(2)}) copy-start(s32[576]{0:T(1024)} %iota_sign_fusion) | copy-start | bytes 6916
  169.4 42.5 %copy-start.12 = (bf16[1,144,1536]{2,1,0:T(8,128)(2,1)S(1)}, bf16[1,144,1536]{2,1,0:T(8,128)(2,1)}, u32[]{:S(2)}) copy-start(bf16[1,144,1536]{2,1,0:T(8,128)(2,1)} %param.28) | copy-start | bytes 1327108
  169.4 42.5 %copy-start.21 = (bf16[1,144,1536]{2,1,0:T(8,128)(2,1)S(1)}, bf16[1,144,1536]{2,1,0:T(8,128)(2,1)}, u32[]{:S(2)}) copy-start(bf16[1,144,1536]{2,1,0:T(8,128)(2,1)} %param.51) | copy-start | bytes 1327108
  169.4 42.5 %copy-start.54 = (f32[1536]{0:T(1024)S(1)}, f32[1536]{0:T(1024)}, u32[]{:S(2)}) copy-start(f32[1536]{0:T(1024)} %reshape.939) | copy-start | bytes 18436
  169.4 42.5 %copy-start.71 = (f32[144]{0:T(256)S(1)}, f32[144]{0:T(256)}, u32[]{:S(2)}) copy-start(f32[144]{0:T(256)} %get-tuple-element.184) | copy-start | bytes 1732
  215.0 266.2 %reduce-scatter.3.cloned.1.call-start = ((), (), s32[]{:S(2)}) async-start(), calls=%async_computation.3 | async-start | bytes 3981312 | tf_op jit(solution)/shard_map/reduce_scatter | solution.py:885
  338.6 360.0 %reduce-scatter.5.cloned.1.call-start = ((), (), s32[]{:S(2)}) async-start(), calls=%async_computation.4 | async-start | bytes 2949120 | tf_op jit(solution)/shard_map/reduce_scatter | solution.py:951
  485.6 46.8 %copy-start.20 = (bf16[1152,768]{1,0:T(8,128)(2,1)S(1)}, bf16[1152,768]{1,0:T(8,128)(2,1)}, u32[]{:S(2)}) copy-start(bf16[1152,768]{1,0:T(8,128)(2,1)} %copy-done.19) | copy-start | bytes 5308420
  587.0 55.9 %copy-start.5 = (f32[144,1536]{1,0:T(8,128)S(1)}, f32[144,1536]{1,0:T(8,128)}, u32[]{:S(2)}) copy-start(f32[144,1536]{1,0:T(8,128)} %copy-done.4) | copy-start | bytes 2654212
  587.0 55.9 %copy-start.69 = (f32[144]{0:T(256)S(1)}, f32[144]{0:T(256)}, u32[]{:S(2)}) copy-start(f32[144]{0:T(256)} %copy-done.68) | copy-start | bytes 1732
  587.0 55.9 %copy-start.75 = (f32[144]{0:T(256)S(1)}, f32[144]{0:T(256)}, u32[]{:S(2)}) copy-start(f32[144]{0:T(256)} %copy-done.74) | copy-start | bytes 1732
  643.3 35.0 %copy-start.29 = (bf16[4,48,384]{2,1,0:T(8,128)(2,1)S(1)}, bf16[4,48,384]{2,1,0:T(8,128)(2,1)}, u32[]{:S(2)}) copy-start(bf16[4,48,384]{2,1,0:T(8,128)(2,1)} %get-tuple-element.113) | copy-start | bytes 442372
  647.5 33.0 %copy-start.30 = (bf16[8,48,192]{2,1,0:T(8,128)(2,1)S(1)}, bf16[8,48,192]{2,1,0:T(8,128)(2,1)}, u32[]{:S(2)}) copy-start(bf16[8,48,192]{2,1,0:T(8,128)(2,1)} %get-tuple-element.111) | copy-start | bytes 442372
  (78 other events, 484.4 us)
Sparse Core Ops, SparseCore 0:
  215.1 48.1 all-gather.1
  338.7 91.1 reduce-scatter.2
  556.7 36.4 reduce-scatter.4

commit v3 on v2

v3 whole, which is shorter than its diff:
```python
import functools

import jax
import jax.numpy as jnp
from jax import lax
from jax.experimental import pallas as pl
from jax.experimental.pallas import tpu as pltpu
from jax.sharding import Mesh, PartitionSpec as P

HEAD = 64
TXT = 77
UNIT = 8
EDGE = 48

norm_eps = 1e-06
grn_eps = 1e-06
masked_score = -1000000000.0

AXES = ("grp", "duo", "rows")
MESH_ID = pl.DeviceIdType.MESH
F32 = jnp.float32
BF16 = jnp.bfloat16


class Place:
    def __init__(self):
        self.q, self.c, self.z = (lax.axis_index(axis) for axis in AXES)
        self.G, self.D, self.R = (lax.axis_size(axis) for axis in AXES)

    def team(self):
        for step in range(1, self.D * self.R):
            dc, dz = step // self.R, step % self.R
            yield lax.rem(self.c + dc, self.D), lax.rem(self.z + dz, self.R)

    def groups(self):
        for step in range(1, self.G):
            yield lax.rem(self.q + step, self.G)


def signal_all(barrier, targets):
    for target in targets:
        pl.semaphore_signal(barrier, inc=1, device_id=target, device_id_type=MESH_ID)


def guarded(when, act):
    if when is None:
        act()
    else:
        pl.when(when)(act)


class Flow:
    def __init__(self, send_sem, recv_sem, local_sem=None):
        self.send_sem, self.recv_sem, self.local_sem = send_sem, recv_sem, local_sem
        self.used = 0
        self.kept = 0
        self.open = []
        self.posted = []

    def take(self, count=1):
        at = self.used
        self.used += count
        return at

    def copy(self, src, dst, target, at):
        return pltpu.make_async_remote_copy(
            src_ref=src,
            dst_ref=dst,
            send_sem=self.send_sem.at[at],
            recv_sem=self.recv_sem.at[at],
            device_id=target,
            device_id_type=MESH_ID,
        )

    def post(self, src, dst, target, when=None, lands=None):
        copy = self.copy(src, dst, target, self.take())
        guarded(when, copy.start)
        item = Posted(copy, when if lands is None else lands)
        self.posted.append(item)
        self.open.append((copy.wait_send, when))
        return item

    def land(self, item):
        if not item.landed:
            item.landed = True
            guarded(item.lands, item.copy.wait_recv)

    def keep(self, src, dst, when=None):
        copy = pltpu.make_async_copy(src, dst, self.local_sem.at[self.kept])
        self.kept += 1
        guarded(when, copy.start)
        self.open.append((copy.wait, when))

    def gather_group(self, p, src, dst):
        self.keep(src, dst.at[p.q])
        for q in p.groups():
            self.post(src, dst.at[p.q], {"grp": q})

    def swap_group(self, p, src, dst):
        self.keep(src.at[p.q], dst.at[p.q])
        for q in p.groups():
            self.post(src.at[q], dst.at[p.q], {"grp": q})

    def swap_team(self, p, src, dst):
        mine = p.c * p.R + p.z
        self.keep(src.at[mine], dst.at[mine])
        for c, z in p.team():
            self.post(src.at[c * p.R + z], dst.at[mine], {"duo": c, "rows": z})

    def finish(self):
        for item in self.posted:
            self.land(item)
        for act, when in self.open:
            guarded(when, act)


class LineGather:
    def __init__(self, flow, place, src, dst):
        self.flow, self.p, self.src, self.dst = flow, place, src, dst
        self.up = flow.take(place.R - 1)
        self.down = flow.take(place.R - 1)
        self.side = flow.take(2 * place.R - 1)

    def send(self, block, hop, direction):
        p, dst = self.p, self.dst
        src = self.src if hop == 0 else dst.at[p.c, block]
        at = (self.up if direction > 0 else self.down) + hop
        return self.flow.copy(src, dst.at[p.c, block], {"rows": p.z + direction}, at)

    def across(self, block, number):
        p, dst = self.p, self.dst
        src = self.src if number == 0 else dst.at[p.c, block]
        other = {"duo": lax.rem(p.c + 1, p.D)}
        return self.flow.copy(src, dst.at[p.c, block], other, self.side + number)

    def start(self):
        p = self.p
        for direction, ok in ((1, p.z < p.R - 1), (-1, p.z > 0)):
            copy = self.send(p.z, 0, direction)
            guarded(ok, copy.start)
            self.flow.open.append((copy.wait_send, ok))
        copy = self.across(p.z, 0)
        copy.start()
        self.flow.open += [(copy.wait_recv, None), (copy.wait_send, None)]

    def hop(self, step):
        p = self.p
        for direction, number in ((1, step), (-1, p.R - 1 + step)):
            block = p.z - direction * step
            ok = (block >= 0) if direction > 0 else (block < p.R)
            last = (p.z < p.R - 1) if direction > 0 else (p.z > 0)
            arrived = self.send(block, step - 1, direction)
            side = self.across(block, number)

            def relay(arrived=arrived, side=side, block=block, direction=direction, last=last):
                arrived.wait_recv()
                if step < p.R - 1:
                    pl.when(last)(self.send(block, step, direction).start)
                side.start()

            pl.when(ok)(relay)
            if step < p.R - 1:
                self.flow.open.append((self.send(block, step, direction).wait_send, ok & last))
            self.flow.open += [(side.wait_recv, ok), (side.wait_send, ok)]


class LineReduce:
    def __init__(self, flow, place, part, total_ref, mate, passed, landed):
        self.flow, self.p, self.part, self.total = flow, place, part, total_ref
        self.mate, self.passed, self.landed = mate, passed, landed
        self.side = flow.take(place.R)
        self.line = flow.take(2 * place.R)

    def across(self, block):
        p = self.p
        other = lax.rem(p.c + 1, p.D)
        return self.flow.copy(
            self.part.at[other, block], self.mate.at[block], {"duo": other}, self.side + block
        )

    def along(self, upward, block):
        p = self.p
        way = jnp.where(upward, 1, 0)
        target = {"rows": jnp.where(upward, p.z + 1, p.z - 1)}
        return self.flow.copy(
            self.passed.at[way, block],
            self.landed.at[way, block],
            target,
            self.line + way * p.R + block,
        )

    def steps(self):
        p = self.p
        low = p.z < p.R // 2
        for k in range(p.R - 1):
            for first in (True, False):
                upward = low if first else jnp.logical_not(low)
                block = jnp.where(upward, p.R - 1 - k, k)
                yield upward, block, jnp.where(upward, block > p.z, block < p.z)

    def start(self):
        p = self.p
        for k in range(p.R):
            block = jnp.where(p.z < p.R // 2, p.R - 1 - k, k)
            copy = self.across(block)
            copy.start()
            self.flow.open.append((copy.wait_send, None))

    def rows_of(self, act):
        count = self.part.shape[2]
        step = 16

        @pl.loop(0, count // step)
        def _(number):
            act(pl.ds(pl.multiple_of(number * step, step), step))

    def step(self, upward, block, ok):
        p = self.p
        way = jnp.where(upward, 1, 0)
        behind = jnp.where(upward, p.z > 0, p.z < p.R - 1)

        def act():
            self.across(block).wait_recv()

            @pl.when(behind)
            def _():
                self.along(upward, block).wait_recv()

                def add(rows):
                    self.passed[way, block, rows] = (
                        self.part[p.c, block, rows].astype(F32)
                        + self.mate[block, rows].astype(F32)
                        + self.landed[way, block, rows].astype(F32)
                    ).astype(BF16)

                self.rows_of(add)

            @pl.when(jnp.logical_not(behind))
            def _():
                def add(rows):
                    self.passed[way, block, rows] = (
                        self.part[p.c, block, rows].astype(F32) + self.mate[block, rows].astype(F32)
                    ).astype(BF16)

                self.rows_of(add)

            self.along(upward, block).start()

        pl.when(ok)(act)
        self.flow.open.append((self.along(upward, block).wait_send, ok))

    def close(self):
        p = self.p
        self.across(p.z).wait_recv()

        def base(rows):
            self.total[rows] = self.part[p.c, p.z, rows].astype(F32) + self.mate[
                p.z, rows
            ].astype(F32)

        self.rows_of(base)
        for way, ok in ((1, p.z > 0), (0, p.z < p.R - 1)):

            def more(way=way):
                self.along(way == 1, p.z).wait_recv()

                def add(rows):
                    self.total[rows] += self.landed[way, p.z, rows].astype(F32)

                self.rows_of(add)

            pl.when(ok)(more)

    def steps_all(self):
        for upward, block, ok in self.steps():
            self.step(upward, block, ok)
        self.close()

    def run(self, produce=None, between=None):
        p = self.p
        if produce is None:
            self.steps_all()
            return
        ready = 0

        def more():
            block = line_order(p, ready)
            produce(block)
            copy = self.across(block)
            copy.start()
            self.flow.open.append((copy.wait_send, None))

        for number, (upward, block, ok) in enumerate(self.steps()):
            while ready < min(number + 2, p.R):
                more()
                ready += 1
            self.step(upward, block, ok)
            if between is not None:
                between(number)
        self.close()


def team_kernel(
    ident, name, plan, arrays, results, gathers=(), reduces=(), messages=0, local=1, late=None
):
    D, R = lax.axis_size("duo"), lax.axis_size("rows")
    count_a, count_g, count_r = len(arrays), len(gathers), len(reduces)
    extra = 0 if late is None else 1
    total_sems = messages + (count_g + extra) * (4 * R - 3) + count_r * 3 * R

    def kernel(*refs):
        refs = list(refs)
        ins = refs[:count_a]
        g_in = refs[count_a : count_a + count_g]
        r_in = refs[count_a + count_g : count_a + count_g + count_r]
        refs = refs[count_a + count_g + count_r :]
        outs = refs[: len(results)]
        refs = refs[len(results) :]
        late_out = refs[:extra]
        g_out = refs[extra : extra + count_g]
        r_out = refs[extra + count_g : extra + count_g + count_r]
        refs = refs[extra + count_g + count_r :]
        send_sem, recv_sem, local_sem = refs[:3]
        buffers = refs[3:]
        p = Place()
        flow = Flow(send_sem, recv_sem)
        greet, direct, stay = plan(p, ins, outs)
        barrier = pltpu.get_barrier_semaphore()
        waits = 0
        for target, when in greet:
            if when is None:
                waits = waits + 1
            else:
                waits = waits + jnp.where(when, 1, 0).astype(jnp.int32)
            guarded(when, lambda target=target: signal_all(barrier, [target]))
        pl.semaphore_wait(barrier, waits)
        lines = [LineGather(flow, p, src, dst) for src, dst in zip(g_in, g_out)]
        sums = [
            LineReduce(flow, p, src, dst, *buffers[3 * n : 3 * n + 3])
            for n, (src, dst) in enumerate(zip(r_in, r_out))
        ]
        base = flow.take(messages)
        copies = {}
        arrived = set()

        stays = []

        def landed(number):
            if number not in arrived:
                arrived.add(number)
                guarded(copies[number][2], copies[number][0].wait_recv)

        def run_stage(stage):
            for number, (src, dst, target, after, when, when_stage, lands) in enumerate(direct):
                if when_stage != stage:
                    continue
                for earlier in after:
                    landed(earlier)
                copy = flow.copy(src, dst, target, base + number)
                guarded(when, copy.start)
                copies[number] = (copy, when, lands)
            if late is not None and late[1] == stage:
                for number in range(late[2]):
                    landed(number)
                stays[0][0].wait()
                line = LineGather(flow, p, outs[late[0]], late_out[0])
                line.start()
                own = pltpu.make_async_copy(
                    outs[late[0]], late_out[0].at[p.c, p.z], local_sem.at[local + count_g]
                )
                own.start()
                stays[0] = (own, None)
                if stage:
                    for earlier in range(1, stage + 1):
                        line.hop(earlier)
                lines.append(line)

        for item in sums:
            item.start()
        for line in lines:
            line.start()
        for number, (src, dst, when) in enumerate(
            list(stay) + [(src, dst.at[p.c, p.z], None) for src, dst in zip(g_in, g_out)]
        ):
            copy = pltpu.make_async_copy(src, dst, local_sem.at[number])
            guarded(when, copy.start)
            stays.append((copy, when))
        run_stage(0)
        for step in range(1, R):
            for line in lines:
                line.hop(step)
            run_stage(step)
        for item in sums:
            item.run()
        for copy, when in stays:
            guarded(when, copy.wait)
        for number in copies:
            landed(number)
        for copy, when, _ in copies.values():
            guarded(when, copy.wait_send)
        flow.finish()

    spot = pl.BlockSpec(memory_space=pl.ANY)
    near = pl.BlockSpec(memory_space=pltpu.VMEM)
    out_shape = [jax.ShapeDtypeStruct(shape, kind) for shape, kind in results]
    if late is not None:
        shape, kind = results[late[0]]
        out_shape.append(jax.ShapeDtypeStruct((D, R) + shape, kind))
    out_shape += [jax.ShapeDtypeStruct((D, R) + g.shape, g.dtype) for g in gathers]
    out_shape += [jax.ShapeDtypeStruct(r.shape[2:], F32) for r in reduces]
    scratch = [
        pltpu.SemaphoreType.DMA((total_sems,)),
        pltpu.SemaphoreType.DMA((total_sems,)),
        pltpu.SemaphoreType.DMA((local + count_g + extra,)),
    ]
    for r in reduces:
        block = r.shape[1:]
        scratch += [
            pltpu.VMEM(block, BF16),
            pltpu.VMEM((2,) + block, BF16),
            pltpu.VMEM((2,) + block, BF16),
        ]
    return pl.pallas_call(
        kernel,
        out_shape=out_shape,
        in_specs=[spot] * (count_a + count_g) + [near] * count_r,
        out_specs=[spot] * (len(results) + extra + count_g) + [near] * count_r,
        scratch_shapes=scratch,
        compiler_params=pltpu.CompilerParams(
            collective_id=ident, has_side_effects=True, vmem_limit_bytes=56 * 2**20
        ),
        name=name,
    )(*arrays, *gathers, *reduces)


def team_greet(p):
    return [({"duo": c, "rows": z}, None) for c, z in p.team()]


def group_greet(p):
    return [({"grp": q}, None) for q in p.groups()]


class Plan:
    def __init__(self, p):
        self.p = p
        self.messages, self.local, self.greet = [], [], []

    def add(self, src, dst, target, after=(), when=None, stage=0, lands=None):
        self.messages.append((src, dst, target, after, when, stage, when if lands is None else lands))
        return len(self.messages) - 1

    def team_swap(self, src, dst, stage=0):
        p = self.p
        mine = p.c * p.R + p.z
        for c, z in p.team():
            self.add(src.at[c * p.R + z], dst.at[mine], {"duo": c, "rows": z}, stage=stage)
        self.local.append((src.at[mine], dst.at[mine], None))

    def team_gather(self, src, dst, stage=0):
        p = self.p
        mine = p.c * p.R + p.z
        for c, z in p.team():
            self.add(src, dst.at[mine], {"duo": c, "rows": z}, stage=stage)
        self.local.append((src, dst.at[mine], None))

    def group_gather(self, src, dst, late=None):
        p = self.p
        self.local.append((src, dst.at[p.q], None))
        if late is None or p.G != 4:
            for q in p.groups():
                self.add(src, dst.at[p.q], {"grp": q})
            return
        across = p.q + 1 - 2 * lax.rem(p.q, 2)
        along = lax.rem(p.q + 2, 4)
        one = self.add(src, dst.at[p.q], {"grp": across})
        two = self.add(src, dst.at[p.q], {"grp": along})
        half = src.shape[0] // 2
        top, bottom = pl.ds(0, half), pl.ds(half, half)
        self.add(
            dst.at[across, top], dst.at[across, top], {"grp": along}, after=(one,), stage=late
        )
        self.add(
            dst.at[along, bottom],
            dst.at[along, bottom],
            {"grp": across},
            after=(two,),
            stage=late,
        )

    def group_swap(self, src, dst, stage=0):
        p = self.p
        for q in p.groups():
            self.add(src.at[q], dst.at[p.q], {"grp": q}, stage=stage)
        self.local.append((src.at[p.q], dst.at[p.q], None))

    def done(self):
        p = self.p
        return team_greet(p) + group_greet(p) + self.greet, self.messages, self.local


def layer_stats(values):
    center = values - jnp.mean(values, axis=-1, keepdims=True)
    spread = jnp.mean(center * center, axis=-1, keepdims=True)
    inverse = lax.rsqrt(spread + norm_eps)
    return center * inverse, inverse


def layer_back(grad, hat, inverse):
    first = jnp.mean(grad, axis=-1, keepdims=True)
    second = jnp.mean(grad * hat, axis=-1, keepdims=True)
    return inverse * (grad - first - hat * second)


def mm(left, right):
    return jnp.dot(left, right, preferred_element_type=F32)


def mm_t(left, right):
    return lax.dot_general(left, right, (((1,), (1,)), ((), ())), preferred_element_type=F32)


def t_mm(left, right):
    return lax.dot_general(left, right, (((0,), (0,)), ((), ())), preferred_element_type=F32)


def columns_of(bucket_ids):
    return jnp.where(
        bucket_ids == 0, 9 * UNIT // 2, jnp.where(bucket_ids == 1, 3 * UNIT, 9 * UNIT // 4)
    )


def pixel_mask(positions, height, width, cols):
    row_at = positions // cols
    col_at = positions % cols
    return ((row_at < height) & (col_at < width)).astype(F32)


def spots(shapes):
    return [jax.ShapeDtypeStruct(shape, kind) for shape, kind in shapes]


def local_kernel(name, kernel, arrays, results, scratch=(), scalars=0):
    near = pl.BlockSpec(memory_space=pltpu.VMEM)
    numbers = pl.BlockSpec(memory_space=pltpu.SMEM)
    return pl.pallas_call(
        kernel,
        out_shape=spots(results),
        in_specs=[numbers] * scalars + [near] * (len(arrays) - scalars),
        out_specs=[near] * len(results),
        scratch_shapes=list(scratch),
        compiler_params=pltpu.CompilerParams(vmem_limit_bytes=56 * 2**20),
        name=name,
    )(*arrays)


class Sizes:
    def __init__(self, latents, clip_tokens, in_weight, in_bias, conv_bias, map_weight):
        self.G, self.D, self.R = (lax.axis_size(axis) for axis in AXES)
        self.T = self.D * self.R
        self.S = self.T * self.G
        self.N, self.C = latents.shape[1:]
        self.pixels = self.R * self.N
        self.FFS = in_bias.shape[0]
        self.FL = self.G * self.FFS
        self.FF = in_weight.shape[1]
        self.cs = conv_bias.shape[0]
        self.ms = map_weight.shape[0]
        self.mp = -(-self.ms // 16) * 16
        self.slots = clip_tokens.shape[1]
        self.sp = -(-self.slots // 16) * 16
        self.texts = self.R * self.slots
        self.HW = self.C // self.T
        self.even = self.G == self.R
        self.Q = self.G if self.even else 1
        self.places = [(g, d, r) for g in range(self.G) for d in range(self.D) for r in range(self.R)]


def rows_cols(first, count, cols):
    position = (first + lax.broadcasted_iota(jnp.int32, (count, 1), 0)).astype(F32)
    row = jnp.floor((position + 0.5) / cols)
    return row, position - row * cols


def float_cols(bucket):
    return jnp.where(bucket == 0, 9.0 * UNIT / 2, jnp.where(bucket == 1, 3.0 * UNIT, 9.0 * UNIT / 4))


WIDTHS = (9 * UNIT // 2, 3 * UNIT, 9 * UNIT // 4)
SMALL = 32
VEC = 16


def cut_kernel(m, arrays):
    def kernel(h_ref, w_ref, b_ref, in_ref, qkv_ref, map_ref, clip_ref, lat_ref, cot_ref, cw_ref, *refs):
        vectors, refs = refs[:5], refs[5:]
        te_ref, tm_ref, f0, f1, f2 = refs[:5]
        in_out, qkv_out, map_out, clip_out, masked_out, gres_out, small_out, f_out, small, fv = refs[5:]
        for g in range(m.G):
            for t in range(m.T):
                start = m.FFS * (g * m.T + t)
                in_out[t, :, pl.ds(g * m.FFS, m.FFS)] = in_ref[:, pl.ds(start, m.FFS)]
        for d in range(m.D):
            for r in range(m.R):
                for j in range(3):
                    start = m.C * j + m.HW * (m.D * r + d)
                    qkv_out[d * m.R + r, :, pl.ds(j * m.HW, m.HW)] = qkv_ref[:, pl.ds(start, m.HW)]
        map_out[...] = jnp.zeros_like(map_out)
        for t in range(m.T):
            map_out[t, pl.ds(0, m.ms)] = map_ref[:, pl.ds(t * m.HW, m.HW)]
        clip_out[...] = jnp.zeros_like(clip_out)
        clip_out[pl.ds(0, m.slots)] = clip_ref[0]
        z = lax.axis_index("rows")
        row, col = rows_cols(z * m.N, m.N, float_cols(b_ref[0]))
        keep = (row < h_ref[0].astype(F32)) & (col < w_ref[0].astype(F32))
        masked_out[...] = jnp.where(keep, lat_ref[0].astype(F32), 0.0).astype(BF16)
        gres_out[...] = jnp.where(keep, cot_ref[0].astype(F32), 0.0).astype(BF16)
        small[...] = jnp.zeros_like(small)
        small[pl.ds(0, 9), pl.ds(0, m.cs)] = cw_ref[...].astype(F32)
        for number, ref in enumerate(vectors):
            small[pl.ds(9 + number, 1), pl.ds(0, ref.shape[1])] = ref[...].astype(F32)
        small[pl.ds(14, 1), pl.ds(0, te_ref.shape[1])] = te_ref[...].astype(F32)
        lane = lax.broadcasted_iota(jnp.int32, (1, 128), 1)
        facts = jnp.where(lane == 0, h_ref[0], jnp.where(lane == 1, w_ref[0], b_ref[0]))
        small[pl.ds(15, 1)] = facts.astype(F32)
        small[pl.ds(16, 1), pl.ds(0, m.texts)] = tm_ref[...].astype(F32)
        small_out[...] = small[...].astype(BF16)
        fv[...] = jnp.zeros_like(fv)
        for number, ref in enumerate((f0, f1, f2)):
            fv[pl.ds(number, 1)] = ref[...].astype(F32)
        f_out[...] = fv[...].astype(BF16)

    return local_kernel(
        "cut_weights",
        kernel,
        arrays,
        [
            ((m.T, m.cs, m.FL), BF16),
            ((m.T, m.cs, 3 * m.HW), BF16),
            ((m.T, m.mp, m.HW), BF16),
            ((m.sp, arrays[6].shape[2]), BF16),
            ((m.N, m.C), BF16),
            ((m.N, m.C), BF16),
            ((SMALL, 128), BF16),
            ((16, m.FFS), BF16),
        ],
        [pltpu.VMEM((SMALL, 128), F32), pltpu.VMEM((16, m.FFS), F32)],
        scalars=3,
    )


def fill_extended(m, extended, edges_ref, mid_ref):
    z = lax.axis_index("rows")
    extended[pl.ds(0, EDGE)] = jnp.where(z > 0, edges_ref[0].astype(F32), 0.0)
    extended[pl.ds(EDGE, m.N)] = mid_ref[...].astype(F32)
    extended[pl.ds(EDGE + m.N, EDGE)] = jnp.where(z < m.R - 1, edges_ref[1].astype(F32), 0.0)


def each_bucket(bucket, act):
    for number, width in enumerate(WIDTHS):
        pl.when(bucket == number)(functools.partial(act, width))


def each_column_block(m, act):
    @pl.loop(0, m.C // 128)
    def _(number):
        act(pl.ds(pl.multiple_of(number * 128, 128), 128))


def tap_steps():
    return [(index, index // 3 - 1, index % 3 - 1) for index in range(9)]


def conv_kernel(m, b_ref, edges, masked, small_all, time_weight, time_bias):
    def kernel(b_ref, edges_ref, mid_ref, small_ref, tw_ref, tb_ref, normed, hat, inv, vec, mod, keys, pix, extended, conv, item, te):
        vec[...] = jnp.zeros_like(vec)
        for s, (g, d, r) in enumerate(m.places):
            piece = small_ref[d, r, g].astype(F32)
            vec[pl.ds(0, 13), pl.ds(s * m.cs, m.cs)] = piece[:13, : m.cs]
            half = m.S // 2
            vec[pl.ds(13 + s // half, 1), pl.ds(2 * m.cs * (s % half), 2 * m.cs)] = piece[
                13:14, : 2 * m.cs
            ]
            if r == 0:
                item[pl.ds(m.D * g + d, 1)] = piece[14:15]
        te[...] = item[...][:, : te.shape[1]].astype(BF16)
        mod[...] = jnp.zeros_like(mod)
        mod[pl.ds(0, te.shape[0]), pl.ds(0, 2 * m.cs)] = mm(te[...], tw_ref[...]) + tb_ref[...].astype(F32)
        q = lax.axis_index("grp")
        for d in range(m.D):
            facts = small_ref[d, 0, q].astype(F32)
            row, col = rows_cols(0, m.pixels, float_cols(facts[15:16, 2:3]))
            inside = (row < facts[15:16, 0:1]) & (col < facts[15:16, 1:2])
            keys[d, pl.ds(0, m.pixels)] = jnp.where(inside, 1.0, 0.0)
            text = facts.T[: m.texts, 16:17]
            slot = lax.broadcasted_iota(jnp.int32, (m.texts, 1), 0)
            keys[d, pl.ds(m.pixels, m.texts)] = jnp.where(slot < TXT, text, 0.0)
        fill_extended(m, extended, edges_ref, mid_ref)
        z = lax.axis_index("rows")

        def taps(width):
            _, col = rows_cols(z * m.N, m.N, float(width))

            def block(lanes):
                total = jnp.zeros((m.N, 128), F32) + vec[pl.ds(9, 1), lanes]
                for index, dy, dx in tap_steps():
                    piece = extended[pl.ds(EDGE + dy * width + dx, m.N), lanes]
                    ok = (col + dx >= 0) & (col + dx < width)
                    total = total + jnp.where(ok, piece, 0.0) * vec[pl.ds(index, 1), lanes]
                conv[:, lanes] = total

            each_column_block(m, block)

        each_bucket(b_ref[0], taps)
        values, inverse = layer_stats(conv[...])
        hat[...] = values
        normed[...] = values.astype(BF16)
        inv[...] = inverse
        pix[...] = keys[lax.axis_index("duo"), pl.ds(pl.multiple_of(z * m.N, 8), m.N)]

    items = m.G * m.D
    return local_kernel(
        "convolve",
        kernel,
        [b_ref, edges, masked, small_all, time_weight, time_bias],
        [
            ((m.N, m.C), BF16),
            ((m.N, m.C), F32),
            ((m.N, 1), F32),
            ((VEC, m.C), F32),
            ((-(-items // 8) * 8, 128), F32),
            ((m.D, m.pixels + m.texts, 1), F32),
            ((m.N, 1), F32),
        ],
        [
            pltpu.VMEM((m.N + 2 * EDGE, m.C), F32),
            pltpu.VMEM((m.N, m.C), F32),
            pltpu.VMEM((items, 128), F32),
            pltpu.VMEM((items, time_weight.shape[0]), BF16),
        ],
        scalars=1,
    )


def attention_kernel(m, two_all, gres_all, mapped_all, weight, proj, bias, key_keep):
    heads = m.HW // HEAD
    keys = m.pixels + m.texts
    scale = HEAD ** (-0.5)
    HW, C, pixels, texts = m.HW, m.C, m.pixels, m.texts
    wide = C // m.Q

    def kernel(two_ref, gres_ref, map_ref, w_ref, p_ref, bias_ref, keep_ref, res_out, two_out, map_out, gw_out, gp_out, gb_out,
               qkv, k_all, v_all, dk, dv, o_t, dq_t, g_all, dqkv, dtext, att, gw, gp):
        step = pl.program_id(0)

        @pl.when(step == 0)
        def _():
            gw[...] = jnp.zeros_like(gw)
            gp[...] = jnp.zeros_like(gp)
            gb_out[...] = jnp.zeros_like(gb_out)

        qkv[...] = (mm(two_ref[0], w_ref[...]) + bias_ref[...]).astype(BF16)
        text = jnp.zeros((texts, 3 * HW), F32) + bias_ref[...]
        for t in range(m.T):
            text = text + mm(map_ref[t], w_ref[pl.ds(t * HW, HW)])
        text = text.astype(BF16)
        g = jnp.zeros((pixels, HW), F32)
        for n in range(m.Q):
            g = g + mm_t(gres_ref[0, :, pl.ds(n * wide, wide)], p_ref[n])
        g_all[...] = g.astype(BF16)
        k_all[pl.ds(0, pixels)] = qkv[:, HW : 2 * HW]
        k_all[pl.ds(pixels, texts)] = text[:, HW : 2 * HW]
        v_all[pl.ds(0, pixels)] = qkv[:, 2 * HW :]
        v_all[pl.ds(pixels, texts)] = text[:, 2 * HW :]
        k_t = k_all[...].T
        v_t = v_all[...].T
        dk[...] = jnp.zeros_like(dk)
        dv[...] = jnp.zeros_like(dv)
        o_t[...] = jnp.zeros_like(o_t)
        dq_t[...] = jnp.zeros_like(dq_t)
        lane = lax.broadcasted_iota(jnp.int32, (1, HW), 1)
        line = lax.broadcasted_iota(jnp.int32, (HW, 1), 0)
        alive = keep_ref[0] > 0

        @pl.loop(0, heads)
        def _(head):
            low = head * HEAD
            in_head = (lane >= low) & (lane < low + HEAD)
            in_line = (line >= low) & (line < low + HEAD)
            q_h = jnp.where(in_head, qkv[:, :HW], 0).astype(BF16)
            g_h = jnp.where(in_head, g_all[...], 0).astype(BF16)
            scores = mm_t(k_all[...], q_h) * scale
            scores = jnp.where(alive, scores, masked_score)
            top = jnp.max(scores, axis=0, keepdims=True)
            weights = jnp.exp(scores - top)
            probs = weights / jnp.sum(weights, axis=0, keepdims=True)
            probs_low = probs.astype(BF16)
            v_h = jnp.where(in_line, v_t, 0).astype(BF16)
            o_t[...] += mm(v_h, probs_low)
            dv[...] += mm(probs_low, g_h)
            grad_probs = mm_t(v_all[...], g_h)
            sums = jnp.sum(probs * grad_probs, axis=0, keepdims=True)
            grad_scores = (probs * (grad_probs - sums)).astype(BF16)
            k_h = jnp.where(in_line, k_t, 0).astype(BF16)
            dq_t[...] += mm(k_h, grad_scores)
            dk[...] += mm(grad_scores, q_h)

        o_low = o_t[...].astype(BF16)
        att[...] = o_t[...].T.astype(BF16)
        dqkv[:, :HW] = (dq_t[...].T * scale).astype(BF16)
        dqkv[:, HW : 2 * HW] = (dk[pl.ds(0, pixels)] * scale).astype(BF16)
        dqkv[:, 2 * HW :] = dv[pl.ds(0, pixels)].astype(BF16)
        dtext[:, :HW] = jnp.zeros((texts, HW), BF16)
        dtext[:, HW : 2 * HW] = (dk[pl.ds(pixels, texts)] * scale).astype(BF16)
        dtext[:, 2 * HW :] = dv[pl.ds(pixels, texts)].astype(BF16)
        gb_out[pl.ds(0, 1)] += jnp.sum(dqkv[...].astype(F32), axis=0, keepdims=True) + jnp.sum(
            dtext[...].astype(F32), axis=0, keepdims=True
        )
        for n in range(m.Q):
            block = pl.ds(n * wide, wide)
            res_out[0, :, block] = mm(att[...], p_ref[n]).astype(BF16)
            gp[n] += mm(o_low, gres_ref[0, :, block])
        two_out[0] = mm_t(dqkv[...], w_ref[...]).astype(BF16)
        gw[...] += t_mm(two_ref[0], dqkv[...])
        for t in range(m.T):
            rows = pl.ds(t * HW, HW)
            map_out[t] = mm_t(dtext[...], w_ref[rows]).astype(BF16)
            gw[rows] += t_mm(map_ref[t], dtext[...])

        @pl.when(step == m.D - 1)
        def _():
            gw_out[...] = gw[...].astype(BF16)
            gp_out[...] = gp[...].astype(BF16)

    def item(shape):
        return pl.BlockSpec((1,) + shape, lambda i: (i, 0, 0))

    def fixed(shape):
        return pl.BlockSpec(shape, lambda i: (0,) * len(shape))

    slots = pl.BlockSpec((m.T, texts, HW), lambda i: (0, i, 0))
    return pl.pallas_call(
        kernel,
        grid=(m.D,),
        out_shape=spots(
            [
                ((m.D, pixels, C), BF16),
                ((m.D, pixels, C), BF16),
                ((m.T, m.D * texts, HW), BF16),
                ((C, 3 * HW), BF16),
                ((m.Q, HW, wide), BF16),
                ((8, 3 * HW), F32),
            ]
        ),
        in_specs=[
            item((pixels, C)),
            item((pixels, C)),
            slots,
            fixed((C, 3 * HW)),
            fixed((m.Q, HW, wide)),
            fixed((1, 3 * HW)),
            item((keys, 1)),
        ],
        out_specs=[
            item((pixels, C)),
            item((pixels, C)),
            slots,
            fixed((C, 3 * HW)),
            fixed((m.Q, HW, wide)),
            fixed((8, 3 * HW)),
        ],
        scratch_shapes=[
            pltpu.VMEM((pixels, 3 * HW), BF16),
            pltpu.VMEM((keys, HW), BF16),
            pltpu.VMEM((keys, HW), BF16),
            pltpu.VMEM((keys, HW), F32),
            pltpu.VMEM((keys, HW), F32),
            pltpu.VMEM((HW, pixels), F32),
            pltpu.VMEM((HW, pixels), F32),
            pltpu.VMEM((pixels, HW), BF16),
            pltpu.VMEM((pixels, 3 * HW), BF16),
            pltpu.VMEM((texts, 3 * HW), BF16),
            pltpu.VMEM((pixels, HW), BF16),
            pltpu.VMEM((C, 3 * HW), F32),
            pltpu.VMEM((m.Q, HW, wide), F32),
        ],
        compiler_params=pltpu.CompilerParams(vmem_limit_bytes=60 * 2**20),
        name="attention_block",
    )(two_all, gres_all, mapped_all, weight, proj, bias, key_keep)


def conv_back_kernel(m, b_ref, grad_in, hat, inv, edges, masked, vec_grads, qv_grads, modulate_grads):
    def kernel(b_ref, g_ref, hat_ref, inv_ref, edges_ref, mid_ref, vec_ref, qv_ref, gm_ref, grad, low, tiny, extended, vec):
        values = layer_back(g_ref[...], hat_ref[...], inv_ref[...])
        grad[...] = values
        low[...] = values.astype(BF16)
        fill_extended(m, extended, edges_ref, mid_ref)
        vec[pl.ds(9, 1)] = jnp.sum(values, axis=0, keepdims=True)
        vec[pl.ds(10, 3)] = vec_ref[pl.ds(0, 3)]
        vec[pl.ds(13, 3)] = jnp.zeros((3, m.C), F32)
        z = lax.axis_index("rows")

        def taps(width):
            _, col = rows_cols(z * m.N, m.N, float(width))

            def block(lanes):
                value = grad[:, lanes]
                for index, dy, dx in tap_steps():
                    piece = extended[pl.ds(EDGE + dy * width + dx, m.N), lanes]
                    ok = (col + dx >= 0) & (col + dx < width)
                    vec[pl.ds(index, 1), lanes] = jnp.sum(
                        jnp.where(ok, piece, 0.0) * value, axis=0, keepdims=True
                    )

            each_column_block(m, block)

        each_bucket(b_ref[0], taps)
        tiny[...] = jnp.zeros_like(tiny)
        half = m.S // 2
        pair = 2 * m.cs
        for s, (g, d, r) in enumerate(m.places):
            t = d * m.R + r
            tiny[t, g, pl.ds(0, 13), pl.ds(0, m.cs)] = vec[pl.ds(0, 13), pl.ds(s * m.cs, m.cs)]
            side, at = pl.ds(s // half, 1), pl.ds(pair * (s % half), pair)
            tiny[t, g, pl.ds(13, 1), pl.ds(0, pair)] = qv_ref[side, at]
            tiny[t, g, pl.ds(14, 1), pl.ds(0, pair)] = gm_ref[side, at]

    return local_kernel(
        "convolve_back",
        kernel,
        [b_ref, grad_in, hat, inv, edges, masked, vec_grads, qv_grads, modulate_grads],
        [((m.N, m.C), F32), ((m.N, m.C), BF16), ((m.T, m.G, 16, 128), F32)],
        [pltpu.VMEM((m.N + 2 * EDGE, m.C), F32), pltpu.VMEM((VEC, m.C), F32)],
        scalars=1,
    )


def finish_kernel(m, b_ref, edges, low, after, pix, vec, in_team, qkv_team, map_team, proj_team):
    def kernel(b_ref, edges_ref, low_ref, after_ref, pix_ref, vec_ref, in_ref, qkv_ref, map_ref, proj_ref,
               lat_out, in_out, qkv_out, map_out, proj_out, extended):
        fill_extended(m, extended, edges_ref, low_ref)
        z = lax.axis_index("rows")
        keep = pix_ref[...] > 0

        def taps(width):
            _, col = rows_cols(z * m.N, m.N, float(width))

            def block(lanes):
                total = jnp.zeros((m.N, 128), F32)
                for index, dy, dx in tap_steps():
                    piece = extended[pl.ds(EDGE - dy * width - dx, m.N), lanes]
                    ok = (col - dx >= 0) & (col - dx < width)
                    total = total + jnp.where(ok, piece, 0.0) * vec_ref[pl.ds(index, 1), lanes]
                lat_out[0, :, lanes] = after_ref[:, lanes] + jnp.where(keep, total, 0.0)

            each_column_block(m, block)

        each_bucket(b_ref[0], taps)
        for g in range(m.G):
            for t in range(m.T):
                start = m.FFS * (g * m.T + t)
                in_out[:, pl.ds(start, m.FFS)] = in_ref[t, :, pl.ds(g * m.FFS, m.FFS)].astype(F32)
        for d in range(m.D):
            for r in range(m.R):
                for j in range(3):
                    start = m.C * j + m.HW * (m.D * r + d)
                    qkv_out[:, pl.ds(start, m.HW)] = qkv_ref[
                        d * m.R + r, :, pl.ds(j * m.HW, m.HW)
                    ].astype(F32)
        for t in range(m.T):
            map_out[:, pl.ds(t * m.HW, m.HW)] = map_ref[t].astype(F32)[: m.ms]
        wide = m.C // m.Q
        for n in range(m.Q):
            proj_out[:, pl.ds(n * wide, wide)] = proj_ref[n].astype(F32)

    return local_kernel(
        "finish",
        kernel,
        [b_ref, edges, low, after, pix, vec, in_team, qkv_team, map_team, proj_team],
        [
            ((1, m.N, m.C), F32),
            ((m.cs, m.FF), F32),
            ((m.cs, 3 * m.C), F32),
            ((m.ms, m.C), F32),
            ((m.cs, m.C), F32),
        ],
        [pltpu.VMEM((m.N + 2 * EDGE, m.C), F32)],
        scalars=1,
    )


class Posted:
    def __init__(self, copy, lands):
        self.copy, self.lands, self.landed = copy, lands, False


def line_order(p, number):
    low = p.z < p.R // 2
    far, near = p.R - 1 - number // 2, number // 2
    if number % 2:
        far, near = near, far
    return jnp.where(low, far, near)


def chunks(count, act, step=16):
    @pl.loop(0, count // step)
    def _(number):
        act(pl.ds(pl.multiple_of(number * step, step), step))


def greet_all(p, targets):
    barrier = pltpu.get_barrier_semaphore()
    waits = 0
    for target, when in targets:
        if when is None:
            waits = waits + 1
        else:
            waits = waits + jnp.where(when, 1, 0).astype(jnp.int32)
        guarded(when, lambda target=target: signal_all(barrier, [target]))
    pl.semaphore_wait(barrier, waits)


def fused_kernel(ident, name, greet, act, near, loads, far, near_out, far_out, scratch, sems, local):
    close = pl.BlockSpec(memory_space=pltpu.VMEM)
    spot = pl.BlockSpec(memory_space=pl.ANY)
    counts = [len(near), len(loads), len(far), len(near_out), len(far_out), len(scratch), len(loads)]

    def kernel(*refs):
        groups = []
        for count in counts:
            groups.append(refs[:count])
            refs = refs[count:]
        send_sem, recv_sem, local_sem, load_sem = refs
        near, sources, far, near_out, far_out, scratch, held = groups
        brought = []
        for number, (source, place) in enumerate(zip(sources, held)):
            copy = pltpu.make_async_copy(source, place, load_sem.at[number])
            copy.start()
            brought.append(Brought(copy, place))
        p = Place()
        flow = Flow(send_sem, recv_sem, local_sem)
        greet_all(p, greet(p))
        act(p, flow, near, brought, far, near_out, far_out, scratch)
        flow.finish()

    return pl.pallas_call(
        kernel,
        out_shape=spots(near_out + far_out),
        in_specs=[close] * len(near) + [spot] * (len(loads) + len(far)),
        out_specs=[close] * len(near_out) + [spot] * len(far_out),
        scratch_shapes=list(scratch)
        + [pltpu.VMEM(array.shape, array.dtype) for array in loads]
        + [
            pltpu.SemaphoreType.DMA((sems,)),
            pltpu.SemaphoreType.DMA((sems,)),
            pltpu.SemaphoreType.DMA((local,)),
            pltpu.SemaphoreType.DMA((max(len(loads), 1),)),
        ],
        compiler_params=pltpu.CompilerParams(
            collective_id=ident, has_side_effects=True, vmem_limit_bytes=63 * 2**20
        ),
        name=name,
    )(*near, *loads, *far)


class Brought:
    def __init__(self, copy, place):
        self.copy, self.place, self.here = copy, place, False

    def get(self):
        if not self.here:
            self.copy.wait()
            self.here = True
        return self.place


def gather_sems(m):
    return 4 * m.R - 3


def reduce_sems(m):
    return 3 * m.R


def reduce_buffers(m, count, width, part=True):
    block = (m.R, count, width)
    mine = [pltpu.VMEM((m.D,) + block, BF16)] if part else []
    return mine + [
        pltpu.VMEM(block, BF16),
        pltpu.VMEM((2,) + block, BF16),
        pltpu.VMEM((2,) + block, BF16),
    ]


def spread_greet(m, p):
    greet = []
    for step in range(m.G):
        source = {"grp": p.z, "duo": p.c, "rows": lax.rem(p.q - step + m.G, m.G)}
        greet.append((source, None if step else p.q != p.z))
    return greet


def common_greet(p):
    return team_greet(p) + group_greet(p)


def up_kernel(m, normed_all, in_full, in_bias, key_keep, clip_all, map_full, vec):
    step = m.N
    per = m.pixels // step
    root = 0.5**0.5

    def kernel(x_ref, w_ref, b_ref, keep_ref, clip_ref, map_ref, vec_ref,
               active, slope, norms, total, silu, mapped, squares, weight, text):
        squares[...] = jnp.zeros_like(squares)

        @pl.loop(0, m.D * per)
        def _(number):
            rows = pl.ds(pl.multiple_of(number * step, 16), step)
            hidden = mm(x_ref[rows], w_ref[...]) + b_ref[...]
            gate = 0.5 * (1.0 + lax.erf(hidden * root))
            value = hidden * gate
            active[rows] = value
            slope[rows] = gate + hidden * (jnp.exp(-0.5 * hidden * hidden) * 0.3989422804014327)
            item = number // per
            inside = pl.ds(pl.multiple_of((number - item * per) * step, 16), step)
            squares[pl.ds(item, 1)] += jnp.sum(
                keep_ref[item, inside] * value * value, axis=0, keepdims=True
            )

        norms[...] = jnp.sqrt(squares[...])
        total[...] = jnp.broadcast_to(jnp.sum(norms[...], axis=1, keepdims=True), total.shape)
        for t in range(m.T):
            piece = clip_ref[t].astype(F32)[: m.slots]
            text[pl.ds(t * m.slots, m.slots)] = piece / (1.0 + jnp.exp(-piece))
        silu[...] = text[...].astype(BF16)
        for g in range(m.G):
            for t in range(m.T):
                at = m.ms * (g * m.T + t)
                piece = map_ref[g, pl.ds(t * m.mp, m.mp)].astype(F32)
                weight[pl.ds(at, m.ms)] = piece[: m.ms]
        for t in range(m.T):
            @pl.when(lax.axis_index("duo") * m.R + lax.axis_index("rows") == t)
            def _():
                bias = vec_ref[pl.ds(11, 1), pl.ds(t * m.HW, m.HW)]
                mapped[...] = (mm(silu[...], weight[...].astype(BF16)) + bias).astype(BF16)

    texts = m.D * m.texts
    cond = clip_all.shape[2]
    return local_kernel(
        "hidden_units",
        kernel,
        [normed_all, in_full, in_bias, key_keep, clip_all, map_full, vec],
        [
            ((m.D * m.pixels, m.FL), F32),
            ((m.D * m.pixels, m.FL), F32),
            ((8, m.FL), F32),
            ((8, 128), F32),
            ((texts, cond), BF16),
            ((texts, m.HW), BF16),
        ],
        [
            pltpu.VMEM((8, m.FL), F32),
            pltpu.VMEM((cond, m.HW), F32),
            pltpu.VMEM((texts, cond), F32),
        ],
    )


def team_sum(m, p, flow, own, everyone):
    mine = p.c * m.R + p.z
    posted = [
        flow.post(own, everyone.at[mine], {"duo": c, "rows": z}) for c, z in p.team()
    ]

    def total():
        for item in posted:
            flow.land(item)
        result = own[...]
        for step, (c, z) in enumerate(p.team()):
            result = result + everyone[c * m.R + z]
        return result

    return total


def branch_kernel(m, active, norms, total, out_full, gain, grn_bias, latents, keep, vec, mod_all, qkv_rows, mapped, gres, proj_part):
    near = [norms, total, gain, grn_bias, keep, mod_all]
    loads = [active, out_full, latents, vec]
    far = [qkv_rows, mapped, gres] + ([proj_part] if m.even else [])
    N, C = m.N, m.C
    rows_all = m.D * m.pixels

    def act(p, flow, near, loads, far, near_out, far_out, scratch):
        norms, total, gain, grn_bias, keep, mod_all = near
        grn, after, hat, inv, two, ratio, means, mods = near_out
        two_all, mapped_all, gres_all, qkv_all = far_out[:4]
        everyone, part, mate, passed, landed, branch, slopes = scratch
        add_up = team_sum(m, p, flow, total, everyone)
        flow.gather_group(p, far[0], qkv_all)
        if m.even:
            flow.gather_group(p, far[3], far_out[4])
        text_line = LineGather(flow, p, far[1], mapped_all)
        grad_line = LineGather(flow, p, far[2], gres_all)
        two_line = LineGather(flow, p, two, two_all)
        half = m.S // 2
        pair = 2 * m.cs
        for s, (g, d, r) in enumerate(m.places):
            item = pl.ds(m.D * p.q + p.c, 1)
            mods[pl.ds(s // half, 1), pl.ds(pair * (s % half), pair)] = mod_all[d, r, g, item, pl.ds(0, pair)]
        mean = add_up() / m.FF + grn_eps
        means[...] = mean
        ratio[...] = norms[...] / mean[:, :1]
        slopes[...] = gain[...] * ratio[...] + 1.0
        line = LineReduce(flow, p, part, branch, mate, passed, landed)
        active, out_w, lat, vec = (load.get() for load in loads)

        def produce(block):
            for d in range(m.D):
                rows = pl.ds(pl.multiple_of(d * m.pixels + block * N, 16), N)
                low = (active[rows] * slopes[pl.ds(d, 1)] + grn_bias[...]).astype(BF16)
                grn[rows] = low
                part[d, block] = mm(low, out_w[...]).astype(BF16)

        line.run(produce)
        text_line.start()

        def tail(rows):
            value = lat[rows].astype(F32) + keep[rows] * (branch[rows] + vec[pl.ds(10, 1)])
            after[rows] = value
            second = value * (1.0 + mods[pl.ds(0, 1)]) + mods[pl.ds(1, 1)]
            normal, inverse = layer_stats(second)
            hat[rows] = normal
            inv[rows] = inverse
            two[rows] = normal.astype(BF16)

        chunks(N, tail)
        two_line.start()
        grad_line.start()
        flow.keep(far[1], mapped_all.at[p.c, p.z])
        flow.keep(two, two_all.at[p.c, p.z])
        flow.keep(far[2], gres_all.at[p.c, p.z])
        for step in range(1, m.R):
            text_line.hop(step)
            two_line.hop(step)
            grad_line.hop(step)

    near_out = [
        ((rows_all, m.FL), BF16),
        ((N, C), F32),
        ((N, C), F32),
        ((N, 1), F32),
        ((N, C), BF16),
        ((8, m.FL), F32),
        ((8, 128), F32),
        ((8, C), F32),
    ]
    far_out = [
        ((m.D, m.R, N, C), BF16),
        ((m.D, m.R) + mapped.shape, BF16),
        ((m.D, m.R, N, C), BF16),
        ((m.G,) + qkv_rows.shape, BF16),
    ]
    if m.even:
        far_out.append(((m.G,) + proj_part.shape, BF16))
    scratch = (
        [pltpu.VMEM((m.T, 8, 128), F32)]
        + reduce_buffers(m, N, C)
        + [pltpu.VMEM((N, C), F32), pltpu.VMEM((8, m.FL), F32)]
    )
    return fused_kernel(
        3,
        "branch",
        common_greet,
        act,
        near,
        loads,
        far,
        near_out,
        far_out,
        scratch,
        (m.T - 1) + 2 * (m.G - 1) + 3 * gather_sems(m) + reduce_sems(m),
        5,
    )


def attended_kernel(m, two_part, text_part, result_part, cot, gres, hat, inv, after, mods, keep, vec, grad_qkv, grad_proj):
    near = [inv, mods, keep]
    loads = [two_part, hat, after, cot, gres, text_part, result_part, vec]
    far = [grad_qkv] + ([grad_proj] if m.even else [])
    N, C = m.N, m.C
    texts = m.D * m.texts

    def act(p, flow, near, loads, far, near_out, far_out, scratch):
        inv, mods, keep = near
        two_part, hat, after, cot, gres, text_part, result_part, vec = (load.get() for load in loads)
        output, grad_after, branch, gm, vecg, text = near_out
        gb_all = far_out[0]
        two_sum, result_sum, text_sum = scratch[:3]
        two_red = LineReduce(flow, p, two_part, two_sum, *scratch[3:6])
        text_red = LineReduce(flow, p, text_part, text_sum, *scratch[6:9])
        result_red = LineReduce(flow, p, result_part, result_sum, *scratch[9:12])
        line = LineGather(flow, p, branch, gb_all)
        two_red.start()
        flow.swap_group(p, far[0], far_out[1])
        if m.even:
            flow.swap_group(p, far[1], far_out[2])
        two_red.steps_all()
        gm[...] = jnp.zeros_like(gm)
        vecg[...] = jnp.zeros_like(vecg)

        def back(rows):
            grad = cot[rows].astype(F32) + layer_back(two_sum[rows], hat[rows], inv[rows])
            gm[pl.ds(0, 1)] += jnp.sum(grad * after[rows], axis=0, keepdims=True)
            gm[pl.ds(1, 1)] += jnp.sum(grad, axis=0, keepdims=True)
            scaled = grad * (1.0 + mods[pl.ds(0, 1)])
            grad_after[rows] = scaled
            low = (keep[rows] * scaled).astype(BF16)
            branch[rows] = low
            vecg[pl.ds(0, 1)] += jnp.sum(low.astype(F32), axis=0, keepdims=True)
            vecg[pl.ds(1, 1)] += jnp.sum(gres[rows].astype(F32), axis=0, keepdims=True)

        chunks(N, back)
        line.start()
        flow.keep(branch, gb_all.at[p.c, p.z])
        text_red.start()
        result_red.start()
        for step in range(1, m.R):
            line.hop(step)
        text_red.steps_all()
        text[...] = text_sum[...].astype(BF16)
        result_red.steps_all()

        def out(rows):
            second = after[rows] * (1.0 + mods[pl.ds(0, 1)]) + mods[pl.ds(1, 1)]
            value = keep[rows] * (result_sum[rows] + vec[pl.ds(12, 1)])
            output[rows] = (second + value).astype(BF16)

        chunks(N, out)

    near_out = [
        ((N, C), BF16),
        ((N, C), F32),
        ((N, C), BF16),
        ((8, C), F32),
        ((8, C), F32),
        ((texts, m.HW), BF16),
    ]
    far_out = [((m.D, m.R, N, C), BF16), (grad_qkv.shape, BF16)]
    if m.even:
        far_out.append((grad_proj.shape, BF16))
    scratch = (
        [pltpu.VMEM((N, C), F32), pltpu.VMEM((N, C), F32), pltpu.VMEM((texts, m.HW), F32)]
        + reduce_buffers(m, N, C, False)
        + reduce_buffers(m, texts, m.HW, False)
        + reduce_buffers(m, N, C, False)
    )
    return fused_kernel(
        5,
        "attended",
        common_greet,
        act,
        near,
        loads,
        far,
        near_out,
        far_out,
        scratch,
        2 * (m.G - 1) + gather_sems(m) + 3 * reduce_sems(m),
        4,
    )


def text_back_kernel(m, silu, grad_mapped):
    def kernel(s_ref, g_ref, out, bias, weight):
        weight[...] = t_mm(s_ref[...], g_ref[...])
        out[...] = jnp.zeros_like(out)
        for g in range(m.G):
            for t in range(m.T):
                at = m.ms * (g * m.T + t)
                out[g, pl.ds(t * m.mp, m.ms)] = weight[pl.ds(at, m.ms)].astype(BF16)
        bias[...] = jnp.sum(g_ref[...].astype(F32), axis=0, keepdims=True)

    return local_kernel(
        "text_back",
        kernel,
        [silu, grad_mapped],
        [((m.G, m.T * m.mp, m.HW), BF16), ((1, m.HW), F32)],
        [pltpu.VMEM((silu.shape[1], m.HW), F32)],
    )


def back_kernel(m, gb_all, out_full, active, slope, grn_out, normed_all, in_full, norms, ratio, means, gain, key_keep,
                hat, inv, qkv_parts, proj_parts, grad_map):
    near = [norms, ratio, means, gain, key_keep]
    loads = [gb_all, out_full, active, grn_out, slope, normed_all, in_full, qkv_parts]
    loads += [proj_parts] if m.even else []
    far = [grad_map]
    N, C, FL, G = m.N, m.C, m.FL, m.G
    rows_in = C // G
    wide = C // m.Q
    per = m.pixels // N

    def act(p, flow, near, loads, far, near_out, far_out, scratch):
        norms, ratio, means, gain, keep = near
        (back,) = near_out
        out_parts, in_parts, f_parts, map_parts, qkv_team = far_out[:5]
        everyone, mine, moments, slopes, shifts, grads, hidden, part, mate, passed, landed = scratch[:11]
        g_out, g_in, f_own, qkv_own = scratch[11:15]
        flow.swap_group(p, far[0], map_parts)
        gb, out_w, active, grn = (load.get() for load in loads[:4])
        moments[...] = jnp.zeros_like(moments)

        @pl.loop(0, m.D * per)
        def _(number):
            rows = pl.ds(pl.multiple_of(number * N, 16), N)
            item = number // per
            grad = mm_t(gb[rows], out_w[...])
            grads[rows] = grad
            moments[pl.ds(item, 1)] += jnp.sum(grad * active[rows], axis=0, keepdims=True)
            moments[pl.ds(m.D, 1)] += jnp.sum(grad, axis=0, keepdims=True)

        scaled = moments[...] * gain[...]
        cross = jnp.sum(scaled * norms[...], axis=1, keepdims=True)
        mine[...] = jnp.broadcast_to(cross, mine.shape)
        add_up = team_sum(m, p, flow, mine, everyone)
        for g in range(G):
            g_out[g] = t_mm(grn[:, g * m.FFS : (g + 1) * m.FFS], gb[...]).astype(BF16)
        slope, x, in_w, qkv_parts = (load.get() for load in loads[4:8])
        step = m.cs

        def add_parts(parts, own, count):
            for t in range(count):
                rows = pl.ds(t * step, step)
                total = parts[0, rows].astype(F32)
                for g in range(1, G):
                    total = total + parts[g, rows].astype(F32)
                own[t] = total.astype(BF16)

        add_parts(qkv_parts, qkv_own, m.T)
        if m.even:
            proj_own = scratch[15]
            add_parts(loads[8].get(), proj_own, m.R)
        flow.swap_group(p, g_out, out_parts)
        mean = means[...][:, :1]
        cross = add_up()[:, :1]
        slopes[...] = gain[...] * ratio[...] + 1.0
        shifts[...] = (scaled / mean - cross / (m.FF * mean * mean)) / norms[...]
        gains = jnp.sum(moments[pl.ds(0, m.D)] * ratio[pl.ds(0, m.D)], axis=0, keepdims=True)
        biases = moments[pl.ds(m.D, 1)]
        moments[pl.ds(m.D + 1, 1)] = jnp.zeros((1, FL), F32)
        flow.swap_team(p, qkv_own, qkv_team)
        if m.even:
            for number in range(G):
                to = lax.rem(p.q + number, G)
                flow.post(
                    proj_own.at[to],
                    far_out[5].at[p.q],
                    {"grp": p.z, "duo": p.c, "rows": to},
                    when=None if number else p.q != p.z,
                )
            flow.keep(proj_own.at[p.z], far_out[5].at[p.q], p.q == p.z)

        @pl.loop(0, m.D * per)
        def _(number):
            rows = pl.ds(pl.multiple_of(number * N, 16), N)
            item = number // per
            inside = pl.ds(pl.multiple_of((number - item * per) * N, 16), N)
            one = pl.ds(item, 1)
            grad = grads[rows] * slopes[one] + keep[item, inside] * (active[rows] * shifts[one])
            low = (grad * slope[rows]).astype(BF16)
            hidden[rows] = low
            moments[pl.ds(m.D + 1, 1)] += jnp.sum(low.astype(F32), axis=0, keepdims=True)

        inner = moments[pl.ds(m.D + 1, 1)]
        f_own[...] = jnp.zeros_like(f_own)
        for g in range(G):
            lanes = slice(g * m.FFS, (g + 1) * m.FFS)
            for row, values in enumerate((inner, gains, biases)):
                f_own[g, pl.ds(row, 1)] = values[:, lanes]
        flow.swap_group(p, f_own, f_parts)
        line = LineReduce(flow, p, part, back, mate, passed, landed)

        def produce(block):
            for d in range(m.D):
                rows = pl.ds(pl.multiple_of(d * m.pixels + block * N, 16), N)
                part[d, block] = mm_t(hidden[rows], in_w[...]).astype(BF16)

        def between(number):
            if number < G:
                g = lax.rem(p.q + 1 + number, G)
                lanes = pl.ds(pl.multiple_of(g * rows_in, 128), rows_in)
                g_in[g] = t_mm(x[:, lanes], hidden[...]).astype(BF16)
                if number < G - 1:
                    flow.post(g_in.at[g], in_parts.at[p.q], {"grp": g})
                else:
                    flow.keep(g_in.at[p.q], in_parts.at[p.q])

        line.run(produce, between)

    near_out = [((N, C), F32)]
    far_out = [
        ((G, m.FFS, C), BF16),
        ((G, rows_in, FL), BF16),
        ((G, 8, m.FFS), F32),
        (grad_map.shape, BF16),
        ((m.T, m.cs, 3 * m.HW), BF16),
    ]
    scratch = [
        pltpu.VMEM((m.T, 8, 128), F32),
        pltpu.VMEM((8, 128), F32),
        pltpu.VMEM((8, FL), F32),
        pltpu.VMEM((8, FL), F32),
        pltpu.VMEM((8, FL), F32),
        pltpu.VMEM((m.D * m.pixels, FL), F32),
        pltpu.VMEM((m.D * m.pixels, FL), BF16),
    ]
    scratch += reduce_buffers(m, N, C)
    scratch += [
        pltpu.VMEM((G, m.FFS, C), BF16),
        pltpu.VMEM((G, rows_in, FL), BF16),
        pltpu.VMEM((G, 8, m.FFS), F32),
        pltpu.VMEM((m.T, m.cs, 3 * m.HW), BF16),
    ]
    if m.even:
        far_out.append(((G, m.cs, wide), BF16))
        scratch.append(pltpu.VMEM((m.R, m.cs, wide), BF16))
    return fused_kernel(
        9,
        "feed_forward_back",
        lambda p: common_greet(p) + (spread_greet(m, p) if m.even else []),
        act,
        near,
        loads,
        far,
        near_out,
        far_out,
        scratch,
        2 * (m.T - 1) + 4 * (G - 1) + reduce_sems(m) + (G if m.even else 0),
        7,
    )


def pad_rows(values, rows):
    return jnp.pad(values, ((0, rows - values.shape[0]),) + ((0, 0),) * (values.ndim - 1))


def body(
    latents,
    clip_tokens,
    time_embed,
    bucket_ids,
    heights,
    widths,
    text_mask,
    conv_weight,
    conv_bias,
    in_weight,
    in_bias,
    grn_gain,
    grn_bias,
    out_weight,
    out_bias,
    time_weight,
    time_bias,
    map_weight,
    map_bias,
    qkv_weight,
    qv_bias,
    proj_weight,
    proj_bias,
    cotangent,
):
    m = Sizes(latents, clip_tokens, in_weight, in_bias, conv_bias, map_weight)
    G, D, R, T, N, C = m.G, m.D, m.R, m.T, m.N, m.C
    pixels, texts, FFS, FL, FF, HW = m.pixels, m.texts, m.FFS, m.FL, m.FF, m.HW
    cs, ms, mp, sp, even, Q = m.cs, m.ms, m.mp, m.sp, m.even, m.Q
    q, c, z = (lax.axis_index(axis) for axis in AXES)
    head_slice = D * z + c

    vectors = [conv_bias, out_bias, map_bias, proj_bias, qv_bias]
    fvectors = [in_bias, grn_gain, grn_bias]
    in_cut, qkv_cut, map_cut, clip_pad, masked, grad_result, small, fvec = cut_kernel(
        m,
        [heights, widths, bucket_ids, in_weight, qkv_weight, map_weight, clip_tokens, latents]
        + [cotangent, conv_weight]
        + [vector[None] for vector in vectors]
        + [time_embed, text_mask]
        + [vector[None] for vector in fvectors],
    )
    latents = latents[0]
    cotangent = cotangent[0]

    def swap_edges(plan, src, dst):
        p = plan.p
        for block, to, sends, lands in (
            (src.at[pl.ds(src.shape[0] - EDGE, EDGE)], p.z + 1, p.z < R - 1, p.z > 0),
            (src.at[pl.ds(0, EDGE)], p.z - 1, p.z > 0, p.z < R - 1),
        ):
            slot = jnp.where(to > p.z, 0, 1)
            plan.add(block, dst.at[slot], {"rows": to}, when=sends, lands=lands)

    def plan_start(p, ins, outs):
        plan = Plan(p)
        plan.group_gather(ins[1], outs[1])
        swap_edges(plan, ins[0], outs[0])
        plan.team_swap(ins[2], outs[2])
        plan.group_gather(ins[3], outs[3])
        plan.team_swap(ins[4], outs[4])
        return plan.done()

    edges, _, in_rows, fvec_all, map_rows, small_all, clip_all = team_kernel(
        0,
        "exchange_start",
        plan_start,
        [masked, small, in_cut, fvec, map_cut],
        [
            ((2, EDGE, C), BF16),
            ((G, SMALL, 128), BF16),
            ((T, cs, FL), BF16),
            ((G, 16, FFS), BF16),
            ((T, mp, HW), BF16),
        ],
        gathers=[clip_pad],
        messages=2 + 2 * (G - 1) + 2 * (T - 1),
        local=4,
        late=(1, 0, G - 1),
    )
    normed, norm_hat, norm_inv, vec, mod_part, key_keep, keep = conv_kernel(
        m, bucket_ids, edges, masked, small_all, time_weight, time_bias[None]
    )
    in_bias_s, gain_s, grn_bias_s = (
        fvec_all[:, row].reshape(1, FL).astype(F32) for row in range(3)
    )

    def plan_first(p, ins, outs):
        plan = Plan(p)
        plan.group_gather(ins[4], outs[4])
        plan.group_gather(ins[0], outs[0], late=1)
        plan.group_gather(ins[1], outs[1], late=2)
        plan.team_swap(ins[2], outs[2])
        plan.group_gather(ins[3], outs[3])
        if even:
            wide = C // G
            for step in range(G):
                to = lax.rem(p.z + step, G)
                when = None if step else p.q != p.z
                piece = ins[5].at[:, pl.ds(pl.multiple_of(to * wide, 128), wide)]
                plan.add(
                    piece, outs[5].at[p.z], {"grp": to, "duo": p.c, "rows": p.q}, when=when
                )
                source = {"grp": p.z, "duo": p.c, "rows": lax.rem(p.q - step + G, G)}
                plan.greet.append((source, when))
            piece = ins[5].at[:, pl.ds(pl.multiple_of(p.z * wide, 128), wide)]
            plan.local.append((piece, outs[5].at[p.z], p.q == p.z))
        return plan.done()

    group_count = 4 if G == 4 else G - 1
    arrays = [in_rows.reshape(T * cs, FL), out_weight, qkv_cut, map_rows.reshape(T * mp, HW)]
    arrays.append(mod_part)
    results = [
        ((G, T * cs, FL), BF16),
        ((G,) + out_weight.shape, BF16),
        ((T, cs, 3 * HW), BF16),
        ((G, T * mp, HW), BF16),
        ((G,) + mod_part.shape, F32),
    ]
    if even:
        arrays.append(proj_weight)
        results.append(((R, cs, C // G), BF16))
    gathered = team_kernel(
        1,
        "exchange_normed",
        plan_first,
        arrays,
        results,
        gathers=[normed],
        messages=2 * group_count + (T - 1) + 2 * (G - 1) + (G if even else 0),
        local=5 + (1 if even else 0),
        late=(4, 1, G - 1),
    )
    in_full, out_full, qkv_rows, map_full = gathered[:4]
    proj_part = gathered[5].reshape(HW, C // G) if even else None
    mod_all, normed_all = gathered[-2:]
    normed_all = normed_all.reshape(D * pixels, C)
    in_full = in_full.reshape(C, FL)
    out_full = out_full.reshape(FL, C)
    active, slope, norms, total, silu, mapped_s = up_kernel(
        m,
        normed_all,
        in_full,
        in_bias_s,
        key_keep,
        clip_all.reshape(T, sp, -1),
        map_full,
        vec,
    )
    outs = branch_kernel(
        m,
        active,
        norms,
        total,
        out_full,
        gain_s,
        grn_bias_s,
        latents,
        keep,
        vec,
        mod_all,
        qkv_rows.reshape(T * cs, 3 * HW),
        mapped_s,
        grad_result,
        proj_part,
    )
    grn_out, after_res, two_hat, two_inv, _, ratio, means, mods, two_all, mapped, gres_all = outs[:11]
    qkv_full = outs[11].reshape(C, 3 * HW)
    if even:
        proj_s = outs[12]
    else:
        proj_whole = lax.all_gather(proj_weight, AXES, axis=0, tiled=True)
        proj_s = lax.dynamic_slice_in_dim(proj_whole, head_slice * HW, HW, axis=0)[None]
    q_bias = lax.dynamic_slice_in_dim(vec[13], head_slice * HW, HW)
    v_bias = lax.dynamic_slice_in_dim(vec[14], head_slice * HW, HW)
    bias = jnp.concatenate([q_bias, jnp.zeros_like(q_bias), v_bias])[None]
    result_part, two_part, mapped_part, grad_qkv, grad_proj, qkv_bias_grad = attention_kernel(
        m,
        two_all.reshape(D, pixels, C),
        gres_all.reshape(D, pixels, C),
        mapped.reshape(T, D * texts, HW),
        qkv_full,
        proj_s,
        bias,
        key_keep,
    )
    outs = attended_kernel(
        m,
        two_part.reshape(D, R, N, C),
        mapped_part.reshape(D, R, D * texts, HW),
        result_part.reshape(D, R, N, C),
        cotangent,
        grad_result,
        two_hat,
        two_inv,
        after_res,
        mods,
        keep,
        vec,
        grad_qkv.reshape(G, T * cs, 3 * HW),
        grad_proj,
    )
    output, grad_after, _, grad_modulate, vec_sums, grad_mapped, gb_all, qkv_parts = outs[:8]
    if even:
        proj_parts = outs[8]
    else:
        proj_parts = None
        spread = jnp.zeros((C, C), F32)
        spread = lax.dynamic_update_slice_in_dim(
            spread, grad_proj[0].astype(F32), head_slice * HW, axis=0
        )
        proj_team = lax.psum_scatter(spread, AXES, scatter_dimension=0, tiled=True)[None]
    grad_map, map_bias_grad = text_back_kernel(m, silu, grad_mapped)
    outs = back_kernel(
        m,
        gb_all.reshape(D * pixels, C),
        out_full,
        active,
        slope,
        grn_out,
        normed_all,
        in_full,
        norms,
        ratio,
        means,
        gain_s,
        key_keep,
        norm_hat,
        norm_inv,
        qkv_parts,
        proj_parts,
        grad_map,
    )
    grad_conv_in, out_sum, in_sum, f_sum, map_sum, qkv_team = outs[:6]
    if even:
        proj_team = outs[6]
    grad_out_shard = jnp.sum(out_sum.astype(F32), axis=0)
    in_back = jnp.sum(in_sum.astype(F32), axis=0).astype(BF16).reshape(T, cs, FL)
    map_back = jnp.sum(map_sum.astype(F32), axis=0).astype(BF16).reshape(T, mp, HW)

    def placed(values, start):
        return lax.dynamic_update_slice_in_dim(jnp.zeros((C,), F32), values, start, axis=0)

    vec_grads = jnp.concatenate(
        [vec_sums[:2], placed(map_bias_grad[0], (c * R + z) * HW)[None]], axis=0
    )
    qv_grads = jnp.stack(
        [
            placed(qkv_bias_grad[0, :HW], head_slice * HW),
            placed(qkv_bias_grad[0, 2 * HW :], head_slice * HW),
        ]
    )
    grad_conv, conv_low, tiny = conv_back_kernel(
        m,
        bucket_ids,
        grad_conv_in,
        norm_hat,
        norm_inv,
        edges,
        masked,
        vec_grads,
        qv_grads,
        grad_modulate,
    )
    trows = 16

    def plan_fifth(p, ins, outs):
        plan = Plan(p)
        swap_edges(plan, ins[0], outs[0])
        plan.team_swap(ins[1], outs[1])
        plan.team_swap(ins[2], outs[2])
        plan.team_swap(ins[3], outs[3])
        return plan.done()

    conv_edges, tiny_team, in_team, map_team = team_kernel(
        11,
        "exchange_tail",
        plan_fifth,
        [conv_low, tiny, in_back, map_back],
        [((2, EDGE, C), BF16), (tiny.shape, F32), (in_back.shape, BF16), (map_back.shape, BF16)],
        messages=2 + 3 * (T - 1),
        local=3,
    )
    tiny_items = jnp.sum(tiny_team.reshape(D, R, G, trows, 128), axis=1).transpose(1, 0, 2, 3)

    def plan_sixth(p, ins, outs):
        plan = Plan(p)
        plan.group_swap(ins[0], outs[0])
        return group_greet(p), plan.messages, plan.local

    (tiny_all,) = team_kernel(
        12,
        "exchange_tiny",
        plan_sixth,
        [tiny_items],
        [((G, D, trows, 128), F32)],
        messages=G - 1,
    )
    tiny_all = tiny_all.reshape(G * D, trows, 128)
    tiny_sum = jnp.sum(tiny_all, axis=0)
    modulate_items = tiny_all[:, 14, : 2 * cs]
    embed_all = small_all.reshape(D, R, G, SMALL, 128)[:, 0, :, 14, : time_embed.shape[1]]
    embed_all = embed_all.transpose(1, 0, 2).reshape(G * D, -1)
    grad_time = lax.dot_general(
        embed_all.astype(F32),
        modulate_items,
        (((0,), (0,)), ((), ())),
        precision=lax.Precision.HIGHEST,
    )
    grad_time_bias = jnp.sum(modulate_items, axis=0)
    grad_latents, grad_in_shard, grad_qkv_shard, grad_map_shard, grad_proj_shard = finish_kernel(
        m,
        bucket_ids,
        conv_edges,
        conv_low,
        grad_after,
        keep,
        vec,
        in_team,
        qkv_team,
        map_team,
        proj_team,
    )
    f_total = jnp.sum(f_sum, axis=0)
    return (
        output[None],
        grad_latents,
        tiny_sum[:9, :cs],
        tiny_sum[9, :cs],
        grad_in_shard,
        f_total[0],
        f_total[1],
        f_total[2],
        grad_out_shard,
        tiny_sum[10, :cs],
        grad_time,
        grad_time_bias,
        grad_map_shard,
        tiny_sum[12, :cs],
        grad_qkv_shard,
        tiny_sum[13, : 2 * cs],
        grad_proj_shard,
        tiny_sum[11, :cs],
    )


def solution(mesh):
    items, rows = mesh.devices.shape
    fine = Mesh(mesh.devices.reshape(items // 2, 2, rows), AXES)
    item = ("grp", "duo")
    full = AXES
    ins = (
        P(item, "rows", None),
        P(item, "rows", None),
        P(item, None),
        P(item),
        P(item),
        P(item),
        P(item, None),
        P(None, full),
        P(full),
        P(full, None),
        P(full),
        P(full),
        P(full),
        P(full, None),
        P(full),
        P(None, full),
        P(full),
        P(full, None),
        P(full),
        P(full, None),
        P(full),
        P(full, None),
        P(full),
        P(item, "rows", None),
    )
    outs = (
        P(item, "rows", None),
        P(item, "rows", None),
        P(None, full),
        P(full),
        P(full, None),
        P(full),
        P(full),
        P(full),
        P(full, None),
        P(full),
        P(None, full),
        P(full),
        P(full, None),
        P(full),
        P(full, None),
        P(full),
        P(full, None),
        P(full),
    )
    return jax.shard_map(body, mesh=fine, in_specs=ins, out_specs=outs, check_vma=False)
```

time: 718 us -> 553 us (0.77)
  Pallas kernels: 412 us -> 517 us
  local copies, waits for them, and re-layouts: 115 us -> 13.6 us
  matrix products: 85.9 us -> 0.83 us
  other arithmetic: 76 us -> 10.1 us
  between operations: 17.8 us -> 3.2 us
    pallas_call x1 -> x10, Pallas kernels: 20.1 us -> 372 us  [the longest x3 298 us: fused_kernel(): pl.pallas_call(kernel, out_shape=spots(near_out + far_out), in_specs=[clo...]
    pallas_call x11 -> x4, Pallas kernels: 392 us -> 145 us  [team_kernel(): pl.pallas_call(kernel, out_shape=out_shape, in_specs=[spot] * (count_a +...]
    dot_general x18 -> x0, matrix products: 85.1 us -> none  [the longest x7 33.8 us: mm(): return jnp.dot(left, right, preferred_element_type=F32)]
    reduce_sum x23 -> x3, other arithmetic: 40.7 us -> 3.35 us  [the longest x1 2 us: body(): jnp.sum(map_sum.astype(F32), axis=0).astype(BF16).reshape(T, mp, HW)]
    reshape x31 -> x0, local copies, waits for them, and re-layouts: 36.3 us -> none  [the longest x3 7.2 us: body(): grad_qkv_shard = qkv_team.astype(F32).reshape(D, R, cs, 3, HW).transpose(...]
    convert_element_type x13 -> x3, local copies, waits for them, and re-layouts: 18.3 us -> 2 us  [body(): fvec_all[:, row].reshape(1, FL).astype(F32)]
    convert_element_type x17 -> x1, other arithmetic: 15.3 us -> 0.9 us  [body(): fvec_all[:, row].reshape(1, FL).astype(F32)]
    pad x13 -> x0, local copies, waits for them, and re-layouts: 9.43 us -> none  [the longest x8 4.67 us: lanes(): return jnp.pad(piece, ((0, 0), (0, 128 - piece.shape[1])))]
  transfers between devices with their start and end apart: 3 -> 0, of which waited for: 0 -> 0; matrix products, arithmetic and copies ran while one was open for 25% -> 0% of each run, Pallas kernels for 29% -> 0%
where the time goes in v3:
time: 553 us; the launch traced here: 545 us
  Pallas kernels  517 us (93%)
  local copies, waits for them, and re-layouts  13.6 us (2%)
  other arithmetic  10.1 us (2%)
    pallas_call x3, Pallas kernels, fused_kernel(): pl.pallas_call(kernel, out_shape=spots(near_out + far_out), in_specs=[clo...  298 us
    pallas_call x4, Pallas kernels, team_kernel(): pl.pallas_call(kernel, out_shape=out_shape, in_specs=[spot] * (count_a +...  145 us
    pallas_call x1, Pallas kernels, attention_kernel(): pl.pallas_call(kernel, grid=(m.D,), out_shape=spots([((m.D, pixels, C), B...  39.5 us
    pallas_call x6, Pallas kernels, local_kernel(): pl.pallas_call(kernel, out_shape=spots(results), in_specs=[numbers] * sca...  34.7 us

profile of v3, /device:TPU:0, one launch (start us, length us, event | category | flops | bytes accessed | tf_op | source)
XLA Modules:
  0.0 545.3 jit_solution(4529521085933310792)
XLA Ops:
  2.6 1.2 broadcast_in_dim.44.refs_7_
  3.8 1.2 broadcast_in_dim.45.refs_8_
  5.0 1.2 broadcast_in_dim.46.refs_9_
  6.3 3.2 cut_weights.1
  9.5 38.5 %exchange_start.1 = (bf16[2,48,1536]{2,1,0:T(8,128)(2,1)}, bf16[4,32,128]{2,1,0:T(8,128)(2,1)}, bf16[8,48,768]{2,1,0:T(8,128)(2,1)}, bf16[4,16,192]{2,1,0:T(8,12...) custom-call(bf16[144,1536]{1,0:T(8,128)(2,1)} %get-tuple-element.98.refs, ...), custom_call_target="tpu_custom_call" | custom-call | tf_op jit(solution)/shard_map/exchange_start/pallas_call | solution.py:423
  48.7 0.9 convert_reduce_fusion.1
  51.6 5.1 convolve.1
  56.8 0.9 fusion
  58.4 63.1 %exchange_normed.1 = (bf16[4,384,768]{2,1,0:T(8,128)(2,1)}, bf16[4,192,1536]{2,1,0:T(8,128)(2,1)}, bf16[8,48,576]{2,1,0:T(8,128)(2,1)}, bf16[4,384,192]{2,1,0:T(...) custom-call(bf16[384,768]{1,0:T(8,128)(2,1)} %bitcast.79, ...), custom_call_target="tpu_custom_call" | custom-call | tf_op jit(solution)/shard_map/exchange_normed/pallas_call | solution.py:423
  121.5 12.4 %hidden_units.1 = (f32[1152,768]{1,0:T(8,128)}, f32[1152,768]{1,0:T(8,128)}, f32[8,768]{1,0:T(8,128)}, f32[8,128]{1,0:T(8,128)}, bf16[160,1280]{1,0:T(8,128)(2,1)}, /*index=5*/bf16[160,192]{1,0:T(8,128)(2,1)}) custom-call(bf16[1152,1536]{1,0:T(8,128)(2,1)} %bitcast.59, bf16[1536,768]{1,0:T(8,128)(2,1)} %bitcast.61, f32[1,768]{1,0:T(1,128)} %reshape.177.b_ref, ...), custom_call_target="tpu_custom_call" | custom-call | tf_op jit(solution)/shard_map/hidden_units/pallas_call | solution.py:546
  133.9 113.5 %branch.1 = (bf16[1152,768]{1,0:T(8,128)(2,1)}, f32[144,1536]{1,0:T(8,128)}, f32[144,1536]{1,0:T(8,128)}, f32[144,1]{1,0:T(8,128)}, bf16[144,1536]{1,0:T(8,128)(...) custom-call(f32[8,768]{1,0:T(8,128)} %get-tuple-element.118.refs_0_,, ...), custom_call_target="tpu_custom_call" | custom-call | tf_op jit(solution)/shard_map/branch/pallas_call | solution.py:1046
  247.4 39.5 %attention_block.1 = (bf16[2,576,1536]{2,1,0:T(8,128)(2,1)}, bf16[2,576,1536]{2,1,0:T(8,128)(2,1)}, bf16[8,160,192]{2,1,0:T(8,128)(2,1)}, bf16[1536,576]{1,0:T(8...) custom-call(bf16[2,576,1536]{2,1,0:T(8,128)(2,1)} %bitcast.65, bf16[2,576,1536]{2,1,0:T(8,128)(2,1)} %bitcast.66, ...), custom_call_target="tpu_custom_call" | custom-call | tf_op jit(solution)/shard_map/attention_block/pallas_call | solution.py:842
  286.9 113.1 %attended.1 = (bf16[144,1536]{1,0:T(8,128)(2,1)}, f32[144,1536]{1,0:T(8,128)}, bf16[144,1536]{1,0:T(8,128)(2,1)}, f32[8,1536]{1,0:T(8,128)}, f32[8,1536]{1,0:T(8...) custom-call(f32[144,1]{1,0:T(8,128)} %get-tuple-element.128.refs_0_,, ...), custom_call_target="tpu_custom_call" | custom-call | tf_op jit(solution)/shard_map/attended/pallas_call | solution.py:1046
  402.5 2.4 text_back.1
  405.6 71.3 %feed_forward_back.1 = (f32[144,1536]{1,0:T(8,128)}, bf16[4,192,1536]{2,1,0:T(8,128)(2,1)}, bf16[4,384,768]{2,1,0:T(8,128)(2,1)}, f32[4,8,192]{2,1,0:T(8,128)}, ...) custom-call(f32[8,768]{1,0:T(8,128)} %get-tuple-element.118.refs_0_, ...), custom_call_target="tpu_custom_call" | custom-call | tf_op jit(solution)/shard_map/feed_forward_back/pallas_call | solution.py:1046
  477.6 5.8 %convolve_back.1 = (f32[144,1536]{1,0:T(8,128)}, bf16[144,1536]{1,0:T(8,128)(2,1)}, f32[8,4,16,128]{3,2,1,0:T(8,128)}) custom-call(s32[1]{0:T(128)S(6)} %copy.56.b_ref, f32[144,1536]{1,0:T(8,128)} %get-tuple-element.153.g_ref, f32[144,1536]{1,0:T(8,128)} %get-tuple-element.154.hat_ref, f32[144,1]{1,0:T(8,128)} %get-tuple-element.155.inv_ref, ...), custom_call_target="tpu_custom_call" | custom-call | tf_op jit(solution)/shard_map/convolve_back/pallas_call | solution.py:546
  484.0 2.0 reduce_sum.70
  486.0 1.3 reduce_sum.69
  487.3 36.0 %exchange_tail.1 = (bf16[2,48,1536]{2,1,0:T(8,128)(2,1)}, f32[8,4,16,128]{3,2,1,0:T(8,128)}, bf16[8,48,768]{2,1,0:T(8,128)(2,1)}, bf16[8,48,192]{2,1,0:T(8,128)(2,1)}) custom-call(bf16[144,1536]{1,0:T(8,128)(2,1)} %get-tuple-element.160.refs_0_.low_ref, f32[8,4,16,128]{3,2,1,0:T(8,128)} %get-tuple-element.161.refs_1_, bf16[8,48,768]{2,1,0:T(8,128)(2,1)} %bitcast.70, ...), custom_call_target="tpu_custom_call" | custom-call | tf_op jit(solution)/shard_map/exchange_tail/pallas_call | solution.py:423
  523.3 1.1 bitcast_reduce_fusion
  525.1 7.7 %exchange_tiny.1 = f32[4,2,16,128]{3,2,1,0:T(8,128)} custom-call(f32[4,2,16,128]{3,2,1,0:T(8,128)} %bitcast.83), custom_call_target="tpu_custom_call" | custom-call | tf_op jit(solution)/shard_map/exchange_tiny/pallas_call | solution.py:423
  532.8 1.3 slice_reduce_fusion
  536.8 5.9 %finish.1 = (f32[1,144,1536]{2,1,0:T(8,128)}, f32[48,6144]{1,0:T(8,128)}, f32[48,4608]{1,0:T(8,128)}, f32[40,1536]{1,0:T(8,128)}, f32[48,1536]{1,0:T(8,128)}) custom-call(s32[1]{0:T(128)S(6)} %copy.56.b_ref, bf16[2,48,1536]{2,1,0:T(8,128)(2,1)} %get-tuple-element.164.edges_ref, bf16[144,1536]{1,0:T(8,128)(2,1)} %get-tuple-element.160.refs_0_.low_ref, ...), custom_call_target="tpu_custom_call" | custom-call | tf_op jit(solution)/shard_map/finish/pallas_call | solution.py:546
  542.7 1.3 convert_reduce_fusion
  (38 shorter events, 12.1 us)
Async XLA Ops:
  477.0 6.5 %copy-start.3 = (f32[4,8,192]{2,1,0:T(8,128)S(1)}, f32[4,8,192]{2,1,0:T(8,128)}, u32[]{:S(2)}) copy-start(f32[4,8,192]{2,1,0:T(8,128)} %get-tuple-element.173) | copy-start | bytes 73732
  477.0 9.0 %copy-start.1 = (bf16[4,384,768]{2,1,0:T(8,128)(2,1)S(1)}, bf16[4,384,768]{2,1,0:T(8,128)(2,1)}, u32[]{:S(2)}) copy-start(bf16[4,384,768]{2,1,0:T(8,128)(2,1)} %get-tuple-element.162) | copy-start | bytes 7077892
  523.3 19.4 %copy-start = (bf16[4,192,1536]{2,1,0:T(8,128)(2,1)S(1)}, bf16[4,192,1536]{2,1,0:T(8,128)(2,1)}, u32[]{:S(2)}) copy-start(bf16[4,192,1536]{2,1,0:T(8,128)(2,1)} %get-tuple-element.174) | copy-start | bytes 7077892
  534.9 9.1 %copy-start.4 = (f32[16,128]{1,0:T(8,128)}, f32[16,128]{1,0:T(8,128)S(1)}, u32[]{:S(2)}) copy-start(f32[16,128]{1,0:T(8,128)S(1)} %reduce_sum.72) | copy-start | bytes 24580
  542.7 1.4 copy-start.2

commit v4 on v3

--- a/solution.py
+++ b/solution.py
@@ -56,6 +56,8 @@
         self.kept = 0
         self.open = []
         self.posted = []
+        self.lines = []
+        self.stays = []
 
     def take(self, count=1):
         at = self.used
@@ -85,16 +87,47 @@
             item.landed = True
             guarded(item.lands, item.copy.wait_recv)
 
-    def keep(self, src, dst, when=None):
+    def keep(self, src, dst, when=None, now=False):
         copy = pltpu.make_async_copy(src, dst, self.local_sem.at[self.kept])
         self.kept += 1
         guarded(when, copy.start)
-        self.open.append((copy.wait, when))
+        if now:
+            guarded(when, copy.wait)
+        else:
+            self.stays.append((copy.wait, when))
+
+    def square(self, p, src, dst):
+        across = p.q + 1 - 2 * lax.rem(p.q, 2)
+        along = lax.rem(p.q + 2, 4)
+        one = self.post(src, dst.at[p.q], {"grp": across})
+        two = self.post(src, dst.at[p.q], {"grp": along})
+        half = dst.shape[1] // 2
+        top, bottom = pl.ds(0, half), pl.ds(half, half)
+
+        def relay():
+            self.land(one)
+            block = dst.at[across, top]
+            first = self.post(block, block, {"grp": along})
+            self.land(two)
+            block = dst.at[along, bottom]
+            second = self.post(block, block, {"grp": across})
+            return first, second
+
+        return relay
+
+    def settle_kept(self):
+        for act, when in self.stays:
+            guarded(when, act)
+        self.stays = []
+
+    def gather_team(self, p, src, dst):
+        mine = p.c * p.R + p.z
+        self.keep(src, dst.at[mine])
+        return [self.post(src, dst.at[mine], {"duo": c, "rows": z}) for c, z in p.team()]
 
     def gather_group(self, p, src, dst):
         self.keep(src, dst.at[p.q])
-        for q in p.groups():
-            self.post(src, dst.at[p.q], {"grp": q})
+        return [self.post(src, dst.at[p.q], {"grp": q}) for q in p.groups()]
 
     def swap_group(self, p, src, dst):
         self.keep(src.at[p.q], dst.at[p.q])
@@ -104,10 +137,14 @@
     def swap_team(self, p, src, dst):
         mine = p.c * p.R + p.z
         self.keep(src.at[mine], dst.at[mine])
-        for c, z in p.team():
-            self.post(src.at[c * p.R + z], dst.at[mine], {"duo": c, "rows": z})
+        return [
+            self.post(src.at[c * p.R + z], dst.at[mine], {"duo": c, "rows": z}) for c, z in p.team()
+        ]
 
     def finish(self):
+        self.settle_kept()
+        for line in self.lines:
+            line.settle(line.p.R)
         for item in self.posted:
             self.land(item)
         for act, when in self.open:
@@ -129,7 +166,7 @@
 
     def across(self, block, number):
         p, dst = self.p, self.dst
-        src = self.src if number == 0 else dst.at[p.c, block]
+        src = self.src if isinstance(number, int) and number == 0 else dst.at[p.c, block]
         other = {"duo": lax.rem(p.c + 1, p.D)}
         return self.flow.copy(src, dst.at[p.c, block], other, self.side + number)
 
@@ -141,7 +178,9 @@
             self.flow.open.append((copy.wait_send, ok))
         copy = self.across(p.z, 0)
         copy.start()
-        self.flow.open += [(copy.wait_recv, None), (copy.wait_send, None)]
+        self.flow.open.append((copy.wait_send, None))
+        self.flow.lines.append(self)
+        self.settled = 0
 
     def hop(self, step):
         p = self.p
@@ -161,7 +200,28 @@
             pl.when(ok)(relay)
             if step < p.R - 1:
                 self.flow.open.append((self.send(block, step, direction).wait_send, ok & last))
-            self.flow.open += [(side.wait_recv, ok), (side.wait_send, ok)]
+            self.flow.open.append((side.wait_send, ok))
+
+
+    def nth(self, number):
+        p = self.p
+        reach = [p.z]
+        for step in range(1, p.R):
+            reach += [p.z - step, p.z + step]
+        seen, found = 0, jnp.int32(0)
+        for block in reach:
+            ok = (block >= 0) & (block < p.R)
+            found = jnp.where(ok & (seen == number), block, found)
+            seen = seen + jnp.where(ok, 1, 0)
+        return found
+
+    def settle(self, upto):
+        p = self.p
+        while self.settled < upto:
+            block = self.nth(self.settled)
+            number = jnp.where(block <= p.z, p.z - block, p.R - 1 + block - p.z)
+            self.across(block, number).wait_recv()
+            self.settled += 1
 
 
 class LineReduce:
@@ -214,13 +274,33 @@
         def _(number):
             act(pl.ds(pl.multiple_of(number * step, step), step))
 
-    def step(self, upward, block, ok):
+    def early(self):
+        for upward, block, ok in self.steps():
+            behind = jnp.where(upward, self.p.z > 0, self.p.z < self.p.R - 1)
+            self.step(upward, block, ok & jnp.logical_not(behind), False)
+
+    def later(self):
+        for upward, block, ok in self.steps():
+            behind = jnp.where(upward, self.p.z > 0, self.p.z < self.p.R - 1)
+            yield functools.partial(self.step, upward, block, ok & behind, True)
+
+    def step(self, upward, block, ok, relays=None):
         p = self.p
         way = jnp.where(upward, 1, 0)
         behind = jnp.where(upward, p.z > 0, p.z < p.R - 1)
 
         def act():
             self.across(block).wait_recv()
+            if relays is False:
+
+                def add(rows):
+                    self.passed[way, block, rows] = (
+                        self.part[p.c, block, rows].astype(F32) + self.mate[block, rows].astype(F32)
+                    ).astype(BF16)
+
+                self.rows_of(add)
+                self.along(upward, block).start()
+                return
 
             @pl.when(behind)
             def _():
@@ -235,14 +315,17 @@
 
                 self.rows_of(add)
 
-            @pl.when(jnp.logical_not(behind))
-            def _():
-                def add(rows):
-                    self.passed[way, block, rows] = (
-                        self.part[p.c, block, rows].astype(F32) + self.mate[block, rows].astype(F32)
-                    ).astype(BF16)
-
-                self.rows_of(add)
+            if relays is None:
+
+                @pl.when(jnp.logical_not(behind))
+                def _():
+                    def add(rows):
+                        self.passed[way, block, rows] = (
+                            self.part[p.c, block, rows].astype(F32)
+                            + self.mate[block, rows].astype(F32)
+                        ).astype(BF16)
+
+                    self.rows_of(add)
 
             self.along(upward, block).start()
 
@@ -272,8 +355,9 @@
             pl.when(ok)(more)
 
     def steps_all(self):
-        for upward, block, ok in self.steps():
-            self.step(upward, block, ok)
+        self.early()
+        for act in self.later():
+            act()
         self.close()
 
     def run(self, produce=None, between=None):
@@ -587,8 +671,9 @@
 
 
 WIDTHS = (9 * UNIT // 2, 3 * UNIT, 9 * UNIT // 4)
-SMALL = 32
+SMALL = 16
 VEC = 16
+FACTS = 96
 
 
 def cut_kernel(m, arrays):
@@ -618,16 +703,18 @@
         small[...] = jnp.zeros_like(small)
         small[pl.ds(0, 9), pl.ds(0, m.cs)] = cw_ref[...].astype(F32)
         for number, ref in enumerate(vectors):
-            small[pl.ds(9 + number, 1), pl.ds(0, ref.shape[1])] = ref[...].astype(F32)
+            small[pl.ds(9 + number, 1), pl.ds(0, ref.shape[0])] = ref[...].astype(F32).reshape(1, -1)
         small[pl.ds(14, 1), pl.ds(0, te_ref.shape[1])] = te_ref[...].astype(F32)
         lane = lax.broadcasted_iota(jnp.int32, (1, 128), 1)
-        facts = jnp.where(lane == 0, h_ref[0], jnp.where(lane == 1, w_ref[0], b_ref[0]))
-        small[pl.ds(15, 1)] = facts.astype(F32)
-        small[pl.ds(16, 1), pl.ds(0, m.texts)] = tm_ref[...].astype(F32)
+        for number, ref in enumerate((h_ref, w_ref, b_ref)):
+            fact = jnp.full((1, 128), ref[0]).astype(F32)
+            row = small[pl.ds(14, 1)]
+            small[pl.ds(14, 1)] = jnp.where(lane == FACTS + number, fact, row)
+        small[pl.ds(15, 1), pl.ds(0, m.texts)] = tm_ref[...].astype(F32)
         small_out[...] = small[...].astype(BF16)
         fv[...] = jnp.zeros_like(fv)
         for number, ref in enumerate((f0, f1, f2)):
-            fv[pl.ds(number, 1)] = ref[...].astype(F32)
+            fv[pl.ds(number, 1)] = ref[...].astype(F32).reshape(1, -1)
         f_out[...] = fv[...].astype(BF16)
 
     return local_kernel(
@@ -656,9 +743,17 @@
     extended[pl.ds(EDGE + m.N, EDGE)] = jnp.where(z < m.R - 1, edges_ref[1].astype(F32), 0.0)
 
 
-def each_bucket(bucket, act):
-    for number, width in enumerate(WIDTHS):
-        pl.when(bucket == number)(functools.partial(act, width))
+def width_of(bucket):
+    return jnp.where(bucket == 0, WIDTHS[0], jnp.where(bucket == 1, WIDTHS[1], WIDTHS[2]))
+
+
+def shifted_rows(ref, count, shift, lanes):
+    start = EDGE + shift
+    whole = start // 8
+    tall = count + 8
+    block = ref[pl.ds(pl.multiple_of(whole * 8, 8), tall), lanes]
+    extra = start - whole * 8
+    return pltpu.roll(block, jnp.where(extra == 0, 0, tall - extra), 0)[:count]
 
 
 def each_column_block(m, act):
@@ -669,224 +764,6 @@
 
 def tap_steps():
     return [(index, index // 3 - 1, index % 3 - 1) for index in range(9)]
-
-
-def conv_kernel(m, b_ref, edges, masked, small_all, time_weight, time_bias):
-    def kernel(b_ref, edges_ref, mid_ref, small_ref, tw_ref, tb_ref, normed, hat, inv, vec, mod, keys, pix, extended, conv, item, te):
-        vec[...] = jnp.zeros_like(vec)
-        for s, (g, d, r) in enumerate(m.places):
-            piece = small_ref[d, r, g].astype(F32)
-            vec[pl.ds(0, 13), pl.ds(s * m.cs, m.cs)] = piece[:13, : m.cs]
-            half = m.S // 2
-            vec[pl.ds(13 + s // half, 1), pl.ds(2 * m.cs * (s % half), 2 * m.cs)] = piece[
-                13:14, : 2 * m.cs
-            ]
-            if r == 0:
-                item[pl.ds(m.D * g + d, 1)] = piece[14:15]
-        te[...] = item[...][:, : te.shape[1]].astype(BF16)
-        mod[...] = jnp.zeros_like(mod)
-        mod[pl.ds(0, te.shape[0]), pl.ds(0, 2 * m.cs)] = mm(te[...], tw_ref[...]) + tb_ref[...].astype(F32)
-        q = lax.axis_index("grp")
-        for d in range(m.D):
-            facts = small_ref[d, 0, q].astype(F32)
-            row, col = rows_cols(0, m.pixels, float_cols(facts[15:16, 2:3]))
-            inside = (row < facts[15:16, 0:1]) & (col < facts[15:16, 1:2])
-            keys[d, pl.ds(0, m.pixels)] = jnp.where(inside, 1.0, 0.0)
-            text = facts.T[: m.texts, 16:17]
-            slot = lax.broadcasted_iota(jnp.int32, (m.texts, 1), 0)
-            keys[d, pl.ds(m.pixels, m.texts)] = jnp.where(slot < TXT, text, 0.0)
-        fill_extended(m, extended, edges_ref, mid_ref)
-        z = lax.axis_index("rows")
-
-        def taps(width):
-            _, col = rows_cols(z * m.N, m.N, float(width))
-
-            def block(lanes):
-                total = jnp.zeros((m.N, 128), F32) + vec[pl.ds(9, 1), lanes]
-                for index, dy, dx in tap_steps():
-                    piece = extended[pl.ds(EDGE + dy * width + dx, m.N), lanes]
-                    ok = (col + dx >= 0) & (col + dx < width)
-                    total = total + jnp.where(ok, piece, 0.0) * vec[pl.ds(index, 1), lanes]
-                conv[:, lanes] = total
-
-            each_column_block(m, block)
-
-        each_bucket(b_ref[0], taps)
-        values, inverse = layer_stats(conv[...])
-        hat[...] = values
-        normed[...] = values.astype(BF16)
-        inv[...] = inverse
-        pix[...] = keys[lax.axis_index("duo"), pl.ds(pl.multiple_of(z * m.N, 8), m.N)]
-
-    items = m.G * m.D
-    return local_kernel(
-        "convolve",
-        kernel,
-        [b_ref, edges, masked, small_all, time_weight, time_bias],
-        [
-            ((m.N, m.C), BF16),
-            ((m.N, m.C), F32),
-            ((m.N, 1), F32),
-            ((VEC, m.C), F32),
-            ((-(-items // 8) * 8, 128), F32),
-            ((m.D, m.pixels + m.texts, 1), F32),
-            ((m.N, 1), F32),
-        ],
-        [
-            pltpu.VMEM((m.N + 2 * EDGE, m.C), F32),
-            pltpu.VMEM((m.N, m.C), F32),
-            pltpu.VMEM((items, 128), F32),
-            pltpu.VMEM((items, time_weight.shape[0]), BF16),
-        ],
-        scalars=1,
-    )
-
-
-def attention_kernel(m, two_all, gres_all, mapped_all, weight, proj, bias, key_keep):
-    heads = m.HW // HEAD
-    keys = m.pixels + m.texts
-    scale = HEAD ** (-0.5)
-    HW, C, pixels, texts = m.HW, m.C, m.pixels, m.texts
-    wide = C // m.Q
-
-    def kernel(two_ref, gres_ref, map_ref, w_ref, p_ref, bias_ref, keep_ref, res_out, two_out, map_out, gw_out, gp_out, gb_out,
-               qkv, k_all, v_all, dk, dv, o_t, dq_t, g_all, dqkv, dtext, att, gw, gp):
-        step = pl.program_id(0)
-
-        @pl.when(step == 0)
-        def _():
-            gw[...] = jnp.zeros_like(gw)
-            gp[...] = jnp.zeros_like(gp)
-            gb_out[...] = jnp.zeros_like(gb_out)
-
-        qkv[...] = (mm(two_ref[0], w_ref[...]) + bias_ref[...]).astype(BF16)
-        text = jnp.zeros((texts, 3 * HW), F32) + bias_ref[...]
-        for t in range(m.T):
-            text = text + mm(map_ref[t], w_ref[pl.ds(t * HW, HW)])
-        text = text.astype(BF16)
-        g = jnp.zeros((pixels, HW), F32)
-        for n in range(m.Q):
-            g = g + mm_t(gres_ref[0, :, pl.ds(n * wide, wide)], p_ref[n])
-        g_all[...] = g.astype(BF16)
-        k_all[pl.ds(0, pixels)] = qkv[:, HW : 2 * HW]
-        k_all[pl.ds(pixels, texts)] = text[:, HW : 2 * HW]
-        v_all[pl.ds(0, pixels)] = qkv[:, 2 * HW :]
-        v_all[pl.ds(pixels, texts)] = text[:, 2 * HW :]
-        k_t = k_all[...].T
-        v_t = v_all[...].T
-        dk[...] = jnp.zeros_like(dk)
-        dv[...] = jnp.zeros_like(dv)
-        o_t[...] = jnp.zeros_like(o_t)
-        dq_t[...] = jnp.zeros_like(dq_t)
-        lane = lax.broadcasted_iota(jnp.int32, (1, HW), 1)
-        line = lax.broadcasted_iota(jnp.int32, (HW, 1), 0)
-        alive = keep_ref[0] > 0
-
-        @pl.loop(0, heads)
-        def _(head):
-            low = head * HEAD
-            in_head = (lane >= low) & (lane < low + HEAD)
-            in_line = (line >= low) & (line < low + HEAD)
-            q_h = jnp.where(in_head, qkv[:, :HW], 0).astype(BF16)
-            g_h = jnp.where(in_head, g_all[...], 0).astype(BF16)
-            scores = mm_t(k_all[...], q_h) * scale
-            scores = jnp.where(alive, scores, masked_score)
-            top = jnp.max(scores, axis=0, keepdims=True)
-            weights = jnp.exp(scores - top)
-            probs = weights / jnp.sum(weights, axis=0, keepdims=True)
-            probs_low = probs.astype(BF16)
-            v_h = jnp.where(in_line, v_t, 0).astype(BF16)
-            o_t[...] += mm(v_h, probs_low)
-            dv[...] += mm(probs_low, g_h)
-            grad_probs = mm_t(v_all[...], g_h)
-            sums = jnp.sum(probs * grad_probs, axis=0, keepdims=True)
-            grad_scores = (probs * (grad_probs - sums)).astype(BF16)
-            k_h = jnp.where(in_line, k_t, 0).astype(BF16)
-            dq_t[...] += mm(k_h, grad_scores)
-            dk[...] += mm(grad_scores, q_h)
-
-        o_low = o_t[...].astype(BF16)
-        att[...] = o_t[...].T.astype(BF16)
-        dqkv[:, :HW] = (dq_t[...].T * scale).astype(BF16)
-        dqkv[:, HW : 2 * HW] = (dk[pl.ds(0, pixels)] * scale).astype(BF16)
-        dqkv[:, 2 * HW :] = dv[pl.ds(0, pixels)].astype(BF16)
-        dtext[:, :HW] = jnp.zeros((texts, HW), BF16)
-        dtext[:, HW : 2 * HW] = (dk[pl.ds(pixels, texts)] * scale).astype(BF16)
-        dtext[:, 2 * HW :] = dv[pl.ds(pixels, texts)].astype(BF16)
-        gb_out[pl.ds(0, 1)] += jnp.sum(dqkv[...].astype(F32), axis=0, keepdims=True) + jnp.sum(
-            dtext[...].astype(F32), axis=0, keepdims=True
-        )
-        for n in range(m.Q):
-            block = pl.ds(n * wide, wide)
-            res_out[0, :, block] = mm(att[...], p_ref[n]).astype(BF16)
-            gp[n] += mm(o_low, gres_ref[0, :, block])
-        two_out[0] = mm_t(dqkv[...], w_ref[...]).astype(BF16)
-        gw[...] += t_mm(two_ref[0], dqkv[...])
-        for t in range(m.T):
-            rows = pl.ds(t * HW, HW)
-            map_out[t] = mm_t(dtext[...], w_ref[rows]).astype(BF16)
-            gw[rows] += t_mm(map_ref[t], dtext[...])
-
-        @pl.when(step == m.D - 1)
-        def _():
-            gw_out[...] = gw[...].astype(BF16)
-            gp_out[...] = gp[...].astype(BF16)
-
-    def item(shape):
-        return pl.BlockSpec((1,) + shape, lambda i: (i, 0, 0))
-
-    def fixed(shape):
-        return pl.BlockSpec(shape, lambda i: (0,) * len(shape))
-
-    slots = pl.BlockSpec((m.T, texts, HW), lambda i: (0, i, 0))
-    return pl.pallas_call(
-        kernel,
-        grid=(m.D,),
-        out_shape=spots(
-            [
-                ((m.D, pixels, C), BF16),
-                ((m.D, pixels, C), BF16),
-                ((m.T, m.D * texts, HW), BF16),
-                ((C, 3 * HW), BF16),
-                ((m.Q, HW, wide), BF16),
-                ((8, 3 * HW), F32),
-            ]
-        ),
-        in_specs=[
-            item((pixels, C)),
-            item((pixels, C)),
-            slots,
-            fixed((C, 3 * HW)),
-            fixed((m.Q, HW, wide)),
-            fixed((1, 3 * HW)),
-            item((keys, 1)),
-        ],
-        out_specs=[
-            item((pixels, C)),
-            item((pixels, C)),
-            slots,
-            fixed((C, 3 * HW)),
-            fixed((m.Q, HW, wide)),
-            fixed((8, 3 * HW)),
-        ],
-        scratch_shapes=[
-            pltpu.VMEM((pixels, 3 * HW), BF16),
-            pltpu.VMEM((keys, HW), BF16),
-            pltpu.VMEM((keys, HW), BF16),
-            pltpu.VMEM((keys, HW), F32),
-            pltpu.VMEM((keys, HW), F32),
-            pltpu.VMEM((HW, pixels), F32),
-            pltpu.VMEM((HW, pixels), F32),
-            pltpu.VMEM((pixels, HW), BF16),
-            pltpu.VMEM((pixels, 3 * HW), BF16),
-            pltpu.VMEM((texts, 3 * HW), BF16),
-            pltpu.VMEM((pixels, HW), BF16),
-            pltpu.VMEM((C, 3 * HW), F32),
-            pltpu.VMEM((m.Q, HW, wide), F32),
-        ],
-        compiler_params=pltpu.CompilerParams(vmem_limit_bytes=60 * 2**20),
-        name="attention_block",
-    )(two_all, gres_all, mapped_all, weight, proj, bias, key_keep)
 
 
 def conv_back_kernel(m, b_ref, grad_in, hat, inv, edges, masked, vec_grads, qv_grads, modulate_grads):
@@ -901,12 +778,12 @@
         z = lax.axis_index("rows")
 
         def taps(width):
-            _, col = rows_cols(z * m.N, m.N, float(width))
+            _, col = rows_cols(z * m.N, m.N, width.astype(F32))
 
             def block(lanes):
                 value = grad[:, lanes]
                 for index, dy, dx in tap_steps():
-                    piece = extended[pl.ds(EDGE + dy * width + dx, m.N), lanes]
+                    piece = shifted_rows(extended, m.N, dy * width + dx, lanes)
                     ok = (col + dx >= 0) & (col + dx < width)
                     vec[pl.ds(index, 1), lanes] = jnp.sum(
                         jnp.where(ok, piece, 0.0) * value, axis=0, keepdims=True
@@ -914,7 +791,7 @@
 
             each_column_block(m, block)
 
-        each_bucket(b_ref[0], taps)
+        taps(width_of(b_ref[0]))
         tiny[...] = jnp.zeros_like(tiny)
         half = m.S // 2
         pair = 2 * m.cs
@@ -935,27 +812,27 @@
     )
 
 
-def finish_kernel(m, b_ref, edges, low, after, pix, vec, in_team, qkv_team, map_team, proj_team):
-    def kernel(b_ref, edges_ref, low_ref, after_ref, pix_ref, vec_ref, in_ref, qkv_ref, map_ref, proj_ref,
-               lat_out, in_out, qkv_out, map_out, proj_out, extended):
+def finish_kernel(m, b_ref, edges, low, after, pix, vec, in_team, qkv_team, map_team, proj_team, out_parts):
+    def kernel(b_ref, edges_ref, low_ref, after_ref, pix_ref, vec_ref, in_ref, qkv_ref, map_ref, proj_ref, parts_ref,
+               lat_out, in_out, qkv_out, map_out, proj_out, out_out, extended):
         fill_extended(m, extended, edges_ref, low_ref)
         z = lax.axis_index("rows")
         keep = pix_ref[...] > 0
 
         def taps(width):
-            _, col = rows_cols(z * m.N, m.N, float(width))
+            _, col = rows_cols(z * m.N, m.N, width.astype(F32))
 
             def block(lanes):
                 total = jnp.zeros((m.N, 128), F32)
                 for index, dy, dx in tap_steps():
-                    piece = extended[pl.ds(EDGE - dy * width - dx, m.N), lanes]
+                    piece = shifted_rows(extended, m.N, -dy * width - dx, lanes)
                     ok = (col - dx >= 0) & (col - dx < width)
                     total = total + jnp.where(ok, piece, 0.0) * vec_ref[pl.ds(index, 1), lanes]
                 lat_out[0, :, lanes] = after_ref[:, lanes] + jnp.where(keep, total, 0.0)
 
             each_column_block(m, block)
 
-        each_bucket(b_ref[0], taps)
+        taps(width_of(b_ref[0]))
         for g in range(m.G):
             for t in range(m.T):
                 start = m.FFS * (g * m.T + t)
@@ -969,6 +846,10 @@
                     ].astype(F32)
         for t in range(m.T):
             map_out[:, pl.ds(t * m.HW, m.HW)] = map_ref[t].astype(F32)[: m.ms]
+        total = parts_ref[0].astype(F32)
+        for g in range(1, m.G):
+            total = total + parts_ref[g].astype(F32)
+        out_out[...] = total
         wide = m.C // m.Q
         for n in range(m.Q):
             proj_out[:, pl.ds(n * wide, wide)] = proj_ref[n].astype(F32)
@@ -976,13 +857,14 @@
     return local_kernel(
         "finish",
         kernel,
-        [b_ref, edges, low, after, pix, vec, in_team, qkv_team, map_team, proj_team],
+        [b_ref, edges, low, after, pix, vec, in_team, qkv_team, map_team, proj_team, out_parts],
         [
             ((1, m.N, m.C), F32),
             ((m.cs, m.FF), F32),
             ((m.cs, 3 * m.C), F32),
             ((m.ms, m.C), F32),
             ((m.cs, m.C), F32),
+            ((m.FFS, m.C), F32),
         ],
         [pltpu.VMEM((m.N + 2 * EDGE, m.C), F32)],
         scalars=1,
@@ -1006,6 +888,17 @@
     @pl.loop(0, count // step)
     def _(number):
         act(pl.ds(pl.multiple_of(number * step, step), step))
+
+
+def each_rows(count, step, act):
+    if step % 16:
+        for number in range(count):
+            act(number, pl.ds(number * step, step))
+    else:
+
+        @pl.loop(0, count)
+        def _(number):
+            act(number, pl.ds(pl.multiple_of(number * step, 16), step))
 
 
 def greet_all(p, targets):
@@ -1020,7 +913,9 @@
     pl.semaphore_wait(barrier, waits)
 
 
-def fused_kernel(ident, name, greet, act, near, loads, far, near_out, far_out, scratch, sems, local):
+def fused_kernel(
+    ident, name, greet, act, near, loads, far, near_out, far_out, scratch, sems, local, numbers=0
+):
     close = pl.BlockSpec(memory_space=pltpu.VMEM)
     spot = pl.BlockSpec(memory_space=pl.ANY)
     counts = [len(near), len(loads), len(far), len(near_out), len(far_out), len(scratch), len(loads)]
@@ -1042,11 +937,15 @@
         greet_all(p, greet(p))
         act(p, flow, near, brought, far, near_out, far_out, scratch)
         flow.finish()
+        if flow.used > sems or flow.kept > local:
+            raise ValueError(f"{name}: {flow.used} {flow.kept}")
 
     return pl.pallas_call(
         kernel,
         out_shape=spots(near_out + far_out),
-        in_specs=[close] * len(near) + [spot] * (len(loads) + len(far)),
+        in_specs=[pl.BlockSpec(memory_space=pltpu.SMEM)] * numbers
+        + [close] * (len(near) - numbers)
+        + [spot] * (len(loads) + len(far)),
         out_specs=[close] * len(near_out) + [spot] * len(far_out),
         scratch_shapes=list(scratch)
         + [pltpu.VMEM(array.shape, array.dtype) for array in loads]
@@ -1104,66 +1003,291 @@
     return team_greet(p) + group_greet(p)
 
 
-def up_kernel(m, normed_all, in_full, in_bias, key_keep, clip_all, map_full, vec):
-    step = m.N
-    per = m.pixels // step
+def front_kernel(m, time_weight, time_bias, masked, small, fvec, in_cut, out_weight, map_cut, qkv_cut, clip_pad, proj_weight):
+    near = [time_weight, time_bias]
+    loads = [masked]
+    far = [masked, small, fvec, in_cut, out_weight, map_cut, qkv_cut, clip_pad]
+    far += [proj_weight] if m.even else []
+    N, C, FL, G, T = m.N, m.C, m.FL, m.G, m.T
     root = 0.5**0.5
-
-    def kernel(x_ref, w_ref, b_ref, keep_ref, clip_ref, map_ref, vec_ref,
-               active, slope, norms, total, silu, mapped, squares, weight, text):
+    texts = m.D * m.texts
+    cond = clip_pad.shape[1]
+    wide = C // m.Q
+    square = G == 4
+    items = m.G * m.D
+    mod_rows = -(-items // 8) * 8
+    pair = 2 * m.cs
+
+    def act(p, flow, near, loads, far, near_out, far_out, scratch):
+        tw_ref, tb_ref = near
+        norms, total, silu, mapped, x_all, in_all, active, slope = near_out[:8]
+        hat, inv, vec, fv, keep, pix, qkv_bias, embed, edges, normed = near_out[8:]
+        out_all, qkv_rows, mod_all, mod_line = far_out[:4]
+        map_all, clip_all, squares, weight, text, small_all, f_all, extended, conv, te, mod = scratch
+        mid, small_ref, fvec_ref, in_cut, out_own, map_cut, qkv_cut, clip = far[:8]
+        mine = p.c * p.R + p.z
+        own_in = in_all.at[p.q]
+        small_posts = [
+            flow.post(small_ref, small_all.at[mine, p.q], {"grp": to}) for to in p.groups()
+        ]
+        edge_posts = []
+        for block, to, sends, lands in (
+            (mid.at[pl.ds(N - EDGE, EDGE)], p.z + 1, p.z < p.R - 1, p.z > 0),
+            (mid.at[pl.ds(0, EDGE)], p.z - 1, p.z > 0, p.z < p.R - 1),
+        ):
+            slot = jnp.where(to > p.z, 0, 1)
+            edge_posts.append(
+                flow.post(block, edges.at[slot], {"rows": to}, when=sends, lands=lands)
+            )
+        f_posts = [flow.post(fvec_ref, f_all.at[p.q], {"grp": to}) for to in p.groups()]
+        flow.keep(small_ref, small_all.at[mine, p.q], now=True)
+        for item in small_posts:
+            flow.land(item)
+        spread = [
+            flow.post(small_all.at[mine], small_all.at[mine], {"duo": c, "rows": z})
+            for c, z in p.team()
+        ]
+        in_team = [
+            flow.post(in_cut.at[c * p.R + z], own_in.at[mine], {"duo": c, "rows": z})
+            for c, z in p.team()
+        ]
+        if square:
+            out_relay = flow.square(p, out_own, out_all)
+            flow.keep(out_own, out_all.at[p.q])
+        else:
+            flow.gather_group(p, out_own, out_all)
+        own_map = map_all.at[p.q]
+        map_team = [
+            flow.post(map_cut.at[c * p.R + z], own_map.at[mine], {"duo": c, "rows": z})
+            for c, z in p.team()
+        ]
+        clip_line = LineGather(flow, p, clip, clip_all)
+        clip_line.start()
+        if m.even:
+            for number in range(G):
+                to = lax.rem(p.z + number, G)
+                piece = far[8].at[:, pl.ds(pl.multiple_of(to * wide, 128), wide)]
+                flow.post(
+                    piece,
+                    far_out[4].at[p.z],
+                    {"grp": to, "duo": p.c, "rows": p.q},
+                    when=None if number else p.q != p.z,
+                )
+            piece = far[8].at[:, pl.ds(pl.multiple_of(p.z * wide, 128), wide)]
+            flow.keep(piece, far_out[4].at[p.z], p.q == p.z)
+        flow.keep(in_cut.at[mine], own_in.at[mine], now=True)
+        flow.keep(map_cut.at[mine], own_map.at[mine], now=True)
+        flow.keep(clip, clip_all.at[p.c, p.z], now=True)
+        flow.keep(fvec_ref, f_all.at[p.q], now=True)
+        for item in spread + edge_posts:
+            flow.land(item)
+        half = m.S // 2
+        vec[...] = jnp.zeros_like(vec)
+        for s, (g, d, r) in enumerate(m.places):
+            piece = small_all[d * m.R + r, g].astype(F32)
+            vec[pl.ds(0, 13), pl.ds(s * m.cs, m.cs)] = piece[:13, : m.cs]
+            vec[pl.ds(13 + s // half, 1), pl.ds(pair * (s % half), pair)] = piece[13:14, :pair]
+            if r == 0:
+                embed[pl.ds(m.D * g + d, 1)] = piece[14:15]
+        extended[pl.ds(0, EDGE)] = jnp.where(p.z > 0, edges[0].astype(F32), 0.0)
+        extended[pl.ds(EDGE, N)] = loads[0].get()[...].astype(F32)
+        extended[pl.ds(EDGE + N, EDGE)] = jnp.where(p.z < m.R - 1, edges[1].astype(F32), 0.0)
+        kind = small_all[mine, p.q].astype(F32)[14:15, FACTS + 2 : FACTS + 3]
+        real = float_cols(kind)
+        _, col = rows_cols(p.z * N, N, real)
+
+        def taps(lanes):
+            sum_of = jnp.zeros((N, 128), F32) + vec[pl.ds(9, 1), lanes]
+            for index, dy, dx in tap_steps():
+                pieces = [
+                    extended[pl.ds(EDGE + dy * width + dx, N), lanes]
+                    for width in (WIDTHS if dy else WIDTHS[:1])
+                ]
+                piece = pieces[0]
+                if dy:
+                    piece = jnp.where(kind == 0, piece, jnp.where(kind == 1, pieces[1], pieces[2]))
+                ok = (col + dx >= 0) & (col + dx < real)
+                sum_of = sum_of + jnp.where(ok, piece, 0.0) * vec[pl.ds(index, 1), lanes]
+            conv[:, lanes] = sum_of
+
+        each_column_block(m, taps)
+        values, inverse = layer_stats(conv[...])
+        hat[...] = values
+        normed[...] = values.astype(BF16)
+        inv[...] = inverse
+        line = LineGather(flow, p, normed, x_all)
+        line.start()
+        flow.keep(normed, x_all.at[p.c, p.z], now=True)
+        te[...] = embed[...][:items, : te.shape[1]].astype(BF16)
+        mod[...] = jnp.zeros_like(mod)
+        mod[pl.ds(0, items), pl.ds(0, pair)] = mm(te[...], tw_ref[...]) + tb_ref[...].astype(F32)
+        mod_posts = flow.gather_group(p, mod, mod_all)
+        for item in in_team:
+            flow.land(item)
+        if square:
+            in_relay = flow.square(p, own_in, in_all)
+        else:
+            in_posts = [flow.post(own_in, in_all.at[p.q], {"grp": q}) for q in p.groups()]
+        for d in range(m.D):
+            facts = small_all[d * m.R, p.q].astype(F32)
+            row, col_all = rows_cols(0, m.pixels, float_cols(facts[14:15, FACTS + 2 : FACTS + 3]))
+            inside = (row < facts[14:15, FACTS : FACTS + 1]) & (
+                col_all < facts[14:15, FACTS + 1 : FACTS + 2]
+            )
+            keep[d, pl.ds(0, m.pixels)] = jnp.where(inside, 1.0, 0.0)
+            shown = facts.T[: m.texts, 15:16]
+            slot = lax.broadcasted_iota(jnp.int32, (m.texts, 1), 0)
+            keep[d, pl.ds(m.pixels, m.texts)] = jnp.where(slot < TXT, shown, 0.0)
+        pix[...] = keep[p.c, pl.ds(pl.multiple_of(p.z * N, 8), N)]
+        for item in f_posts:
+            flow.land(item)
+        for g in range(G):
+            fv[:, pl.ds(g * m.FFS, m.FFS)] = f_all[g].astype(F32)[:8]
+        qkv_bias[...] = jnp.zeros_like(qkv_bias)
+        for h in range(T):
+
+            @pl.when(p.D * p.z + p.c == h)
+            def _():
+                at = pl.ds(h * m.HW, m.HW)
+                qkv_bias[:, : m.HW] = vec[pl.ds(13, 1), at]
+                qkv_bias[:, 2 * m.HW :] = vec[pl.ds(14, 1), at]
+
+        line.hop(1)
+        if square:
+            out_relay()
+        line.hop(2)
+        for item in map_team:
+            flow.land(item)
+        map_posts = [flow.post(own_map, map_all.at[p.q], {"grp": q}) for q in p.groups()]
+        flow.swap_team(p, qkv_cut, qkv_rows)
+        if square:
+            in_posts = in_relay()
+        for item in mod_posts:
+            flow.land(item)
+        flow.settle_kept()
+        mods = LineGather(flow, p, mod_all, mod_line)
+        mods.start()
+        flow.keep(mod_all, mod_line.at[p.c, p.z])
         squares[...] = jnp.zeros_like(squares)
-
-        @pl.loop(0, m.D * per)
-        def _(number):
-            rows = pl.ds(pl.multiple_of(number * step, 16), step)
-            hidden = mm(x_ref[rows], w_ref[...]) + b_ref[...]
-            gate = 0.5 * (1.0 + lax.erf(hidden * root))
-            value = hidden * gate
-            active[rows] = value
-            slope[rows] = gate + hidden * (jnp.exp(-0.5 * hidden * hidden) * 0.3989422804014327)
-            item = number // per
-            inside = pl.ds(pl.multiple_of((number - item * per) * step, 16), step)
-            squares[pl.ds(item, 1)] += jnp.sum(
-                keep_ref[item, inside] * value * value, axis=0, keepdims=True
-            )
-
+        for item in in_posts:
+            flow.land(item)
+
+        def multiply(first, count):
+            line.settle(first + count)
+
+            @pl.loop(0, count * m.D)
+            def _(number):
+                d = number // count
+                block = jnp.where(
+                    number - d * count == 0, line.nth(first), line.nth(first + count - 1)
+                )
+                base = pl.multiple_of(block * N, 16)
+                hidden = mm(x_all[d, block], in_all[...].reshape(C, FL)) + fv[pl.ds(0, 1)]
+                gate = 0.5 * (1.0 + lax.erf(hidden * root))
+                value = hidden * gate
+                rows = pl.ds(pl.multiple_of(d * m.pixels + base, 16), N)
+                active[rows] = value
+                slope[rows] = gate + hidden * (
+                    jnp.exp(-0.5 * hidden * hidden) * 0.3989422804014327
+                )
+                squares[pl.ds(d, 1)] += jnp.sum(
+                    keep[d, pl.ds(base, N)] * value * value, axis=0, keepdims=True
+                )
+
+        first = m.R // 2
+        multiply(0, first)
+        line.hop(3)
+        for step in range(4, m.R):
+            line.hop(step)
+        multiply(first, m.R - first)
         norms[...] = jnp.sqrt(squares[...])
         total[...] = jnp.broadcast_to(jnp.sum(norms[...], axis=1, keepdims=True), total.shape)
-        for t in range(m.T):
-            piece = clip_ref[t].astype(F32)[: m.slots]
-            text[pl.ds(t * m.slots, m.slots)] = piece / (1.0 + jnp.exp(-piece))
+        for step in range(1, m.R):
+            clip_line.hop(step)
+            mods.hop(step)
+        clip_line.settle(m.R)
+        for item in map_posts:
+            flow.land(item)
+        for d in range(m.D):
+            for r in range(m.R):
+                piece = clip_all[d, r].astype(F32)[: m.slots]
+                text[pl.ds((d * m.R + r) * m.slots, m.slots)] = piece / (1.0 + jnp.exp(-piece))
         silu[...] = text[...].astype(BF16)
-        for g in range(m.G):
-            for t in range(m.T):
-                at = m.ms * (g * m.T + t)
-                piece = map_ref[g, pl.ds(t * m.mp, m.mp)].astype(F32)
-                weight[pl.ds(at, m.ms)] = piece[: m.ms]
-        for t in range(m.T):
-            @pl.when(lax.axis_index("duo") * m.R + lax.axis_index("rows") == t)
+        for g in range(G):
+            for t in range(T):
+                piece = map_all[g, t].astype(F32)
+                weight[pl.ds(m.ms * (g * T + t), m.ms)] = piece[: m.ms]
+        product = mm(silu[...], weight[...].astype(BF16))
+        for t in range(T):
+
+            @pl.when(mine == t)
             def _():
-                bias = vec_ref[pl.ds(11, 1), pl.ds(t * m.HW, m.HW)]
-                mapped[...] = (mm(silu[...], weight[...].astype(BF16)) + bias).astype(BF16)
-
-    texts = m.D * m.texts
-    cond = clip_all.shape[2]
-    return local_kernel(
-        "hidden_units",
-        kernel,
-        [normed_all, in_full, in_bias, key_keep, clip_all, map_full, vec],
-        [
-            ((m.D * m.pixels, m.FL), F32),
-            ((m.D * m.pixels, m.FL), F32),
-            ((8, m.FL), F32),
-            ((8, 128), F32),
-            ((texts, cond), BF16),
-            ((texts, m.HW), BF16),
-        ],
-        [
-            pltpu.VMEM((8, m.FL), F32),
-            pltpu.VMEM((cond, m.HW), F32),
-            pltpu.VMEM((texts, cond), F32),
-        ],
-    )
+                mapped[...] = (product + vec[pl.ds(11, 1), pl.ds(t * m.HW, m.HW)]).astype(BF16)
+
+    near_out = [
+        ((8, FL), F32),
+        ((8, 128), F32),
+        ((texts, cond), BF16),
+        ((texts, m.HW), BF16),
+        ((m.D, m.R, N, C), BF16),
+        ((G, T, m.cs, FL), BF16),
+        ((m.D * m.pixels, FL), F32),
+        ((m.D * m.pixels, FL), F32),
+        ((N, C), F32),
+        ((N, 1), F32),
+        ((VEC, C), F32),
+        ((8, FL), F32),
+        ((m.D, m.pixels + m.texts, 1), F32),
+        ((N, 1), F32),
+        ((1, 3 * m.HW), F32),
+        ((mod_rows, 128), F32),
+        ((2, EDGE, C), BF16),
+        ((N, C), BF16),
+    ]
+    far_out = [
+        ((G,) + out_weight.shape, BF16),
+        (qkv_cut.shape, BF16),
+        ((G, mod_rows, 128), F32),
+        ((m.D, m.R, G, mod_rows, 128), F32),
+    ]
+    if m.even:
+        far_out.append(((m.R, m.cs, wide), BF16))
+    scratch = [
+        pltpu.VMEM((G, T, m.mp, m.HW), BF16),
+        pltpu.VMEM((m.D, m.R) + clip_pad.shape, BF16),
+        pltpu.VMEM((8, FL), F32),
+        pltpu.VMEM((cond, m.HW), F32),
+        pltpu.VMEM((texts, cond), F32),
+        pltpu.VMEM((T, G, SMALL, 128), BF16),
+        pltpu.VMEM((G,) + fvec.shape, BF16),
+        pltpu.VMEM((N + 2 * EDGE, C), F32),
+        pltpu.VMEM((N, C), F32),
+        pltpu.VMEM((items, time_weight.shape[0]), BF16),
+        pltpu.VMEM((mod_rows, 128), F32),
+    ]
+    columns = 4 if square else G - 1
+    return fused_kernel(
+        1,
+        "front",
+        lambda p: common_greet(p) + (sources_greet(m, p) if m.even else []),
+        act,
+        near,
+        loads,
+        far,
+        near_out,
+        far_out,
+        scratch,
+        4 * (T - 1) + 2 + 2 * columns + 4 * (G - 1) + (G if m.even else 0) + 3 * gather_sems(m),
+        12,
+    )
+
+
+def sources_greet(m, p):
+    greet = []
+    for step in range(m.G):
+        source = {"grp": p.z, "duo": p.c, "rows": lax.rem(p.q - step + m.G, m.G)}
+        greet.append((source, None if step else p.q != p.z))
+    return greet
 
 
 def team_sum(m, p, flow, own, everyone):
@@ -1183,24 +1307,24 @@
     return total
 
 
-def branch_kernel(m, active, norms, total, out_full, gain, grn_bias, latents, keep, vec, mod_all, qkv_rows, mapped, gres, proj_part):
-    near = [norms, total, gain, grn_bias, keep, mod_all]
+def branch_kernel(m, active, norms, total, out_full, fv, latents, keep, vec, mod_all, qkv_rows, mapped, proj_part):
+    near = [norms, total, fv, keep, mod_all]
     loads = [active, out_full, latents, vec]
-    far = [qkv_rows, mapped, gres] + ([proj_part] if m.even else [])
+    far = [qkv_rows, mapped] + ([proj_part] if m.even else [])
     N, C = m.N, m.C
     rows_all = m.D * m.pixels
 
     def act(p, flow, near, loads, far, near_out, far_out, scratch):
-        norms, total, gain, grn_bias, keep, mod_all = near
+        norms, total, fv, keep, mod_all = near
+        gain, grn_bias = fv[pl.ds(1, 1)], fv[pl.ds(2, 1)]
         grn, after, hat, inv, two, ratio, means, mods = near_out
-        two_all, mapped_all, gres_all, qkv_all = far_out[:4]
+        two_all, mapped_all, qkv_all = far_out[:3]
         everyone, part, mate, passed, landed, branch, slopes = scratch
         add_up = team_sum(m, p, flow, total, everyone)
         flow.gather_group(p, far[0], qkv_all)
         if m.even:
-            flow.gather_group(p, far[3], far_out[4])
+            flow.gather_group(p, far[2], far_out[3])
         text_line = LineGather(flow, p, far[1], mapped_all)
-        grad_line = LineGather(flow, p, far[2], gres_all)
         two_line = LineGather(flow, p, two, two_all)
         half = m.S // 2
         pair = 2 * m.cs
@@ -1210,14 +1334,15 @@
         mean = add_up() / m.FF + grn_eps
         means[...] = mean
         ratio[...] = norms[...] / mean[:, :1]
-        slopes[...] = gain[...] * ratio[...] + 1.0
+        slopes[...] = gain * ratio[...] + 1.0
         line = LineReduce(flow, p, part, branch, mate, passed, landed)
         active, out_w, lat, vec = (load.get() for load in loads)
 
         def produce(block):
-            for d in range(m.D):
+            @pl.loop(0, m.D)
+            def _(d):
                 rows = pl.ds(pl.multiple_of(d * m.pixels + block * N, 16), N)
-                low = (active[rows] * slopes[pl.ds(d, 1)] + grn_bias[...]).astype(BF16)
+                low = (active[rows] * slopes[pl.ds(d, 1)] + grn_bias).astype(BF16)
                 grn[rows] = low
                 part[d, block] = mm(low, out_w[...]).astype(BF16)
 
@@ -1235,14 +1360,11 @@
 
         chunks(N, tail)
         two_line.start()
-        grad_line.start()
         flow.keep(far[1], mapped_all.at[p.c, p.z])
         flow.keep(two, two_all.at[p.c, p.z])
-        flow.keep(far[2], gres_all.at[p.c, p.z])
         for step in range(1, m.R):
             text_line.hop(step)
             two_line.hop(step)
-            grad_line.hop(step)
 
     near_out = [
         ((rows_all, m.FL), BF16),
@@ -1257,7 +1379,6 @@
     far_out = [
         ((m.D, m.R, N, C), BF16),
         ((m.D, m.R) + mapped.shape, BF16),
-        ((m.D, m.R, N, C), BF16),
         ((m.G,) + qkv_rows.shape, BF16),
     ]
     if m.even:
@@ -1278,27 +1399,231 @@
         near_out,
         far_out,
         scratch,
-        (m.T - 1) + 2 * (m.G - 1) + 3 * gather_sems(m) + reduce_sems(m),
+        (m.T - 1) + 2 * (m.G - 1) + 2 * gather_sems(m) + reduce_sems(m),
         5,
     )
 
 
-def attended_kernel(m, two_part, text_part, result_part, cot, gres, hat, inv, after, mods, keep, vec, grad_qkv, grad_proj):
+def attention_kernel(m, two_all, gres, mapped_all, weight, proj, bias, key_keep):
+    near = [bias, key_keep]
+    loads = [two_all, weight, proj, mapped_all]
+    far = [gres]
+    heads = m.HW // HEAD
+    keys = m.pixels + m.texts
+    scale = HEAD ** (-0.5)
+    HW, C, N, D, R, G, pixels, texts = m.HW, m.C, m.N, m.D, m.R, m.G, m.pixels, m.texts
+    wide = C // m.Q
+    block_rows = 2 * HW
+
+    def act(p, flow, near, loads, far, near_out, far_out, scratch):
+        bias, keep = near
+        result, two_out, map_out, gw_out, gp_out, gb_out = near_out
+        (gres_all, part, mate, passed, landed, qkv, k_all, v_all, k_t, v_t, dk, dv, o_t, dq_t, o_low, att, g_all, probs, dqkv,
+         dtext, piece, words) = scratch
+        line = LineGather(flow, p, far[0], gres_all)
+        line.start()
+        flow.keep(far[0], gres_all.at[p.c, p.z], now=True)
+        two, w, proj, mapped = (load.get() for load in loads)
+        red = LineReduce(flow, p, part, result, mate, passed, landed)
+
+        @pl.loop(0, D)
+        def _(d):
+            qkv[d] = (mm(two[d], w[...]) + bias[...]).astype(BF16)
+            words[...] = jnp.zeros((texts, 3 * HW), F32) + bias[...]
+
+            @pl.loop(0, m.T)
+            def _(t):
+                words[...] += mm(mapped[t, d], w[pl.ds(pl.multiple_of(t * HW, 16), HW)])
+
+            text = words[...].astype(BF16)
+            k_all[d, pl.ds(0, pixels)] = qkv[d, :, HW : 2 * HW]
+            k_all[d, pl.ds(pixels, texts)] = text[:, HW : 2 * HW]
+            v_all[d, pl.ds(0, pixels)] = qkv[d, :, 2 * HW :]
+            v_all[d, pl.ds(pixels, texts)] = text[:, 2 * HW :]
+            k_t[d] = k_all[d].T
+            v_t[d] = v_all[d].T
+            dk[d] = jnp.zeros_like(dk[d])
+            dv[d] = jnp.zeros_like(dv[d])
+            o_t[d] = jnp.zeros_like(o_t[d])
+            dq_t[d] = jnp.zeros_like(dq_t[d])
+
+        lane = lax.broadcasted_iota(jnp.int32, (1, HW), 1)
+        row = lax.broadcasted_iota(jnp.int32, (HW, 1), 0)
+
+        def masks(number):
+            d = number // heads
+            low = (number - d * heads) * HEAD
+            return d, (lane >= low) & (lane < low + HEAD), (row >= low) & (row < low + HEAD)
+
+        def forward(number):
+            d, in_head, in_row = masks(number)
+            q_h = jnp.where(in_head, qkv[d, :, :HW], 0).astype(BF16)
+            scores = mm_t(k_all[d], q_h) * scale
+            scores = jnp.where(keep[d] > 0, scores, masked_score)
+            weights = jnp.exp(scores - jnp.max(scores, axis=0, keepdims=True))
+            low = (weights / jnp.sum(weights, axis=0, keepdims=True)).astype(BF16)
+            probs[number] = low
+            o_t[d] += mm(jnp.where(in_row, v_t[d], 0).astype(BF16), low)
+
+        pl.loop(0, D * heads // 2)(forward)
+        line.hop(1)
+        pl.loop(D * heads // 2, D * heads)(forward)
+
+        @pl.loop(0, D)
+        def _(d):
+            o_low[d] = o_t[d].astype(BF16)
+            att[d] = o_t[d].T.astype(BF16)
+
+        def lanes_of(n):
+            return pl.ds(pl.multiple_of(n * wide, 128), wide)
+
+        @pl.loop(0, D * R)
+        def _(number):
+            d = number // R
+            block = number - d * R
+            mine = att[d, pl.ds(pl.multiple_of(block * N, 16), N)]
+            for n in range(m.Q):
+                part[d, block, :, pl.ds(n * wide, wide)] = mm(mine, proj[n]).astype(BF16)
+
+        red.start()
+        line.hop(2)
+        red.early()
+        steps = list(red.later())
+        for number in range(3, R):
+            line.hop(number)
+        line.settle(R)
+
+        @pl.loop(0, D * R)
+        def _(number):
+            d = number // R
+            block = number - d * R
+            total = jnp.zeros((N, HW), F32)
+            for n in range(m.Q):
+                total = total + mm_t(gres_all[d, block, :, pl.ds(n * wide, wide)], proj[n])
+            g_all[d, pl.ds(pl.multiple_of(block * N, 16), N)] = total.astype(BF16)
+
+        def back(first, last):
+            @pl.loop(first, last)
+            def _(number):
+                d, in_head, in_row = masks(number)
+                q_h = jnp.where(in_head, qkv[d, :, :HW], 0).astype(BF16)
+                g_h = jnp.where(in_head, g_all[d], 0).astype(BF16)
+                low = probs[number]
+                dv[d] += mm(low, g_h)
+                grad_probs = mm_t(v_all[d], g_h)
+                high = low.astype(F32)
+                sums = jnp.sum(high * grad_probs, axis=0, keepdims=True)
+                grad_scores = (high * (grad_probs - sums)).astype(BF16)
+                dq_t[d] += mm(jnp.where(in_row, k_t[d], 0).astype(BF16), grad_scores)
+                dk[d] += mm(grad_scores, q_h)
+
+        cut = D * heads // 2
+        steps[0]()
+        back(0, cut)
+        for step in steps[1:3]:
+            step()
+        back(cut, D * heads)
+        for step in steps[3:]:
+            step()
+        gb_out[...] = jnp.zeros_like(gb_out)
+
+        @pl.loop(0, D)
+        def _(d):
+            dqkv[d, :, :HW] = (dq_t[d].T * scale).astype(BF16)
+            dqkv[d, :, HW : 2 * HW] = (dk[d, pl.ds(0, pixels)] * scale).astype(BF16)
+            dqkv[d, :, 2 * HW :] = dv[d, pl.ds(0, pixels)].astype(BF16)
+            dtext[d, :, :HW] = jnp.zeros((texts, HW), BF16)
+            dtext[d, :, HW : 2 * HW] = (dk[d, pl.ds(pixels, texts)] * scale).astype(BF16)
+            dtext[d, :, 2 * HW :] = dv[d, pl.ds(pixels, texts)].astype(BF16)
+            gb_out[pl.ds(0, 1)] += jnp.sum(dqkv[d].astype(F32), axis=0, keepdims=True) + jnp.sum(
+                dtext[d].astype(F32), axis=0, keepdims=True
+            )
+            two_out[d] = mm_t(dqkv[d], w[...]).astype(BF16)
+            @pl.loop(0, m.T)
+            def _(t):
+                rows = pl.ds(pl.multiple_of(t * HW, 16), HW)
+                map_out[t, d] = mm_t(dtext[d], w[rows]).astype(BF16)
+
+        @pl.loop(0, C // block_rows)
+        def _(g):
+            lanes = pl.ds(pl.multiple_of(g * block_rows, 128), block_rows)
+            piece[...] = t_mm(two[0, :, lanes], dqkv[0])
+            for d in range(1, D):
+                piece[...] += t_mm(two[d, :, lanes], dqkv[d])
+            for side in range(2):
+                rows = pl.ds(side * HW, HW)
+                for d in range(D):
+                    piece[rows] += t_mm(mapped[2 * g + side, d], dtext[d])
+            gw_out[pl.ds(pl.multiple_of(g * block_rows, 16), block_rows)] = piece[...].astype(BF16)
+
+        @pl.loop(0, m.Q)
+        def _(n):
+            total = jnp.zeros((HW, wide), F32)
+            for d in range(D):
+                columns = gres_all[d, :, :, lanes_of(n)].reshape(pixels, wide)
+                total = total + mm(o_low[d], columns)
+            gp_out[n] = total.astype(BF16)
+        red.close()
+
+    near_out = [
+        ((N, C), F32),
+        ((D, pixels, C), BF16),
+        ((m.T, D, texts, HW), BF16),
+        ((C, 3 * HW), BF16),
+        ((m.Q, HW, wide), BF16),
+        ((8, 3 * HW), F32),
+    ]
+    scratch = [pltpu.VMEM((D, R, N, C), BF16)] + reduce_buffers(m, N, C)
+    scratch += [
+        pltpu.VMEM((D, pixels, 3 * HW), BF16),
+        pltpu.VMEM((D, keys, HW), BF16),
+        pltpu.VMEM((D, keys, HW), BF16),
+        pltpu.VMEM((D, HW, keys), BF16),
+        pltpu.VMEM((D, HW, keys), BF16),
+        pltpu.VMEM((D, keys, HW), F32),
+        pltpu.VMEM((D, keys, HW), F32),
+        pltpu.VMEM((D, HW, pixels), F32),
+        pltpu.VMEM((D, HW, pixels), F32),
+        pltpu.VMEM((D, HW, pixels), BF16),
+        pltpu.VMEM((D, pixels, HW), BF16),
+        pltpu.VMEM((D, pixels, HW), BF16),
+        pltpu.VMEM((D * heads, keys, pixels), BF16),
+        pltpu.VMEM((D, pixels, 3 * HW), BF16),
+        pltpu.VMEM((D, texts, 3 * HW), BF16),
+        pltpu.VMEM((block_rows, 3 * HW), F32),
+        pltpu.VMEM((texts, 3 * HW), F32),
+    ]
+    return fused_kernel(
+        4,
+        "attention_block",
+        team_greet,
+        act,
+        near,
+        loads,
+        far,
+        near_out,
+        [],
+        scratch,
+        gather_sems(m) + reduce_sems(m),
+        1,
+    )
+
+
+def attended_kernel(m, two_part, text_part, result, cot, gres, hat, inv, after, mods, keep, vec, grad_qkv, grad_proj):
     near = [inv, mods, keep]
-    loads = [two_part, hat, after, cot, gres, text_part, result_part, vec]
+    loads = [two_part, hat, after, cot, gres, text_part, result, vec]
     far = [grad_qkv] + ([grad_proj] if m.even else [])
     N, C = m.N, m.C
     texts = m.D * m.texts
 
     def act(p, flow, near, loads, far, near_out, far_out, scratch):
         inv, mods, keep = near
-        two_part, hat, after, cot, gres, text_part, result_part, vec = (load.get() for load in loads)
+        two_part, hat, after, cot, gres, text_part, result, vec = (load.get() for load in loads)
         output, grad_after, branch, gm, vecg, text = near_out
         gb_all = far_out[0]
-        two_sum, result_sum, text_sum = scratch[:3]
-        two_red = LineReduce(flow, p, two_part, two_sum, *scratch[3:6])
-        text_red = LineReduce(flow, p, text_part, text_sum, *scratch[6:9])
-        result_red = LineReduce(flow, p, result_part, result_sum, *scratch[9:12])
+        two_sum, text_sum = scratch[:2]
+        two_red = LineReduce(flow, p, two_part, two_sum, *scratch[2:5])
+        text_red = LineReduce(flow, p, text_part, text_sum, *scratch[5:8])
         line = LineGather(flow, p, branch, gb_all)
         two_red.start()
         flow.swap_group(p, far[0], far_out[1])
@@ -1323,19 +1648,18 @@
         line.start()
         flow.keep(branch, gb_all.at[p.c, p.z])
         text_red.start()
-        result_red.start()
-        for step in range(1, m.R):
+        line.hop(1)
+
+        def out(rows):
+            second = after[rows] * (1.0 + mods[pl.ds(0, 1)]) + mods[pl.ds(1, 1)]
+            value = keep[rows] * (result[rows] + vec[pl.ds(12, 1)])
+            output[rows] = (second + value).astype(BF16)
+
+        chunks(N, out)
+        for step in range(2, m.R):
             line.hop(step)
         text_red.steps_all()
         text[...] = text_sum[...].astype(BF16)
-        result_red.steps_all()
-
-        def out(rows):
-            second = after[rows] * (1.0 + mods[pl.ds(0, 1)]) + mods[pl.ds(1, 1)]
-            value = keep[rows] * (result_sum[rows] + vec[pl.ds(12, 1)])
-            output[rows] = (second + value).astype(BF16)
-
-        chunks(N, out)
 
     near_out = [
         ((N, C), BF16),
@@ -1349,10 +1673,9 @@
     if m.even:
         far_out.append((grad_proj.shape, BF16))
     scratch = (
-        [pltpu.VMEM((N, C), F32), pltpu.VMEM((N, C), F32), pltpu.VMEM((texts, m.HW), F32)]
+        [pltpu.VMEM((N, C), F32), pltpu.VMEM((texts, m.HW), F32)]
         + reduce_buffers(m, N, C, False)
         + reduce_buffers(m, texts, m.HW, False)
-        + reduce_buffers(m, N, C, False)
     )
     return fused_kernel(
         5,
@@ -1365,7 +1688,7 @@
         near_out,
         far_out,
         scratch,
-        2 * (m.G - 1) + gather_sems(m) + 3 * reduce_sems(m),
+        2 * (m.G - 1) + gather_sems(m) + 2 * reduce_sems(m),
         4,
     )
 
@@ -1389,9 +1712,9 @@
     )
 
 
-def back_kernel(m, gb_all, out_full, active, slope, grn_out, normed_all, in_full, norms, ratio, means, gain, key_keep,
-                hat, inv, qkv_parts, proj_parts, grad_map):
-    near = [norms, ratio, means, gain, key_keep]
+def back_kernel(m, gb_all, out_full, active, slope, grn_out, normed_all, in_full, norms, ratio, means, fv, key_keep,
+                qkv_parts, proj_parts, grad_map):
+    near = [norms, ratio, means, fv, key_keep]
     loads = [gb_all, out_full, active, grn_out, slope, normed_all, in_full, qkv_parts]
     loads += [proj_parts] if m.even else []
     far = [grad_map]
@@ -1401,11 +1724,12 @@
     per = m.pixels // N
 
     def act(p, flow, near, loads, far, near_out, far_out, scratch):
-        norms, ratio, means, gain, keep = near
-        (back,) = near_out
-        out_parts, in_parts, f_parts, map_parts, qkv_team = far_out[:5]
+        norms, ratio, means, fv, keep = near
+        gain = fv[pl.ds(1, 1)]
+        back, g_out = near_out
+        in_parts, f_parts, map_parts, qkv_team = far_out[:4]
         everyone, mine, moments, slopes, shifts, grads, hidden, part, mate, passed, landed = scratch[:11]
-        g_out, g_in, f_own, qkv_own = scratch[11:15]
+        turned_g, turned_x, g_in, f_own, qkv_own = scratch[11:16]
         flow.swap_group(p, far[0], map_parts)
         gb, out_w, active, grn = (load.get() for load in loads[:4])
         moments[...] = jnp.zeros_like(moments)
@@ -1419,12 +1743,17 @@
             moments[pl.ds(item, 1)] += jnp.sum(grad * active[rows], axis=0, keepdims=True)
             moments[pl.ds(m.D, 1)] += jnp.sum(grad, axis=0, keepdims=True)
 
-        scaled = moments[...] * gain[...]
+        scaled = moments[...] * gain
         cross = jnp.sum(scaled * norms[...], axis=1, keepdims=True)
         mine[...] = jnp.broadcast_to(cross, mine.shape)
         add_up = team_sum(m, p, flow, mine, everyone)
-        for g in range(G):
-            g_out[g] = t_mm(grn[:, g * m.FFS : (g + 1) * m.FFS], gb[...]).astype(BF16)
+        turned_g[...] = grn[...].T
+
+        def multiply_out(g, rows):
+            g_out[g] = mm(turned_g[rows], gb[...]).astype(BF16)
+
+        each_rows(G, m.FFS, multiply_out)
+
         slope, x, in_w, qkv_parts = (load.get() for load in loads[4:8])
         step = m.cs
 
@@ -1438,12 +1767,11 @@
 
         add_parts(qkv_parts, qkv_own, m.T)
         if m.even:
-            proj_own = scratch[15]
+            proj_own = scratch[16]
             add_parts(loads[8].get(), proj_own, m.R)
-        flow.swap_group(p, g_out, out_parts)
         mean = means[...][:, :1]
         cross = add_up()[:, :1]
-        slopes[...] = gain[...] * ratio[...] + 1.0
+        slopes[...] = gain * ratio[...] + 1.0
         shifts[...] = (scaled / mean - cross / (m.FF * mean * mean)) / norms[...]
         gains = jnp.sum(moments[pl.ds(0, m.D)] * ratio[pl.ds(0, m.D)], axis=0, keepdims=True)
         biases = moments[pl.ds(m.D, 1)]
@@ -1454,11 +1782,11 @@
                 to = lax.rem(p.q + number, G)
                 flow.post(
                     proj_own.at[to],
-                    far_out[5].at[p.q],
+                    far_out[4].at[p.q],
                     {"grp": p.z, "duo": p.c, "rows": to},
                     when=None if number else p.q != p.z,
                 )
-            flow.keep(proj_own.at[p.z], far_out[5].at[p.q], p.q == p.z)
+            flow.keep(proj_own.at[p.z], far_out[4].at[p.q], p.q == p.z)
 
         @pl.loop(0, m.D * per)
         def _(number):
@@ -1481,25 +1809,38 @@
         line = LineReduce(flow, p, part, back, mate, passed, landed)
 
         def produce(block):
-            for d in range(m.D):
+            @pl.loop(0, m.D)
+            def _(d):
                 rows = pl.ds(pl.multiple_of(d * m.pixels + block * N, 16), N)
                 part[d, block] = mm_t(hidden[rows], in_w[...]).astype(BF16)
 
+        turned_x[...] = x[...].T
+        first = flow.take(G - 1)
+
+        def send_in(number):
+            g = lax.rem(p.q + 1 + number, G)
+            return flow.copy(g_in.at[g], in_parts.at[p.q], {"grp": g}, first + number)
+
         def between(number):
-            if number < G:
+            if number != 1:
+                return
+
+            @pl.loop(0, G)
+            def _(number):
                 g = lax.rem(p.q + 1 + number, G)
-                lanes = pl.ds(pl.multiple_of(g * rows_in, 128), rows_in)
-                g_in[g] = t_mm(x[:, lanes], hidden[...]).astype(BF16)
-                if number < G - 1:
-                    flow.post(g_in.at[g], in_parts.at[p.q], {"grp": g})
-                else:
-                    flow.keep(g_in.at[p.q], in_parts.at[p.q])
+                rows = pl.ds(pl.multiple_of(g * rows_in, 16), rows_in)
+                g_in[g] = mm(turned_x[rows], hidden[...]).astype(BF16)
+                pl.when(number < G - 1)(lambda: send_in(number).start())
+
+            flow.keep(g_in.at[p.q], in_parts.at[p.q])
 
         line.run(produce, between)
-
-    near_out = [((N, C), F32)]
+        for number in range(G - 1):
+            send_in(number).wait_recv()
+            send_in(number).wait_send()
+
+    near_out = [((N, C), F32), ((G, m.FFS, C), BF16)]
     far_out = [
-        ((G, m.FFS, C), BF16),
         ((G, rows_in, FL), BF16),
         ((G, 8, m.FFS), F32),
         (grad_map.shape, BF16),
@@ -1516,7 +1857,8 @@
     ]
     scratch += reduce_buffers(m, N, C)
     scratch += [
-        pltpu.VMEM((G, m.FFS, C), BF16),
+        pltpu.VMEM((FL, m.D * m.pixels), BF16),
+        pltpu.VMEM((C, m.D * m.pixels), BF16),
         pltpu.VMEM((G, rows_in, FL), BF16),
         pltpu.VMEM((G, 8, m.FFS), F32),
         pltpu.VMEM((m.T, m.cs, 3 * m.HW), BF16),
@@ -1537,6 +1879,74 @@
         scratch,
         2 * (m.T - 1) + 4 * (G - 1) + reduce_sems(m) + (G if m.even else 0),
         7,
+    )
+
+
+def tail_kernel(m, grad_low, tiny, g_out, in_parts, map_parts):
+    loads = [in_parts, map_parts]
+    far = [grad_low, tiny, g_out]
+    N, C, G, T = m.N, m.C, m.G, m.T
+
+    def act(p, flow, near, loads, far, near_out, far_out, scratch):
+        low, tiny, g_out = far
+        edges, tiny_all, in_team, map_team, out_parts = far_out
+        in_own, map_own, tiny_in, tiny_own = scratch
+        for block, to, sends, lands in (
+            (low.at[pl.ds(N - EDGE, EDGE)], p.z + 1, p.z < p.R - 1, p.z > 0),
+            (low.at[pl.ds(0, EDGE)], p.z - 1, p.z > 0, p.z < p.R - 1),
+        ):
+            slot = jnp.where(to > p.z, 0, 1)
+            flow.post(block, edges.at[slot], {"rows": to}, when=sends, lands=lands)
+        posts = flow.swap_team(p, tiny, tiny_in)
+        flow.swap_group(p, g_out, out_parts)
+        for load, own, step in ((loads[0], in_own, m.cs), (loads[1], map_own, m.mp)):
+            parts = load.get()
+
+            def add(t, rows, parts=parts, own=own):
+                total = parts[0, rows].astype(F32)
+                for g in range(1, G):
+                    total = total + parts[g, rows].astype(F32)
+                own[t] = total.astype(BF16)
+
+            each_rows(T, step, add)
+
+        flow.swap_team(p, in_own, in_team)
+        flow.swap_team(p, map_own, map_team)
+        for item in posts:
+            flow.land(item)
+        flow.settle_kept()
+        for d in range(m.D):
+            for g in range(G):
+                total = tiny_in[d * m.R, g]
+                for r in range(1, m.R):
+                    total = total + tiny_in[d * m.R + r, g]
+                tiny_own[g, d] = total
+        flow.swap_group(p, tiny_own, tiny_all)
+
+    return fused_kernel(
+        11,
+        "tail",
+        common_greet,
+        act,
+        [],
+        loads,
+        far,
+        [],
+        [
+            ((2, EDGE, C), BF16),
+            ((G, m.D) + tiny.shape[2:], F32),
+            ((T, m.cs, m.FL), BF16),
+            ((T, m.mp, m.HW), BF16),
+            (g_out.shape, BF16),
+        ],
+        [
+            pltpu.VMEM((T, m.cs, m.FL), BF16),
+            pltpu.VMEM((T, m.mp, m.HW), BF16),
+            pltpu.VMEM(tiny.shape, F32),
+            pltpu.VMEM((G, m.D) + tiny.shape[2:], F32),
+        ],
+        2 + 3 * (T - 1) + 2 * (G - 1),
+        5,
     )
 
 
@@ -1583,9 +1993,9 @@
         m,
         [heights, widths, bucket_ids, in_weight, qkv_weight, map_weight, clip_tokens, latents]
         + [cotangent, conv_weight]
-        + [vector[None] for vector in vectors]
+        + vectors
         + [time_embed, text_mask]
-        + [vector[None] for vector in fvectors],
+        + fvectors,
     )
     latents = latents[0]
     cotangent = cotangent[0]
@@ -1599,133 +2009,54 @@
             slot = jnp.where(to > p.z, 0, 1)
             plan.add(block, dst.at[slot], {"rows": to}, when=sends, lands=lands)
 
-    def plan_start(p, ins, outs):
-        plan = Plan(p)
-        plan.group_gather(ins[1], outs[1])
-        swap_edges(plan, ins[0], outs[0])
-        plan.team_swap(ins[2], outs[2])
-        plan.group_gather(ins[3], outs[3])
-        plan.team_swap(ins[4], outs[4])
-        return plan.done()
-
-    edges, _, in_rows, fvec_all, map_rows, small_all, clip_all = team_kernel(
-        0,
-        "exchange_start",
-        plan_start,
-        [masked, small, in_cut, fvec, map_cut],
-        [
-            ((2, EDGE, C), BF16),
-            ((G, SMALL, 128), BF16),
-            ((T, cs, FL), BF16),
-            ((G, 16, FFS), BF16),
-            ((T, mp, HW), BF16),
-        ],
-        gathers=[clip_pad],
-        messages=2 + 2 * (G - 1) + 2 * (T - 1),
-        local=4,
-        late=(1, 0, G - 1),
-    )
-    normed, norm_hat, norm_inv, vec, mod_part, key_keep, keep = conv_kernel(
-        m, bucket_ids, edges, masked, small_all, time_weight, time_bias[None]
-    )
-    in_bias_s, gain_s, grn_bias_s = (
-        fvec_all[:, row].reshape(1, FL).astype(F32) for row in range(3)
-    )
-
-    def plan_first(p, ins, outs):
-        plan = Plan(p)
-        plan.group_gather(ins[4], outs[4])
-        plan.group_gather(ins[0], outs[0], late=1)
-        plan.group_gather(ins[1], outs[1], late=2)
-        plan.team_swap(ins[2], outs[2])
-        plan.group_gather(ins[3], outs[3])
-        if even:
-            wide = C // G
-            for step in range(G):
-                to = lax.rem(p.z + step, G)
-                when = None if step else p.q != p.z
-                piece = ins[5].at[:, pl.ds(pl.multiple_of(to * wide, 128), wide)]
-                plan.add(
-                    piece, outs[5].at[p.z], {"grp": to, "duo": p.c, "rows": p.q}, when=when
-                )
-                source = {"grp": p.z, "duo": p.c, "rows": lax.rem(p.q - step + G, G)}
-                plan.greet.append((source, when))
-            piece = ins[5].at[:, pl.ds(pl.multiple_of(p.z * wide, 128), wide)]
-            plan.local.append((piece, outs[5].at[p.z], p.q == p.z))
-        return plan.done()
-
-    group_count = 4 if G == 4 else G - 1
-    arrays = [in_rows.reshape(T * cs, FL), out_weight, qkv_cut, map_rows.reshape(T * mp, HW)]
-    arrays.append(mod_part)
-    results = [
-        ((G, T * cs, FL), BF16),
-        ((G,) + out_weight.shape, BF16),
-        ((T, cs, 3 * HW), BF16),
-        ((G, T * mp, HW), BF16),
-        ((G,) + mod_part.shape, F32),
-    ]
-    if even:
-        arrays.append(proj_weight)
-        results.append(((R, cs, C // G), BF16))
-    gathered = team_kernel(
-        1,
-        "exchange_normed",
-        plan_first,
-        arrays,
-        results,
-        gathers=[normed],
-        messages=2 * group_count + (T - 1) + 2 * (G - 1) + (G if even else 0),
-        local=5 + (1 if even else 0),
-        late=(4, 1, G - 1),
-    )
-    in_full, out_full, qkv_rows, map_full = gathered[:4]
-    proj_part = gathered[5].reshape(HW, C // G) if even else None
-    mod_all, normed_all = gathered[-2:]
+    outs = front_kernel(
+        m,
+        time_weight,
+        time_bias[None],
+        masked,
+        small,
+        fvec,
+        in_cut,
+        out_weight,
+        map_cut,
+        qkv_cut,
+        clip_pad,
+        proj_weight,
+    )
+    norms, total, silu, mapped_s, normed_all, in_full, active, slope = outs[:8]
+    norm_hat, norm_inv, vec, fv, key_keep, keep, bias, embed, edges, _ = outs[8:18]
+    out_full, qkv_rows, _, mod_all = outs[18:22]
+    proj_part = outs[22].reshape(HW, C // G) if even else None
     normed_all = normed_all.reshape(D * pixels, C)
     in_full = in_full.reshape(C, FL)
     out_full = out_full.reshape(FL, C)
-    active, slope, norms, total, silu, mapped_s = up_kernel(
-        m,
-        normed_all,
-        in_full,
-        in_bias_s,
-        key_keep,
-        clip_all.reshape(T, sp, -1),
-        map_full,
-        vec,
-    )
     outs = branch_kernel(
         m,
         active,
         norms,
         total,
         out_full,
-        gain_s,
-        grn_bias_s,
+        fv,
         latents,
         keep,
         vec,
         mod_all,
         qkv_rows.reshape(T * cs, 3 * HW),
         mapped_s,
-        grad_result,
         proj_part,
     )
-    grn_out, after_res, two_hat, two_inv, _, ratio, means, mods, two_all, mapped, gres_all = outs[:11]
-    qkv_full = outs[11].reshape(C, 3 * HW)
+    grn_out, after_res, two_hat, two_inv, _, ratio, means, mods, two_all, mapped = outs[:10]
+    qkv_full = outs[10].reshape(C, 3 * HW)
     if even:
-        proj_s = outs[12]
+        proj_s = outs[11]
     else:
         proj_whole = lax.all_gather(proj_weight, AXES, axis=0, tiled=True)
         proj_s = lax.dynamic_slice_in_dim(proj_whole, head_slice * HW, HW, axis=0)[None]
-    q_bias = lax.dynamic_slice_in_dim(vec[13], head_slice * HW, HW)
-    v_bias = lax.dynamic_slice_in_dim(vec[14], head_slice * HW, HW)
-    bias = jnp.concatenate([q_bias, jnp.zeros_like(q_bias), v_bias])[None]
-    result_part, two_part, mapped_part, grad_qkv, grad_proj, qkv_bias_grad = attention_kernel(
+    result, two_part, mapped_part, grad_qkv, grad_proj, qkv_bias_grad = attention_kernel(
         m,
         two_all.reshape(D, pixels, C),
-        gres_all.reshape(D, pixels, C),
-        mapped.reshape(T, D * texts, HW),
+        grad_result,
+        mapped.reshape(T, D, texts, HW),
         qkv_full,
         proj_s,
         bias,
@@ -1735,7 +2066,7 @@
         m,
         two_part.reshape(D, R, N, C),
         mapped_part.reshape(D, R, D * texts, HW),
-        result_part.reshape(D, R, N, C),
+        result,
         cotangent,
         grad_result,
         two_hat,
@@ -1770,20 +2101,15 @@
         norms,
         ratio,
         means,
-        gain_s,
+        fv,
         key_keep,
-        norm_hat,
-        norm_inv,
         qkv_parts,
         proj_parts,
         grad_map,
     )
-    grad_conv_in, out_sum, in_sum, f_sum, map_sum, qkv_team = outs[:6]
+    grad_conv_in, grad_out, in_parts, f_sum, map_parts, qkv_team = outs[:6]
     if even:
         proj_team = outs[6]
-    grad_out_shard = jnp.sum(out_sum.astype(F32), axis=0)
-    in_back = jnp.sum(in_sum.astype(F32), axis=0).astype(BF16).reshape(T, cs, FL)
-    map_back = jnp.sum(map_sum.astype(F32), axis=0).astype(BF16).reshape(T, mp, HW)
 
     def placed(values, start):
         return lax.dynamic_update_slice_in_dim(jnp.zeros((C,), F32), values, start, axis=0)
@@ -1809,53 +2135,22 @@
         qv_grads,
         grad_modulate,
     )
+    conv_edges, tiny_all, in_team, map_team, out_parts = tail_kernel(
+        m, conv_low, tiny, grad_out, in_parts, map_parts
+    )
     trows = 16
-
-    def plan_fifth(p, ins, outs):
-        plan = Plan(p)
-        swap_edges(plan, ins[0], outs[0])
-        plan.team_swap(ins[1], outs[1])
-        plan.team_swap(ins[2], outs[2])
-        plan.team_swap(ins[3], outs[3])
-        return plan.done()
-
-    conv_edges, tiny_team, in_team, map_team = team_kernel(
-        11,
-        "exchange_tail",
-        plan_fifth,
-        [conv_low, tiny, in_back, map_back],
-        [((2, EDGE, C), BF16), (tiny.shape, F32), (in_back.shape, BF16), (map_back.shape, BF16)],
-        messages=2 + 3 * (T - 1),
-        local=3,
-    )
-    tiny_items = jnp.sum(tiny_team.reshape(D, R, G, trows, 128), axis=1).transpose(1, 0, 2, 3)
-
-    def plan_sixth(p, ins, outs):
-        plan = Plan(p)
-        plan.group_swap(ins[0], outs[0])
-        return group_greet(p), plan.messages, plan.local
-
-    (tiny_all,) = team_kernel(
-        12,
-        "exchange_tiny",
-        plan_sixth,
-        [tiny_items],
-        [((G, D, trows, 128), F32)],
-        messages=G - 1,
-    )
     tiny_all = tiny_all.reshape(G * D, trows, 128)
     tiny_sum = jnp.sum(tiny_all, axis=0)
     modulate_items = tiny_all[:, 14, : 2 * cs]
-    embed_all = small_all.reshape(D, R, G, SMALL, 128)[:, 0, :, 14, : time_embed.shape[1]]
-    embed_all = embed_all.transpose(1, 0, 2).reshape(G * D, -1)
+    embed_all = embed[: G * D, : time_embed.shape[1]]
     grad_time = lax.dot_general(
-        embed_all.astype(F32),
+        embed_all,
         modulate_items,
         (((0,), (0,)), ((), ())),
         precision=lax.Precision.HIGHEST,
     )
     grad_time_bias = jnp.sum(modulate_items, axis=0)
-    grad_latents, grad_in_shard, grad_qkv_shard, grad_map_shard, grad_proj_shard = finish_kernel(
+    outs = finish_kernel(
         m,
         bucket_ids,
         conv_edges,
@@ -1867,7 +2162,10 @@
         qkv_team,
         map_team,
         proj_team,
-    )
+        out_parts,
+    )
+    grad_latents, grad_in_shard, grad_qkv_shard, grad_map_shard, grad_proj_shard = outs[:5]
+    grad_out_shard = outs[5]
     f_total = jnp.sum(f_sum, axis=0)
     return (
         output[None],

time: 553 us -> 482 us (0.87); the launches traced: 545 us -> 482 us
  Pallas kernels: 517 us -> 470 us
  local copies, waits for them, and re-layouts: 13.6 us -> 5.01 us
  other arithmetic: 10.1 us -> 2.55 us
    pallas_call x8 -> x6, Pallas kernels: 483 us -> 448 us  [fused_kernel(): pl.pallas_call(kernel, out_shape=spots(near_out + far_out), in_specs=[pl....]
    pallas_call x6 -> x4, Pallas kernels: 34.7 us -> 22.1 us  [local_kernel(): pl.pallas_call(kernel, out_shape=spots(results), in_specs=[numbers] * sca...]
    reduce_sum x4 -> x0, other arithmetic: 5.78 us -> none  [the longest x1 2 us: body(): jnp.sum(map_sum.astype(F32), axis=0).astype(BF16).reshape(T, mp, HW)]
where the time goes in v4:
time: 482 us
  Pallas kernels  470 us (98%)
  local copies, waits for them, and re-layouts  5.01 us (1%)
    pallas_call x6, Pallas kernels, fused_kernel(): pl.pallas_call(kernel, out_shape=spots(near_out + far_out), in_specs=[pl....  448 us
    pallas_call x4, Pallas kernels, local_kernel(): pl.pallas_call(kernel, out_shape=spots(results), in_specs=[numbers] * sca...  22.1 us

profile of v4, /device:TPU:0, one launch (start us, length us, event | category | flops | bytes accessed | tf_op | source)
XLA Modules:
  0.0 481.6 jit_solution(4201332107769296261)
XLA Ops:
  2.6 3.2 cut_weights.1
  5.8 99.1 %front.1 = (f32[8,768]{1,0:T(8,128)}, f32[8,128]{1,0:T(8,128)}, bf16[160,1280]{1,0:T(8,128)(2,1)}, bf16[160,192]{1,0:T(8,128)(2,1)}, bf16[2,4,144,1536]{3,2,1,0:...) custom-call(bf16[64,96]{1,0:T(8,128)(2,1)} %refs_0_.3, ...), custom_call_target="tpu_custom_call" | custom-call | tf_op jit(solution)/shard_map/front/pallas_call | solution.py:943
  104.9 85.9 %branch.1 = (bf16[1152,768]{1,0:T(8,128)(2,1)}, f32[144,1536]{1,0:T(8,128)}, f32[144,1536]{1,0:T(8,128)}, f32[144,1]{1,0:T(8,128)}, bf16[144,1536]{1,0:T(8,128)(...) custom-call(f32[8,768]{1,0:T(8,128)} %get-tuple-element.101.refs_0_,, ...), custom_call_target="tpu_custom_call" | custom-call | tf_op jit(solution)/shard_map/branch/pallas_call | solution.py:943
  190.8 71.0 %attention_block.1 = (f32[144,1536]{1,0:T(8,128)}, bf16[2,576,1536]{2,1,0:T(8,128)(2,1)}, bf16[8,2,80,192]{3,2,1,0:T(8,128)(2,1)}, bf16[1536,576]{1,0:T(8,128)(2...) custom-call(f32[1,576]{1,0:T(1,128)} %get-tuple-element.114.refs_0_, ...), custom_call_target="tpu_custom_call" | custom-call | tf_op jit(solution)/shard_map/attention_block/pallas_call | solution.py:943
  261.8 0.7 fusion.2
  262.5 0.1 dynamic_update_slice.13
  262.6 0.2 dynamic_update_slice.14
  262.8 0.6 pad_maximum_fusion.1.qv_ref
  263.4 82.5 %attended.1 = (bf16[144,1536]{1,0:T(8,128)(2,1)}, f32[144,1536]{1,0:T(8,128)}, bf16[144,1536]{1,0:T(8,128)(2,1)}, f32[8,1536]{1,0:T(8,128)}, f32[8,1536]{1,0:T(8...) custom-call(f32[144,1]{1,0:T(8,128)} %get-tuple-element.112.refs_0_,, ...), custom_call_target="tpu_custom_call" | custom-call | tf_op jit(solution)/shard_map/attended/pallas_call | solution.py:943
  346.0 2.4 text_back.1
  348.3 0.8 dynamic_update_slice.12
  349.1 0.8 slice.42
  349.9 0.6 pad_maximum_fusion.vec_ref
  350.5 62.6 %feed_forward_back.1 = (f32[144,1536]{1,0:T(8,128)}, bf16[4,192,1536]{2,1,0:T(8,128)(2,1)}, bf16[4,384,768]{2,1,0:T(8,128)(2,1)}, f32[4,8,192]{2,1,0:T(8,128)}, ...) custom-call(f32[8,768]{1,0:T(8,128)} %get-tuple-element.101.refs_0_, ...), custom_call_target="tpu_custom_call" | custom-call | tf_op jit(solution)/shard_map/feed_forward_back/pallas_call | solution.py:943
  413.1 7.4 %convolve_back.1 = (f32[144,1536]{1,0:T(8,128)}, bf16[144,1536]{1,0:T(8,128)(2,1)}, f32[8,4,16,128]{3,2,1,0:T(8,128)}) custom-call(s32[1]{0:T(128)S(6)} %copy.48.b_ref, f32[144,1536]{1,0:T(8,128)} %get-tuple-element.143.g_ref, f32[144,1536]{1,0:T(8,128)} %get-tuple-element.144.hat_ref, f32[144,1]{1,0:T(8,128)} %get-tuple-element.145.inv_ref, ...), custom_call_target="tpu_custom_call" | custom-call | tf_op jit(solution)/shard_map/convolve_back/pallas_call | solution.py:630
  420.6 47.3 %tail.1 = (bf16[2,48,1536]{2,1,0:T(8,128)(2,1)}, f32[4,2,16,128]{3,2,1,0:T(8,128)}, bf16[8,48,768]{2,1,0:T(8,128)(2,1)}, bf16[8,48,192]{2,1,0:T(8,128)(2,1)}, bf16[4,192,1536]{2,1,0:T(8,128)(2,1)}) custom-call(bf16[4,384,768]{2,1,0:T(8,128)(2,1)} %get-tuple-element.141.refs_0_, bf16[4,384,192]{2,1,0:T(8,128)(2,1)} %get-tuple-element.142.refs_1_, ...), custom_call_target="tpu_custom_call" | custom-call | tf_op jit(solution)/shard_map/tail/pallas_call | solution.py:943
  467.9 1.3 slice_reduce_fusion
  469.1 0.8 fusion
  470.0 9.1 %finish.1 = (f32[1,144,1536]{2,1,0:T(8,128)}, f32[48,6144]{1,0:T(8,128)}, f32[48,4608]{1,0:T(8,128)}, f32[40,1536]{1,0:T(8,128)}, f32[48,1536]{1,0:T(8,128)}, /*index=5*/f32[192,1536]{1,0:T(8,128)}) custom-call(s32[1]{0:T(128)S(6)} %copy.48.b_ref, bf16[2,48,1536]{2,1,0:T(8,128)(2,1)} %get-tuple-element.154.edges_ref, ...), custom_call_target="tpu_custom_call" | custom-call | tf_op jit(solution)/shard_map/finish/pallas_call | solution.py:630
  479.2 0.0 copy-start.3
  479.2 0.5 slice_bitcast_fusion
  479.7 0.5 slice_bitcast_fusion.1
  480.2 0.6 fusion.3
  480.8 0.8 copy.51
  (14 shorter events, 0.0 us)
Async XLA Ops:
  420.6 48.6 %copy-start.4 = (f32[8,128]{1,0:T(8,128)S(1)}, f32[8,128]{1,0:T(8,128)}, u32[]{:S(2)}) copy-start(f32[8,128]{1,0:T(8,128)} %get-tuple-element.166) | copy-start | bytes 12292
  470.0 9.1 %copy-start.1 = (f32[4,2,16,128]{3,2,1,0:T(8,128)S(1)}, f32[4,2,16,128]{3,2,1,0:T(8,128)}, u32[]{:S(2)}) copy-start(f32[4,2,16,128]{3,2,1,0:T(8,128)} %get-tuple-element.162) | copy-start | bytes 196612
  470.0 10.2 %copy-start.2 = (f32[4,8,192]{2,1,0:T(8,128)S(1)}, f32[4,8,192]{2,1,0:T(8,128)}, u32[]{:S(2)}) copy-start(f32[4,8,192]{2,1,0:T(8,128)} %get-tuple-element.164) | copy-start | bytes 73732
  470.0 10.8 %copy-start = (bf16[144,1536]{1,0:T(8,128)(2,1)S(1)}, bf16[144,1536]{1,0:T(8,128)(2,1)}, u32[]{:S(2)}) copy-start(bf16[144,1536]{1,0:T(8,128)(2,1)} %get-tuple-element.128) | copy-start | bytes 1327108
  479.2 2.4 copy-start.3

commit v5 on v4

--- a/solution.py
+++ b/solution.py
@@ -273,6 +273,11 @@
         @pl.loop(0, count // step)
         def _(number):
             act(pl.ds(pl.multiple_of(number * step, step), step))
+
+    def offer(self, block):
+        copy = self.across(block)
+        copy.start()
+        self.flow.open.append((copy.wait_send, None))
 
     def early(self):
         for upward, block, ok in self.steps():
@@ -743,17 +748,9 @@
     extended[pl.ds(EDGE + m.N, EDGE)] = jnp.where(z < m.R - 1, edges_ref[1].astype(F32), 0.0)
 
 
-def width_of(bucket):
-    return jnp.where(bucket == 0, WIDTHS[0], jnp.where(bucket == 1, WIDTHS[1], WIDTHS[2]))
-
-
-def shifted_rows(ref, count, shift, lanes):
-    start = EDGE + shift
-    whole = start // 8
-    tall = count + 8
-    block = ref[pl.ds(pl.multiple_of(whole * 8, 8), tall), lanes]
-    extra = start - whole * 8
-    return pltpu.roll(block, jnp.where(extra == 0, 0, tall - extra), 0)[:count]
+def each_bucket(bucket, act):
+    for number, width in enumerate(WIDTHS):
+        pl.when(bucket == number)(functools.partial(act, width))
 
 
 def each_column_block(m, act):
@@ -766,24 +763,25 @@
     return [(index, index // 3 - 1, index % 3 - 1) for index in range(9)]
 
 
-def conv_back_kernel(m, b_ref, grad_in, hat, inv, edges, masked, vec_grads, qv_grads, modulate_grads):
-    def kernel(b_ref, g_ref, hat_ref, inv_ref, edges_ref, mid_ref, vec_ref, qv_ref, gm_ref, grad, low, tiny, extended, vec):
+def conv_back_kernel(m, b_ref, grad_in, hat, inv, edges, masked, vec_grads, map_grad, qv_grads, modulate_grads):
+    def kernel(b_ref, g_ref, hat_ref, inv_ref, edges_ref, mid_ref, vec_ref, map_ref, qv_ref, gm_ref, grad, low, tiny, extended, vec):
         values = layer_back(g_ref[...], hat_ref[...], inv_ref[...])
         grad[...] = values
         low[...] = values.astype(BF16)
         fill_extended(m, extended, edges_ref, mid_ref)
         vec[pl.ds(9, 1)] = jnp.sum(values, axis=0, keepdims=True)
-        vec[pl.ds(10, 3)] = vec_ref[pl.ds(0, 3)]
+        vec[pl.ds(10, 2)] = vec_ref[pl.ds(0, 2)]
+        vec[pl.ds(12, 1)] = map_ref[pl.ds(0, 1)]
         vec[pl.ds(13, 3)] = jnp.zeros((3, m.C), F32)
         z = lax.axis_index("rows")
 
         def taps(width):
-            _, col = rows_cols(z * m.N, m.N, width.astype(F32))
+            _, col = rows_cols(z * m.N, m.N, float(width))
 
             def block(lanes):
                 value = grad[:, lanes]
                 for index, dy, dx in tap_steps():
-                    piece = shifted_rows(extended, m.N, dy * width + dx, lanes)
+                    piece = extended[pl.ds(EDGE + dy * width + dx, m.N), lanes]
                     ok = (col + dx >= 0) & (col + dx < width)
                     vec[pl.ds(index, 1), lanes] = jnp.sum(
                         jnp.where(ok, piece, 0.0) * value, axis=0, keepdims=True
@@ -791,7 +789,7 @@
 
             each_column_block(m, block)
 
-        taps(width_of(b_ref[0]))
+        each_bucket(b_ref[0], taps)
         tiny[...] = jnp.zeros_like(tiny)
         half = m.S // 2
         pair = 2 * m.cs
@@ -805,34 +803,54 @@
     return local_kernel(
         "convolve_back",
         kernel,
-        [b_ref, grad_in, hat, inv, edges, masked, vec_grads, qv_grads, modulate_grads],
+        [b_ref, grad_in, hat, inv, edges, masked, vec_grads, map_grad, qv_grads, modulate_grads],
         [((m.N, m.C), F32), ((m.N, m.C), BF16), ((m.T, m.G, 16, 128), F32)],
         [pltpu.VMEM((m.N + 2 * EDGE, m.C), F32), pltpu.VMEM((VEC, m.C), F32)],
         scalars=1,
     )
 
 
-def finish_kernel(m, b_ref, edges, low, after, pix, vec, in_team, qkv_team, map_team, proj_team, out_parts):
-    def kernel(b_ref, edges_ref, low_ref, after_ref, pix_ref, vec_ref, in_ref, qkv_ref, map_ref, proj_ref, parts_ref,
-               lat_out, in_out, qkv_out, map_out, proj_out, out_out, extended):
+def finish_kernel(m, b_ref, edges, low, after, pix, vec, in_team, qkv_team, map_team, proj_team, out_parts, tiny_all, f_parts, embed, rdim):
+    def kernel(b_ref, edges_ref, low_ref, after_ref, pix_ref, vec_ref, in_ref, qkv_ref, map_ref, proj_ref, parts_ref, tiny_ref, f_ref, te_ref,
+               lat_out, in_out, qkv_out, map_out, proj_out, out_out, cw_out, time_out, *refs):
+        singles, (extended,) = refs[:10], refs[10:]
+        total = jnp.zeros(tiny_ref.shape[2:], F32)
+        times = jnp.zeros((128, 128), F32)
+        turned = te_ref[...].T
+        for g in range(m.G):
+            for d in range(m.D):
+                item = tiny_ref[g, d]
+                total = total + item
+                at = m.D * g + d
+                times = times + turned[:, at : at + 1] * item[14:15]
+        cw_out[...] = total[:9, : m.cs]
+        time_out[...] = times[:rdim, : 2 * m.cs]
+        for number, ref in enumerate(singles[:6]):
+            ref[...] = total[9 + number, : ref.shape[0]]
+        sums = f_ref[0]
+        for g in range(1, m.G):
+            sums = sums + f_ref[g]
+        for number, ref in enumerate(singles[6:9]):
+            ref[...] = sums[number, :]
+        singles[9][...] = total[15, :]
         fill_extended(m, extended, edges_ref, low_ref)
         z = lax.axis_index("rows")
         keep = pix_ref[...] > 0
 
         def taps(width):
-            _, col = rows_cols(z * m.N, m.N, width.astype(F32))
+            _, col = rows_cols(z * m.N, m.N, float(width))
 
             def block(lanes):
                 total = jnp.zeros((m.N, 128), F32)
                 for index, dy, dx in tap_steps():
-                    piece = shifted_rows(extended, m.N, -dy * width - dx, lanes)
+                    piece = extended[pl.ds(EDGE - dy * width - dx, m.N), lanes]
                     ok = (col - dx >= 0) & (col - dx < width)
                     total = total + jnp.where(ok, piece, 0.0) * vec_ref[pl.ds(index, 1), lanes]
                 lat_out[0, :, lanes] = after_ref[:, lanes] + jnp.where(keep, total, 0.0)
 
             each_column_block(m, block)
 
-        taps(width_of(b_ref[0]))
+        each_bucket(b_ref[0], taps)
         for g in range(m.G):
             for t in range(m.T):
                 start = m.FFS * (g * m.T + t)
@@ -857,7 +875,8 @@
     return local_kernel(
         "finish",
         kernel,
-        [b_ref, edges, low, after, pix, vec, in_team, qkv_team, map_team, proj_team, out_parts],
+        [b_ref, edges, low, after, pix, vec, in_team, qkv_team, map_team, proj_team, out_parts]
+        + [tiny_all, f_parts, embed],
         [
             ((1, m.N, m.C), F32),
             ((m.cs, m.FF), F32),
@@ -865,7 +884,13 @@
             ((m.ms, m.C), F32),
             ((m.cs, m.C), F32),
             ((m.FFS, m.C), F32),
-        ],
+            ((9, m.cs), F32),
+            ((rdim, 2 * m.cs), F32),
+        ]
+        + [((m.cs,), F32)] * 4
+        + [((2 * m.cs,), F32)] * 2
+        + [((m.FFS,), F32)] * 3
+        + [((128,), F32)],
         [pltpu.VMEM((m.N + 2 * EDGE, m.C), F32)],
         scalars=1,
     )
@@ -884,10 +909,14 @@
     return jnp.where(low, far, near)
 
 
-def chunks(count, act, step=16):
+STRIPES = 3
+AHEAD = 2
+
+
+def chunks(count, act, step=16, first=0):
     @pl.loop(0, count // step)
     def _(number):
-        act(pl.ds(pl.multiple_of(number * step, step), step))
+        act(pl.ds(pl.multiple_of(first + number * step, step), step))
 
 
 def each_rows(count, step, act):
@@ -973,6 +1002,61 @@
         return self.place
 
 
+class Stripes:
+    def __init__(self, flow, p, part, total, buffers, src, dst):
+        count = part.shape[2]
+        self.p, self.flow, self.src, self.dst = p, flow, src, dst
+        step = count // STRIPES
+        self.rows = [pl.ds(number * step, step) for number in range(STRIPES)]
+        mate, passed, landed = buffers
+        self.sums = [
+            LineReduce(
+                flow,
+                p,
+                part.at[:, :, rows],
+                total.at[rows],
+                mate.at[:, rows],
+                passed.at[:, :, rows],
+                landed.at[:, :, rows],
+            )
+            for rows in self.rows
+        ]
+        self.lines = [LineGather(flow, p, src.at[rows], dst.at[:, :, rows]) for rows in self.rows]
+
+    def run(self, act, before=None, between=None):
+        p = self.p
+        for item in self.sums:
+            for number in range(p.R):
+                item.offer(line_order(p, number))
+        for number, item in enumerate(self.sums[:AHEAD]):
+            item.early()
+            if before is not None and number == 0:
+                before()
+        size = self.rows[0].size
+        hops = [0] * STRIPES
+
+        def hop(number):
+            if hops[number] < p.R - 1:
+                hops[number] += 1
+                self.lines[number].hop(hops[number])
+
+        for number, item in enumerate(self.sums):
+            for step in item.later():
+                step()
+            item.close()
+            chunks(size, act, first=number * size)
+            self.lines[number].start()
+            rows = self.rows[number]
+            self.flow.keep(self.src.at[rows], self.dst.at[p.c, p.z, rows])
+            if number + AHEAD < STRIPES:
+                self.sums[number + AHEAD].early()
+            if between is not None:
+                between(number)
+        while min(hops) < p.R - 1:
+            for number in range(STRIPES):
+                hop(number)
+
+
 def gather_sems(m):
     return 4 * m.R - 3
 
@@ -1020,10 +1104,11 @@
 
     def act(p, flow, near, loads, far, near_out, far_out, scratch):
         tw_ref, tb_ref = near
-        norms, total, silu, mapped, x_all, in_all, active, slope = near_out[:8]
-        hat, inv, vec, fv, keep, pix, qkv_bias, embed, edges, normed = near_out[8:]
-        out_all, qkv_rows, mod_all, mod_line = far_out[:4]
-        map_all, clip_all, squares, weight, text, small_all, f_all, extended, conv, te, mod = scratch
+        norms, total, silu, mapped = near_out[:4]
+        hat, inv, vec, fv, keep, pix, qkv_bias, embed, edges, normed = near_out[4:]
+        x_out, in_out, active_out, slope_out, out_all, qkv_rows, mod_all, mod_line = far_out[:8]
+        map_all, clip_all, squares, weight, text, small_all, f_all, extended, conv, te, mod = scratch[:11]
+        x_all, in_all, active, slope = scratch[11:]
         mid, small_ref, fvec_ref, in_cut, out_own, map_cut, qkv_cut, clip = far[:8]
         mine = p.c * p.R + p.z
         own_in = in_all.at[p.q]
@@ -1063,18 +1148,6 @@
         ]
         clip_line = LineGather(flow, p, clip, clip_all)
         clip_line.start()
-        if m.even:
-            for number in range(G):
-                to = lax.rem(p.z + number, G)
-                piece = far[8].at[:, pl.ds(pl.multiple_of(to * wide, 128), wide)]
-                flow.post(
-                    piece,
-                    far_out[4].at[p.z],
-                    {"grp": to, "duo": p.c, "rows": p.q},
-                    when=None if number else p.q != p.z,
-                )
-            piece = far[8].at[:, pl.ds(pl.multiple_of(p.z * wide, 128), wide)]
-            flow.keep(piece, far_out[4].at[p.z], p.q == p.z)
         flow.keep(in_cut.at[mine], own_in.at[mine], now=True)
         flow.keep(map_cut.at[mine], own_map.at[mine], now=True)
         flow.keep(clip, clip_all.at[p.c, p.z], now=True)
@@ -1152,14 +1225,34 @@
                 qkv_bias[:, : m.HW] = vec[pl.ds(13, 1), at]
                 qkv_bias[:, 2 * m.HW :] = vec[pl.ds(14, 1), at]
 
+        for item in map_team:
+            flow.land(item)
+        map_posts = [flow.post(own_map, map_all.at[p.q], {"grp": q}) for q in p.groups()]
+        for step in range(1, m.R):
+            clip_line.hop(step)
         line.hop(1)
         if square:
             out_relay()
+        clip_line.settle(m.R)
+        for item in map_posts:
+            flow.land(item)
+        for d in range(m.D):
+            for r in range(m.R):
+                piece = clip_all[d, r].astype(F32)[: m.slots]
+                text[pl.ds((d * m.R + r) * m.slots, m.slots)] = piece / (1.0 + jnp.exp(-piece))
+        silu[...] = text[...].astype(BF16)
+        for g in range(G):
+            for t in range(T):
+                piece = map_all[g, t].astype(F32)
+                weight[pl.ds(m.ms * (g * T + t), m.ms)] = piece[: m.ms]
+        product = mm(silu[...], weight[...].astype(BF16))
+        for t in range(T):
+
+            @pl.when(mine == t)
+            def _():
+                mapped[...] = (product + vec[pl.ds(11, 1), pl.ds(t * m.HW, m.HW)]).astype(BF16)
+
         line.hop(2)
-        for item in map_team:
-            flow.land(item)
-        map_posts = [flow.post(own_map, map_all.at[p.q], {"grp": q}) for q in p.groups()]
-        flow.swap_team(p, qkv_cut, qkv_rows)
         if square:
             in_posts = in_relay()
         for item in mod_posts:
@@ -1168,9 +1261,23 @@
         mods = LineGather(flow, p, mod_all, mod_line)
         mods.start()
         flow.keep(mod_all, mod_line.at[p.c, p.z])
+        flow.swap_team(p, qkv_cut, qkv_rows)
+        if m.even:
+            for number in range(G):
+                to = lax.rem(p.z + number, G)
+                piece = far[8].at[:, pl.ds(pl.multiple_of(to * wide, 128), wide)]
+                flow.post(
+                    piece,
+                    far_out[8].at[p.z],
+                    {"grp": to, "duo": p.c, "rows": p.q},
+                    when=None if number else p.q != p.z,
+                )
+            piece = far[8].at[:, pl.ds(pl.multiple_of(p.z * wide, 128), wide)]
+            flow.keep(piece, far_out[8].at[p.z], p.q == p.z)
         squares[...] = jnp.zeros_like(squares)
         for item in in_posts:
             flow.land(item)
+        flow.keep(in_all, in_out)
 
         def multiply(first, count):
             line.settle(first + count)
@@ -1196,43 +1303,23 @@
 
         first = m.R // 2
         multiply(0, first)
-        line.hop(3)
-        for step in range(4, m.R):
+        for step in range(3, m.R):
             line.hop(step)
+        mods.hop(1)
         multiply(first, m.R - first)
+        flow.keep(x_all, x_out)
+        flow.keep(active, active_out)
+        flow.keep(slope, slope_out)
         norms[...] = jnp.sqrt(squares[...])
         total[...] = jnp.broadcast_to(jnp.sum(norms[...], axis=1, keepdims=True), total.shape)
-        for step in range(1, m.R):
-            clip_line.hop(step)
+        for step in range(2, m.R):
             mods.hop(step)
-        clip_line.settle(m.R)
-        for item in map_posts:
-            flow.land(item)
-        for d in range(m.D):
-            for r in range(m.R):
-                piece = clip_all[d, r].astype(F32)[: m.slots]
-                text[pl.ds((d * m.R + r) * m.slots, m.slots)] = piece / (1.0 + jnp.exp(-piece))
-        silu[...] = text[...].astype(BF16)
-        for g in range(G):
-            for t in range(T):
-                piece = map_all[g, t].astype(F32)
-                weight[pl.ds(m.ms * (g * T + t), m.ms)] = piece[: m.ms]
-        product = mm(silu[...], weight[...].astype(BF16))
-        for t in range(T):
-
-            @pl.when(mine == t)
-            def _():
-                mapped[...] = (product + vec[pl.ds(11, 1), pl.ds(t * m.HW, m.HW)]).astype(BF16)
 
     near_out = [
         ((8, FL), F32),
         ((8, 128), F32),
         ((texts, cond), BF16),
         ((texts, m.HW), BF16),
-        ((m.D, m.R, N, C), BF16),
-        ((G, T, m.cs, FL), BF16),
-        ((m.D * m.pixels, FL), F32),
-        ((m.D * m.pixels, FL), F32),
         ((N, C), F32),
         ((N, 1), F32),
         ((VEC, C), F32),
@@ -1245,6 +1332,10 @@
         ((N, C), BF16),
     ]
     far_out = [
+        ((m.D, m.R, N, C), BF16),
+        ((G, T, m.cs, FL), BF16),
+        ((m.D * m.pixels, FL), F32),
+        ((m.D * m.pixels, FL), F32),
         ((G,) + out_weight.shape, BF16),
         (qkv_cut.shape, BF16),
         ((G, mod_rows, 128), F32),
@@ -1264,6 +1355,10 @@
         pltpu.VMEM((N, C), F32),
         pltpu.VMEM((items, time_weight.shape[0]), BF16),
         pltpu.VMEM((mod_rows, 128), F32),
+        pltpu.VMEM((m.D, m.R, N, C), BF16),
+        pltpu.VMEM((G, T, m.cs, FL), BF16),
+        pltpu.VMEM((m.D * m.pixels, FL), F32),
+        pltpu.VMEM((m.D * m.pixels, FL), F32),
     ]
     columns = 4 if square else G - 1
     return fused_kernel(
@@ -1278,7 +1373,7 @@
         far_out,
         scratch,
         4 * (T - 1) + 2 + 2 * columns + 4 * (G - 1) + (G if m.even else 0) + 3 * gather_sems(m),
-        12,
+        16,
     )
 
 
@@ -1325,7 +1420,6 @@
         if m.even:
             flow.gather_group(p, far[2], far_out[3])
         text_line = LineGather(flow, p, far[1], mapped_all)
-        two_line = LineGather(flow, p, two, two_all)
         half = m.S // 2
         pair = 2 * m.cs
         for s, (g, d, r) in enumerate(m.places):
@@ -1335,19 +1429,14 @@
         means[...] = mean
         ratio[...] = norms[...] / mean[:, :1]
         slopes[...] = gain * ratio[...] + 1.0
-        line = LineReduce(flow, p, part, branch, mate, passed, landed)
         active, out_w, lat, vec = (load.get() for load in loads)
 
-        def produce(block):
-            @pl.loop(0, m.D)
-            def _(d):
-                rows = pl.ds(pl.multiple_of(d * m.pixels + block * N, 16), N)
-                low = (active[rows] * slopes[pl.ds(d, 1)] + grn_bias).astype(BF16)
-                grn[rows] = low
-                part[d, block] = mm(low, out_w[...]).astype(BF16)
-
-        line.run(produce)
-        text_line.start()
+        @pl.loop(0, m.D)
+        def _(d):
+            rows = pl.ds(pl.multiple_of(d * m.pixels, 16), m.pixels)
+            low = (active[rows] * slopes[pl.ds(d, 1)] + grn_bias).astype(BF16)
+            grn[rows] = low
+            part[d] = mm(low, out_w[...]).astype(BF16).reshape(m.R, N, C)
 
         def tail(rows):
             value = lat[rows].astype(F32) + keep[rows] * (branch[rows] + vec[pl.ds(10, 1)])
@@ -1358,13 +1447,12 @@
             inv[rows] = inverse
             two[rows] = normal.astype(BF16)
 
-        chunks(N, tail)
-        two_line.start()
+        stripes = Stripes(flow, p, part, branch, (mate, passed, landed), two, two_all)
+        text_line.start()
         flow.keep(far[1], mapped_all.at[p.c, p.z])
-        flow.keep(two, two_all.at[p.c, p.z])
-        for step in range(1, m.R):
+        stripes.run(tail, None, lambda number: text_line.hop(number + 1))
+        for step in range(STRIPES + 1, m.R):
             text_line.hop(step)
-            two_line.hop(step)
 
     near_out = [
         ((rows_all, m.FL), BF16),
@@ -1399,8 +1487,8 @@
         near_out,
         far_out,
         scratch,
-        (m.T - 1) + 2 * (m.G - 1) + 2 * gather_sems(m) + reduce_sems(m),
-        5,
+        (m.T - 1) + 2 * (m.G - 1) + (1 + STRIPES) * gather_sems(m) + STRIPES * reduce_sems(m),
+        4 + STRIPES,
     )
 
 
@@ -1417,9 +1505,10 @@
 
     def act(p, flow, near, loads, far, near_out, far_out, scratch):
         bias, keep = near
-        result, two_out, map_out, gw_out, gp_out, gb_out = near_out
+        result, map_out, gw_out, gp_out, qv_out = near_out
+        (two_far,) = far_out
         (gres_all, part, mate, passed, landed, qkv, k_all, v_all, k_t, v_t, dk, dv, o_t, dq_t, o_low, att, g_all, probs, dqkv,
-         dtext, piece, words) = scratch
+         dtext, piece, words, gb_out, two_out) = scratch
         line = LineGather(flow, p, far[0], gres_all)
         line.start()
         flow.keep(far[0], gres_all.at[p.c, p.z], now=True)
@@ -1544,6 +1633,15 @@
                 rows = pl.ds(pl.multiple_of(t * HW, 16), HW)
                 map_out[t, d] = mm_t(dtext[d], w[rows]).astype(BF16)
 
+        flow.keep(two_out, two_far)
+        qv_out[...] = jnp.zeros_like(qv_out)
+        for h in range(m.T):
+
+            @pl.when(D * p.z + p.c == h)
+            def _():
+                qv_out[pl.ds(0, 1), pl.ds(h * HW, HW)] = gb_out[pl.ds(0, 1), pl.ds(0, HW)]
+                qv_out[pl.ds(1, 1), pl.ds(h * HW, HW)] = gb_out[pl.ds(0, 1), pl.ds(2 * HW, HW)]
+
         @pl.loop(0, C // block_rows)
         def _(g):
             lanes = pl.ds(pl.multiple_of(g * block_rows, 128), block_rows)
@@ -1567,11 +1665,10 @@
 
     near_out = [
         ((N, C), F32),
-        ((D, pixels, C), BF16),
         ((m.T, D, texts, HW), BF16),
         ((C, 3 * HW), BF16),
         ((m.Q, HW, wide), BF16),
-        ((8, 3 * HW), F32),
+        ((8, C), F32),
     ]
     scratch = [pltpu.VMEM((D, R, N, C), BF16)] + reduce_buffers(m, N, C)
     scratch += [
@@ -1592,6 +1689,8 @@
         pltpu.VMEM((D, texts, 3 * HW), BF16),
         pltpu.VMEM((block_rows, 3 * HW), F32),
         pltpu.VMEM((texts, 3 * HW), F32),
+        pltpu.VMEM((8, 3 * HW), F32),
+        pltpu.VMEM((D, pixels, C), BF16),
     ]
     return fused_kernel(
         4,
@@ -1602,10 +1701,10 @@
         loads,
         far,
         near_out,
-        [],
+        [((D, pixels, C), BF16)],
         scratch,
         gather_sems(m) + reduce_sems(m),
-        1,
+        2,
     )
 
 
@@ -1622,14 +1721,11 @@
         output, grad_after, branch, gm, vecg, text = near_out
         gb_all = far_out[0]
         two_sum, text_sum = scratch[:2]
-        two_red = LineReduce(flow, p, two_part, two_sum, *scratch[2:5])
         text_red = LineReduce(flow, p, text_part, text_sum, *scratch[5:8])
-        line = LineGather(flow, p, branch, gb_all)
-        two_red.start()
+        stripes = Stripes(flow, p, two_part, two_sum, scratch[2:5], branch, gb_all)
         flow.swap_group(p, far[0], far_out[1])
         if m.even:
             flow.swap_group(p, far[1], far_out[2])
-        two_red.steps_all()
         gm[...] = jnp.zeros_like(gm)
         vecg[...] = jnp.zeros_like(vecg)
 
@@ -1644,11 +1740,19 @@
             vecg[pl.ds(0, 1)] += jnp.sum(low.astype(F32), axis=0, keepdims=True)
             vecg[pl.ds(1, 1)] += jnp.sum(gres[rows].astype(F32), axis=0, keepdims=True)
 
-        chunks(N, back)
-        line.start()
-        flow.keep(branch, gb_all.at[p.c, p.z])
         text_red.start()
-        line.hop(1)
+        steps = list(text_red.later())
+
+        def between(number):
+            if number == 0:
+                steps[0]()
+            elif number == 1:
+                for step in steps[1:]:
+                    step()
+                text_red.close()
+                text[...] = text_sum[...].astype(BF16)
+
+        stripes.run(back, text_red.early, between)
 
         def out(rows):
             second = after[rows] * (1.0 + mods[pl.ds(0, 1)]) + mods[pl.ds(1, 1)]
@@ -1656,10 +1760,6 @@
             output[rows] = (second + value).astype(BF16)
 
         chunks(N, out)
-        for step in range(2, m.R):
-            line.hop(step)
-        text_red.steps_all()
-        text[...] = text_sum[...].astype(BF16)
 
     near_out = [
         ((N, C), BF16),
@@ -1688,8 +1788,8 @@
         near_out,
         far_out,
         scratch,
-        2 * (m.G - 1) + gather_sems(m) + 2 * reduce_sems(m),
-        4,
+        2 * (m.G - 1) + STRIPES * gather_sems(m) + (1 + STRIPES) * reduce_sems(m),
+        3 + STRIPES,
     )
 
 
@@ -1701,13 +1801,19 @@
             for t in range(m.T):
                 at = m.ms * (g * m.T + t)
                 out[g, pl.ds(t * m.mp, m.ms)] = weight[pl.ds(at, m.ms)].astype(BF16)
-        bias[...] = jnp.sum(g_ref[...].astype(F32), axis=0, keepdims=True)
+        total = jnp.sum(g_ref[...].astype(F32), axis=0, keepdims=True)
+        bias[...] = jnp.zeros_like(bias)
+        for t in range(m.T):
+
+            @pl.when(lax.axis_index("duo") * m.R + lax.axis_index("rows") == t)
+            def _():
+                bias[pl.ds(0, 1), pl.ds(t * m.HW, m.HW)] = total
 
     return local_kernel(
         "text_back",
         kernel,
         [silu, grad_mapped],
-        [((m.G, m.T * m.mp, m.HW), BF16), ((1, m.HW), F32)],
+        [((m.G, m.T * m.mp, m.HW), BF16), ((8, m.C), F32)],
         [pltpu.VMEM((silu.shape[1], m.HW), F32)],
     )
 
@@ -1726,10 +1832,12 @@
     def act(p, flow, near, loads, far, near_out, far_out, scratch):
         norms, ratio, means, fv, keep = near
         gain = fv[pl.ds(1, 1)]
-        back, g_out = near_out
+        (back,) = near_out
         in_parts, f_parts, map_parts, qkv_team = far_out[:4]
+        g_far = far_out[-1]
         everyone, mine, moments, slopes, shifts, grads, hidden, part, mate, passed, landed = scratch[:11]
         turned_g, turned_x, g_in, f_own, qkv_own = scratch[11:16]
+        g_out = scratch[-1]
         flow.swap_group(p, far[0], map_parts)
         gb, out_w, active, grn = (load.get() for load in loads[:4])
         moments[...] = jnp.zeros_like(moments)
@@ -1753,6 +1861,7 @@
             g_out[g] = mm(turned_g[rows], gb[...]).astype(BF16)
 
         each_rows(G, m.FFS, multiply_out)
+        flow.keep(g_out, g_far)
 
         slope, x, in_w, qkv_parts = (load.get() for load in loads[4:8])
         step = m.cs
@@ -1808,12 +1917,14 @@
         flow.swap_group(p, f_own, f_parts)
         line = LineReduce(flow, p, part, back, mate, passed, landed)
 
-        def produce(block):
-            @pl.loop(0, m.D)
-            def _(d):
-                rows = pl.ds(pl.multiple_of(d * m.pixels + block * N, 16), N)
-                part[d, block] = mm_t(hidden[rows], in_w[...]).astype(BF16)
-
+        @pl.loop(0, m.D)
+        def _(d):
+            rows = pl.ds(pl.multiple_of(d * m.pixels, 16), m.pixels)
+            part[d] = mm_t(hidden[rows], in_w[...]).astype(BF16).reshape(m.R, N, C)
+
+        for number in range(m.R):
+            line.offer(line_order(p, number))
+        line.early()
         turned_x[...] = x[...].T
         first = flow.take(G - 1)
 
@@ -1821,25 +1932,22 @@
             g = lax.rem(p.q + 1 + number, G)
             return flow.copy(g_in.at[g], in_parts.at[p.q], {"grp": g}, first + number)
 
-        def between(number):
-            if number != 1:
-                return
-
-            @pl.loop(0, G)
-            def _(number):
-                g = lax.rem(p.q + 1 + number, G)
-                rows = pl.ds(pl.multiple_of(g * rows_in, 16), rows_in)
-                g_in[g] = mm(turned_x[rows], hidden[...]).astype(BF16)
-                pl.when(number < G - 1)(lambda: send_in(number).start())
-
-            flow.keep(g_in.at[p.q], in_parts.at[p.q])
-
-        line.run(produce, between)
+        @pl.loop(0, G)
+        def _(number):
+            g = lax.rem(p.q + 1 + number, G)
+            rows = pl.ds(pl.multiple_of(g * rows_in, 16), rows_in)
+            g_in[g] = mm(turned_x[rows], hidden[...]).astype(BF16)
+            pl.when(number < G - 1)(lambda: send_in(number).start())
+
+        flow.keep(g_in.at[p.q], in_parts.at[p.q])
+        for act_of in line.later():
+            act_of()
+        line.close()
         for number in range(G - 1):
             send_in(number).wait_recv()
             send_in(number).wait_send()
 
-    near_out = [((N, C), F32), ((G, m.FFS, C), BF16)]
+    near_out = [((N, C), F32)]
     far_out = [
         ((G, rows_in, FL), BF16),
         ((G, 8, m.FFS), F32),
@@ -1866,6 +1974,8 @@
     if m.even:
         far_out.append(((G, m.cs, wide), BF16))
         scratch.append(pltpu.VMEM((m.R, m.cs, wide), BF16))
+    far_out.append(((G, m.FFS, C), BF16))
+    scratch.append(pltpu.VMEM((G, m.FFS, C), BF16))
     return fused_kernel(
         9,
         "feed_forward_back",
@@ -2023,9 +2133,9 @@
         clip_pad,
         proj_weight,
     )
-    norms, total, silu, mapped_s, normed_all, in_full, active, slope = outs[:8]
-    norm_hat, norm_inv, vec, fv, key_keep, keep, bias, embed, edges, _ = outs[8:18]
-    out_full, qkv_rows, _, mod_all = outs[18:22]
+    norms, total, silu, mapped_s = outs[:4]
+    norm_hat, norm_inv, vec, fv, key_keep, keep, bias, embed, edges, _ = outs[4:14]
+    normed_all, in_full, active, slope, out_full, qkv_rows, _, mod_all = outs[14:22]
     proj_part = outs[22].reshape(HW, C // G) if even else None
     normed_all = normed_all.reshape(D * pixels, C)
     in_full = in_full.reshape(C, FL)
@@ -2052,7 +2162,7 @@
     else:
         proj_whole = lax.all_gather(proj_weight, AXES, axis=0, tiled=True)
         proj_s = lax.dynamic_slice_in_dim(proj_whole, head_slice * HW, HW, axis=0)[None]
-    result, two_part, mapped_part, grad_qkv, grad_proj, qkv_bias_grad = attention_kernel(
+    result, mapped_part, grad_qkv, grad_proj, qv_grads, two_part = attention_kernel(
         m,
         two_all.reshape(D, pixels, C),
         grad_result,
@@ -2107,22 +2217,11 @@
         proj_parts,
         grad_map,
     )
-    grad_conv_in, grad_out, in_parts, f_sum, map_parts, qkv_team = outs[:6]
+    grad_conv_in, in_parts, f_sum, map_parts, qkv_team = outs[:5]
+    grad_out = outs[-1]
     if even:
-        proj_team = outs[6]
-
-    def placed(values, start):
-        return lax.dynamic_update_slice_in_dim(jnp.zeros((C,), F32), values, start, axis=0)
-
-    vec_grads = jnp.concatenate(
-        [vec_sums[:2], placed(map_bias_grad[0], (c * R + z) * HW)[None]], axis=0
-    )
-    qv_grads = jnp.stack(
-        [
-            placed(qkv_bias_grad[0, :HW], head_slice * HW),
-            placed(qkv_bias_grad[0, 2 * HW :], head_slice * HW),
-        ]
-    )
+        proj_team = outs[5]
+
     grad_conv, conv_low, tiny = conv_back_kernel(
         m,
         bucket_ids,
@@ -2131,25 +2230,14 @@
         norm_inv,
         edges,
         masked,
-        vec_grads,
+        vec_sums,
+        map_bias_grad,
         qv_grads,
         grad_modulate,
     )
     conv_edges, tiny_all, in_team, map_team, out_parts = tail_kernel(
         m, conv_low, tiny, grad_out, in_parts, map_parts
     )
-    trows = 16
-    tiny_all = tiny_all.reshape(G * D, trows, 128)
-    tiny_sum = jnp.sum(tiny_all, axis=0)
-    modulate_items = tiny_all[:, 14, : 2 * cs]
-    embed_all = embed[: G * D, : time_embed.shape[1]]
-    grad_time = lax.dot_general(
-        embed_all,
-        modulate_items,
-        (((0,), (0,)), ((), ())),
-        precision=lax.Precision.HIGHEST,
-    )
-    grad_time_bias = jnp.sum(modulate_items, axis=0)
     outs = finish_kernel(
         m,
         bucket_ids,
@@ -2163,29 +2251,33 @@
         map_team,
         proj_team,
         out_parts,
+        tiny_all,
+        f_sum,
+        embed,
+        time_embed.shape[1],
     )
     grad_latents, grad_in_shard, grad_qkv_shard, grad_map_shard, grad_proj_shard = outs[:5]
-    grad_out_shard = outs[5]
-    f_total = jnp.sum(f_sum, axis=0)
+    grad_out_shard, grad_kernel, grad_time = outs[5:8]
+    conv_b, out_b, proj_b, map_b, qv_b, time_b, in_b, gain_g, grn_b = outs[8:17]
     return (
         output[None],
         grad_latents,
-        tiny_sum[:9, :cs],
-        tiny_sum[9, :cs],
+        grad_kernel,
+        conv_b,
         grad_in_shard,
-        f_total[0],
-        f_total[1],
-        f_total[2],
+        in_b,
+        gain_g,
+        grn_b,
         grad_out_shard,
-        tiny_sum[10, :cs],
+        out_b,
         grad_time,
-        grad_time_bias,
+        time_b,
         grad_map_shard,
-        tiny_sum[12, :cs],
+        map_b,
         grad_qkv_shard,
-        tiny_sum[13, : 2 * cs],
+        qv_b,
         grad_proj_shard,
-        tiny_sum[11, :cs],
+        proj_b,
     )
 
 

time: 482 us -> 440 us (0.913)
  Pallas kernels: 470 us -> 435 us
    pallas_call x6, Pallas kernels: 448 us -> 417 us  [fused_kernel(): pl.pallas_call(kernel, out_shape=spots(near_out + far_out), in_specs=[pl....]
where the time goes in v5:
time: 440 us; the launch traced here: 439 us
  Pallas kernels  435 us (99%)
    pallas_call x6, Pallas kernels, fused_kernel(): pl.pallas_call(kernel, out_shape=spots(near_out + far_out), in_specs=[pl....  417 us
    pallas_call x4, Pallas kernels, local_kernel(): pl.pallas_call(kernel, out_shape=spots(results), in_specs=[numbers] * sca...  18.6 us

profile of v5, /device:TPU:0, one launch (start us, length us, event | category | flops | bytes accessed | tf_op | source)
XLA Modules:
  0.0 438.9 jit_solution(17101199175503698286)
XLA Ops:
  2.6 3.2 cut_weights.1
  5.8 88.4 %front.1 = (f32[8,768]{1,0:T(8,128)}, f32[8,128]{1,0:T(8,128)}, bf16[160,1280]{1,0:T(8,128)(2,1)}, bf16[160,192]{1,0:T(8,128)(2,1)}, f32[144,1536]{1,0:T(8,128)}...) custom-call(bf16[64,96]{1,0:T(8,128)(2,1)} %refs_0_.3, ...), custom_call_target="tpu_custom_call" | custom-call | tf_op jit(solution)/shard_map/front/pallas_call | solution.py:972
  94.2 81.6 %branch.1 = (bf16[1152,768]{1,0:T(8,128)(2,1)}, f32[144,1536]{1,0:T(8,128)}, f32[144,1536]{1,0:T(8,128)}, f32[144,1]{1,0:T(8,128)}, bf16[144,1536]{1,0:T(8,128)(...) custom-call(f32[8,768]{1,0:T(8,128)} %get-tuple-element.112.refs_0_,, ...), custom_call_target="tpu_custom_call" | custom-call | tf_op jit(solution)/shard_map/branch/pallas_call | solution.py:972
  175.8 70.1 %attention_block.1 = (f32[144,1536]{1,0:T(8,128)}, bf16[8,2,80,192]{3,2,1,0:T(8,128)(2,1)}, bf16[1536,576]{1,0:T(8,128)(2,1)}, bf16[4,192,384]{2,1,0:T(8,128)(2,...) custom-call(f32[1,576]{1,0:T(1,128)} %get-tuple-element.125.refs_0_, ...), custom_call_target="tpu_custom_call" | custom-call | tf_op jit(solution)/shard_map/attention_block/pallas_call | solution.py:972
  245.9 81.2 %attended.1 = (bf16[144,1536]{1,0:T(8,128)(2,1)}, f32[144,1536]{1,0:T(8,128)}, bf16[144,1536]{1,0:T(8,128)(2,1)}, f32[8,1536]{1,0:T(8,128)}, f32[8,1536]{1,0:T(8...) custom-call(f32[144,1]{1,0:T(8,128)} %get-tuple-element.123.refs_0_,, ...), custom_call_target="tpu_custom_call" | custom-call | tf_op jit(solution)/shard_map/attended/pallas_call | solution.py:972
  327.1 2.4 text_back.1
  329.5 66.1 %feed_forward_back.1 = (f32[144,1536]{1,0:T(8,128)}, bf16[4,384,768]{2,1,0:T(8,128)(2,1)}, f32[4,8,192]{2,1,0:T(8,128)}, bf16[4,384,192]{2,1,0:T(8,128)(2,1)}, b...) custom-call(f32[8,768]{1,0:T(8,128)} %get-tuple-element.112.refs_0_, ...), custom_call_target="tpu_custom_call" | custom-call | tf_op jit(solution)/shard_map/feed_forward_back/pallas_call | solution.py:972
  395.6 5.8 %convolve_back.1 = (f32[144,1536]{1,0:T(8,128)}, bf16[144,1536]{1,0:T(8,128)(2,1)}, f32[8,4,16,128]{3,2,1,0:T(8,128)}) custom-call(s32[1]{0:T(128)S(6)} %copy.43.b_ref, f32[144,1536]{1,0:T(8,128)} %get-tuple-element.154.g_ref, f32[144,1536]{1,0:T(8,128)} %get-tuple-element.155.hat_ref, f32[144,1]{1,0:T(8,128)} %get-tuple-element.156.inv_ref, ...), custom_call_target="tpu_custom_call" | custom-call | tf_op jit(solution)/shard_map/convolve_back/pallas_call | solution.py:635
  401.4 29.5 %tail.1 = (bf16[2,48,1536]{2,1,0:T(8,128)(2,1)}, f32[4,2,16,128]{3,2,1,0:T(8,128)}, bf16[8,48,768]{2,1,0:T(8,128)(2,1)}, bf16[8,48,192]{2,1,0:T(8,128)(2,1)}, bf16[4,192,1536]{2,1,0:T(8,128)(2,1)}) custom-call(bf16[4,384,768]{2,1,0:T(8,128)(2,1)} %get-tuple-element.152.refs_0_, bf16[4,384,192]{2,1,0:T(8,128)(2,1)} %get-tuple-element.153.refs_1_, ...), custom_call_target="tpu_custom_call" | custom-call | tf_op jit(solution)/shard_map/tail/pallas_call | solution.py:972
  430.9 0.0 copy-start
  431.0 7.2 %finish.1 = (f32[1,144,1536]{2,1,0:T(8,128)}, f32[48,6144]{1,0:T(8,128)}, f32[48,4608]{1,0:T(8,128)}, f32[40,1536]{1,0:T(8,128)}, f32[48,1536]{1,0:T(8,128)}, /*...) custom-call(s32[1]{0:T(128)S(6)} %copy.43.b_ref, ...), custom_call_target="tpu_custom_call" | custom-call | tf_op jit(solution)/shard_map/finish/pallas_call | solution.py:635
  438.1 0.0 copy-done
  438.2 0.8 copy.46
Async XLA Ops:
  430.9 7.2 %copy-start = (bf16[144,1536]{1,0:T(8,128)(2,1)S(1)}, bf16[144,1536]{1,0:T(8,128)(2,1)}, u32[]{:S(2)}) copy-start(bf16[144,1536]{1,0:T(8,128)(2,1)} %get-tuple-element.139) | copy-start | bytes 1327108

commit v6 on v5

--- a/solution.py
+++ b/solution.py
@@ -222,6 +222,33 @@
             number = jnp.where(block <= p.z, p.z - block, p.R - 1 + block - p.z)
             self.across(block, number).wait_recv()
             self.settled += 1
+
+
+class LineGatherOn(LineGather):
+    def start_from(self, near):
+        p, flow = self.p, self.flow
+        flow.lines.append(self)
+        self.settled = 0
+        flow.keep(near.at[0], self.dst.at[p.c, jnp.maximum(p.z - 1, 0)], p.z > 0)
+        flow.keep(near.at[1], self.dst.at[p.c, jnp.minimum(p.z + 1, p.R - 1)], p.z < p.R - 1)
+        flow.keep(self.src, self.dst.at[p.c, p.z])
+        flow.settle_kept()
+        copy = self.across(p.z, 0)
+        copy.start()
+        flow.open.append((copy.wait_send, None))
+        for direction, number in ((1, 1), (-1, p.R)):
+            block = p.z - direction
+            ok = (block >= 0) if direction > 0 else (block < p.R)
+            last = (p.z < p.R - 1) if direction > 0 else (p.z > 0)
+            side = self.across(block, number)
+
+            def relay(side=side, block=block, direction=direction, last=last):
+                pl.when(last)(self.send(block, 1, direction).start)
+                side.start()
+
+            pl.when(ok)(relay)
+            flow.open.append((self.send(block, 1, direction).wait_send, ok & last))
+            flow.open.append((side.wait_send, ok))
 
 
 class LineReduce:
@@ -1402,10 +1429,10 @@
     return total
 
 
-def branch_kernel(m, active, norms, total, out_full, fv, latents, keep, vec, mod_all, qkv_rows, mapped, proj_part):
+def branch_kernel(m, active, norms, total, out_full, fv, latents, keep, vec, mod_all, qkv_rows, mapped, gres, proj_part):
     near = [norms, total, fv, keep, mod_all]
     loads = [active, out_full, latents, vec]
-    far = [qkv_rows, mapped] + ([proj_part] if m.even else [])
+    far = [qkv_rows, mapped, gres] + ([proj_part] if m.even else [])
     N, C = m.N, m.C
     rows_all = m.D * m.pixels
 
@@ -1413,12 +1440,17 @@
         norms, total, fv, keep, mod_all = near
         gain, grn_bias = fv[pl.ds(1, 1)], fv[pl.ds(2, 1)]
         grn, after, hat, inv, two, ratio, means, mods = near_out
-        two_all, mapped_all, qkv_all = far_out[:3]
+        two_all, mapped_all, qkv_all, gres_near = far_out[:4]
         everyone, part, mate, passed, landed, branch, slopes = scratch
         add_up = team_sum(m, p, flow, total, everyone)
+        for slot, to, sends, lands in (
+            (0, p.z + 1, p.z < p.R - 1, p.z > 0),
+            (1, p.z - 1, p.z > 0, p.z < p.R - 1),
+        ):
+            flow.post(far[2], gres_near.at[slot], {"rows": to}, when=sends, lands=lands)
         flow.gather_group(p, far[0], qkv_all)
         if m.even:
-            flow.gather_group(p, far[2], far_out[3])
+            flow.gather_group(p, far[3], far_out[4])
         text_line = LineGather(flow, p, far[1], mapped_all)
         half = m.S // 2
         pair = 2 * m.cs
@@ -1468,6 +1500,7 @@
         ((m.D, m.R, N, C), BF16),
         ((m.D, m.R) + mapped.shape, BF16),
         ((m.G,) + qkv_rows.shape, BF16),
+        ((2, N, C), BF16),
     ]
     if m.even:
         far_out.append(((m.G,) + proj_part.shape, BF16))
@@ -1487,15 +1520,15 @@
         near_out,
         far_out,
         scratch,
-        (m.T - 1) + 2 * (m.G - 1) + (1 + STRIPES) * gather_sems(m) + STRIPES * reduce_sems(m),
+        (m.T + 1) + 2 * (m.G - 1) + (1 + STRIPES) * gather_sems(m) + STRIPES * reduce_sems(m),
         4 + STRIPES,
     )
 
 
-def attention_kernel(m, two_all, gres, mapped_all, weight, proj, bias, key_keep):
+def attention_kernel(m, two_all, gres, gres_near, mapped_all, weight, proj, bias, key_keep):
     near = [bias, key_keep]
     loads = [two_all, weight, proj, mapped_all]
-    far = [gres]
+    far = [gres, gres_near]
     heads = m.HW // HEAD
     keys = m.pixels + m.texts
     scale = HEAD ** (-0.5)
@@ -1509,9 +1542,8 @@
         (two_far,) = far_out
         (gres_all, part, mate, passed, landed, qkv, k_all, v_all, k_t, v_t, dk, dv, o_t, dq_t, o_low, att, g_all, probs, dqkv,
          dtext, piece, words, gb_out, two_out) = scratch
-        line = LineGather(flow, p, far[0], gres_all)
-        line.start()
-        flow.keep(far[0], gres_all.at[p.c, p.z], now=True)
+        line = LineGatherOn(flow, p, far[0], gres_all)
+        line.start_from(far[1])
         two, w, proj, mapped = (load.get() for load in loads)
         red = LineReduce(flow, p, part, result, mate, passed, landed)
 
@@ -1555,7 +1587,7 @@
             o_t[d] += mm(jnp.where(in_row, v_t[d], 0).astype(BF16), low)
 
         pl.loop(0, D * heads // 2)(forward)
-        line.hop(1)
+        line.hop(2)
         pl.loop(D * heads // 2, D * heads)(forward)
 
         @pl.loop(0, D)
@@ -1575,7 +1607,6 @@
                 part[d, block, :, pl.ds(n * wide, wide)] = mm(mine, proj[n]).astype(BF16)
 
         red.start()
-        line.hop(2)
         red.early()
         steps = list(red.later())
         for number in range(3, R):
@@ -1606,13 +1637,11 @@
                 dq_t[d] += mm(jnp.where(in_row, k_t[d], 0).astype(BF16), grad_scores)
                 dk[d] += mm(grad_scores, q_h)
 
-        cut = D * heads // 2
+        cut = D * heads // 3
+        back(0, cut)
         steps[0]()
-        back(0, cut)
-        for step in steps[1:3]:
-            step()
         back(cut, D * heads)
-        for step in steps[3:]:
+        for step in steps[1:]:
             step()
         gb_out[...] = jnp.zeros_like(gb_out)
 
@@ -1704,7 +1733,7 @@
         [((D, pixels, C), BF16)],
         scratch,
         gather_sems(m) + reduce_sems(m),
-        2,
+        4,
     )
 
 
@@ -1855,14 +1884,6 @@
         cross = jnp.sum(scaled * norms[...], axis=1, keepdims=True)
         mine[...] = jnp.broadcast_to(cross, mine.shape)
         add_up = team_sum(m, p, flow, mine, everyone)
-        turned_g[...] = grn[...].T
-
-        def multiply_out(g, rows):
-            g_out[g] = mm(turned_g[rows], gb[...]).astype(BF16)
-
-        each_rows(G, m.FFS, multiply_out)
-        flow.keep(g_out, g_far)
-
         slope, x, in_w, qkv_parts = (load.get() for load in loads[4:8])
         step = m.cs
 
@@ -1940,7 +1961,17 @@
             pl.when(number < G - 1)(lambda: send_in(number).start())
 
         flow.keep(g_in.at[p.q], in_parts.at[p.q])
-        for act_of in line.later():
+        acts = list(line.later())
+        acts[0]()
+        turned_g[...] = grn[...].T
+
+        def multiply_out(g, rows):
+            g_out[g] = mm(turned_g[rows], gb[...]).astype(BF16)
+
+        each_rows(G, m.FFS, multiply_out)
+        flow.keep(g_out, g_far)
+
+        for act_of in acts[1:]:
             act_of()
         line.close()
         for number in range(G - 1):
@@ -2153,12 +2184,13 @@
         mod_all,
         qkv_rows.reshape(T * cs, 3 * HW),
         mapped_s,
+        grad_result,
         proj_part,
     )
     grn_out, after_res, two_hat, two_inv, _, ratio, means, mods, two_all, mapped = outs[:10]
-    qkv_full = outs[10].reshape(C, 3 * HW)
+    qkv_full, gres_near = outs[10].reshape(C, 3 * HW), outs[11]
     if even:
-        proj_s = outs[11]
+        proj_s = outs[12]
     else:
         proj_whole = lax.all_gather(proj_weight, AXES, axis=0, tiled=True)
         proj_s = lax.dynamic_slice_in_dim(proj_whole, head_slice * HW, HW, axis=0)[None]
@@ -2166,6 +2198,7 @@
         m,
         two_all.reshape(D, pixels, C),
         grad_result,
+        gres_near,
         mapped.reshape(T, D, texts, HW),
         qkv_full,
         proj_s,

time: 440 us -> 433 us (0.984)
  Pallas kernels: 435 us -> 429 us
    pallas_call x6, Pallas kernels: 417 us -> 410 us  [fused_kernel(): pl.pallas_call(kernel, out_shape=spots(near_out + far_out), in_specs=[pl....]
where the time goes in v6:
time: 433 us
  Pallas kernels  429 us (99%)
    pallas_call x6, Pallas kernels, fused_kernel(): pl.pallas_call(kernel, out_shape=spots(near_out + far_out), in_specs=[pl....  410 us
    pallas_call x4, Pallas kernels, local_kernel(): pl.pallas_call(kernel, out_shape=spots(results), in_specs=[numbers] * sca...  18.8 us

profile of v6, /device:TPU:0, one launch (start us, length us, event | category | flops | bytes accessed | tf_op | source)
XLA Modules:
  0.0 432.6 jit_solution(13469845136706829978)
XLA Ops:
  2.6 3.2 cut_weights.1
  5.8 88.4 %front.1 = (f32[8,768]{1,0:T(8,128)}, f32[8,128]{1,0:T(8,128)}, bf16[160,1280]{1,0:T(8,128)(2,1)}, bf16[160,192]{1,0:T(8,128)(2,1)}, f32[144,1536]{1,0:T(8,128)}...) custom-call(bf16[64,96]{1,0:T(8,128)(2,1)} %refs_0_.3, ...), custom_call_target="tpu_custom_call" | custom-call | tf_op jit(solution)/shard_map/front/pallas_call | solution.py:999
  94.2 88.2 %branch.1 = (bf16[1152,768]{1,0:T(8,128)(2,1)}, f32[144,1536]{1,0:T(8,128)}, f32[144,1536]{1,0:T(8,128)}, f32[144,1]{1,0:T(8,128)}, bf16[144,1536]{1,0:T(8,128)(...) custom-call(f32[8,768]{1,0:T(8,128)} %get-tuple-element.113.refs_0_,, ...), custom_call_target="tpu_custom_call" | custom-call | tf_op jit(solution)/shard_map/branch/pallas_call | solution.py:999
  182.4 61.1 %attention_block.1 = (f32[144,1536]{1,0:T(8,128)}, bf16[8,2,80,192]{3,2,1,0:T(8,128)(2,1)}, bf16[1536,576]{1,0:T(8,128)(2,1)}, bf16[4,192,384]{2,1,0:T(8,128)(2,...) custom-call(f32[1,576]{1,0:T(1,128)} %get-tuple-element.127.refs_0_, ...), custom_call_target="tpu_custom_call" | custom-call | tf_op jit(solution)/shard_map/attention_block/pallas_call | solution.py:999
  243.5 79.5 %attended.1 = (bf16[144,1536]{1,0:T(8,128)(2,1)}, f32[144,1536]{1,0:T(8,128)}, bf16[144,1536]{1,0:T(8,128)(2,1)}, f32[8,1536]{1,0:T(8,128)}, f32[8,1536]{1,0:T(8...) custom-call(f32[144,1]{1,0:T(8,128)} %get-tuple-element.125.refs_0_,, ...), custom_call_target="tpu_custom_call" | custom-call | tf_op jit(solution)/shard_map/attended/pallas_call | solution.py:999
  323.1 2.4 text_back.1
  325.5 62.0 %feed_forward_back.1 = (f32[144,1536]{1,0:T(8,128)}, bf16[4,384,768]{2,1,0:T(8,128)(2,1)}, f32[4,8,192]{2,1,0:T(8,128)}, bf16[4,384,192]{2,1,0:T(8,128)(2,1)}, b...) custom-call(f32[8,768]{1,0:T(8,128)} %get-tuple-element.113.refs_0_, ...), custom_call_target="tpu_custom_call" | custom-call | tf_op jit(solution)/shard_map/feed_forward_back/pallas_call | solution.py:999
  387.5 6.0 %convolve_back.1 = (f32[144,1536]{1,0:T(8,128)}, bf16[144,1536]{1,0:T(8,128)(2,1)}, f32[8,4,16,128]{3,2,1,0:T(8,128)}) custom-call(s32[1]{0:T(128)S(6)} %copy.43.b_ref, f32[144,1536]{1,0:T(8,128)} %get-tuple-element.156.g_ref, f32[144,1536]{1,0:T(8,128)} %get-tuple-element.157.hat_ref, f32[144,1]{1,0:T(8,128)} %get-tuple-element.158.inv_ref, ...), custom_call_target="tpu_custom_call" | custom-call | tf_op jit(solution)/shard_map/convolve_back/pallas_call | solution.py:662
  393.6 31.0 %tail.1 = (bf16[2,48,1536]{2,1,0:T(8,128)(2,1)}, f32[4,2,16,128]{3,2,1,0:T(8,128)}, bf16[8,48,768]{2,1,0:T(8,128)(2,1)}, bf16[8,48,192]{2,1,0:T(8,128)(2,1)}, bf16[4,192,1536]{2,1,0:T(8,128)(2,1)}) custom-call(bf16[4,384,768]{2,1,0:T(8,128)(2,1)} %get-tuple-element.154.refs_0_, bf16[4,384,192]{2,1,0:T(8,128)(2,1)} %get-tuple-element.155.refs_1_, ...), custom_call_target="tpu_custom_call" | custom-call | tf_op jit(solution)/shard_map/tail/pallas_call | solution.py:999
  424.6 0.0 copy-start
  424.6 7.2 %finish.1 = (f32[1,144,1536]{2,1,0:T(8,128)}, f32[48,6144]{1,0:T(8,128)}, f32[48,4608]{1,0:T(8,128)}, f32[40,1536]{1,0:T(8,128)}, f32[48,1536]{1,0:T(8,128)}, /*...) custom-call(s32[1]{0:T(128)S(6)} %copy.43.b_ref, ...), custom_call_target="tpu_custom_call" | custom-call | tf_op jit(solution)/shard_map/finish/pallas_call | solution.py:662
  431.8 0.0 copy-done
  431.8 0.8 copy.46
Async XLA Ops:
  424.6 7.2 %copy-start = (bf16[144,1536]{1,0:T(8,128)(2,1)S(1)}, bf16[144,1536]{1,0:T(8,128)(2,1)}, u32[]{:S(2)}) copy-start(bf16[144,1536]{1,0:T(8,128)(2,1)} %get-tuple-element.141) | copy-start | bytes 1327108

commit v7 on v6

--- a/solution.py
+++ b/solution.py
@@ -682,9 +682,9 @@
         self.FF = in_weight.shape[1]
         self.cs = conv_bias.shape[0]
         self.ms = map_weight.shape[0]
-        self.mp = -(-self.ms // 16) * 16
+        self.mp = -(-self.ms // 8) * 8
         self.slots = clip_tokens.shape[1]
-        self.sp = -(-self.slots // 16) * 16
+        self.sp = -(-self.slots // 8) * 8
         self.texts = self.R * self.slots
         self.HW = self.C // self.T
         self.even = self.G == self.R
@@ -791,7 +791,7 @@
 
 
 def conv_back_kernel(m, b_ref, grad_in, hat, inv, edges, masked, vec_grads, map_grad, qv_grads, modulate_grads):
-    def kernel(b_ref, g_ref, hat_ref, inv_ref, edges_ref, mid_ref, vec_ref, map_ref, qv_ref, gm_ref, grad, low, tiny, extended, vec):
+    def kernel(b_ref, g_ref, hat_ref, inv_ref, edges_ref, mid_ref, vec_ref, map_ref, qv_ref, gm_ref, grad, low, tiny_low, extended, vec, tiny):
         values = layer_back(g_ref[...], hat_ref[...], inv_ref[...])
         grad[...] = values
         low[...] = values.astype(BF16)
@@ -826,13 +826,18 @@
             side, at = pl.ds(s // half, 1), pl.ds(pair * (s % half), pair)
             tiny[t, g, pl.ds(13, 1), pl.ds(0, pair)] = qv_ref[side, at]
             tiny[t, g, pl.ds(14, 1), pl.ds(0, pair)] = gm_ref[side, at]
+        tiny_low[...] = tiny[...].astype(BF16)
 
     return local_kernel(
         "convolve_back",
         kernel,
         [b_ref, grad_in, hat, inv, edges, masked, vec_grads, map_grad, qv_grads, modulate_grads],
-        [((m.N, m.C), F32), ((m.N, m.C), BF16), ((m.T, m.G, 16, 128), F32)],
-        [pltpu.VMEM((m.N + 2 * EDGE, m.C), F32), pltpu.VMEM((VEC, m.C), F32)],
+        [((m.N, m.C), F32), ((m.N, m.C), BF16), ((m.T, m.G, 16, 128), BF16)],
+        [
+            pltpu.VMEM((m.N + 2 * EDGE, m.C), F32),
+            pltpu.VMEM((VEC, m.C), F32),
+            pltpu.VMEM((m.T, m.G, 16, 128), F32),
+        ],
         scalars=1,
     )
 
@@ -2058,9 +2063,9 @@
         flow.settle_kept()
         for d in range(m.D):
             for g in range(G):
-                total = tiny_in[d * m.R, g]
+                total = tiny_in[d * m.R, g].astype(F32)
                 for r in range(1, m.R):
-                    total = total + tiny_in[d * m.R + r, g]
+                    total = total + tiny_in[d * m.R + r, g].astype(F32)
                 tiny_own[g, d] = total
         flow.swap_group(p, tiny_own, tiny_all)
 
@@ -2083,7 +2088,7 @@
         [
             pltpu.VMEM((T, m.cs, m.FL), BF16),
             pltpu.VMEM((T, m.mp, m.HW), BF16),
-            pltpu.VMEM(tiny.shape, F32),
+            pltpu.VMEM(tiny.shape, BF16),
             pltpu.VMEM((G, m.D) + tiny.shape[2:], F32),
         ],
         2 + 3 * (T - 1) + 2 * (G - 1),

time: 433 us -> 430 us (level)
  no operation moved by 1% of the time
where the time goes in v7:
time: 430 us; the launch traced here: 429 us
  Pallas kernels  426 us (99%)
    pallas_call x6, Pallas kernels, fused_kernel(): pl.pallas_call(kernel, out_shape=spots(near_out + far_out), in_specs=[pl....  407 us
    pallas_call x4, Pallas kernels, local_kernel(): pl.pallas_call(kernel, out_shape=spots(results), in_specs=[numbers] * sca...  18.7 us

profile of v7, /device:TPU:0, one launch (start us, length us, event | category | flops | bytes accessed | tf_op | source)
XLA Modules:
  0.0 429.2 jit_solution(14147861888340746539)
XLA Ops:
  2.6 3.2 cut_weights.1
  5.8 86.4 %front.1 = (f32[8,768]{1,0:T(8,128)}, f32[8,128]{1,0:T(8,128)}, bf16[160,1280]{1,0:T(8,128)(2,1)}, bf16[160,192]{1,0:T(8,128)(2,1)}, f32[144,1536]{1,0:T(8,128)}...) custom-call(bf16[64,96]{1,0:T(8,128)(2,1)} %refs_0_.3, ...), custom_call_target="tpu_custom_call" | custom-call | tf_op jit(solution)/shard_map/front/pallas_call | solution.py:1004
  92.2 86.4 %branch.1 = (bf16[1152,768]{1,0:T(8,128)(2,1)}, f32[144,1536]{1,0:T(8,128)}, f32[144,1536]{1,0:T(8,128)}, f32[144,1]{1,0:T(8,128)}, bf16[144,1536]{1,0:T(8,128)(...) custom-call(f32[8,768]{1,0:T(8,128)} %get-tuple-element.113.refs_0_,, ...), custom_call_target="tpu_custom_call" | custom-call | tf_op jit(solution)/shard_map/branch/pallas_call | solution.py:1004
  178.6 61.0 %attention_block.1 = (f32[144,1536]{1,0:T(8,128)}, bf16[8,2,80,192]{3,2,1,0:T(8,128)(2,1)}, bf16[1536,576]{1,0:T(8,128)(2,1)}, bf16[4,192,384]{2,1,0:T(8,128)(2,...) custom-call(f32[1,576]{1,0:T(1,128)} %get-tuple-element.127.refs_0_, ...), custom_call_target="tpu_custom_call" | custom-call | tf_op jit(solution)/shard_map/attention_block/pallas_call | solution.py:1004
  239.7 79.6 %attended.1 = (bf16[144,1536]{1,0:T(8,128)(2,1)}, f32[144,1536]{1,0:T(8,128)}, bf16[144,1536]{1,0:T(8,128)(2,1)}, f32[8,1536]{1,0:T(8,128)}, f32[8,1536]{1,0:T(8...) custom-call(f32[144,1]{1,0:T(8,128)} %get-tuple-element.125.refs_0_,, ...), custom_call_target="tpu_custom_call" | custom-call | tf_op jit(solution)/shard_map/attended/pallas_call | solution.py:1004
  319.2 2.3 text_back.1
  321.6 62.1 %feed_forward_back.1 = (f32[144,1536]{1,0:T(8,128)}, bf16[4,384,768]{2,1,0:T(8,128)(2,1)}, f32[4,8,192]{2,1,0:T(8,128)}, bf16[4,320,192]{2,1,0:T(8,128)(2,1)}, b...) custom-call(f32[8,768]{1,0:T(8,128)} %get-tuple-element.113.refs_0_, ...), custom_call_target="tpu_custom_call" | custom-call | tf_op jit(solution)/shard_map/feed_forward_back/pallas_call | solution.py:1004
  383.7 6.0 %convolve_back.1 = (f32[144,1536]{1,0:T(8,128)}, bf16[144,1536]{1,0:T(8,128)(2,1)}, bf16[8,4,16,128]{3,2,1,0:T(8,128)(2,1)}) custom-call(s32[1]{0:T(128)S(6)} %copy.43.b_ref, f32[144,1536]{1,0:T(8,128)} %get-tuple-element.156.g_ref, f32[144,1536]{1,0:T(8,128)} %get-tuple-element.157.hat_ref, f32[144,1]{1,0:T(8,128)} %get-tuple-element.158.inv_ref, ...), custom_call_target="tpu_custom_call" | custom-call | tf_op jit(solution)/shard_map/convolve_back/pallas_call | solution.py:662
  389.6 31.6 %tail.1 = (bf16[2,48,1536]{2,1,0:T(8,128)(2,1)}, f32[4,2,16,128]{3,2,1,0:T(8,128)}, bf16[8,48,768]{2,1,0:T(8,128)(2,1)}, bf16[8,40,192]{2,1,0:T(8,128)(2,1)}, bf16[4,192,1536]{2,1,0:T(8,128)(2,1)}) custom-call(bf16[4,384,768]{2,1,0:T(8,128)(2,1)} %get-tuple-element.154.refs_0_, bf16[4,320,192]{2,1,0:T(8,128)(2,1)} %get-tuple-element.155.refs_1_, ...), custom_call_target="tpu_custom_call" | custom-call | tf_op jit(solution)/shard_map/tail/pallas_call | solution.py:1004
  421.2 0.0 copy-start
  421.2 7.2 %finish.1 = (f32[1,144,1536]{2,1,0:T(8,128)}, f32[48,6144]{1,0:T(8,128)}, f32[48,4608]{1,0:T(8,128)}, f32[40,1536]{1,0:T(8,128)}, f32[48,1536]{1,0:T(8,128)}, /*...) custom-call(s32[1]{0:T(128)S(6)} %copy.43.b_ref, ...), custom_call_target="tpu_custom_call" | custom-call | tf_op jit(solution)/shard_map/finish/pallas_call | solution.py:662
  428.4 0.0 copy-done
  428.4 0.8 copy.46
Async XLA Ops:
  421.2 7.2 %copy-start = (bf16[144,1536]{1,0:T(8,128)(2,1)S(1)}, bf16[144,1536]{1,0:T(8,128)(2,1)}, u32[]{:S(2)}) copy-start(bf16[144,1536]{1,0:T(8,128)(2,1)} %get-tuple-element.141) | copy-start | bytes 1327108
